TPU v7x, 32 devices: a whole 2x2x4 slice. The times are simulated.
32 devices in a mesh: slab: 4 (over z), row: 2 (over core), pole: 4 (over y, x).
Axes of the slice: x: 2, y: 2, z: 4, core: 2. Of those that a mesh axis runs over, the one named last changes fastest.
Arguments:
- local_green: bfloat16 [2, 4, 2, 4096, 1024], P(None, 'pole', None, ('slab', 'row')), may hold values from -6 to 6
- coupling: bfloat16 [2, 4, 2, 4096, 1024], P(None, 'pole', None, ('slab', 'row')), may hold values from -0.1875 to 0.1875
- block_mask: int32 [2, 4, 32, 8], P(None, 'pole', ('slab', 'row')), may hold values from 0 to 1, as said below
- state_in: bfloat16 [4, 2, 4096, 1024], P('pole', None, ('slab', 'row')), may hold values from -6 to 6
- pole_weight: float32 [2, 16], replicated, may hold values from -4 to 4
- pole_index: int32 [2, 4, 4], P(None, 'pole', 'slab'), may hold values from 0 to 15
Outputs:
- state_out: bfloat16 [4, 2, 4096, 1024], P('pole', None, ('slab', 'row'))
- density: float32 [2, 4096, 1024], P(None, ('slab', 'row'), 'pole')
Inputs may be any that keep to these rules, and one draw needn't show every extreme that they name: `block_mask`: every block row of every slab's mask has exactly 4 ones.
All inputs are finite; a program needn't handle non-finite values.
Results may differ from a plain program's by a relative error of at most 0.0095.
Values may be sent and summed in bfloat16 or wider, within the bound.
No kernel may reach another device: no remote copies, remote signals or barrier semaphores. Data moves between devices by JAX's collectives and lax.ppermute only.
A program may use at most 64 MiB of HBM per device.

v0:
```python
import jax
import jax.numpy as jnp
from jax import lax
from jax.sharding import PartitionSpec as P

BLK = 128
NBLK = 8
KEEP = 4
TICKS = 2
NTAB = 16


def from_behind(block, axis, distance):
    devices = range(lax.axis_size(axis))
    route = [(i - distance, i) for i in devices if i - distance in devices]
    return lax.ppermute(block, axis, route)


def left_rows(masked, piece):
    real_part = jnp.dot(masked[0], piece[0], preferred_element_type=jnp.float32) - jnp.dot(
        masked[1], piece[1], preferred_element_type=jnp.float32
    )
    imag_part = jnp.dot(masked[0], piece[1], preferred_element_type=jnp.float32) + jnp.dot(
        masked[1], piece[0], preferred_element_type=jnp.float32
    )
    return (real_part, imag_part)


def right_rows(half, piece):
    real_part = jnp.einsum(
        "ik,jk->ij", half[0], piece[0], preferred_element_type=jnp.float32
    ) - jnp.einsum("ik,jk->ij", half[1], piece[1], preferred_element_type=jnp.float32)
    imag_part = jnp.einsum(
        "ik,jk->ij", half[0], piece[1], preferred_element_type=jnp.float32
    ) + jnp.einsum("ik,jk->ij", half[1], piece[0], preferred_element_type=jnp.float32)
    return jnp.stack([real_part, imag_part])


def packed_rows_fold(half, pieces):
    values, positions = pieces
    count = values.shape[0]
    onehot = (positions[:, :, None] == jnp.arange(NBLK, dtype=jnp.int32)).astype(jnp.bfloat16)
    blocks = values.reshape(count, 2, KEEP, BLK)
    dense_rows = jnp.einsum("nkb,ncke->cnbe", onehot, blocks, preferred_element_type=jnp.float32)
    dense_rows = dense_rows.astype(jnp.bfloat16).reshape(2, count, NBLK * BLK)
    block = right_rows(half, dense_rows)
    return block


def body(local_green, coupling, block_mask, state_in, pole_weight, pole_index):
    rows = coupling.shape[3]
    width = coupling.shape[4]
    block_rows = block_mask.shape[2]
    state = state_in[0]
    density = None
    for tick in range(TICKS):
        mask_rows = block_mask[tick, 0]
        wide = jnp.broadcast_to(
            mask_rows.astype(jnp.bfloat16)[:, None, :, None], (block_rows, BLK, NBLK, BLK)
        )
        masked = coupling[tick, 0] * wide.reshape(rows, width)[None]
        incoming = from_behind(state, "slab", -1)
        real_part, imag_part = left_rows(
            masked, lax.all_gather(incoming, "row", axis=1, tiled=True)
        )
        half = jnp.stack([real_part, imag_part]).astype(jnp.bfloat16)
        order = jnp.argsort(1 - mask_rows, axis=1, stable=True)[:, :KEEP]
        blocks = masked.reshape(2, block_rows, BLK, NBLK, BLK)
        picked = jnp.take_along_axis(blocks, order[None, :, None, :, None], axis=3)
        packed = jnp.transpose(picked.reshape(2, rows, KEEP * BLK), (1, 0, 2))
        row_order = jnp.broadcast_to(order[:, None, :], (block_rows, BLK, KEEP)).reshape(rows, KEEP)
        sandwich = packed_rows_fold(
            half,
            (
                lax.all_gather(packed, "row", axis=0, tiled=True),
                lax.all_gather(row_order, "row", axis=0, tiled=True),
            ),
        )
        green = (local_green[tick, 0].astype(jnp.float32) + sandwich).astype(jnp.bfloat16)
        selector = (jnp.arange(NTAB, dtype=jnp.int32) == pole_index[tick, 0, 0]).astype(jnp.float32)
        weights = jnp.sum(pole_weight * selector[None, :], axis=1)
        green_real = green[0].astype(jnp.float32)
        green_imag = green[1].astype(jnp.float32)
        term = jnp.stack(
            [
                weights[0] * green_real - weights[1] * green_imag,
                weights[0] * green_imag + weights[1] * green_real,
            ]
        ).astype(jnp.bfloat16)
        term = lax.optimization_barrier(term).astype(jnp.float32)
        share = lax.psum_scatter(
            term.astype(jnp.bfloat16), "pole", scatter_dimension=2, tiled=True
        ).astype(jnp.float32)
        density = share if density is None else density + share
        state = green
    return (state[None], density)


def solution(mesh):
    placed = (
        P(None, "pole", None, ("slab", "row"), None),
        P(None, "pole", None, ("slab", "row"), None),
        P(None, "pole", ("slab", "row"), None),
        P("pole", None, ("slab", "row"), None),
        P(),
        P(None, "pole", "slab"),
    )
    return jax.shard_map(
        body,
        mesh=mesh,
        in_specs=placed,
        out_specs=(P("pole", None, ("slab", "row"), None), P(None, ("slab", "row"), "pole")),
        check_vma=False,
    )
```

profile of v0, /device:TPU:0, one launch (start us, length us, event | category | flops | bytes accessed | tf_op | source)
XLA Modules:
  0.0 246.8 jit_solution(9731973650147956543)
XLA Ops:
  7.2 1.3 collective-permute-start
  10.2 2.7 %fusion.64 = (bf16[1,1,2,512,1024]{4,3,2,1,0:T(8,128)(2,1)S(1)}, bf16[1,1,2,512,1024]{4,3,2,1,0:T(8,128)(2,1)S(1)}) fusion(bf16[2,1,2,512,1024]{4,3,2,1,0:T(8,128)(2,1)} %param.9), kind=kLoop, calls=%fused_computation.111 | loop fusion | bytes 8388608 | tf_op jit(solution)/shard_map/slice | solution.py:61
  14.1 1.9 copy_multiply_fusion
  16.0 2.3 gather_fusion
  18.5 0.8 copy.31
  19.4 1.2 reshape.144
  20.7 37.5 %collective-permute-done = bf16[2,512,1024]{2,1,0:T(8,128)(2,1)} collective-permute-done((bf16[2,512,1024]{2,1,0:T(8,128)(2,1)}, bf16[2,512,1024]{2,1,0:T(8,128)(2,1)}, u32[]{:S(2)}, u32[]{:S(2)}) %collective-permute-start) | collective-permute-done | bytes 2097184 | tf_op jit(solution)/shard_map/ppermute | solution.py:16
  60.9 1.2 reshape.147
  62.1 2.2 all_gather.20
  65.3 2.2 copy-done
  67.5 1.7 bitcast_multiply_fusion.1
  69.2 4.5 %reshape.145 = bf16[1024,2,4,128]{3,2,1,0:T(4,128)(2,1)} reshape(bf16[1024,2,512]{2,1,0:T(2,128)(2,1)} %all-gather.7.cloned.1.call-done) | data formatting | bytes 4194304 | tf_op jit(solution)/shard_map/reshape | solution.py:43
  73.8 4.6 %convert_bitcast_fusion.3 = bf16[2,1024,8,128]{3,2,0,1:T(8,128)(2,1)S(1)} fusion(bf16[1024,2,4,128]{3,2,1,0:T(4,128)(2,1)} %reshape.145, s32[1024,4]{1,0:T(8,128)S(1)} %all_gather.20), kind=kOutput, calls=%fused_computation.11 | convolution fusion | flops 18907136 | bytes 6307840 | tf_op jit(solution)/shard_map/nkb,ncke->cnbe/dot_general | solution.py:44
  78.4 2.3 fusion.65
  80.7 3.0 %fusion.36 = f32[512,1024]{1,0:T(8,128)S(1)} fusion(bf16[2,1024,1024]{2,1,0:T(8,128)(2,1)} %all-gather.5.cloned.1.call-done, bf16[2,512,1024]{2,1,0:T(8,128)(2,1)S(1)} %get-tuple-element.14), kind=kOutput, calls=%fused_computation.67 | convolution fusion | flops 1073741824 | bytes 5242880 | tf_op jit(solution)/shard_map/dot_general | solution.py:20
  83.7 1.3 subtract_convert_fusion.1
  85.3 1.3 fusion.21
  86.6 1.3 fusion.33
  87.9 1.3 add_convert_fusion.1
  89.2 1.3 fusion.23
  90.7 1.3 add_bitcast_fusion
  92.0 1.3 subtract_bitcast_fusion
  93.3 0.9 copy-done.1
  94.2 0.8 fusion.4
  95.1 1.3 collective-permute-start.1
  96.5 48.3 %collective-permute-done.1 = bf16[2,512,1024]{2,1,0:T(8,128)(2,1)} collective-permute-done((bf16[2,512,1024]{2,1,0:T(8,128)(2,1)S(1)}, bf16[2,512,1024]{2,1,0:T(8,128)(2,1)}, u32[]{:S(2)}, u32[]{:S(2)}) %collective-permute-start.1) | collective-permute-done | bytes 2097184 | tf_op jit(solution)/shard_map/ppermute | solution.py:16
  144.9 2.2 all_gather.23
  149.7 4.4 %reshape.148 = bf16[1024,2,4,128]{3,2,1,0:T(4,128)(2,1)} reshape(bf16[1024,2,512]{2,1,0:T(2,128)(2,1)} %all-gather.11.cloned.1.call-done) | data formatting | bytes 4194304 | tf_op jit(solution)/shard_map/reshape | solution.py:43
  154.2 6.3 %convert_bitcast_fusion.2 = bf16[2,1024,8,128]{3,2,0,1:T(8,128)(2,1)} fusion(bf16[1024,2,4,128]{3,2,1,0:T(4,128)(2,1)} %reshape.148, s32[1024,4]{1,0:T(8,128)S(1)} %all_gather.23), kind=kOutput, calls=%fused_computation.10 | convolution fusion | flops 18907136 | bytes 6307840 | tf_op jit(solution)/shard_map/nkb,ncke->cnbe/dot_general | solution.py:44
  160.5 2.0 fusion.6
  162.4 1.5 pad_maximum_fusion
  164.0 4.6 %fusion.63 = (bf16[1,1024,8,128]{3,2,0,1:T(8,128)(2,1)}, bf16[1,1024,8,128]{3,2,0,1:T(8,128)(2,1)}) fusion(bf16[2,1024,8,128]{3,2,0,1:T(8,128)(2,1)} %convert_bitcast_fusion.2), kind=kLoop, calls=%fused_computation.110 | loop fusion | bytes 8388608 | tf_op jit(solution)/shard_map/slice | solution.py:31
  168.6 3.0 %fusion.37 = f32[512,1024]{1,0:T(8,128)S(1)} fusion(bf16[2,1024,1024]{2,1,0:T(8,128)(2,1)} %all-gather.9.cloned.1.call-done, bf16[2,512,1024]{2,1,0:T(8,128)(2,1)S(1)} %copy-done.4), kind=kOutput, calls=%fused_computation.68 | convolution fusion | flops 1073741824 | bytes 5242880 | tf_op jit(solution)/shard_map/dot_general | solution.py:23
  171.8 1.3 add_convert_fusion
  173.4 1.3 fusion.15
  174.6 1.3 fusion.40
  175.9 1.3 subtract_convert_fusion
  177.2 1.3 fusion.13
  178.8 1.3 fusion.53
  180.1 1.3 fusion.56
  181.4 0.9 copy-done.2
  182.4 0.8 fusion.3
  183.2 2.0 fusion.10
  185.2 1.5 pad_maximum_fusion.1
  186.7 4.3 %fusion.1 = bf16[1,2,512,1024]{3,2,1,0:T(8,128)(2,1)} fusion(f32[1,1,512,1024]{3,2,1,0:T(8,128)} %bitcast.209, f32[1,1,512,1024]{3,2,1,0:T(8,128)S(1)} %bitcast.207, bf16[2,1,2,512,1024]{4,3,2,1,0:T(8,128)(2,1)} %param.8), kind=kLoop, calls=%fused_computation.5 | loop fusion | flops 4194304 | bytes 8388608 | tf_op jit(solution)/shard_map/convert_element_type | solution.py:79
  191.0 8.7 %reduce-scatter.3.cloned.1.call-done = bf16[2,512,256]{2,1,0:T(8,128)(2,1)} async-done(((bf16[2,512,1024]{2,1,0:T(8,128)(2,1)}), bf16[2,512,256]{2,1,0:T(8,128)(2,1)}) %reduce-scatter.3.cloned.1.call-update) | async-done | bytes 524304 | tf_op jit(solution)/shard_map/reduce_scatter | solution.py:91
  199.7 38.0 %reduce-scatter.5.cloned.1.call-done = bf16[2,512,256]{2,1,0:T(8,128)(2,1)} async-done(((bf16[2,512,1024]{2,1,0:T(8,128)(2,1)}), bf16[2,512,256]{2,1,0:T(8,128)(2,1)}) %reduce-scatter.5.cloned.1.call-update) | async-done | bytes 524304 | tf_op jit(solution)/shard_map/reduce_scatter | solution.py:91
  237.7 2.3 convert_add_fusion
  (72 shorter events, 11.1 us)
Async XLA Ops:
  7.2 62.1 %all-gather.7.cloned.1.call-start = ((), (), s32[]{:S(2)}) async-start(), calls=%async_computation.3 | async-start | bytes 3145728 | tf_op jit(solution)/shard_map/all_gather | solution.py:75
  7.2 50.9 %collective-permute-start = (bf16[2,512,1024]{2,1,0:T(8,128)(2,1)}, bf16[2,512,1024]{2,1,0:T(8,128)(2,1)}, u32[]{:S(2)}, u32[]{:S(2)}) collective-permute-start(bf16[2,512,1024]{2,1,0:T(8,128)(2,1)} %bitcast.226), channel_id=1, source_target_pairs={{8,0},{16,8},{24,16},{9,1},{17,9},{25,17},{10,2},{18,10},{26,18},{... | collective-permute-start | bytes 6291464 | tf_op jit(solution)/shard_map/ppermute | solution.py:16
  20.6 60.1 %all-gather.5.cloned.1.call-start = ((), (), s32[]{:S(2)}) async-start(), calls=%async_computation.2 | async-start | bytes 6291456 | tf_op jit(solution)/shard_map/all_gather | solution.py:64
  58.1 91.6 %all-gather.11.cloned.1.call-start = ((), (), s32[]{:S(2)}) async-start(), calls=%async_computation.5 | async-start | bytes 3145728 | tf_op jit(solution)/shard_map/all_gather | solution.py:75
  64.7 2.8 %copy-start = (bf16[2,1,2,512,1024]{4,3,2,1,0:T(8,128)(2,1)S(1)}, bf16[2,1,2,512,1024]{4,3,2,1,0:T(8,128)(2,1)}, u32[]{:S(2)}) copy-start(bf16[2,1,2,512,1024]{4,3,2,1,0:T(8,128)(2,1)} %param.9) | copy-start | bytes 12582916
  80.7 3.0 %copy-start.11 = (bf16[2,1024,1024]{2,1,0:T(8,128)(2,1)S(1)}, bf16[2,1024,1024]{2,1,0:T(8,128)(2,1)}, u32[]{:S(2)}) copy-start(bf16[2,1024,1024]{2,1,0:T(8,128)(2,1)} %all-gather.5.cloned.1.call-done) | copy-start | bytes 12582916
  83.7 1.6 copy-start.8
  89.2 1.6 copy-start.6
  92.0 2.2 copy-start.1
  95.1 49.7 %collective-permute-start.1 = (bf16[2,512,1024]{2,1,0:T(8,128)(2,1)S(1)}, bf16[2,512,1024]{2,1,0:T(8,128)(2,1)}, u32[]{:S(2)}, u32[]{:S(2)}) collective-permute-start(bf16[2,512,1024]{2,1,0:T(8,128)(2,1)S(1)} %fusion.4), channel_id=1, source_target_pairs={{8,0},{16,8},{24,16},{9,1},{17,9},{25,17},{10,2},{18,10},{26,18},{... | collective-permute-start | bytes 6291464 | tf_op jit(solution)/shard_map/ppermute | solution.py:16
  96.4 50.7 %copy-start.9 = (s32[2,1,1]{0,2,1:T(1,128)S(1)}, s32[2,1,1]{0,2,1:T(1,128)}, u32[]{:S(2)}) copy-start(s32[2,1,1]{0,2,1:T(1,128)} %param.13) | copy-start | bytes 28
  96.4 52.5 %copy-start.10 = (f32[2,16]{1,0:T(2,128)S(1)}, f32[2,16]{1,0:T(2,128)}, u32[]{:S(2)}) copy-start(f32[2,16]{1,0:T(2,128)} %param.12) | copy-start | bytes 388
  96.4 72.2 %all-gather.9.cloned.1.call-start = ((), (), s32[]{:S(2)}) async-start(), calls=%async_computation.4 | async-start | bytes 6291456 | tf_op jit(solution)/shard_map/all_gather | solution.py:64
  144.8 54.8 %reduce-scatter.3.cloned.1.call-start = ((), (), s32[]{:S(2)}) async-start(), calls=%async_computation.6 | async-start | bytes 2621440 | tf_op jit(solution)/shard_map/reduce_scatter | solution.py:91
  164.0 4.6 %copy-start.4 = (bf16[2,512,1024]{2,1,0:T(8,128)(2,1)S(1)}, bf16[2,512,1024]{2,1,0:T(8,128)(2,1)}, u32[]{:S(2)}) copy-start(bf16[2,512,1024]{2,1,0:T(8,128)(2,1)} %get-tuple-element.13) | copy-start | bytes 6291460
  164.0 73.7 %reduce-scatter.5.cloned.1.call-start = ((), (), s32[]{:S(2)}) async-start(), calls=%async_computation.7 | async-start | bytes 2621440 | tf_op jit(solution)/shard_map/reduce_scatter | solution.py:91
  168.6 3.1 %copy-start.12 = (bf16[2,1024,1024]{2,1,0:T(8,128)(2,1)S(1)}, bf16[2,1024,1024]{2,1,0:T(8,128)(2,1)}, u32[]{:S(2)}) copy-start(bf16[2,1024,1024]{2,1,0:T(8,128)(2,1)} %all-gather.9.cloned.1.call-done) | copy-start | bytes 12582916
  171.8 1.6 copy-start.7
  177.2 1.6 copy-start.5
  180.1 2.3 copy-start.2
  181.4 1.8 copy-start.3
Sparse Core Ops, SparseCore 0:
  20.7 15.6 all-gather.6
  58.3 14.0 all-gather.4
  96.5 14.3 all-gather.10
  144.9 13.9 all-gather.8
  164.1 35.5 reduce-scatter.2
  202.5 35.1 reduce-scatter.4
where the time goes:
time: 248 us; the launch traced here: 247 us
  waiting for transfers between devices  133 us (54%)
  local copies, waits for them, and re-layouts  35.1 us (14%)
  matrix products  34.8 us (14%)
  other arithmetic  22.6 us (9%)
  between operations  14.5 us (6%)
  blocking collectives  4.36 us (2%)
  starting transfers between devices  2.82 us (1%)
    ppermute x2, waiting for transfers between devices, from_behind(): return lax.ppermute(block, axis, route)  85.8 us
    reduce_scatter x2, waiting for transfers between devices, body(): lax.psum_scatter(term.astype(jnp.bfloat16), 'pole', scatter_dimension=2,...  46.7 us
    dot_general x2, matrix products, packed_rows_fold(): jnp.einsum('nkb,ncke->cnbe', onehot, blocks, preferred_element_type=jnp.f...  10.9 us
    reshape x2, local copies, waits for them, and re-layouts, packed_rows_fold(): blocks = values.reshape(count, 2, KEEP, BLK)  8.98 us
    slice x2, local copies, waits for them, and re-layouts, right_rows(): piece[0]  6.88 us
    unnamed x28, local copies, waits for them, and re-layouts  6.71 us
    convert_element_type x3, other arithmetic, body(): (local_green[tick, 0].astype(jnp.float32) + sandwich).astype(jnp.bfloat16)  5.93 us
  transfers between devices with their start and end apart: 8, of which 4 were waited for; matrix products, arithmetic and copies ran while one was open for 29% of the time, Pallas kernels for 0%

commit v1 on v0

v1 whole, which is shorter than its diff:
```python
import functools

import jax
import jax.numpy as jnp
from jax import lax
from jax.experimental import pallas as pl
from jax.experimental.pallas import tpu as pltpu
from jax.sharding import PartitionSpec as P


BF16 = jnp.bfloat16
F32 = jnp.float32

LIMIT = pltpu.CompilerParams(vmem_limit_bytes=20 << 20)


def from_behind(block, axis):
    devices = range(lax.axis_size(axis))
    return lax.ppermute(block, axis, [(i + 1, i) for i in devices if i + 1 in devices])


def flip(block, axis, bit):
    return lax.ppermute(block, axis, [(i, i ^ bit) for i in range(lax.axis_size(axis))])


def row_pieces(block):
    rows = block.shape[1]
    count = lax.axis_size("row")
    if count == 1:
        return [block], [0]
    if count == 2:
        here = lax.axis_index("row")
        there = flip(block, "row", 1)
        return [block, there], [here * rows, (1 - here) * rows]
    return [lax.all_gather(block, "row", axis=1, tiled=True)], [0]


def mask_body(mask_ref, coupling_ref, out_ref, *, tick, per_tile):
    tile = pl.program_id(0)
    blocks = mask_ref.shape[3]
    wide = coupling_ref.shape[4] // blocks
    high = coupling_ref.shape[3] // per_tile
    for part in range(per_tile):
        rows = slice(part * high, (part + 1) * high)
        for col in range(blocks):
            cols = slice(col * wide, (col + 1) * wide)
            keep = mask_ref[tick, 0, tile * per_tile + part, col] != 0
            block = coupling_ref[0, 0, :, rows, cols]
            out_ref[:, rows, cols] = jnp.where(keep, block, jnp.zeros_like(block))


def masked_factor(block_mask, coupling, tick):
    rows, width = coupling.shape[3:]
    block_rows = block_mask.shape[2]
    per_tile = 2 if block_rows % 2 == 0 else 1
    tile = rows // block_rows * per_tile
    return pl.pallas_call(
        functools.partial(mask_body, tick=tick, per_tile=per_tile),
        grid_spec=pltpu.PrefetchScalarGridSpec(
            num_scalar_prefetch=1,
            grid=(rows // tile,),
            in_specs=[pl.BlockSpec((1, 1, 2, tile, width), lambda i, m: (tick, 0, 0, i, 0))],
            out_specs=pl.BlockSpec((2, tile, width), lambda i, m: (0, i, 0)),
        ),
        out_shape=jax.ShapeDtypeStruct((2, rows, width), BF16),
        compiler_params=LIMIT,
    )(block_mask, coupling)


def dot(a, b):
    return jnp.dot(a, b, preferred_element_type=F32)


def dot_t(a, b):
    return lax.dot_general(a, b, (((1,), (1,)), ((), ())), preferred_element_type=F32)


def fold_body(*refs, pieces, tick, first, last, start_of_term):
    offs, pidx, pw, here = refs[:4]
    refs = refs[4:]
    own = refs[0]
    factor = refs[1 : 1 + pieces]
    behind = refs[1 + pieces : 1 + 2 * pieces]
    before = refs[1 + 2 * pieces]
    outs = refs[2 + 2 * pieces : -3]
    right, low, high = refs[-3:]
    span = behind[0].shape[2]

    @pl.when(pl.program_id(0) == 0)
    def _():
        for k in range(pieces):
            size = behind[k].shape[1]
            at = pl.ds(pl.multiple_of(offs[k], size), size)
            right[at, :span] = behind[k][0]
            right[at, span:] = behind[k][1]
            low[at, :span] = factor[k][0]
            low[at, span:] = -factor[k][1]
            high[at, :span] = factor[k][1]
            high[at, span:] = factor[k][0]

    a = dot(own[0], right[...])
    b = dot(own[1], right[...])
    half = jnp.concatenate([a[:, :span] - b[:, span:], a[:, span:] + b[:, :span]], axis=1).astype(BF16)
    if first:
        old = (before[0, 0, 0].astype(F32), before[0, 0, 1].astype(F32))
    else:
        old = (before[0], before[1])
    real = old[0] + dot_t(half, low[...])
    imag = old[1] + dot_t(half, high[...])
    if not last:
        outs[0][0] = real
        outs[0][1] = imag
        return
    real = real.astype(BF16)
    imag = imag.astype(BF16)
    start = 0
    for out in outs[:start_of_term]:
        cols = slice(start, start + out.shape[2])
        out[0] = real[:, cols]
        out[1] = imag[:, cols]
        start += out.shape[2]
    if len(outs) > start_of_term:
        write_term(real, imag, pidx, pw, here, tick, outs[start_of_term:])


def write_term(real, imag, pidx, pw, here, tick, outs):
    real = real.astype(F32)
    imag = imag.astype(F32)
    w0 = pw[0, pidx[tick, 0, 0]]
    w1 = pw[1, pidx[tick, 0, 0]]
    term_real = (w0 * real - w1 * imag).astype(BF16)
    term_imag = (w0 * imag + w1 * real).astype(BF16)
    if len(outs) == 1:
        outs[0][0] = term_real
        outs[0][1] = term_imag
        return
    real_send, real_keep, imag_send, imag_keep = outs
    quarter = term_real.shape[1] // 4
    first_major = here[0] // 2 == 0
    first_minor = here[0] % 2 == 0
    lower, upper = term_real[:, : 2 * quarter], term_real[:, 2 * quarter :]
    real_send[...] = jnp.where(first_major, upper, lower)
    real_keep[...] = jnp.where(first_major, lower, upper)
    for pair in range(2):
        at = slice(pair * quarter, (pair + 1) * quarter)
        even = term_imag[:, 2 * pair * quarter : (2 * pair + 1) * quarter]
        odd = term_imag[:, (2 * pair + 1) * quarter : (2 * pair + 2) * quarter]
        imag_send[:, at] = jnp.where(first_minor, odd, even)
        imag_keep[:, at] = jnp.where(first_minor, even, odd)


def term_outs(rows, width, tile):
    if lax.axis_size("pole") == 4:
        spec = pl.BlockSpec((tile, width // 2), lambda i, *_: (i, 0))
        return [spec] * 4, [jax.ShapeDtypeStruct((rows, width // 2), BF16)] * 4
    spec = pl.BlockSpec((2, tile, width), lambda i, *_: (0, i, 0))
    return [spec], [jax.ShapeDtypeStruct((2, rows, width), BF16)]


def fold(scalars, own, factor, behind, before, tick, chunk, first, last, widths, with_term):
    rows, width = own.shape[1:]
    span = behind[0].shape[2]
    tile = min(rows, 256)
    pieces = len(behind)
    flat = pl.BlockSpec((2, tile, width), lambda i, *_: (0, i, 0))
    once = pl.Buffered(1)
    in_specs = [flat]
    for piece in factor:
        in_specs.append(pl.BlockSpec((2, piece.shape[1], span), lambda i, *_: (0, 0, chunk), pipeline_mode=once))
    for piece in behind:
        in_specs.append(pl.BlockSpec(memory_space=pltpu.VMEM))
    if first:
        in_specs.append(pl.BlockSpec((1, 1, 2, tile, width), lambda i, *_: (tick, 0, 0, i, 0)))
    else:
        in_specs.append(flat)
    if last:
        out_specs = [pl.BlockSpec((2, tile, w), lambda i, *_: (0, i, 0)) for w in widths]
        out_shape = [jax.ShapeDtypeStruct((2, rows, w), BF16) for w in widths]
        if with_term:
            more = term_outs(rows, width, tile)
            out_specs += more[0]
            out_shape += more[1]
    else:
        out_specs = [flat]
        out_shape = [jax.ShapeDtypeStruct((2, rows, width), F32)]
    aliases = {} if first or last else {len(scalars) + 1 + 2 * pieces: 0}
    return pl.pallas_call(
        functools.partial(
            fold_body, pieces=pieces, tick=tick, first=first, last=last, start_of_term=len(widths)
        ),
        grid_spec=pltpu.PrefetchScalarGridSpec(
            num_scalar_prefetch=len(scalars),
            grid=(rows // tile,),
            in_specs=in_specs,
            out_specs=out_specs,
            scratch_shapes=[pltpu.VMEM((width, 2 * span), BF16)] * 3,
        ),
        out_shape=out_shape,
        input_output_aliases=aliases,
        compiler_params=LIMIT,
    )(*scalars, own, *factor, *behind, before)


def term_body(pidx, pw, here, *refs, tick, count):
    real = jnp.concatenate([ref[0] for ref in refs[:count]], axis=1)
    imag = jnp.concatenate([ref[1] for ref in refs[:count]], axis=1)
    write_term(real, imag, pidx, pw, here, tick, refs[count:])


def weigh(scalars, state, tick):
    rows = state[0].shape[1]
    tile = min(rows, 256)
    out_specs, out_shape = term_outs(rows, sum(piece.shape[2] for piece in state), tile)
    return pl.pallas_call(
        functools.partial(term_body, tick=tick, count=len(state)),
        grid_spec=pltpu.PrefetchScalarGridSpec(
            num_scalar_prefetch=3,
            grid=(rows // tile,),
            in_specs=[pl.BlockSpec((2, tile, p.shape[2]), lambda i, *_: (0, i, 0)) for p in state],
            out_specs=out_specs,
        ),
        out_shape=out_shape,
        compiler_params=LIMIT,
    )(*scalars[1:], *state)


def cut_body(src, out):
    out[...] = src[0]


def first_piece(state, span):
    rows = state.shape[2]
    return pl.pallas_call(
        cut_body,
        grid=(1,),
        in_specs=[pl.BlockSpec((1, 2, rows, span), lambda i: (0, 0, 0, 0))],
        out_specs=pl.BlockSpec((2, rows, span), lambda i: (0, 0, 0)),
        out_shape=jax.ShapeDtypeStruct((2, rows, span), BF16),
        compiler_params=LIMIT,
        name="cut",
    )(state)


def pass_on_body(here, real_keep, real_got, imag_keep, imag_got, real_send, imag_send):
    real_send[...] = (real_keep[...].astype(F32) + real_got[...].astype(F32)).astype(BF16)
    imag_send[...] = (imag_keep[...].astype(F32) + imag_got[...].astype(F32)).astype(BF16)


def retain_body(here, real_keep, real_got, imag_keep, imag_got, *refs):
    out = refs[-1]
    real = real_keep[...].astype(F32) + real_got[...].astype(F32)
    imag = imag_keep[...].astype(F32) + imag_got[...].astype(F32)
    if len(refs) == 2:
        real = refs[0][0] + real
        imag = refs[0][1] + imag
    out[0] = real
    out[1] = imag


def close_body(base, real_last, imag_last, out):
    out[0] = base[0] + real_last[...].astype(F32)
    out[1] = base[1] + imag_last[...].astype(F32)


def scatter_sum(parts, before, here):
    if len(parts) == 1:
        share = lax.psum_scatter(parts[0], "pole", scatter_dimension=2, tiled=True).astype(F32)
        return share if before is None else before + share
    real_out, real_keep, imag_out, imag_keep = parts
    rows, half = real_out.shape
    quarter = half // 2
    tile = min(rows, 256)
    real_got = flip(real_out, "pole", 2)
    imag_got = flip(imag_out, "pole", 1)
    fields = (real_keep, real_got, imag_keep, imag_got)
    block = (tile, quarter)

    def picked(mine):
        real_at = pl.BlockSpec(block, lambda i, h: (i, h[0] % 2 if mine else 1 - h[0] % 2))
        imag_at = pl.BlockSpec(block, lambda i, h: (i, h[0] // 2 if mine else 1 - h[0] // 2))
        return [real_at, real_at, imag_at, imag_at]

    flat = pl.BlockSpec(block, lambda i, *_: (i, 0))
    both = pl.BlockSpec((2, tile, quarter), lambda i, *_: (0, i, 0))
    real_send, imag_send = pl.pallas_call(
        pass_on_body,
        grid_spec=pltpu.PrefetchScalarGridSpec(
            num_scalar_prefetch=1, grid=(rows // tile,), in_specs=picked(False), out_specs=[flat, flat]
        ),
        out_shape=[jax.ShapeDtypeStruct((rows, quarter), BF16)] * 2,
        compiler_params=LIMIT,
    )(here, *fields)
    real_last = flip(real_send, "pole", 1)
    imag_last = flip(imag_send, "pole", 2)
    extra = [] if before is None else [before]
    shape = jax.ShapeDtypeStruct((2, rows, quarter), F32)
    base = pl.pallas_call(
        retain_body,
        grid_spec=pltpu.PrefetchScalarGridSpec(
            num_scalar_prefetch=1, grid=(rows // tile,), in_specs=picked(True) + [both] * len(extra), out_specs=both
        ),
        out_shape=shape,
        compiler_params=LIMIT,
    )(here, *fields, *extra)
    return pl.pallas_call(
        close_body,
        grid=(rows // tile,),
        in_specs=[both, flat, flat],
        out_specs=both,
        out_shape=shape,
        compiler_params=LIMIT,
    )(base, real_last, imag_last)


def body(local_green, coupling, block_mask, state_in, pole_weight, pole_index):
    ticks = coupling.shape[0]
    width = coupling.shape[4]
    span = min(128, width)
    chunks = width // span
    state = [first_piece(state_in, span)]
    state += [state_in[0, :, :, c * span : (c + 1) * span] for c in range(1, chunks)]
    here = jnp.reshape(lax.axis_index("pole").astype(jnp.int32), (1,))
    factors = []
    density = None
    for tick in range(ticks):
        own = masked_factor(block_mask, coupling, tick)
        factors.append((own, *row_pieces(own)))
    for tick in range(ticks):
        incoming = []
        for c in range(chunks):
            incoming.append(from_behind(state[c], "slab"))
        own, factor, offsets = factors[tick]
        scalars = (jnp.stack([jnp.int32(o) for o in offsets]), pole_index, pole_weight, here)
        before = local_green
        last_tick = tick == ticks - 1
        widths = [width] if last_tick else [span] * chunks
        for c in range(chunks):
            behind, _ = row_pieces(incoming[c])
            last = c == chunks - 1
            outs = fold(
                scalars, own, factor, behind, before, tick, c, c == 0, last, widths if last else [], last_tick
            )
            before = outs[0]
        state = outs[: len(widths)]
        parts = outs[len(widths) :] or weigh(scalars, state, tick)
        density = scatter_sum(parts, density, here)
    return (state[0][None], density)


def solution(mesh):
    placed = (
        P(None, "pole", None, ("slab", "row"), None),
        P(None, "pole", None, ("slab", "row"), None),
        P(None, "pole", ("slab", "row"), None),
        P("pole", None, ("slab", "row"), None),
        P(),
        P(None, "pole", "slab"),
    )
    return jax.shard_map(
        body,
        mesh=mesh,
        in_specs=placed,
        out_specs=(P("pole", None, ("slab", "row"), None), P(None, ("slab", "row"), "pole")),
        check_vma=False,
    )
```

time: 248 us -> 216 us (0.87)
  Pallas kernels: 0 us -> 70.8 us
  waiting for transfers between devices: 133 us -> 95.5 us
  matrix products: 34.8 us -> 0 us
  starting transfers between devices: 2.82 us -> 33.3 us
  other arithmetic: 22.6 us -> 0.07 us
  local copies, waits for them, and re-layouts: 35.1 us -> 14.1 us
  between operations: 14.5 us -> 1.18 us
  blocking collectives: 4.36 us -> 0 us
    pallas_call x0 -> x26, Pallas kernels: none -> 70.8 us  [the longest x16 62.7 us: fold(): pl.pallas_call(functools.partial(fold_body, pieces=pieces, tick=tick, fir...]
    reduce_scatter x2 -> x0, waiting for transfers between devices: 46.7 us -> none  [body(): lax.psum_scatter(term.astype(jnp.bfloat16), 'pole', scatter_dimension=2,...]
    dot_general x18 -> x0, matrix products: 34.8 us -> none  [the longest x2 10.9 us: packed_rows_fold(): jnp.einsum('nkb,ncke->cnbe', onehot, blocks, preferred_element_type=jnp.f...]
    ppermute x2 -> x42, starting transfers between devices: 2.58 us -> 33.3 us  [the longest x16 20.6 us: from_behind(): lax.ppermute(block, axis, [(i + 1, i) for i in devices if i + 1 in devices])]
    reshape x4 -> x0, local copies, waits for them, and re-layouts: 11.4 us -> none  [the longest x2 8.98 us: packed_rows_fold(): blocks = values.reshape(count, 2, KEEP, BLK)]
    slice x9 -> x0, local copies, waits for them, and re-layouts: 11 us -> none  [the longest x2 6.88 us: right_rows(): piece[0]]
    ppermute x2 -> x42, waiting for transfers between devices: 85.8 us -> 95.5 us  [the longest x16 79 us: from_behind(): lax.ppermute(block, axis, [(i + 1, i) for i in devices if i + 1 in devices])]
    convert_element_type x5 -> x0, other arithmetic: 7.15 us -> none  [the longest x3 5.93 us: body(): (local_green[tick, 0].astype(jnp.float32) + sandwich).astype(jnp.bfloat16)]
  transfers between devices with their start and end apart: 8 -> 42, of which waited for: 4 -> 20; matrix products, arithmetic and copies ran while one was open for 29% -> 0% of each run, Pallas kernels for 0% -> 32%
where the time goes in v1:
time: 216 us; the launch traced here: 215 us
  waiting for transfers between devices  95.5 us (44%)
  Pallas kernels  70.8 us (33%)
  starting transfers between devices  33.3 us (15%)
  local copies, waits for them, and re-layouts  14.1 us (7%)
    ppermute x16, waiting for transfers between devices, from_behind(): lax.ppermute(block, axis, [(i + 1, i) for i in devices if i + 1 in devices])  79 us
    pallas_call x16, Pallas kernels, fold(): pl.pallas_call(functools.partial(fold_body, pieces=pieces, tick=tick, fir...  62.7 us
    ppermute x16, starting transfers between devices, from_behind(): lax.ppermute(block, axis, [(i + 1, i) for i in devices if i + 1 in devices])  20.6 us
    ppermute x26, waiting for transfers between devices, flip(): lax.ppermute(block, axis, [(i, i ^ bit) for i in range(lax.axis_size(axis...  16.6 us
    unnamed x39, local copies, waits for them, and re-layouts  13.7 us
    ppermute x26, starting transfers between devices, flip(): lax.ppermute(block, axis, [(i, i ^ bit) for i in range(lax.axis_size(axis...  12.7 us
  transfers between devices with their start and end apart: 42, of which 20 were waited for; matrix products, arithmetic and copies ran while one was open for 0% of the time, Pallas kernels for 32%

profile of v1, /device:TPU:0, one launch (start us, length us, event | category | flops | bytes accessed | tf_op | source)
XLA Modules:
  0.0 215.0 jit_solution(13005711484890986806)
XLA Ops:
  0.6 2.2 %copy-done.4 = bf16[2,1,2,512,1024]{4,3,2,1,0:T(8,128)(2,1)S(1)} copy-done((bf16[2,1,2,512,1024]{4,3,2,1,0:T(8,128)(2,1)S(1)}, bf16[2,1,2,512,1024]{4,3,2,1,0:T(8,128)(2,1)}, u32[]{:S(2)}) %copy-start.4) | copy-done | bytes 4194328
  3.5 1.5 shard_map.78.refs_4_.refs_5_
  5.6 1.5 shard_map.77.refs_4_.refs_5_
  11.8 7.8 %collective-permute-done.16.refs_7_ = bf16[2,512,128]{2,1,0:T(8,128)(2,1)S(1)} collective-permute-done((bf16[2,512,128]{2,1,0:T(8,128)(2,1)S(1)}, bf16[2,512,128]{2,1,0:T(8,128)(2,1)S(1)}, u32[]{:S(2)}, u32[]{:S(2)}) %collective-permute-start.16) | collective-permute-done | bytes 262176 | tf_op jit(solution)/shard_map/ppermute | solution.py:19
  20.9 4.3 %collective-permute-done.14.refs_7_ = bf16[2,512,128]{2,1,0:T(8,128)(2,1)S(1)} collective-permute-done((bf16[2,512,128]{2,1,0:T(8,128)(2,1)S(1)}, bf16[2,512,128]{2,1,0:T(8,128)(2,1)S(1)}, u32[]{:S(2)}, u32[]{:S(2)}) %collective-permute-start.14) | collective-permute-done | bytes 262176 | tf_op jit(solution)/shard_map/ppermute | solution.py:19
  26.5 4.3 %collective-permute-done.12.refs_7_ = bf16[2,512,128]{2,1,0:T(8,128)(2,1)S(1)} collective-permute-done((bf16[2,512,128]{2,1,0:T(8,128)(2,1)S(1)}, bf16[2,512,128]{2,1,0:T(8,128)(2,1)S(1)}, u32[]{:S(2)}, u32[]{:S(2)}) %collective-permute-start.12) | collective-permute-done | bytes 262176 | tf_op jit(solution)/shard_map/ppermute | solution.py:19
  32.1 4.3 %collective-permute-done.10.refs_7_ = bf16[2,512,128]{2,1,0:T(8,128)(2,1)S(1)} collective-permute-done((bf16[2,512,128]{2,1,0:T(8,128)(2,1)S(1)}, bf16[2,512,128]{2,1,0:T(8,128)(2,1)S(1)}, u32[]{:S(2)}, u32[]{:S(2)}) %collective-permute-start.10) | collective-permute-done | bytes 262176 | tf_op jit(solution)/shard_map/ppermute | solution.py:19
  37.7 4.3 %collective-permute-done.8.refs_7_ = bf16[2,512,128]{2,1,0:T(8,128)(2,1)S(1)} collective-permute-done((bf16[2,512,128]{2,1,0:T(8,128)(2,1)S(1)}, bf16[2,512,128]{2,1,0:T(8,128)(2,1)S(1)}, u32[]{:S(2)}, u32[]{:S(2)}) %collective-permute-start.8) | collective-permute-done | bytes 262176 | tf_op jit(solution)/shard_map/ppermute | solution.py:19
  43.3 4.4 %collective-permute-done.6.refs_7_ = bf16[2,512,128]{2,1,0:T(8,128)(2,1)} collective-permute-done((bf16[2,512,128]{2,1,0:T(8,128)(2,1)S(1)}, bf16[2,512,128]{2,1,0:T(8,128)(2,1)}, u32[]{:S(2)}, u32[]{:S(2)}) %collective-permute-start.6) | collective-permute-done | bytes 262176 | tf_op jit(solution)/shard_map/ppermute | solution.py:19
  47.8 5.6 %collective-permute-done.4.refs_7_ = bf16[2,512,128]{2,1,0:T(8,128)(2,1)} collective-permute-done((bf16[2,512,128]{2,1,0:T(8,128)(2,1)S(1)}, bf16[2,512,128]{2,1,0:T(8,128)(2,1)}, u32[]{:S(2)}, u32[]{:S(2)}) %collective-permute-start.4) | collective-permute-done | bytes 262176 | tf_op jit(solution)/shard_map/ppermute | solution.py:19
  53.4 4.8 %collective-permute-done.2.refs_7_ = bf16[2,512,128]{2,1,0:T(8,128)(2,1)} collective-permute-done((bf16[2,512,128]{2,1,0:T(8,128)(2,1)S(1)}, bf16[2,512,128]{2,1,0:T(8,128)(2,1)}, u32[]{:S(2)}, u32[]{:S(2)}) %collective-permute-start.2) | collective-permute-done | bytes 262176 | tf_op jit(solution)/shard_map/ppermute | solution.py:19
  62.0 1.4 copy-done.2
  64.1 1.6 copy-done.1
  65.7 1.6 copy-done.3
  67.3 2.2 %copy-done.5 = bf16[2,1,2,512,1024]{4,3,2,1,0:T(8,128)(2,1)S(1)} copy-done((bf16[2,1,2,512,1024]{4,3,2,1,0:T(8,128)(2,1)S(1)}, bf16[2,1,2,512,1024]{4,3,2,1,0:T(8,128)(2,1)}, u32[]{:S(2)}) %copy-start.5) | copy-done | bytes 4194328
  70.4 3.2 %shard_map.79.refs_9_ = f32[2,512,1024]{2,1,0:T(8,128)S(1)} custom-call(s32[2]{0:T(128)S(1)} %pad_add_fusion.refs_0_, s32[2,1,1]{2,1,0:T(1,128)S(1)} %copy.35.refs_1_.pidx, f32[2,16]{1,0:T(2,128)S(1)} %copy-done.8, s32[1]{0:T(128)} %bitcast.2.refs_3_.here, bf16[2,512,1024]{2,1,0:T(8,128)(2,1)S(1)} %copy-done.1, bf16[2,512,1024]{2,1,0:T(8,128)(2,1)S(1)} %copy-done.1, ...), custom_call_target="tpu_custom_call" | custom-call | tf_op jit(solution)/shard_map/pallas_call | solution.py:187
  73.6 3.3 %shard_map.80.refs_9_ = f32[2,512,1024]{2,1,0:T(8,128)S(1)} custom-call(s32[2]{0:T(128)S(1)} %pad_add_fusion.refs_0_, s32[2,1,1]{2,1,0:T(1,128)S(1)} %copy.35.refs_1_.pidx, f32[2,16]{1,0:T(2,128)S(1)} %copy-done.8, s32[1]{0:T(128)} %bitcast.2.refs_3_.here, bf16[2,512,1024]{2,1,0:T(8,128)(2,1)S(1)} %copy-done.1, ...), custom_call_target="tpu_custom_call", output_to_operand_aliasing={{}: (9, {})} | custom-call | tf_op jit(solution)/shard_map/pallas_call | solution.py:187
  76.9 3.3 %shard_map.81.refs_9_ = f32[2,512,1024]{2,1,0:T(8,128)S(1)} custom-call(s32[2]{0:T(128)S(1)} %pad_add_fusion.refs_0_, s32[2,1,1]{2,1,0:T(1,128)S(1)} %copy.35.refs_1_.pidx, f32[2,16]{1,0:T(2,128)S(1)} %copy-done.8, s32[1]{0:T(128)} %bitcast.2.refs_3_.here, bf16[2,512,1024]{2,1,0:T(8,128)(2,1)S(1)} %copy-done.1, ...), custom_call_target="tpu_custom_call", output_to_operand_aliasing={{}: (9, {})} | custom-call | tf_op jit(solution)/shard_map/pallas_call | solution.py:187
  80.2 3.3 %shard_map.82.refs_9_ = f32[2,512,1024]{2,1,0:T(8,128)S(1)} custom-call(s32[2]{0:T(128)S(1)} %pad_add_fusion.refs_0_, s32[2,1,1]{2,1,0:T(1,128)S(1)} %copy.35.refs_1_.pidx, f32[2,16]{1,0:T(2,128)S(1)} %copy-done.8, s32[1]{0:T(128)} %bitcast.2.refs_3_.here, bf16[2,512,1024]{2,1,0:T(8,128)(2,1)S(1)} %copy-done.1, ...), custom_call_target="tpu_custom_call", output_to_operand_aliasing={{}: (9, {})} | custom-call | tf_op jit(solution)/shard_map/pallas_call | solution.py:187
  83.6 4.0 %shard_map.83.refs_9_ = f32[2,512,1024]{2,1,0:T(8,128)S(1)} custom-call(s32[2]{0:T(128)S(1)} %pad_add_fusion.refs_0_, s32[2,1,1]{2,1,0:T(1,128)S(1)} %copy.35.refs_1_.pidx, f32[2,16]{1,0:T(2,128)S(1)} %copy-done.8, s32[1]{0:T(128)} %bitcast.2.refs_3_.here, bf16[2,512,1024]{2,1,0:T(8,128)(2,1)S(1)} %copy-done.1, ...), custom_call_target="tpu_custom_call", output_to_operand_aliasing={{}: (9, {})} | custom-call | tf_op jit(solution)/shard_map/pallas_call | solution.py:187
  87.6 4.1 %shard_map.84.refs_9_ = f32[2,512,1024]{2,1,0:T(8,128)S(1)} custom-call(s32[2]{0:T(128)S(1)} %pad_add_fusion.refs_0_, s32[2,1,1]{2,1,0:T(1,128)S(1)} %copy.35.refs_1_.pidx, f32[2,16]{1,0:T(2,128)S(1)} %copy-done.8, s32[1]{0:T(128)} %bitcast.2.refs_3_.here, bf16[2,512,1024]{2,1,0:T(8,128)(2,1)S(1)} %copy-done.1, ...), custom_call_target="tpu_custom_call", output_to_operand_aliasing={{}: (9, {})} | custom-call | tf_op jit(solution)/shard_map/pallas_call | solution.py:187
  91.8 4.1 %shard_map.85.refs_9_ = f32[2,512,1024]{2,1,0:T(8,128)S(1)} custom-call(s32[2]{0:T(128)S(1)} %pad_add_fusion.refs_0_, s32[2,1,1]{2,1,0:T(1,128)S(1)} %copy.35.refs_1_.pidx, f32[2,16]{1,0:T(2,128)S(1)} %copy-done.8, s32[1]{0:T(128)} %bitcast.2.refs_3_.here, bf16[2,512,1024]{2,1,0:T(8,128)(2,1)S(1)} %copy-done.1, ...), custom_call_target="tpu_custom_call", output_to_operand_aliasing={{}: (9, {})} | custom-call | tf_op jit(solution)/shard_map/pallas_call | solution.py:187
  95.9 4.3 %shard_map.86 = (bf16[2,512,128]{2,1,0:T(8,128)(2,1)S(1)}, bf16[2,512,128]{2,1,0:T(8,128)(2,1)S(1)}, bf16[2,512,128]{2,1,0:T(8,128)(2,1)S(1)}, bf16[2,512,128]{2...) custom-call(s32[2]{0:T(128)S(1)} %pad_add_fusion.refs_0_, ...), custom_call_target="tpu_custom_call" | custom-call | tf_op jit(solution)/shard_map/pallas_call | solution.py:187
  106.8 4.6 %collective-permute-done.32.refs_7_ = bf16[2,512,128]{2,1,0:T(8,128)(2,1)S(1)} collective-permute-done((bf16[2,512,128]{2,1,0:T(8,128)(2,1)S(1)}, bf16[2,512,128]{2,1,0:T(8,128)(2,1)S(1)}, u32[]{:S(2)}, u32[]{:S(2)}) %collective-permute-start.32) | collective-permute-done | bytes 262176 | tf_op jit(solution)/shard_map/ppermute | solution.py:19
  112.6 4.3 %collective-permute-done.30.refs_7_ = bf16[2,512,128]{2,1,0:T(8,128)(2,1)S(1)} collective-permute-done((bf16[2,512,128]{2,1,0:T(8,128)(2,1)S(1)}, bf16[2,512,128]{2,1,0:T(8,128)(2,1)S(1)}, u32[]{:S(2)}, u32[]{:S(2)}) %collective-permute-start.30) | collective-permute-done | bytes 262176 | tf_op jit(solution)/shard_map/ppermute | solution.py:19
  118.2 4.3 %collective-permute-done.28.refs_7_ = bf16[2,512,128]{2,1,0:T(8,128)(2,1)S(1)} collective-permute-done((bf16[2,512,128]{2,1,0:T(8,128)(2,1)S(1)}, bf16[2,512,128]{2,1,0:T(8,128)(2,1)S(1)}, u32[]{:S(2)}, u32[]{:S(2)}) %collective-permute-start.28) | collective-permute-done | bytes 262176 | tf_op jit(solution)/shard_map/ppermute | solution.py:19
  123.8 4.3 %collective-permute-done.26.refs_7_ = bf16[2,512,128]{2,1,0:T(8,128)(2,1)S(1)} collective-permute-done((bf16[2,512,128]{2,1,0:T(8,128)(2,1)S(1)}, bf16[2,512,128]{2,1,0:T(8,128)(2,1)S(1)}, u32[]{:S(2)}, u32[]{:S(2)}) %collective-permute-start.26) | collective-permute-done | bytes 262176 | tf_op jit(solution)/shard_map/ppermute | solution.py:19
  128.2 5.6 %collective-permute-done.24.refs_7_ = bf16[2,512,128]{2,1,0:T(8,128)(2,1)S(1)} collective-permute-done((bf16[2,512,128]{2,1,0:T(8,128)(2,1)S(1)}, bf16[2,512,128]{2,1,0:T(8,128)(2,1)S(1)}, u32[]{:S(2)}, u32[]{:S(2)}) %collective-permute-start.24) | collective-permute-done | bytes 262176 | tf_op jit(solution)/shard_map/ppermute | solution.py:19
  133.8 5.6 %collective-permute-done.22.refs_7_ = bf16[2,512,128]{2,1,0:T(8,128)(2,1)S(1)} collective-permute-done((bf16[2,512,128]{2,1,0:T(8,128)(2,1)S(1)}, bf16[2,512,128]{2,1,0:T(8,128)(2,1)S(1)}, u32[]{:S(2)}, u32[]{:S(2)}) %collective-permute-start.22) | collective-permute-done | bytes 262176 | tf_op jit(solution)/shard_map/ppermute | solution.py:19
  139.4 5.6 %collective-permute-done.20.refs_7_ = bf16[2,512,128]{2,1,0:T(8,128)(2,1)S(1)} collective-permute-done((bf16[2,512,128]{2,1,0:T(8,128)(2,1)S(1)}, bf16[2,512,128]{2,1,0:T(8,128)(2,1)S(1)}, u32[]{:S(2)}, u32[]{:S(2)}) %collective-permute-start.20) | collective-permute-done | bytes 262176 | tf_op jit(solution)/shard_map/ppermute | solution.py:19
  145.0 4.7 %collective-permute-done.18.refs_7_ = bf16[2,512,128]{2,1,0:T(8,128)(2,1)S(1)} collective-permute-done((bf16[2,512,128]{2,1,0:T(8,128)(2,1)S(1)}, bf16[2,512,128]{2,1,0:T(8,128)(2,1)S(1)}, u32[]{:S(2)}, u32[]{:S(2)}) %collective-permute-start.18) | collective-permute-done | bytes 262176 | tf_op jit(solution)/shard_map/ppermute | solution.py:19
  150.7 1.9 shard_map.95
  152.6 3.9 %shard_map.87.refs_9_ = f32[2,512,1024]{2,1,0:T(8,128)S(1)} custom-call(s32[2]{0:T(128)S(1)} %pad_add_fusion.refs_0_, s32[2,1,1]{2,1,0:T(1,128)S(1)} %copy.35.refs_1_.pidx, f32[2,16]{1,0:T(2,128)S(1)} %copy-done.8, s32[1]{0:T(128)} %bitcast.2.refs_3_.here, bf16[2,512,1024]{2,1,0:T(8,128)(2,1)S(1)} %shard_map.77.refs_4_.refs_5_, ...), custom_call_target="tpu_custom_call" | custom-call | tf_op jit(solution)/shard_map/pallas_call | solution.py:187
  156.5 4.0 %shard_map.88.refs_9_ = f32[2,512,1024]{2,1,0:T(8,128)S(1)} custom-call(s32[2]{0:T(128)S(1)} %pad_add_fusion.refs_0_, s32[2,1,1]{2,1,0:T(1,128)S(1)} %copy.35.refs_1_.pidx, f32[2,16]{1,0:T(2,128)S(1)} %copy-done.8, s32[1]{0:T(128)} %bitcast.2.refs_3_.here, bf16[2,512,1024]{2,1,0:T(8,128)(2,1)S(1)} %shard_map.77.refs_4_.refs_5_, ...), custom_call_target="tpu_custom_call", output_to_operand_aliasing={{}: (9, {})} | custom-call | tf_op jit(solution)/shard_map/pallas_call | solution.py:187
  160.5 4.0 %shard_map.89.refs_9_ = f32[2,512,1024]{2,1,0:T(8,128)S(1)} custom-call(s32[2]{0:T(128)S(1)} %pad_add_fusion.refs_0_, s32[2,1,1]{2,1,0:T(1,128)S(1)} %copy.35.refs_1_.pidx, f32[2,16]{1,0:T(2,128)S(1)} %copy-done.8, s32[1]{0:T(128)} %bitcast.2.refs_3_.here, bf16[2,512,1024]{2,1,0:T(8,128)(2,1)S(1)} %shard_map.77.refs_4_.refs_5_, ...), custom_call_target="tpu_custom_call", output_to_operand_aliasing={{}: (9, {})} | custom-call | tf_op jit(solution)/shard_map/pallas_call | solution.py:187
  164.5 1.7 collective-permute-start.36
  166.2 4.0 %shard_map.90.refs_9_ = f32[2,512,1024]{2,1,0:T(8,128)S(1)} custom-call(s32[2]{0:T(128)S(1)} %pad_add_fusion.refs_0_, s32[2,1,1]{2,1,0:T(1,128)S(1)} %copy.35.refs_1_.pidx, f32[2,16]{1,0:T(2,128)S(1)} %copy-done.8, s32[1]{0:T(128)} %bitcast.2.refs_3_.here, bf16[2,512,1024]{2,1,0:T(8,128)(2,1)S(1)} %shard_map.77.refs_4_.refs_5_, ...), custom_call_target="tpu_custom_call", output_to_operand_aliasing={{}: (9, {})} | custom-call | tf_op jit(solution)/shard_map/pallas_call | solution.py:187
  170.2 1.6 collective-permute-start.37
  171.8 4.0 %shard_map.91.refs_9_ = f32[2,512,1024]{2,1,0:T(8,128)S(1)} custom-call(s32[2]{0:T(128)S(1)} %pad_add_fusion.refs_0_, s32[2,1,1]{2,1,0:T(1,128)S(1)} %copy.35.refs_1_.pidx, f32[2,16]{1,0:T(2,128)S(1)} %copy-done.8, s32[1]{0:T(128)} %bitcast.2.refs_3_.here, bf16[2,512,1024]{2,1,0:T(8,128)(2,1)S(1)} %shard_map.77.refs_4_.refs_5_, ...), custom_call_target="tpu_custom_call", output_to_operand_aliasing={{}: (9, {})} | custom-call | tf_op jit(solution)/shard_map/pallas_call | solution.py:187
  175.8 4.0 %shard_map.92.refs_9_ = f32[2,512,1024]{2,1,0:T(8,128)S(1)} custom-call(s32[2]{0:T(128)S(1)} %pad_add_fusion.refs_0_, s32[2,1,1]{2,1,0:T(1,128)S(1)} %copy.35.refs_1_.pidx, f32[2,16]{1,0:T(2,128)S(1)} %copy-done.8, s32[1]{0:T(128)} %bitcast.2.refs_3_.here, bf16[2,512,1024]{2,1,0:T(8,128)(2,1)S(1)} %shard_map.77.refs_4_.refs_5_, ...), custom_call_target="tpu_custom_call", output_to_operand_aliasing={{}: (9, {})} | custom-call | tf_op jit(solution)/shard_map/pallas_call | solution.py:187
  179.8 4.0 %shard_map.93.refs_9_ = f32[2,512,1024]{2,1,0:T(8,128)S(1)} custom-call(s32[2]{0:T(128)S(1)} %pad_add_fusion.refs_0_, s32[2,1,1]{2,1,0:T(1,128)S(1)} %copy.35.refs_1_.pidx, f32[2,16]{1,0:T(2,128)S(1)} %copy-done.8, s32[1]{0:T(128)} %bitcast.2.refs_3_.here, bf16[2,512,1024]{2,1,0:T(8,128)(2,1)S(1)} %shard_map.77.refs_4_.refs_5_, ...), custom_call_target="tpu_custom_call", output_to_operand_aliasing={{}: (9, {})} | custom-call | tf_op jit(solution)/shard_map/pallas_call | solution.py:187
  183.8 5.3 %shard_map.94 = (bf16[2,512,1024]{2,1,0:T(8,128)(2,1)}, bf16[512,512]{1,0:T(8,128)(2,1)S(1)}, bf16[512,512]{1,0:T(8,128)(2,1)S(1)}, bf16[512,512]{1,0:T(8,128)(2,1)S(1)}, bf16[512,512]{1,0:T(8,128)(2,1)S(1)}) custom-call(s32[2]{0:T(128)S(1)} %pad_add_fusion.refs_0_, s32[2,1,1]{2,1,0:T(1,128)S(1)} %copy.35.refs_1_.pidx, f32[2,16]{1,0:T(2,128)S(1)} %copy-done.8, ...), custom_call_target="tpu_custom_call" | custom-call | tf_op jit(solution)/shard_map/pallas_call | solution.py:187
  190.3 1.7 collective-permute-start.38
  192.0 1.5 collective-permute-start.39
  193.6 10.3 %collective-permute-done.34.real_got = bf16[512,512]{1,0:T(8,128)(2,1)S(1)} collective-permute-done((bf16[512,512]{1,0:T(8,128)(2,1)S(1)}, bf16[512,512]{1,0:T(8,128)(2,1)S(1)}, u32[]{:S(2)}, u32[]{:S(2)}) %collective-permute-start.34) | collective-permute-done | bytes 524320 | tf_op jit(solution)/shard_map/ppermute | solution.py:23
  205.2 1.7 collective-permute-start.41
  207.3 2.7 %collective-permute-done.38.real_last = bf16[512,256]{1,0:T(8,128)(2,1)S(1)} collective-permute-done((bf16[512,256]{1,0:T(8,128)(2,1)S(1)}, bf16[512,256]{1,0:T(8,128)(2,1)S(1)}, u32[]{:S(2)}, u32[]{:S(2)}) %collective-permute-start.38) | collective-permute-done | bytes 262176 | tf_op jit(solution)/shard_map/ppermute | solution.py:23
  210.8 3.0 %collective-permute-done.40.real_last = bf16[512,256]{1,0:T(8,128)(2,1)S(1)} collective-permute-done((bf16[512,256]{1,0:T(8,128)(2,1)S(1)}, bf16[512,256]{1,0:T(8,128)(2,1)S(1)}, u32[]{:S(2)}, u32[]{:S(2)}) %collective-permute-start.40) | collective-permute-done | bytes 262176 | tf_op jit(solution)/shard_map/ppermute | solution.py:23
  (103 shorter events, 34.1 us)
Async XLA Ops:
  5.0 57.0 %collective-permute-start.1 = (bf16[2,512,1024]{2,1,0:T(8,128)(2,1)S(1)}, bf16[2,512,1024]{2,1,0:T(8,128)(2,1)S(1)}, u32[]{:S(2)}, u32[]{:S(2)}) collective-permute-start(bf16[2,512,1024]{2,1,0:T(8,128)(2,1)S(1)} %shard_map.78.refs_4_.refs_5_), channel_id=1, source_target_pairs={{0,4},{4,0},{1,5},{5,1},{2,6},{6,2},{3,7},{7,3},{8,12},{12,8},{9,1... | collective-permute-start | bytes 6291464 | tf_op jit(solution)/shard_map/ppermute | solution.py:23
  7.1 56.8 %copy-start.18 = (s32[2,1,1]{0,2,1:T(1,128)S(1)}, s32[2,1,1]{0,2,1:T(1,128)}, u32[]{:S(2)}) copy-start(s32[2,1,1]{0,2,1:T(1,128)} %param.11) | copy-start | bytes 28
  7.1 57.0 %copy-start.8 = (f32[2,16]{1,0:T(2,128)S(1)}, f32[2,16]{1,0:T(2,128)}, u32[]{:S(2)}) copy-start(f32[2,16]{1,0:T(2,128)} %pw.1) | copy-start | bytes 388
  7.1 98.3 %collective-permute-start = (bf16[2,512,1024]{2,1,0:T(8,128)(2,1)S(1)}, bf16[2,512,1024]{2,1,0:T(8,128)(2,1)}, u32[]{:S(2)}, u32[]{:S(2)}) collective-permute-start(bf16[2,512,1024]{2,1,0:T(8,128)(2,1)S(1)} %shard_map.77.refs_4_.refs_5_), channel_id=1, source_target_pairs={{0,4},{4,0},{1,5},{5,1},{2,6},{6,2},{3,7},{7,3},{8,12},{12,8},{9,1... | collective-permute-start | bytes 6291464 | tf_op jit(solution)/shard_map/ppermute | solution.py:23
  7.5 12.1 %collective-permute-start.16 = (bf16[2,512,128]{2,1,0:T(8,128)(2,1)S(1)}, bf16[2,512,128]{2,1,0:T(8,128)(2,1)S(1)}, u32[]{:S(2)}, u32[]{:S(2)}) collective-permute-start(bf16[2,512,128]{2,1,0:T(8,128)(2,1)S(1)} %cut.1), channel_id=1, source_target_pairs={{8,0},{16,8},{24,16},{9,1},{17,9},{25,17},{10,2},{18,10},{26,18},{... | collective-permute-start | bytes 786440 | tf_op jit(solution)/shard_map/ppermute | solution.py:19
  9.2 16.0 %collective-permute-start.14 = (bf16[2,512,128]{2,1,0:T(8,128)(2,1)S(1)}, bf16[2,512,128]{2,1,0:T(8,128)(2,1)S(1)}, u32[]{:S(2)}, u32[]{:S(2)}) collective-permute-start(bf16[2,512,128]{2,1,0:T(8,128)(2,1)S(1)} %get-tuple-element.44), channel_id=1, source_target_pairs={{8,0},{16,8},{24,16},{9,1},{17,9},{25,17},{10,2},{18,10},{26,18},{... | collective-permute-start | bytes 786440 | tf_op jit(solution)/shard_map/ppermute | solution.py:19
  10.5 20.3 %collective-permute-start.12 = (bf16[2,512,128]{2,1,0:T(8,128)(2,1)S(1)}, bf16[2,512,128]{2,1,0:T(8,128)(2,1)S(1)}, u32[]{:S(2)}, u32[]{:S(2)}) collective-permute-start(bf16[2,512,128]{2,1,0:T(8,128)(2,1)S(1)} %get-tuple-element.45), channel_id=1, source_target_pairs={{8,0},{16,8},{24,16},{9,1},{17,9},{25,17},{10,2},{18,10},{26,18},{... | collective-permute-start | bytes 786440 | tf_op jit(solution)/shard_map/ppermute | solution.py:19
  19.6 16.9 %collective-permute-start.10 = (bf16[2,512,128]{2,1,0:T(8,128)(2,1)S(1)}, bf16[2,512,128]{2,1,0:T(8,128)(2,1)S(1)}, u32[]{:S(2)}, u32[]{:S(2)}) collective-permute-start(bf16[2,512,128]{2,1,0:T(8,128)(2,1)S(1)} %get-tuple-element.46), channel_id=1, source_target_pairs={{8,0},{16,8},{24,16},{9,1},{17,9},{25,17},{10,2},{18,10},{26,18},{... | collective-permute-start | bytes 786440 | tf_op jit(solution)/shard_map/ppermute | solution.py:19
  25.2 16.9 %collective-permute-start.8 = (bf16[2,512,128]{2,1,0:T(8,128)(2,1)S(1)}, bf16[2,512,128]{2,1,0:T(8,128)(2,1)S(1)}, u32[]{:S(2)}, u32[]{:S(2)}) collective-permute-start(bf16[2,512,128]{2,1,0:T(8,128)(2,1)S(1)} %get-tuple-element.47), channel_id=1, source_target_pairs={{8,0},{16,8},{24,16},{9,1},{17,9},{25,17},{10,2},{18,10},{26,18},{... | collective-permute-start | bytes 786440 | tf_op jit(solution)/shard_map/ppermute | solution.py:19
  30.8 17.0 %collective-permute-start.6 = (bf16[2,512,128]{2,1,0:T(8,128)(2,1)S(1)}, bf16[2,512,128]{2,1,0:T(8,128)(2,1)}, u32[]{:S(2)}, u32[]{:S(2)}) collective-permute-start(bf16[2,512,128]{2,1,0:T(8,128)(2,1)S(1)} %get-tuple-element.48), channel_id=1, source_target_pairs={{8,0},{16,8},{24,16},{9,1},{17,9},{25,17},{10,2},{18,10},{26,18},{... | collective-permute-start | bytes 786440 | tf_op jit(solution)/shard_map/ppermute | solution.py:19
  36.4 17.0 %collective-permute-start.4 = (bf16[2,512,128]{2,1,0:T(8,128)(2,1)S(1)}, bf16[2,512,128]{2,1,0:T(8,128)(2,1)}, u32[]{:S(2)}, u32[]{:S(2)}) collective-permute-start(bf16[2,512,128]{2,1,0:T(8,128)(2,1)S(1)} %get-tuple-element.49), channel_id=1, source_target_pairs={{8,0},{16,8},{24,16},{9,1},{17,9},{25,17},{10,2},{18,10},{26,18},{... | collective-permute-start | bytes 786440 | tf_op jit(solution)/shard_map/ppermute | solution.py:19
  42.0 16.1 %collective-permute-start.2 = (bf16[2,512,128]{2,1,0:T(8,128)(2,1)S(1)}, bf16[2,512,128]{2,1,0:T(8,128)(2,1)}, u32[]{:S(2)}, u32[]{:S(2)}) collective-permute-start(bf16[2,512,128]{2,1,0:T(8,128)(2,1)S(1)} %get-tuple-element.50), channel_id=1, source_target_pairs={{8,0},{16,8},{24,16},{9,1},{17,9},{25,17},{10,2},{18,10},{26,18},{... | collective-permute-start | bytes 786440 | tf_op jit(solution)/shard_map/ppermute | solution.py:19
  47.8 10.4 %collective-permute-start.17 = (bf16[2,512,128]{2,1,0:T(8,128)(2,1)S(1)}, bf16[2,512,128]{2,1,0:T(8,128)(2,1)S(1)}, u32[]{:S(2)}, u32[]{:S(2)}) collective-permute-start(bf16[2,512,128]{2,1,0:T(8,128)(2,1)S(1)} %collective-permute-done.16.refs_7_), channel_id=1, source_target_pairs={{0,4},{4,0},{1,5},{5,1},{2,6},{6,2},{3,7},{7,3},{8,12},{12,8},{9,1... | collective-permute-start | bytes 786440 | tf_op jit(solution)/shard_map/ppermute | solution.py:23
  53.4 6.0 %collective-permute-start.15 = (bf16[2,512,128]{2,1,0:T(8,128)(2,1)S(1)}, bf16[2,512,128]{2,1,0:T(8,128)(2,1)S(1)}, u32[]{:S(2)}, u32[]{:S(2)}) collective-permute-start(bf16[2,512,128]{2,1,0:T(8,128)(2,1)S(1)} %collective-permute-done.14.refs_7_), channel_id=1, source_target_pairs={{0,4},{4,0},{1,5},{5,1},{2,6},{6,2},{3,7},{7,3},{8,12},{12,8},{9,1... | collective-permute-start | bytes 786440 | tf_op jit(solution)/shard_map/ppermute | solution.py:23
  58.2 1.9 collective-permute-start.13
  58.9 2.4 %collective-permute-start.11 = (bf16[2,512,128]{2,1,0:T(8,128)(2,1)S(1)}, bf16[2,512,128]{2,1,0:T(8,128)(2,1)S(1)}, u32[]{:S(2)}, u32[]{:S(2)}) collective-permute-start(bf16[2,512,128]{2,1,0:T(8,128)(2,1)S(1)} %collective-permute-done.10.refs_7_), channel_id=1, source_target_pairs={{0,4},{4,0},{1,5},{5,1},{2,6},{6,2},{3,7},{7,3},{8,12},{12,8},{9,1... | collective-permute-start | bytes 786440 | tf_op jit(solution)/shard_map/ppermute | solution.py:23
  60.1 23.4 %collective-permute-start.9 = (bf16[2,512,128]{2,1,0:T(8,128)(2,1)S(1)}, bf16[2,512,128]{2,1,0:T(8,128)(2,1)}, u32[]{:S(2)}, u32[]{:S(2)}) collective-permute-start(bf16[2,512,128]{2,1,0:T(8,128)(2,1)S(1)} %collective-permute-done.8.refs_7_), channel_id=1, source_target_pairs={{0,4},{4,0},{1,5},{5,1},{2,6},{6,2},{3,7},{7,3},{8,12},{12,8},{9,1... | collective-permute-start | bytes 786440 | tf_op jit(solution)/shard_map/ppermute | solution.py:23
  60.8 26.8 %collective-permute-start.7 = (bf16[2,512,128]{2,1,0:T(8,128)(2,1)}, bf16[2,512,128]{2,1,0:T(8,128)(2,1)}, u32[]{:S(2)}, u32[]{:S(2)}) collective-permute-start(bf16[2,512,128]{2,1,0:T(8,128)(2,1)} %collective-permute-done.6.refs_7_), channel_id=1, source_target_pairs={{0,4},{4,0},{1,5},{5,1},{2,6},{6,2},{3,7},{7,3},{8,12},{12,8},{9,1... | collective-permute-start | bytes 786440 | tf_op jit(solution)/shard_map/ppermute | solution.py:23
  62.0 29.7 %collective-permute-start.5 = (bf16[2,512,128]{2,1,0:T(8,128)(2,1)}, bf16[2,512,128]{2,1,0:T(8,128)(2,1)}, u32[]{:S(2)}, u32[]{:S(2)}) collective-permute-start(bf16[2,512,128]{2,1,0:T(8,128)(2,1)} %collective-permute-done.4.refs_7_), channel_id=1, source_target_pairs={{0,4},{4,0},{1,5},{5,1},{2,6},{6,2},{3,7},{7,3},{8,12},{12,8},{9,1... | collective-permute-start | bytes 786440 | tf_op jit(solution)/shard_map/ppermute | solution.py:23
  63.4 32.5 %collective-permute-start.3 = (bf16[2,512,128]{2,1,0:T(8,128)(2,1)}, bf16[2,512,128]{2,1,0:T(8,128)(2,1)}, u32[]{:S(2)}, u32[]{:S(2)}) collective-permute-start(bf16[2,512,128]{2,1,0:T(8,128)(2,1)} %collective-permute-done.2.refs_7_), channel_id=1, source_target_pairs={{0,4},{4,0},{1,5},{5,1},{2,6},{6,2},{3,7},{7,3},{8,12},{12,8},{9,1... | collective-permute-start | bytes 786440 | tf_op jit(solution)/shard_map/ppermute | solution.py:23
  70.4 3.2 %copy-start.12 = (bf16[2,512,128]{2,1,0:T(8,128)(2,1)S(1)}, bf16[2,512,128]{2,1,0:T(8,128)(2,1)}, u32[]{:S(2)}) copy-start(bf16[2,512,128]{2,1,0:T(8,128)(2,1)} %copy-done.11) | copy-start | bytes 786436
  73.6 3.3 %copy-start.14 = (bf16[2,512,128]{2,1,0:T(8,128)(2,1)S(1)}, bf16[2,512,128]{2,1,0:T(8,128)(2,1)}, u32[]{:S(2)}) copy-start(bf16[2,512,128]{2,1,0:T(8,128)(2,1)} %copy-done.13) | copy-start | bytes 786436
  76.9 3.3 %copy-start.16 = (bf16[2,512,128]{2,1,0:T(8,128)(2,1)S(1)}, bf16[2,512,128]{2,1,0:T(8,128)(2,1)}, u32[]{:S(2)}) copy-start(bf16[2,512,128]{2,1,0:T(8,128)(2,1)} %copy-done.15) | copy-start | bytes 786436
  95.9 56.7 %copy-start.6 = (bf16[2,1,2,512,1024]{4,3,2,1,0:T(8,128)(2,1)S(1)}, bf16[2,1,2,512,1024]{4,3,2,1,0:T(8,128)(2,1)}, u32[]{:S(2)}) copy-start(bf16[2,1,2,512,1024]{4,3,2,1,0:T(8,128)(2,1)} %refs_9_.3) | copy-start | bytes 12582916
  100.2 11.1 %collective-permute-start.32 = (bf16[2,512,128]{2,1,0:T(8,128)(2,1)S(1)}, bf16[2,512,128]{2,1,0:T(8,128)(2,1)S(1)}, u32[]{:S(2)}, u32[]{:S(2)}) collective-permute-start(bf16[2,512,128]{2,1,0:T(8,128)(2,1)S(1)} %get-tuple-element.30.refs_0_), channel_id=1, source_target_pairs={{8,0},{16,8},{24,16},{9,1},{17,9},{25,17},{10,2},{18,10},{26,18},{... | collective-permute-start | bytes 786440 | tf_op jit(solution)/shard_map/ppermute | solution.py:19
  101.5 15.4 %collective-permute-start.30 = (bf16[2,512,128]{2,1,0:T(8,128)(2,1)S(1)}, bf16[2,512,128]{2,1,0:T(8,128)(2,1)S(1)}, u32[]{:S(2)}, u32[]{:S(2)}) collective-permute-start(bf16[2,512,128]{2,1,0:T(8,128)(2,1)S(1)} %get-tuple-element.29.refs_1_), channel_id=1, source_target_pairs={{8,0},{16,8},{24,16},{9,1},{17,9},{25,17},{10,2},{18,10},{26,18},{... | collective-permute-start | bytes 786440 | tf_op jit(solution)/shard_map/ppermute | solution.py:19
  102.8 19.7 %collective-permute-start.28 = (bf16[2,512,128]{2,1,0:T(8,128)(2,1)S(1)}, bf16[2,512,128]{2,1,0:T(8,128)(2,1)S(1)}, u32[]{:S(2)}, u32[]{:S(2)}) collective-permute-start(bf16[2,512,128]{2,1,0:T(8,128)(2,1)S(1)} %get-tuple-element.28.refs_2_), channel_id=1, source_target_pairs={{8,0},{16,8},{24,16},{9,1},{17,9},{25,17},{10,2},{18,10},{26,18},{... | collective-permute-start | bytes 786440 | tf_op jit(solution)/shard_map/ppermute | solution.py:19
  104.1 24.0 %collective-permute-start.26 = (bf16[2,512,128]{2,1,0:T(8,128)(2,1)S(1)}, bf16[2,512,128]{2,1,0:T(8,128)(2,1)S(1)}, u32[]{:S(2)}, u32[]{:S(2)}) collective-permute-start(bf16[2,512,128]{2,1,0:T(8,128)(2,1)S(1)} %get-tuple-element.27.refs_3_), channel_id=1, source_target_pairs={{8,0},{16,8},{24,16},{9,1},{17,9},{25,17},{10,2},{18,10},{26,18},{... | collective-permute-start | bytes 786440 | tf_op jit(solution)/shard_map/ppermute | solution.py:19
  105.5 28.3 %collective-permute-start.24 = (bf16[2,512,128]{2,1,0:T(8,128)(2,1)S(1)}, bf16[2,512,128]{2,1,0:T(8,128)(2,1)S(1)}, u32[]{:S(2)}, u32[]{:S(2)}) collective-permute-start(bf16[2,512,128]{2,1,0:T(8,128)(2,1)S(1)} %get-tuple-element.26.refs_4_), channel_id=1, source_target_pairs={{8,0},{16,8},{24,16},{9,1},{17,9},{25,17},{10,2},{18,10},{26,18},{... | collective-permute-start | bytes 786440 | tf_op jit(solution)/shard_map/ppermute | solution.py:19
  111.3 28.1 %collective-permute-start.22 = (bf16[2,512,128]{2,1,0:T(8,128)(2,1)S(1)}, bf16[2,512,128]{2,1,0:T(8,128)(2,1)S(1)}, u32[]{:S(2)}, u32[]{:S(2)}) collective-permute-start(bf16[2,512,128]{2,1,0:T(8,128)(2,1)S(1)} %get-tuple-element.25.refs_5_), channel_id=1, source_target_pairs={{8,0},{16,8},{24,16},{9,1},{17,9},{25,17},{10,2},{18,10},{26,18},{... | collective-permute-start | bytes 786440 | tf_op jit(solution)/shard_map/ppermute | solution.py:19
  116.9 28.1 %collective-permute-start.20 = (bf16[2,512,128]{2,1,0:T(8,128)(2,1)S(1)}, bf16[2,512,128]{2,1,0:T(8,128)(2,1)S(1)}, u32[]{:S(2)}, u32[]{:S(2)}) collective-permute-start(bf16[2,512,128]{2,1,0:T(8,128)(2,1)S(1)} %get-tuple-element.24.refs_6_), channel_id=1, source_target_pairs={{8,0},{16,8},{24,16},{9,1},{17,9},{25,17},{10,2},{18,10},{26,18},{... | collective-permute-start | bytes 786440 | tf_op jit(solution)/shard_map/ppermute | solution.py:19
  122.6 27.1 %collective-permute-start.18 = (bf16[2,512,128]{2,1,0:T(8,128)(2,1)S(1)}, bf16[2,512,128]{2,1,0:T(8,128)(2,1)S(1)}, u32[]{:S(2)}, u32[]{:S(2)}) collective-permute-start(bf16[2,512,128]{2,1,0:T(8,128)(2,1)S(1)} %get-tuple-element.23.refs_7_), channel_id=1, source_target_pairs={{8,0},{16,8},{24,16},{9,1},{17,9},{25,17},{10,2},{18,10},{26,18},{... | collective-permute-start | bytes 786440 | tf_op jit(solution)/shard_map/ppermute | solution.py:19
  128.2 21.5 %collective-permute-start.33 = (bf16[2,512,128]{2,1,0:T(8,128)(2,1)S(1)}, bf16[2,512,128]{2,1,0:T(8,128)(2,1)S(1)}, u32[]{:S(2)}, u32[]{:S(2)}) collective-permute-start(bf16[2,512,128]{2,1,0:T(8,128)(2,1)S(1)} %collective-permute-done.32.refs_7_), channel_id=1, source_target_pairs={{0,4},{4,0},{1,5},{5,1},{2,6},{6,2},{3,7},{7,3},{8,12},{12,8},{9,1... | collective-permute-start | bytes 786440 | tf_op jit(solution)/shard_map/ppermute | solution.py:23
  133.8 16.4 %collective-permute-start.31 = (bf16[2,512,128]{2,1,0:T(8,128)(2,1)S(1)}, bf16[2,512,128]{2,1,0:T(8,128)(2,1)S(1)}, u32[]{:S(2)}, u32[]{:S(2)}) collective-permute-start(bf16[2,512,128]{2,1,0:T(8,128)(2,1)S(1)} %collective-permute-done.30.refs_7_), channel_id=1, source_target_pairs={{0,4},{4,0},{1,5},{5,1},{2,6},{6,2},{3,7},{7,3},{8,12},{12,8},{9,1... | collective-permute-start | bytes 786440 | tf_op jit(solution)/shard_map/ppermute | solution.py:23
  139.4 10.9 %collective-permute-start.29 = (bf16[2,512,128]{2,1,0:T(8,128)(2,1)S(1)}, bf16[2,512,128]{2,1,0:T(8,128)(2,1)S(1)}, u32[]{:S(2)}, u32[]{:S(2)}) collective-permute-start(bf16[2,512,128]{2,1,0:T(8,128)(2,1)S(1)} %collective-permute-done.28.refs_7_), channel_id=1, source_target_pairs={{0,4},{4,0},{1,5},{5,1},{2,6},{6,2},{3,7},{7,3},{8,12},{12,8},{9,1... | collective-permute-start | bytes 786440 | tf_op jit(solution)/shard_map/ppermute | solution.py:23
  145.0 19.5 %collective-permute-start.27 = (bf16[2,512,128]{2,1,0:T(8,128)(2,1)S(1)}, bf16[2,512,128]{2,1,0:T(8,128)(2,1)S(1)}, u32[]{:S(2)}, u32[]{:S(2)}) collective-permute-start(bf16[2,512,128]{2,1,0:T(8,128)(2,1)S(1)} %collective-permute-done.26.refs_7_), channel_id=1, source_target_pairs={{0,4},{4,0},{1,5},{5,1},{2,6},{6,2},{3,7},{7,3},{8,12},{12,8},{9,1... | collective-permute-start | bytes 786440 | tf_op jit(solution)/shard_map/ppermute | solution.py:23
  149.7 20.5 %collective-permute-start.25 = (bf16[2,512,128]{2,1,0:T(8,128)(2,1)S(1)}, bf16[2,512,128]{2,1,0:T(8,128)(2,1)S(1)}, u32[]{:S(2)}, u32[]{:S(2)}) collective-permute-start(bf16[2,512,128]{2,1,0:T(8,128)(2,1)S(1)} %collective-permute-done.24.refs_7_), channel_id=1, source_target_pairs={{0,4},{4,0},{1,5},{5,1},{2,6},{6,2},{3,7},{7,3},{8,12},{12,8},{9,1... | collective-permute-start | bytes 786440 | tf_op jit(solution)/shard_map/ppermute | solution.py:23
  149.7 26.1 %collective-permute-start.23 = (bf16[2,512,128]{2,1,0:T(8,128)(2,1)S(1)}, bf16[2,512,128]{2,1,0:T(8,128)(2,1)S(1)}, u32[]{:S(2)}, u32[]{:S(2)}) collective-permute-start(bf16[2,512,128]{2,1,0:T(8,128)(2,1)S(1)} %collective-permute-done.22.refs_7_), channel_id=1, source_target_pairs={{0,4},{4,0},{1,5},{5,1},{2,6},{6,2},{3,7},{7,3},{8,12},{12,8},{9,1... | collective-permute-start | bytes 786440 | tf_op jit(solution)/shard_map/ppermute | solution.py:23
  150.2 29.6 %collective-permute-start.21 = (bf16[2,512,128]{2,1,0:T(8,128)(2,1)S(1)}, bf16[2,512,128]{2,1,0:T(8,128)(2,1)S(1)}, u32[]{:S(2)}, u32[]{:S(2)}) collective-permute-start(bf16[2,512,128]{2,1,0:T(8,128)(2,1)S(1)} %collective-permute-done.20.refs_7_), channel_id=1, source_target_pairs={{0,4},{4,0},{1,5},{5,1},{2,6},{6,2},{3,7},{7,3},{8,12},{12,8},{9,1... | collective-permute-start | bytes 786440 | tf_op jit(solution)/shard_map/ppermute | solution.py:23
  150.3 33.5 %collective-permute-start.19 = (bf16[2,512,128]{2,1,0:T(8,128)(2,1)S(1)}, bf16[2,512,128]{2,1,0:T(8,128)(2,1)S(1)}, u32[]{:S(2)}, u32[]{:S(2)}) collective-permute-start(bf16[2,512,128]{2,1,0:T(8,128)(2,1)S(1)} %collective-permute-done.18.refs_7_), channel_id=1, source_target_pairs={{0,4},{4,0},{1,5},{5,1},{2,6},{6,2},{3,7},{7,3},{8,12},{12,8},{9,1... | collective-permute-start | bytes 786440 | tf_op jit(solution)/shard_map/ppermute | solution.py:23
  164.5 25.4 %collective-permute-start.36 = (bf16[512,512]{1,0:T(8,128)(2,1)S(1)}, bf16[512,512]{1,0:T(8,128)(2,1)S(1)}, u32[]{:S(2)}, u32[]{:S(2)}) collective-permute-start(bf16[512,512]{1,0:T(8,128)(2,1)S(1)} %get-tuple-element.37), channel_id=1, source_target_pairs={{0,2},{1,3},{2,0},{3,1},{4,6},{5,7},{6,4},{7,5},{8,10},{9,11},{10,... | collective-permute-start | bytes 1572872 | tf_op jit(solution)/shard_map/ppermute | solution.py:23
  170.2 19.7 %collective-permute-start.37 = (bf16[512,512]{1,0:T(8,128)(2,1)S(1)}, bf16[512,512]{1,0:T(8,128)(2,1)S(1)}, u32[]{:S(2)}, u32[]{:S(2)}) collective-permute-start(bf16[512,512]{1,0:T(8,128)(2,1)S(1)} %get-tuple-element.39), channel_id=1, source_target_pairs={{0,1},{1,0},{2,3},{3,2},{4,5},{5,4},{6,7},{7,6},{8,9},{9,8},{10,11... | collective-permute-start | bytes 1572872 | tf_op jit(solution)/shard_map/ppermute | solution.py:23
  189.1 14.8 %collective-permute-start.34 = (bf16[512,512]{1,0:T(8,128)(2,1)S(1)}, bf16[512,512]{1,0:T(8,128)(2,1)S(1)}, u32[]{:S(2)}, u32[]{:S(2)}) collective-permute-start(bf16[512,512]{1,0:T(8,128)(2,1)S(1)} %get-tuple-element.33), channel_id=1, source_target_pairs={{0,2},{1,3},{2,0},{3,1},{4,6},{5,7},{6,4},{7,5},{8,10},{9,11},{10,... | collective-permute-start | bytes 1572872 | tf_op jit(solution)/shard_map/ppermute | solution.py:23
  189.6 14.8 %collective-permute-start.35 = (bf16[512,512]{1,0:T(8,128)(2,1)S(1)}, bf16[512,512]{1,0:T(8,128)(2,1)S(1)}, u32[]{:S(2)}, u32[]{:S(2)}) collective-permute-start(bf16[512,512]{1,0:T(8,128)(2,1)S(1)} %get-tuple-element.35), channel_id=1, source_target_pairs={{0,1},{1,0},{2,3},{3,2},{4,5},{5,4},{6,7},{7,6},{8,9},{9,8},{10,11... | collective-permute-start | bytes 1572872 | tf_op jit(solution)/shard_map/ppermute | solution.py:23
  190.3 19.7 %collective-permute-start.38 = (bf16[512,256]{1,0:T(8,128)(2,1)S(1)}, bf16[512,256]{1,0:T(8,128)(2,1)S(1)}, u32[]{:S(2)}, u32[]{:S(2)}) collective-permute-start(bf16[512,256]{1,0:T(8,128)(2,1)S(1)} %get-tuple-element.40), channel_id=1, source_target_pairs={{0,1},{1,0},{2,3},{3,2},{4,5},{5,4},{6,7},{7,6},{8,9},{9,8},{10,11... | collective-permute-start | bytes 786440 | tf_op jit(solution)/shard_map/ppermute | solution.py:23
  192.0 17.9 %collective-permute-start.39 = (bf16[512,256]{1,0:T(8,128)(2,1)S(1)}, bf16[512,256]{1,0:T(8,128)(2,1)S(1)}, u32[]{:S(2)}, u32[]{:S(2)}) collective-permute-start(bf16[512,256]{1,0:T(8,128)(2,1)S(1)} %get-tuple-element.41), channel_id=1, source_target_pairs={{0,2},{1,3},{2,0},{3,1},{4,6},{5,7},{6,4},{7,5},{8,10},{9,11},{10,... | collective-permute-start | bytes 786440 | tf_op jit(solution)/shard_map/ppermute | solution.py:23
  204.7 9.1 %collective-permute-start.40 = (bf16[512,256]{1,0:T(8,128)(2,1)S(1)}, bf16[512,256]{1,0:T(8,128)(2,1)S(1)}, u32[]{:S(2)}, u32[]{:S(2)}) collective-permute-start(bf16[512,256]{1,0:T(8,128)(2,1)S(1)} %get-tuple-element.42), channel_id=1, source_target_pairs={{0,1},{1,0},{2,3},{3,2},{4,5},{5,4},{6,7},{7,6},{8,9},{9,8},{10,11... | collective-permute-start | bytes 786440 | tf_op jit(solution)/shard_map/ppermute | solution.py:23
  205.2 8.7 %collective-permute-start.41 = (bf16[512,256]{1,0:T(8,128)(2,1)S(1)}, bf16[512,256]{1,0:T(8,128)(2,1)S(1)}, u32[]{:S(2)}, u32[]{:S(2)}) collective-permute-start(bf16[512,256]{1,0:T(8,128)(2,1)S(1)} %get-tuple-element.43), channel_id=1, source_target_pairs={{0,2},{1,3},{2,0},{3,1},{4,6},{5,7},{6,4},{7,5},{8,10},{9,11},{10,... | collective-permute-start | bytes 786440 | tf_op jit(solution)/shard_map/ppermute | solution.py:23
  (13 other events, 18.2 us)

commit v2 on v1

v2 whole, which is shorter than its diff:
```python
import functools

import jax
import jax.numpy as jnp
from jax import lax
from jax.experimental import pallas as pl
from jax.experimental.pallas import tpu as pltpu
from jax.sharding import PartitionSpec as P


BF16 = jnp.bfloat16
F32 = jnp.float32

LIMIT = pltpu.CompilerParams(vmem_limit_bytes=20 << 20)


def from_behind(block, axis):
    devices = range(lax.axis_size(axis))
    return lax.ppermute(block, axis, [(i + 1, i) for i in devices if i + 1 in devices])


def flip(block, axis, bit):
    return lax.ppermute(block, axis, [(i, i ^ bit) for i in range(lax.axis_size(axis))])


def row_pieces(block):
    rows = block.shape[1]
    count = lax.axis_size("row")
    if count == 1:
        return [block], [0]
    if count == 2:
        here = lax.axis_index("row")
        there = flip(block, "row", 1)
        return [block, there], [here * rows, (1 - here) * rows]
    return [lax.all_gather(block, "row", axis=1, tiled=True)], [0]


VMEM = pl.BlockSpec(memory_space=pltpu.VMEM)
HBM = pl.BlockSpec(memory_space=pltpu.HBM)


def mask_body(mask_ref, coupling_ref, out_ref, sems, *, tick):
    block_rows, blocks = mask_ref.shape[2:]
    rows, width = out_ref.shape[1:]
    high, wide = rows // block_rows, width // blocks

    def fetch(k):
        at = pl.ds(k * high, high)
        return pltpu.make_async_copy(coupling_ref.at[tick, 0, :, at, :], out_ref.at[:, at, :], sems.at[k])

    for k in range(block_rows):
        fetch(k).start()
    for k in range(block_rows):
        fetch(k).wait()
        rows_at = slice(k * high, (k + 1) * high)
        for col in range(blocks):
            cols = slice(col * wide, (col + 1) * wide)
            block = out_ref[:, rows_at, cols]
            keep = mask_ref[tick, 0, k, col] != 0
            out_ref[:, rows_at, cols] = jnp.where(keep, block, jnp.zeros_like(block))


def masked_factor(block_mask, coupling, tick):
    rows, width = coupling.shape[3:]
    return pl.pallas_call(
        functools.partial(mask_body, tick=tick),
        grid_spec=pltpu.PrefetchScalarGridSpec(
            num_scalar_prefetch=1,
            grid=(1,),
            in_specs=[HBM],
            out_specs=VMEM,
            scratch_shapes=[pltpu.SemaphoreType.DMA((block_mask.shape[2],))],
        ),
        out_shape=jax.ShapeDtypeStruct((2, rows, width), BF16),
        compiler_params=LIMIT,
    )(block_mask, coupling)


def dot(a, b):
    return jnp.dot(a, b, preferred_element_type=F32)


def dot_t(a, b):
    return lax.dot_general(a, b, (((1,), (1,)), ((), ())), preferred_element_type=F32)


def fold_body(*refs, pieces, tick, start, first, last, chunks):
    offs, pidx, pw, here = refs[:4]
    refs = refs[4:]
    own = refs[0]
    factor = refs[1 : 1 + pieces]
    behind = refs[1 + pieces : 1 + 2 * pieces]
    before = refs[1 + 2 * pieces]
    right, low, high = refs[-3:]
    outs = refs[2 + 2 * pieces : -3]
    rows = own.shape[1]
    span = behind[0].shape[2]
    if first:
        green, sem = outs[-2:]
        outs = outs[:-2]
        fetch = pltpu.make_async_copy(before.at[tick, 0], green, sem)
        fetch.start()
    cols = slice(start, start + span)
    for k in range(pieces):
        size = behind[k].shape[1]
        at = pl.ds(pl.multiple_of(offs[k], size), size)
        right[at, :span] = behind[k][0]
        right[at, span:] = behind[k][1]
        low[at, :span] = factor[k][0, :, cols]
        low[at, span:] = -factor[k][1, :, cols]
        high[at, :span] = factor[k][1, :, cols]
        high[at, span:] = factor[k][0, :, cols]
    tile = min(rows, 256)
    for step in range(rows // tile):
        at = slice(step * tile, (step + 1) * tile)
        a = dot(own[0, at], right[...])
        b = dot(own[1, at], right[...])
        half = jnp.concatenate([a[:, :span] - b[:, span:], a[:, span:] + b[:, :span]], axis=1).astype(BF16)
        real = dot_t(half, low[...])
        imag = dot_t(half, high[...])
        if first:
            if step == 0:
                fetch.wait()
            real = green[0, at].astype(F32) + real
            imag = green[1, at].astype(F32) + imag
        else:
            real = before[0, at] + real
            imag = before[1, at] + imag
        if not last:
            outs[0][0, at] = real
            outs[0][1, at] = imag
            continue
        real = real.astype(BF16)
        imag = imag.astype(BF16)
        left = 0
        for out in outs[:chunks]:
            out[0, at] = real[:, left : left + out.shape[2]]
            out[1, at] = imag[:, left : left + out.shape[2]]
            left += out.shape[2]
        if len(outs) > chunks:
            write_term(real, imag, pidx, pw, here, tick, outs[chunks:], step * tile)


def write_term(real, imag, pidx, pw, here, tick, outs, row):
    real = real.astype(F32)
    imag = imag.astype(F32)
    w0 = pw[0, pidx[tick, 0, 0]]
    w1 = pw[1, pidx[tick, 0, 0]]
    term_real = (w0 * real - w1 * imag).astype(BF16)
    term_imag = (w0 * imag + w1 * real).astype(BF16)
    high, width = real.shape
    if len(outs) == 1:
        outs[0][0, row : row + high] = term_real
        outs[0][1, row : row + high] = term_imag
        return
    part = row // outs[0].shape[0]
    row -= part * outs[0].shape[0]
    at = slice(row, row + high)
    real_send, real_keep, imag_send, imag_keep = outs[4 * part : 4 * part + 4]
    quarter = width // 4
    first_major = here[0] // 2 == 0
    first_minor = here[0] % 2 == 0
    lower, upper = term_real[:, : 2 * quarter], term_real[:, 2 * quarter :]
    real_send[at] = jnp.where(first_major, upper, lower)
    real_keep[at] = jnp.where(first_major, lower, upper)
    for pair in range(2):
        cols = slice(pair * quarter, (pair + 1) * quarter)
        even = term_imag[:, 2 * pair * quarter : (2 * pair + 1) * quarter]
        odd = term_imag[:, (2 * pair + 1) * quarter : (2 * pair + 2) * quarter]
        imag_send[at, cols] = jnp.where(first_minor, odd, even)
        imag_keep[at, cols] = jnp.where(first_minor, even, odd)


def term_shapes(rows, width):
    if lax.axis_size("pole") != 4:
        return [jax.ShapeDtypeStruct((2, rows, width), BF16)]
    parts = 2 if rows % 512 == 0 else 1
    return [jax.ShapeDtypeStruct((rows // parts, width // 2), BF16)] * (4 * parts)


def fold(scalars, own, factor, behind, before, tick, start, first, last, widths, with_term):
    rows, width = own.shape[1:]
    span = behind[0].shape[2]
    pieces = len(behind)
    if last:
        out_shape = [jax.ShapeDtypeStruct((2, rows, w), BF16) for w in widths]
        if with_term:
            out_shape += term_shapes(rows, width)
    else:
        out_shape = [jax.ShapeDtypeStruct((2, rows, width), F32)]
    scratch = [pltpu.VMEM((2, rows, width), BF16), pltpu.SemaphoreType.DMA] if first else []
    return pl.pallas_call(
        functools.partial(
            fold_body, pieces=pieces, tick=tick, start=start, first=first, last=last, chunks=len(widths)
        ),
        grid_spec=pltpu.PrefetchScalarGridSpec(
            num_scalar_prefetch=len(scalars),
            grid=(1,),
            in_specs=[VMEM] * (1 + 2 * pieces) + [HBM if first else VMEM],
            out_specs=[VMEM] * len(out_shape),
            scratch_shapes=scratch + [pltpu.VMEM((width, 2 * span), BF16)] * 3,
        ),
        out_shape=out_shape,
        input_output_aliases={} if first or last else {len(scalars) + 1 + 2 * pieces: 0},
        compiler_params=LIMIT,
    )(*scalars, own, *factor, *behind, before)


def term_body(pidx, pw, here, *refs, tick, count):
    rows = refs[0].shape[1]
    tile = min(rows, 256)
    for row in range(0, rows, tile):
        real = jnp.concatenate([ref[0, row : row + tile] for ref in refs[:count]], axis=1)
        imag = jnp.concatenate([ref[1, row : row + tile] for ref in refs[:count]], axis=1)
        write_term(real, imag, pidx, pw, here, tick, refs[count:], row)


def weigh(scalars, state, tick):
    out_shape = term_shapes(state[0].shape[1], sum(piece.shape[2] for piece in state))
    return pl.pallas_call(
        functools.partial(term_body, tick=tick, count=len(state)),
        grid_spec=pltpu.PrefetchScalarGridSpec(
            num_scalar_prefetch=3,
            grid=(1,),
            in_specs=[VMEM] * len(state),
            out_specs=[VMEM] * len(out_shape),
        ),
        out_shape=out_shape,
        compiler_params=LIMIT,
    )(*scalars[1:], *state)


def cut_body(src, out, sem, *, start):
    fetch = pltpu.make_async_copy(src.at[0, :, :, pl.ds(start, out.shape[2])], out, sem)
    fetch.start()
    fetch.wait()


def cut_piece(state, start, span):
    return pl.pallas_call(
        functools.partial(cut_body, start=start),
        in_specs=[HBM],
        out_specs=VMEM,
        out_shape=jax.ShapeDtypeStruct((2, state.shape[2], span), BF16),
        scratch_shapes=[pltpu.SemaphoreType.DMA],
        compiler_params=LIMIT,
    )(state)


def picked(ref, which):
    quarter = ref.shape[1] // 2
    return jnp.where(which == 0, ref[:, :quarter], ref[:, quarter:]).astype(F32)


def pass_on_body(here, real_keep, real_got, imag_keep, imag_got, real_send, imag_send):
    major, minor = here[0] // 2, here[0] % 2
    real_send[...] = (picked(real_keep, 1 - minor) + picked(real_got, 1 - minor)).astype(BF16)
    imag_send[...] = (picked(imag_keep, 1 - major) + picked(imag_got, 1 - major)).astype(BF16)


def retain_body(here, *refs, parts, extra):
    major, minor = here[0] // 2, here[0] % 2
    out = refs[-1]
    high = refs[0].shape[0]
    for k in range(parts):
        real_keep, real_got, imag_keep, imag_got = refs[4 * k : 4 * k + 4]
        at = slice(k * high, (k + 1) * high)
        real = picked(real_keep, minor) + picked(real_got, minor)
        imag = picked(imag_keep, major) + picked(imag_got, major)
        if extra:
            real = refs[4 * parts][0, at] + real
            imag = refs[4 * parts][1, at] + imag
        out[0, at] = real
        out[1, at] = imag


def close_body(base, *refs):
    out = refs[-1]
    parts = len(refs) // 2
    high = refs[0].shape[0]
    for k in range(parts):
        at = slice(k * high, (k + 1) * high)
        out[0, at] = base[0, at] + refs[2 * k][...].astype(F32)
        out[1, at] = base[1, at] + refs[2 * k + 1][...].astype(F32)


def kernel_call(fn, scalars, args, out_shape):
    many = isinstance(out_shape, list)
    return pl.pallas_call(
        fn,
        grid_spec=pltpu.PrefetchScalarGridSpec(
            num_scalar_prefetch=len(scalars),
            grid=(1,),
            in_specs=[VMEM] * len(args),
            out_specs=[VMEM] * len(out_shape) if many else VMEM,
        ),
        out_shape=out_shape,
        compiler_params=LIMIT,
    )(*scalars, *args)


def scatter_sum(terms, before, here):
    if len(terms) == 1:
        share = lax.psum_scatter(terms[0], "pole", scatter_dimension=2, tiled=True).astype(F32)
        return share if before is None else before + share
    parts = len(terms) // 4
    high, half = terms[0].shape
    quarter = half // 2
    fields = []
    for k in range(parts):
        real_out, real_keep, imag_out, imag_keep = terms[4 * k : 4 * k + 4]
        real_got = flip(real_out, "pole", 2)
        imag_got = flip(imag_out, "pole", 1)
        fields.append((real_keep, real_got, imag_keep, imag_got))
    lasts = []
    for k in range(parts):
        sends = kernel_call(
            pass_on_body, (here,), fields[k], [jax.ShapeDtypeStruct((high, quarter), BF16)] * 2
        )
        lasts.append(flip(sends[0], "pole", 1))
        lasts.append(flip(sends[1], "pole", 2))
    extra = [] if before is None else [before]
    shape = jax.ShapeDtypeStruct((2, parts * high, quarter), F32)
    flat = [value for field in fields for value in field]
    retain = functools.partial(retain_body, parts=parts, extra=len(extra))
    base = kernel_call(retain, (here,), flat + extra, shape)
    return kernel_call(close_body, (), [base, *lasts], shape)


def spans(width):
    unit = width // 8
    if unit % 128:
        return [width]
    return [3 * unit, 2 * unit, 2 * unit, unit]


def body(local_green, coupling, block_mask, state_in, pole_weight, pole_index):
    local_green, coupling, state_in = (
        pltpu.with_memory_space_constraint(value, pltpu.HBM) for value in (local_green, coupling, state_in)
    )
    ticks = coupling.shape[0]
    width = coupling.shape[4]
    sizes = spans(width)
    starts = [sum(sizes[:c]) for c in range(len(sizes))]
    state = []
    for c, start in enumerate(starts):
        state.append(cut_piece(state_in, start, sizes[c]))
    here = jnp.reshape(lax.axis_index("pole").astype(jnp.int32), (1,))
    factors = []
    density = None
    for tick in range(ticks):
        own = masked_factor(block_mask, coupling, tick)
        factors.append((own, *row_pieces(own)))
    for tick in range(ticks):
        incoming = []
        for c in range(len(sizes)):
            incoming.append(from_behind(state[c], "slab"))
        own, factor, offsets = factors[tick]
        scalars = (jnp.stack([jnp.int32(o) for o in offsets]), pole_index, pole_weight, here)
        before = local_green
        last_tick = tick == ticks - 1
        widths = [width] if last_tick else sizes
        for c, start in enumerate(starts):
            behind, _ = row_pieces(incoming[c])
            last = c == len(sizes) - 1
            outs = fold(
                scalars, own, factor, behind, before, tick, start, c == 0, last, widths if last else [], last_tick
            )
            before = outs[0]
        state = outs[: len(widths)]
        terms = outs[len(widths) :] or weigh(scalars, state, tick)
        density = scatter_sum(terms, density, here)
    return (state[0][None], density)


def solution(mesh):
    placed = (
        P(None, "pole", None, ("slab", "row"), None),
        P(None, "pole", None, ("slab", "row"), None),
        P(None, "pole", ("slab", "row"), None),
        P("pole", None, ("slab", "row"), None),
        P(),
        P(None, "pole", "slab"),
    )
    return jax.shard_map(
        body,
        mesh=mesh,
        in_specs=placed,
        out_specs=(P("pole", None, ("slab", "row"), None), P(None, ("slab", "row"), "pole")),
        check_vma=False,
    )
```

time: 216 us -> 201 us (0.931)
  local copies, waits for them, and re-layouts: 14.1 us -> 2.8 us
  Pallas kernels: 70.8 us -> 64.3 us
  waiting for transfers between devices: 95.5 us -> 101 us
  starting transfers between devices: 33.3 us -> 31 us
    unnamed x39 -> x11, local copies, waits for them, and re-layouts: 13.7 us -> 2.8 us
    ppermute x16 -> x8, waiting for transfers between devices: 79 us -> 89.4 us  [from_behind(): lax.ppermute(block, axis, [(i + 1, i) for i in devices if i + 1 in devices])]
    ppermute x16 -> x8, starting transfers between devices: 20.6 us -> 10.5 us  [from_behind(): lax.ppermute(block, axis, [(i + 1, i) for i in devices if i + 1 in devices])]
    ppermute x26, starting transfers between devices: 12.7 us -> 20.5 us  [flip(): lax.ppermute(block, axis, [(i, i ^ bit) for i in range(lax.axis_size(axis...]
    pallas_call x25 -> x22, Pallas kernels: 68.9 us -> 62.8 us  [the longest x8 50.8 us: fold(): pl.pallas_call(functools.partial(fold_body, pieces=pieces, tick=tick, sta...]
    ppermute x26, waiting for transfers between devices: 16.6 us -> 11.4 us  [flip(): lax.ppermute(block, axis, [(i, i ^ bit) for i in range(lax.axis_size(axis...]
  transfers between devices with their start and end apart: 42 -> 34, of which waited for: 20 -> 13; matrix products, arithmetic and copies ran while one was open for 0% -> 0% of each run, Pallas kernels for 32% -> 30%
where the time goes in v2:
time: 201 us; the launch traced here: 200 us
  waiting for transfers between devices  101 us (50%)
  Pallas kernels  64.3 us (32%)
  starting transfers between devices  31 us (15%)
  local copies, waits for them, and re-layouts  2.8 us (1%)
    ppermute x8, waiting for transfers between devices, from_behind(): lax.ppermute(block, axis, [(i + 1, i) for i in devices if i + 1 in devices])  89.4 us
    pallas_call x8, Pallas kernels, fold(): pl.pallas_call(functools.partial(fold_body, pieces=pieces, tick=tick, sta...  50.8 us
    ppermute x26, starting transfers between devices, flip(): lax.ppermute(block, axis, [(i, i ^ bit) for i in range(lax.axis_size(axis...  20.5 us
    ppermute x26, waiting for transfers between devices, flip(): lax.ppermute(block, axis, [(i, i ^ bit) for i in range(lax.axis_size(axis...  11.4 us
    ppermute x8, starting transfers between devices, from_behind(): lax.ppermute(block, axis, [(i + 1, i) for i in devices if i + 1 in devices])  10.5 us
    pallas_call x2, Pallas kernels, masked_factor(): pl.pallas_call(functools.partial(mask_body, tick=tick), grid_spec=pltpu.P...  5.93 us
    pallas_call x4, Pallas kernels, cut_piece(): pl.pallas_call(functools.partial(cut_body, start=start), in_specs=[HBM],...  4.21 us
  transfers between devices with their start and end apart: 34, of which 13 were waited for; matrix products, arithmetic and copies ran while one was open for 0% of the time, Pallas kernels for 30%

profile of v2, /device:TPU:0, one launch (start us, length us, event | category | flops | bytes accessed | tf_op | source)
XLA Modules:
  0.0 199.9 jit_solution(12868897716788389828)
XLA Ops:
  1.3 3.6 %shard_map.78.refs_4_.refs_5_ = bf16[2,512,1024]{2,1,0:T(8,128)(2,1)} custom-call(s32[2,1,4,8]{3,2,1,0:T(4,128)S(1)} %copy-done.3, bf16[2,1,2,512,1024]{4,3,2,1,0:T(8,128)(2,1)} %coupling_ref.3), custom_call_target="tpu_custom_call" | custom-call | tf_op jit(solution)/shard_map/pallas_call | solution.py:65
  5.5 1.1 shard_map.82
  6.6 1.3 collective-permute-start.8
  7.9 1.1 shard_map.81
  9.0 1.3 collective-permute-start.6
  10.3 1.1 shard_map.80
  11.4 1.3 collective-permute-start.4
  12.7 16.8 %collective-permute-done.8.refs_7_ = bf16[2,512,384]{2,1,0:T(8,128)(2,1)S(1)} collective-permute-done((bf16[2,512,384]{2,1,0:T(8,128)(2,1)S(1)}, bf16[2,512,384]{2,1,0:T(8,128)(2,1)S(1)}, u32[]{:S(2)}, u32[]{:S(2)}) %collective-permute-start.8) | collective-permute-done | bytes 786464 | tf_op jit(solution)/shard_map/ppermute | solution.py:19
  29.5 1.0 shard_map.79
  30.5 1.3 collective-permute-start.2
  31.8 2.3 %shard_map.77.refs_4_.refs_5_ = bf16[2,512,1024]{2,1,0:T(8,128)(2,1)S(1)} custom-call(s32[2,1,4,8]{3,2,1,0:T(4,128)S(1)} %copy-done.3, bf16[2,1,2,512,1024]{4,3,2,1,0:T(8,128)(2,1)} %coupling_ref.3), custom_call_target="tpu_custom_call" | custom-call | tf_op jit(solution)/shard_map/pallas_call | solution.py:65
  34.1 23.4 %collective-permute-done.2.refs_7_ = bf16[2,512,128]{2,1,0:T(8,128)(2,1)} collective-permute-done((bf16[2,512,128]{2,1,0:T(8,128)(2,1)S(1)}, bf16[2,512,128]{2,1,0:T(8,128)(2,1)}, u32[]{:S(2)}, u32[]{:S(2)}) %collective-permute-start.2) | collective-permute-done | bytes 262176 | tf_op jit(solution)/shard_map/ppermute | solution.py:19
  58.1 0.9 copy-done
  59.6 1.1 copy-done.1
  60.7 7.8 %shard_map.83.refs_9_ = f32[2,512,1024]{2,1,0:T(8,128)S(1)} custom-call(s32[2]{0:T(128)S(1)} %pad_add_fusion.refs_0_, s32[2,1,1]{2,1,0:T(1,128)S(1)} %copy.19.refs_1_.pidx, f32[2,16]{1,0:T(2,128)S(1)} %copy-done.2, s32[1]{0:T(128)} %bitcast.2.refs_3_.here, bf16[2,512,1024]{2,1,0:T(8,128)(2,1)} %shard_map.78.refs_4_.refs_5_, ...), custom_call_target="tpu_custom_call" | custom-call | tf_op jit(solution)/shard_map/pallas_call | solution.py:192
  68.6 6.9 %shard_map.84.refs_9_ = f32[2,512,1024]{2,1,0:T(8,128)S(1)} custom-call(s32[2]{0:T(128)S(1)} %pad_add_fusion.refs_0_, s32[2,1,1]{2,1,0:T(1,128)S(1)} %copy.19.refs_1_.pidx, f32[2,16]{1,0:T(2,128)S(1)} %copy-done.2, s32[1]{0:T(128)} %bitcast.2.refs_3_.here, bf16[2,512,1024]{2,1,0:T(8,128)(2,1)} %shard_map.78.refs_4_.refs_5_, ...), custom_call_target="tpu_custom_call", output_to_operand_aliasing={{}: (9, {})} | custom-call | tf_op jit(solution)/shard_map/pallas_call | solution.py:192
  75.5 6.8 %shard_map.85.refs_9_ = f32[2,512,1024]{2,1,0:T(8,128)S(1)} custom-call(s32[2]{0:T(128)S(1)} %pad_add_fusion.refs_0_, s32[2,1,1]{2,1,0:T(1,128)S(1)} %copy.19.refs_1_.pidx, f32[2,16]{1,0:T(2,128)S(1)} %copy-done.2, s32[1]{0:T(128)} %bitcast.2.refs_3_.here, bf16[2,512,1024]{2,1,0:T(8,128)(2,1)} %shard_map.78.refs_4_.refs_5_, ...), custom_call_target="tpu_custom_call", output_to_operand_aliasing={{}: (9, {})} | custom-call | tf_op jit(solution)/shard_map/pallas_call | solution.py:192
  82.2 5.2 %shard_map.86 = (bf16[2,512,384]{2,1,0:T(8,128)(2,1)S(1)}, bf16[2,512,256]{2,1,0:T(8,128)(2,1)S(1)}, bf16[2,512,256]{2,1,0:T(8,128)(2,1)S(1)}, bf16[2,512,128]{2,1,0:T(8,128)(2,1)S(1)}) custom-call(s32[2]{0:T(128)S(1)} %pad_add_fusion.refs_0_, s32[2,1,1]{2,1,0:T(1,128)S(1)} %copy.19.refs_1_.pidx, f32[2,16]{1,0:T(2,128)S(1)} %copy-done.2, ...), custom_call_target="tpu_custom_call" | custom-call | tf_op jit(solution)/shard_map/pallas_call | solution.py:192
  87.4 1.3 collective-permute-start.16
  88.7 1.3 collective-permute-start.14
  90.0 1.3 collective-permute-start.12
  91.3 18.4 %collective-permute-done.16.refs_7_ = bf16[2,512,384]{2,1,0:T(8,128)(2,1)S(1)} collective-permute-done((bf16[2,512,384]{2,1,0:T(8,128)(2,1)S(1)}, bf16[2,512,384]{2,1,0:T(8,128)(2,1)S(1)}, u32[]{:S(2)}, u32[]{:S(2)}) %collective-permute-start.16) | collective-permute-done | bytes 786464 | tf_op jit(solution)/shard_map/ppermute | solution.py:19
  109.7 11.2 %collective-permute-done.14.refs_7_ = bf16[2,512,256]{2,1,0:T(8,128)(2,1)S(1)} collective-permute-done((bf16[2,512,256]{2,1,0:T(8,128)(2,1)S(1)}, bf16[2,512,256]{2,1,0:T(8,128)(2,1)S(1)}, u32[]{:S(2)}, u32[]{:S(2)}) %collective-permute-start.14) | collective-permute-done | bytes 524320 | tf_op jit(solution)/shard_map/ppermute | solution.py:19
  120.9 10.4 %collective-permute-done.12.refs_7_ = bf16[2,512,256]{2,1,0:T(8,128)(2,1)S(1)} collective-permute-done((bf16[2,512,256]{2,1,0:T(8,128)(2,1)S(1)}, bf16[2,512,256]{2,1,0:T(8,128)(2,1)S(1)}, u32[]{:S(2)}, u32[]{:S(2)}) %collective-permute-start.12) | collective-permute-done | bytes 524320 | tf_op jit(solution)/shard_map/ppermute | solution.py:19
  131.3 1.5 collective-permute-start.10
  132.8 9.1 %collective-permute-done.10.refs_7_ = bf16[2,512,128]{2,1,0:T(8,128)(2,1)S(1)} collective-permute-done((bf16[2,512,128]{2,1,0:T(8,128)(2,1)S(1)}, bf16[2,512,128]{2,1,0:T(8,128)(2,1)S(1)}, u32[]{:S(2)}, u32[]{:S(2)}) %collective-permute-start.10) | collective-permute-done | bytes 262176 | tf_op jit(solution)/shard_map/ppermute | solution.py:19
  141.9 1.5 shard_map.91
  143.4 1.7 collective-permute-start.24
  145.1 1.5 collective-permute-start.25
  147.1 7.5 %shard_map.87.refs_9_ = f32[2,512,1024]{2,1,0:T(8,128)S(1)} custom-call(s32[2]{0:T(128)S(1)} %pad_add_fusion.refs_0_, s32[2,1,1]{2,1,0:T(1,128)S(1)} %copy.19.refs_1_.pidx, f32[2,16]{1,0:T(2,128)S(1)} %copy-done.2, s32[1]{0:T(128)} %bitcast.2.refs_3_.here, bf16[2,512,1024]{2,1,0:T(8,128)(2,1)S(1)} %shard_map.77.refs_4_.refs_5_, ...), custom_call_target="tpu_custom_call" | custom-call | tf_op jit(solution)/shard_map/pallas_call | solution.py:192
  155.1 5.4 %shard_map.88.refs_9_ = f32[2,512,1024]{2,1,0:T(8,128)S(1)} custom-call(s32[2]{0:T(128)S(1)} %pad_add_fusion.refs_0_, s32[2,1,1]{2,1,0:T(1,128)S(1)} %copy.19.refs_1_.pidx, f32[2,16]{1,0:T(2,128)S(1)} %copy-done.2, s32[1]{0:T(128)} %bitcast.2.refs_3_.here, bf16[2,512,1024]{2,1,0:T(8,128)(2,1)S(1)} %shard_map.77.refs_4_.refs_5_, ...), custom_call_target="tpu_custom_call", output_to_operand_aliasing={{}: (9, {})} | custom-call | tf_op jit(solution)/shard_map/pallas_call | solution.py:192
  160.5 5.4 %shard_map.89.refs_9_ = f32[2,512,1024]{2,1,0:T(8,128)S(1)} custom-call(s32[2]{0:T(128)S(1)} %pad_add_fusion.refs_0_, s32[2,1,1]{2,1,0:T(1,128)S(1)} %copy.19.refs_1_.pidx, f32[2,16]{1,0:T(2,128)S(1)} %copy-done.2, s32[1]{0:T(128)} %bitcast.2.refs_3_.here, bf16[2,512,1024]{2,1,0:T(8,128)(2,1)S(1)} %shard_map.77.refs_4_.refs_5_, ...), custom_call_target="tpu_custom_call", output_to_operand_aliasing={{}: (9, {})} | custom-call | tf_op jit(solution)/shard_map/pallas_call | solution.py:192
  165.9 5.8 %shard_map.90 = (bf16[2,512,1024]{2,1,0:T(8,128)(2,1)}, bf16[256,512]{1,0:T(8,128)(2,1)S(1)}, bf16[256,512]{1,0:T(8,128)(2,1)S(1)}, bf16[256,512]{1,0:T(8,128)(2...) custom-call(s32[2]{0:T(128)S(1)} %pad_add_fusion.refs_0_, ...), custom_call_target="tpu_custom_call" | custom-call | tf_op jit(solution)/shard_map/pallas_call | solution.py:192
  171.8 1.7 collective-permute-start.20
  173.5 1.5 collective-permute-start.21
  176.0 1.7 collective-permute-start.28
  177.8 3.2 %collective-permute-done.20.refs_5_.real_got = bf16[256,512]{1,0:T(8,128)(2,1)S(1)} collective-permute-done((bf16[256,512]{1,0:T(8,128)(2,1)S(1)}, bf16[256,512]{1,0:T(8,128)(2,1)S(1)}, u32[]{:S(2)}, u32[]{:S(2)}) %collective-permute-start.20) | collective-permute-done | bytes 262176 | tf_op jit(solution)/shard_map/ppermute | solution.py:23
  181.0 1.7 collective-permute-start.29
  182.6 1.5 collective-permute-start.26
  184.2 2.4 %collective-permute-done.18.refs_1_.real_got = bf16[256,512]{1,0:T(8,128)(2,1)S(1)} collective-permute-done((bf16[256,512]{1,0:T(8,128)(2,1)S(1)}, bf16[256,512]{1,0:T(8,128)(2,1)S(1)}, u32[]{:S(2)}, u32[]{:S(2)}) %collective-permute-start.18) | collective-permute-done | bytes 262176 | tf_op jit(solution)/shard_map/ppermute | solution.py:23
  186.6 1.7 collective-permute-start.27
  188.3 1.5 collective-permute-start.32
  189.8 1.2 collective-permute-done.28.refs_2_
  191.4 1.6 collective-permute-start.30
  195.1 1.1 collective-permute-done.32.refs_2_
  196.2 1.4 collective-permute-done.30.refs_0_
  197.6 1.2 collective-permute-done.31.refs_1_
  198.8 1.1 shard_map.99
  (55 shorter events, 7.1 us)
Async XLA Ops:
  0.6 0.7 copy-start.3
  4.9 54.7 %collective-permute-start.1 = (bf16[2,512,1024]{2,1,0:T(8,128)(2,1)}, bf16[2,512,1024]{2,1,0:T(8,128)(2,1)}, u32[]{:S(2)}, u32[]{:S(2)}) collective-permute-start(bf16[2,512,1024]{2,1,0:T(8,128)(2,1)} %shard_map.78.refs_4_.refs_5_), channel_id=1, source_target_pairs={{0,4},{4,0},{1,5},{5,1},{2,6},{6,2},{3,7},{7,3},{8,12},{12,8},{9,1... | collective-permute-start | bytes 6291464 | tf_op jit(solution)/shard_map/ppermute | solution.py:23
  6.6 22.9 %collective-permute-start.8 = (bf16[2,512,384]{2,1,0:T(8,128)(2,1)S(1)}, bf16[2,512,384]{2,1,0:T(8,128)(2,1)S(1)}, u32[]{:S(2)}, u32[]{:S(2)}) collective-permute-start(bf16[2,512,384]{2,1,0:T(8,128)(2,1)S(1)} %shard_map.82), channel_id=1, source_target_pairs={{8,0},{16,8},{24,16},{9,1},{17,9},{25,17},{10,2},{18,10},{26,18},{... | collective-permute-start | bytes 2359304 | tf_op jit(solution)/shard_map/ppermute | solution.py:19
  9.0 48.5 %collective-permute-start.6 = (bf16[2,512,256]{2,1,0:T(8,128)(2,1)S(1)}, bf16[2,512,256]{2,1,0:T(8,128)(2,1)}, u32[]{:S(2)}, u32[]{:S(2)}) collective-permute-start(bf16[2,512,256]{2,1,0:T(8,128)(2,1)S(1)} %shard_map.81), channel_id=1, source_target_pairs={{8,0},{16,8},{24,16},{9,1},{17,9},{25,17},{10,2},{18,10},{26,18},{... | collective-permute-start | bytes 1572872 | tf_op jit(solution)/shard_map/ppermute | solution.py:19
  11.4 48.1 %copy-start.4 = (s32[2,1,1]{0,2,1:T(1,128)S(1)}, s32[2,1,1]{0,2,1:T(1,128)}, u32[]{:S(2)}) copy-start(s32[2,1,1]{0,2,1:T(1,128)} %param.11) | copy-start | bytes 28
  11.4 48.2 %copy-start.2 = (f32[2,16]{1,0:T(2,128)S(1)}, f32[2,16]{1,0:T(2,128)}, u32[]{:S(2)}) copy-start(f32[2,16]{1,0:T(2,128)} %pw.1) | copy-start | bytes 388
  11.4 46.6 %collective-permute-start.4 = (bf16[2,512,256]{2,1,0:T(8,128)(2,1)S(1)}, bf16[2,512,256]{2,1,0:T(8,128)(2,1)S(1)}, u32[]{:S(2)}, u32[]{:S(2)}) collective-permute-start(bf16[2,512,256]{2,1,0:T(8,128)(2,1)S(1)} %shard_map.80), channel_id=1, source_target_pairs={{8,0},{16,8},{24,16},{9,1},{17,9},{25,17},{10,2},{18,10},{26,18},{... | collective-permute-start | bytes 1572872 | tf_op jit(solution)/shard_map/ppermute | solution.py:19
  29.5 28.6 %collective-permute-start.9 = (bf16[2,512,384]{2,1,0:T(8,128)(2,1)S(1)}, bf16[2,512,384]{2,1,0:T(8,128)(2,1)S(1)}, u32[]{:S(2)}, u32[]{:S(2)}) collective-permute-start(bf16[2,512,384]{2,1,0:T(8,128)(2,1)S(1)} %collective-permute-done.8.refs_7_), channel_id=1, source_target_pairs={{0,4},{4,0},{1,5},{5,1},{2,6},{6,2},{3,7},{7,3},{8,12},{12,8},{9,1... | collective-permute-start | bytes 2359304 | tf_op jit(solution)/shard_map/ppermute | solution.py:23
  30.5 27.0 %collective-permute-start.2 = (bf16[2,512,128]{2,1,0:T(8,128)(2,1)S(1)}, bf16[2,512,128]{2,1,0:T(8,128)(2,1)}, u32[]{:S(2)}, u32[]{:S(2)}) collective-permute-start(bf16[2,512,128]{2,1,0:T(8,128)(2,1)S(1)} %shard_map.79), channel_id=1, source_target_pairs={{8,0},{16,8},{24,16},{9,1},{17,9},{25,17},{10,2},{18,10},{26,18},{... | collective-permute-start | bytes 786440 | tf_op jit(solution)/shard_map/ppermute | solution.py:19
  57.5 85.9 %collective-permute-start = (bf16[2,512,1024]{2,1,0:T(8,128)(2,1)S(1)}, bf16[2,512,1024]{2,1,0:T(8,128)(2,1)}, u32[]{:S(2)}, u32[]{:S(2)}) collective-permute-start(bf16[2,512,1024]{2,1,0:T(8,128)(2,1)S(1)} %shard_map.77.refs_4_.refs_5_), channel_id=1, source_target_pairs={{0,4},{4,0},{1,5},{5,1},{2,6},{6,2},{3,7},{7,3},{8,12},{12,8},{9,1... | collective-permute-start | bytes 6291464 | tf_op jit(solution)/shard_map/ppermute | solution.py:23
  57.5 11.0 %collective-permute-start.7 = (bf16[2,512,256]{2,1,0:T(8,128)(2,1)}, bf16[2,512,256]{2,1,0:T(8,128)(2,1)}, u32[]{:S(2)}, u32[]{:S(2)}) collective-permute-start(bf16[2,512,256]{2,1,0:T(8,128)(2,1)} %collective-permute-done.6.refs_7_), channel_id=1, source_target_pairs={{0,4},{4,0},{1,5},{5,1},{2,6},{6,2},{3,7},{7,3},{8,12},{12,8},{9,1... | collective-permute-start | bytes 1572872 | tf_op jit(solution)/shard_map/ppermute | solution.py:23
  58.0 17.4 %collective-permute-start.5 = (bf16[2,512,256]{2,1,0:T(8,128)(2,1)S(1)}, bf16[2,512,256]{2,1,0:T(8,128)(2,1)}, u32[]{:S(2)}, u32[]{:S(2)}) collective-permute-start(bf16[2,512,256]{2,1,0:T(8,128)(2,1)S(1)} %collective-permute-done.4.refs_7_), channel_id=1, source_target_pairs={{0,4},{4,0},{1,5},{5,1},{2,6},{6,2},{3,7},{7,3},{8,12},{12,8},{9,1... | collective-permute-start | bytes 1572872 | tf_op jit(solution)/shard_map/ppermute | solution.py:23
  58.1 0.9 copy-start
  59.0 23.2 %collective-permute-start.3 = (bf16[2,512,128]{2,1,0:T(8,128)(2,1)}, bf16[2,512,128]{2,1,0:T(8,128)(2,1)}, u32[]{:S(2)}, u32[]{:S(2)}) collective-permute-start(bf16[2,512,128]{2,1,0:T(8,128)(2,1)} %collective-permute-done.2.refs_7_), channel_id=1, source_target_pairs={{0,4},{4,0},{1,5},{5,1},{2,6},{6,2},{3,7},{7,3},{8,12},{12,8},{9,1... | collective-permute-start | bytes 786440 | tf_op jit(solution)/shard_map/ppermute | solution.py:23
  59.6 1.1 copy-start.1
  87.4 22.3 %collective-permute-start.16 = (bf16[2,512,384]{2,1,0:T(8,128)(2,1)S(1)}, bf16[2,512,384]{2,1,0:T(8,128)(2,1)S(1)}, u32[]{:S(2)}, u32[]{:S(2)}) collective-permute-start(bf16[2,512,384]{2,1,0:T(8,128)(2,1)S(1)} %get-tuple-element.34.refs_0_), channel_id=1, source_target_pairs={{8,0},{16,8},{24,16},{9,1},{17,9},{25,17},{10,2},{18,10},{26,18},{... | collective-permute-start | bytes 2359304 | tf_op jit(solution)/shard_map/ppermute | solution.py:19
  88.7 32.2 %collective-permute-start.14 = (bf16[2,512,256]{2,1,0:T(8,128)(2,1)S(1)}, bf16[2,512,256]{2,1,0:T(8,128)(2,1)S(1)}, u32[]{:S(2)}, u32[]{:S(2)}) collective-permute-start(bf16[2,512,256]{2,1,0:T(8,128)(2,1)S(1)} %get-tuple-element.33.refs_1_), channel_id=1, source_target_pairs={{8,0},{16,8},{24,16},{9,1},{17,9},{25,17},{10,2},{18,10},{26,18},{... | collective-permute-start | bytes 1572872 | tf_op jit(solution)/shard_map/ppermute | solution.py:19
  90.0 41.3 %collective-permute-start.12 = (bf16[2,512,256]{2,1,0:T(8,128)(2,1)S(1)}, bf16[2,512,256]{2,1,0:T(8,128)(2,1)S(1)}, u32[]{:S(2)}, u32[]{:S(2)}) collective-permute-start(bf16[2,512,256]{2,1,0:T(8,128)(2,1)S(1)} %get-tuple-element.32.refs_2_), channel_id=1, source_target_pairs={{8,0},{16,8},{24,16},{9,1},{17,9},{25,17},{10,2},{18,10},{26,18},{... | collective-permute-start | bytes 1572872 | tf_op jit(solution)/shard_map/ppermute | solution.py:19
  109.7 36.9 %collective-permute-start.17 = (bf16[2,512,384]{2,1,0:T(8,128)(2,1)S(1)}, bf16[2,512,384]{2,1,0:T(8,128)(2,1)S(1)}, u32[]{:S(2)}, u32[]{:S(2)}) collective-permute-start(bf16[2,512,384]{2,1,0:T(8,128)(2,1)S(1)} %collective-permute-done.16.refs_7_), channel_id=1, source_target_pairs={{0,4},{4,0},{1,5},{5,1},{2,6},{6,2},{3,7},{7,3},{8,12},{12,8},{9,1... | collective-permute-start | bytes 2359304 | tf_op jit(solution)/shard_map/ppermute | solution.py:23
  120.9 24.2 %collective-permute-start.15 = (bf16[2,512,256]{2,1,0:T(8,128)(2,1)S(1)}, bf16[2,512,256]{2,1,0:T(8,128)(2,1)S(1)}, u32[]{:S(2)}, u32[]{:S(2)}) collective-permute-start(bf16[2,512,256]{2,1,0:T(8,128)(2,1)S(1)} %collective-permute-done.14.refs_7_), channel_id=1, source_target_pairs={{0,4},{4,0},{1,5},{5,1},{2,6},{6,2},{3,7},{7,3},{8,12},{12,8},{9,1... | collective-permute-start | bytes 1572872 | tf_op jit(solution)/shard_map/ppermute | solution.py:23
  131.3 23.3 %collective-permute-start.13 = (bf16[2,512,256]{2,1,0:T(8,128)(2,1)S(1)}, bf16[2,512,256]{2,1,0:T(8,128)(2,1)S(1)}, u32[]{:S(2)}, u32[]{:S(2)}) collective-permute-start(bf16[2,512,256]{2,1,0:T(8,128)(2,1)S(1)} %collective-permute-done.12.refs_7_), channel_id=1, source_target_pairs={{0,4},{4,0},{1,5},{5,1},{2,6},{6,2},{3,7},{7,3},{8,12},{12,8},{9,1... | collective-permute-start | bytes 1572872 | tf_op jit(solution)/shard_map/ppermute | solution.py:23
  131.3 10.6 %collective-permute-start.10 = (bf16[2,512,128]{2,1,0:T(8,128)(2,1)S(1)}, bf16[2,512,128]{2,1,0:T(8,128)(2,1)S(1)}, u32[]{:S(2)}, u32[]{:S(2)}) collective-permute-start(bf16[2,512,128]{2,1,0:T(8,128)(2,1)S(1)} %get-tuple-element.31.refs_3_), channel_id=1, source_target_pairs={{8,0},{16,8},{24,16},{9,1},{17,9},{25,17},{10,2},{18,10},{26,18},{... | collective-permute-start | bytes 786440 | tf_op jit(solution)/shard_map/ppermute | solution.py:19
  141.9 24.0 %collective-permute-start.11 = (bf16[2,512,128]{2,1,0:T(8,128)(2,1)S(1)}, bf16[2,512,128]{2,1,0:T(8,128)(2,1)S(1)}, u32[]{:S(2)}, u32[]{:S(2)}) collective-permute-start(bf16[2,512,128]{2,1,0:T(8,128)(2,1)S(1)} %collective-permute-done.10.refs_7_), channel_id=1, source_target_pairs={{0,4},{4,0},{1,5},{5,1},{2,6},{6,2},{3,7},{7,3},{8,12},{12,8},{9,1... | collective-permute-start | bytes 786440 | tf_op jit(solution)/shard_map/ppermute | solution.py:23
  143.4 30.1 %collective-permute-start.24 = (bf16[256,512]{1,0:T(8,128)(2,1)S(1)}, bf16[256,512]{1,0:T(8,128)(2,1)S(1)}, u32[]{:S(2)}, u32[]{:S(2)}) collective-permute-start(bf16[256,512]{1,0:T(8,128)(2,1)S(1)} %get-tuple-element.49), channel_id=1, source_target_pairs={{0,2},{1,3},{2,0},{3,1},{4,6},{5,7},{6,4},{7,5},{8,10},{9,11},{10,... | collective-permute-start | bytes 786440 | tf_op jit(solution)/shard_map/ppermute | solution.py:23
  145.1 29.8 %collective-permute-start.25 = (bf16[256,512]{1,0:T(8,128)(2,1)S(1)}, bf16[256,512]{1,0:T(8,128)(2,1)S(1)}, u32[]{:S(2)}, u32[]{:S(2)}) collective-permute-start(bf16[256,512]{1,0:T(8,128)(2,1)S(1)} %get-tuple-element.51), channel_id=1, source_target_pairs={{0,1},{1,0},{2,3},{3,2},{4,5},{5,4},{6,7},{7,6},{8,9},{9,8},{10,11... | collective-permute-start | bytes 786440 | tf_op jit(solution)/shard_map/ppermute | solution.py:23
  146.6 28.9 %collective-permute-start.22 = (bf16[256,512]{1,0:T(8,128)(2,1)S(1)}, bf16[256,512]{1,0:T(8,128)(2,1)S(1)}, u32[]{:S(2)}, u32[]{:S(2)}) collective-permute-start(bf16[256,512]{1,0:T(8,128)(2,1)S(1)} %get-tuple-element.45), channel_id=1, source_target_pairs={{0,2},{1,3},{2,0},{3,1},{4,6},{5,7},{6,4},{7,5},{8,10},{9,11},{10,... | collective-permute-start | bytes 786440 | tf_op jit(solution)/shard_map/ppermute | solution.py:23
  154.6 21.4 %collective-permute-start.23 = (bf16[256,512]{1,0:T(8,128)(2,1)S(1)}, bf16[256,512]{1,0:T(8,128)(2,1)S(1)}, u32[]{:S(2)}, u32[]{:S(2)}) collective-permute-start(bf16[256,512]{1,0:T(8,128)(2,1)S(1)} %get-tuple-element.47), channel_id=1, source_target_pairs={{0,1},{1,0},{2,3},{3,2},{4,5},{5,4},{6,7},{7,6},{8,9},{9,8},{10,11... | collective-permute-start | bytes 786440 | tf_op jit(solution)/shard_map/ppermute | solution.py:23
  171.8 9.2 %collective-permute-start.20 = (bf16[256,512]{1,0:T(8,128)(2,1)S(1)}, bf16[256,512]{1,0:T(8,128)(2,1)S(1)}, u32[]{:S(2)}, u32[]{:S(2)}) collective-permute-start(bf16[256,512]{1,0:T(8,128)(2,1)S(1)} %get-tuple-element.41), channel_id=1, source_target_pairs={{0,2},{1,3},{2,0},{3,1},{4,6},{5,7},{6,4},{7,5},{8,10},{9,11},{10,... | collective-permute-start | bytes 786440 | tf_op jit(solution)/shard_map/ppermute | solution.py:23
  173.5 9.2 %collective-permute-start.21 = (bf16[256,512]{1,0:T(8,128)(2,1)S(1)}, bf16[256,512]{1,0:T(8,128)(2,1)S(1)}, u32[]{:S(2)}, u32[]{:S(2)}) collective-permute-start(bf16[256,512]{1,0:T(8,128)(2,1)S(1)} %get-tuple-element.43), channel_id=1, source_target_pairs={{0,1},{1,0},{2,3},{3,2},{4,5},{5,4},{6,7},{7,6},{8,9},{9,8},{10,11... | collective-permute-start | bytes 786440 | tf_op jit(solution)/shard_map/ppermute | solution.py:23
  174.9 11.6 %collective-permute-start.18 = (bf16[256,512]{1,0:T(8,128)(2,1)S(1)}, bf16[256,512]{1,0:T(8,128)(2,1)S(1)}, u32[]{:S(2)}, u32[]{:S(2)}) collective-permute-start(bf16[256,512]{1,0:T(8,128)(2,1)S(1)} %get-tuple-element.37), channel_id=1, source_target_pairs={{0,2},{1,3},{2,0},{3,1},{4,6},{5,7},{6,4},{7,5},{8,10},{9,11},{10,... | collective-permute-start | bytes 786440 | tf_op jit(solution)/shard_map/ppermute | solution.py:23
  175.5 12.8 %collective-permute-start.19 = (bf16[256,512]{1,0:T(8,128)(2,1)S(1)}, bf16[256,512]{1,0:T(8,128)(2,1)S(1)}, u32[]{:S(2)}, u32[]{:S(2)}) collective-permute-start(bf16[256,512]{1,0:T(8,128)(2,1)S(1)} %get-tuple-element.39), channel_id=1, source_target_pairs={{0,1},{1,0},{2,3},{3,2},{4,5},{5,4},{6,7},{7,6},{8,9},{9,8},{10,11... | collective-permute-start | bytes 786440 | tf_op jit(solution)/shard_map/ppermute | solution.py:23
  176.0 15.1 %collective-permute-start.28 = (bf16[256,256]{1,0:T(8,128)(2,1)S(1)}, bf16[256,256]{1,0:T(8,128)(2,1)S(1)}, u32[]{:S(2)}, u32[]{:S(2)}) collective-permute-start(bf16[256,256]{1,0:T(8,128)(2,1)S(1)} %get-tuple-element.54), channel_id=1, source_target_pairs={{0,1},{1,0},{2,3},{3,2},{4,5},{5,4},{6,7},{7,6},{8,9},{9,8},{10,11... | collective-permute-start | bytes 393224 | tf_op jit(solution)/shard_map/ppermute | solution.py:23
  181.0 10.5 %collective-permute-start.29 = (bf16[256,256]{1,0:T(8,128)(2,1)S(1)}, bf16[256,256]{1,0:T(8,128)(2,1)S(1)}, u32[]{:S(2)}, u32[]{:S(2)}) collective-permute-start(bf16[256,256]{1,0:T(8,128)(2,1)S(1)} %get-tuple-element.55), channel_id=1, source_target_pairs={{0,2},{1,3},{2,0},{3,1},{4,6},{5,7},{6,4},{7,5},{8,10},{9,11},{10,... | collective-permute-start | bytes 393224 | tf_op jit(solution)/shard_map/ppermute | solution.py:23
  182.6 11.2 %collective-permute-start.26 = (bf16[256,256]{1,0:T(8,128)(2,1)S(1)}, bf16[256,256]{1,0:T(8,128)(2,1)S(1)}, u32[]{:S(2)}, u32[]{:S(2)}) collective-permute-start(bf16[256,256]{1,0:T(8,128)(2,1)S(1)} %get-tuple-element.52), channel_id=1, source_target_pairs={{0,1},{1,0},{2,3},{3,2},{4,5},{5,4},{6,7},{7,6},{8,9},{9,8},{10,11... | collective-permute-start | bytes 393224 | tf_op jit(solution)/shard_map/ppermute | solution.py:23
  186.6 8.2 %collective-permute-start.27 = (bf16[256,256]{1,0:T(8,128)(2,1)S(1)}, bf16[256,256]{1,0:T(8,128)(2,1)S(1)}, u32[]{:S(2)}, u32[]{:S(2)}) collective-permute-start(bf16[256,256]{1,0:T(8,128)(2,1)S(1)} %get-tuple-element.53), channel_id=1, source_target_pairs={{0,2},{1,3},{2,0},{3,1},{4,6},{5,7},{6,4},{7,5},{8,10},{9,11},{10,... | collective-permute-start | bytes 393224 | tf_op jit(solution)/shard_map/ppermute | solution.py:23
  188.3 8.0 %collective-permute-start.32 = (bf16[256,256]{1,0:T(8,128)(2,1)S(1)}, bf16[256,256]{1,0:T(8,128)(2,1)S(1)}, u32[]{:S(2)}, u32[]{:S(2)}) collective-permute-start(bf16[256,256]{1,0:T(8,128)(2,1)S(1)} %get-tuple-element.58), channel_id=1, source_target_pairs={{0,1},{1,0},{2,3},{3,2},{4,5},{5,4},{6,7},{7,6},{8,9},{9,8},{10,11... | collective-permute-start | bytes 393224 | tf_op jit(solution)/shard_map/ppermute | solution.py:23
  191.1 5.2 %collective-permute-start.33 = (bf16[256,256]{1,0:T(8,128)(2,1)S(1)}, bf16[256,256]{1,0:T(8,128)(2,1)S(1)}, u32[]{:S(2)}, u32[]{:S(2)}) collective-permute-start(bf16[256,256]{1,0:T(8,128)(2,1)S(1)} %get-tuple-element.59), channel_id=1, source_target_pairs={{0,2},{1,3},{2,0},{3,1},{4,6},{5,7},{6,4},{7,5},{8,10},{9,11},{10,... | collective-permute-start | bytes 393224 | tf_op jit(solution)/shard_map/ppermute | solution.py:23
  191.4 6.2 %collective-permute-start.30 = (bf16[256,256]{1,0:T(8,128)(2,1)S(1)}, bf16[256,256]{1,0:T(8,128)(2,1)S(1)}, u32[]{:S(2)}, u32[]{:S(2)}) collective-permute-start(bf16[256,256]{1,0:T(8,128)(2,1)S(1)} %get-tuple-element.56), channel_id=1, source_target_pairs={{0,1},{1,0},{2,3},{3,2},{4,5},{5,4},{6,7},{7,6},{8,9},{9,8},{10,11... | collective-permute-start | bytes 393224 | tf_op jit(solution)/shard_map/ppermute | solution.py:23
  193.9 5.0 %collective-permute-start.31 = (bf16[256,256]{1,0:T(8,128)(2,1)S(1)}, bf16[256,256]{1,0:T(8,128)(2,1)S(1)}, u32[]{:S(2)}, u32[]{:S(2)}) collective-permute-start(bf16[256,256]{1,0:T(8,128)(2,1)S(1)} %get-tuple-element.57), channel_id=1, source_target_pairs={{0,2},{1,3},{2,0},{3,1},{4,6},{5,7},{6,4},{7,5},{8,10},{9,11},{10,... | collective-permute-start | bytes 393224 | tf_op jit(solution)/shard_map/ppermute | solution.py:23

commit v3 on v2

--- a/solution.py
+++ b/solution.py
@@ -24,15 +24,13 @@
 
 
 def row_pieces(block):
-    rows = block.shape[1]
     count = lax.axis_size("row")
     if count == 1:
-        return [block], [0]
+        return [block]
     if count == 2:
-        here = lax.axis_index("row")
         there = flip(block, "row", 1)
-        return [block, there], [here * rows, (1 - here) * rows]
-    return [lax.all_gather(block, "row", axis=1, tiled=True)], [0]
+        return [block, there]
+    return [lax.all_gather(block, "row", axis=1, tiled=True)]
 
 
 VMEM = pl.BlockSpec(memory_space=pltpu.VMEM)
@@ -85,7 +83,7 @@
 
 
 def fold_body(*refs, pieces, tick, start, first, last, chunks):
-    offs, pidx, pw, here = refs[:4]
+    mine, pidx, pw, here = refs[:4]
     refs = refs[4:]
     own = refs[0]
     factor = refs[1 : 1 + pieces]
@@ -103,7 +101,9 @@
     cols = slice(start, start + span)
     for k in range(pieces):
         size = behind[k].shape[1]
-        at = pl.ds(pl.multiple_of(offs[k], size), size)
+        at = slice(0, size)
+        if pieces == 2:
+            at = pl.ds(pl.multiple_of((mine[0] if k == 0 else 1 - mine[0]) * size, size), size)
         right[at, :span] = behind[k][0]
         right[at, span:] = behind[k][1]
         low[at, :span] = factor[k][0, :, cols]
@@ -144,8 +144,8 @@
 def write_term(real, imag, pidx, pw, here, tick, outs, row):
     real = real.astype(F32)
     imag = imag.astype(F32)
-    w0 = pw[0, pidx[tick, 0, 0]]
-    w1 = pw[1, pidx[tick, 0, 0]]
+    w0 = pw[0, pidx[0, 0, tick]]
+    w1 = pw[1, pidx[0, 0, tick]]
     term_real = (w0 * real - w1 * imag).astype(BF16)
     term_imag = (w0 * imag + w1 * real).astype(BF16)
     high, width = real.shape
@@ -230,21 +230,25 @@
     )(*scalars[1:], *state)
 
 
-def cut_body(src, out, sem, *, start):
+def cut_body(mine, here, src, out, sem, *, start):
     fetch = pltpu.make_async_copy(src.at[0, :, :, pl.ds(start, out.shape[2])], out, sem)
     fetch.start()
     fetch.wait()
 
 
-def cut_piece(state, start, span):
+def cut_piece(mine, here, state, start, span):
     return pl.pallas_call(
         functools.partial(cut_body, start=start),
-        in_specs=[HBM],
-        out_specs=VMEM,
+        grid_spec=pltpu.PrefetchScalarGridSpec(
+            num_scalar_prefetch=2,
+            grid=(1,),
+            in_specs=[HBM],
+            out_specs=VMEM,
+            scratch_shapes=[pltpu.SemaphoreType.DMA],
+        ),
         out_shape=jax.ShapeDtypeStruct((2, state.shape[2], span), BF16),
-        scratch_shapes=[pltpu.SemaphoreType.DMA],
-        compiler_params=LIMIT,
-    )(state)
+        compiler_params=LIMIT,
+    )(mine, here, state)
 
 
 def picked(ref, which):
@@ -342,26 +346,29 @@
     width = coupling.shape[4]
     sizes = spans(width)
     starts = [sum(sizes[:c]) for c in range(len(sizes))]
+    here = jnp.reshape(lax.axis_index("pole").astype(jnp.int32), (1,))
+    mine = jnp.reshape(lax.axis_index("row").astype(jnp.int32), (1,))
+    scalars = (mine, jnp.transpose(pole_index, (1, 2, 0)), pole_weight, here)
     state = []
     for c, start in enumerate(starts):
-        state.append(cut_piece(state_in, start, sizes[c]))
-    here = jnp.reshape(lax.axis_index("pole").astype(jnp.int32), (1,))
+        state.append(cut_piece(mine, here, state_in, start, sizes[c]))
+    owns = []
     factors = []
     density = None
     for tick in range(ticks):
         own = masked_factor(block_mask, coupling, tick)
-        factors.append((own, *row_pieces(own)))
+        owns.append(own)
+        factors.append(row_pieces(own))
     for tick in range(ticks):
         incoming = []
         for c in range(len(sizes)):
             incoming.append(from_behind(state[c], "slab"))
-        own, factor, offsets = factors[tick]
-        scalars = (jnp.stack([jnp.int32(o) for o in offsets]), pole_index, pole_weight, here)
+        own, factor = owns[tick], factors[tick]
         before = local_green
         last_tick = tick == ticks - 1
         widths = [width] if last_tick else sizes
         for c, start in enumerate(starts):
-            behind, _ = row_pieces(incoming[c])
+            behind = row_pieces(incoming[c])
             last = c == len(sizes) - 1
             outs = fold(
                 scalars, own, factor, behind, before, tick, start, c == 0, last, widths if last else [], last_tick

time: 201 us -> 186 us (0.925)
  Pallas kernels: 64.3 us -> 52 us
  local copies, waits for them, and re-layouts: 2.8 us -> 0.7 us
    pallas_call x8, Pallas kernels: 50.8 us -> 39.8 us  [fold(): pl.pallas_call(functools.partial(fold_body, pieces=pieces, tick=tick, sta...]
    unnamed x11 -> x8, local copies, waits for them, and re-layouts: 2.8 us -> 0.7 us
  transfers between devices with their start and end apart: 34 -> 34, of which waited for: 13 -> 13; matrix products, arithmetic and copies ran while one was open for 0% -> 0% of each run, Pallas kernels for 30% -> 26%
where the time goes in v3:
time: 186 us; the launch traced here: 185 us
  waiting for transfers between devices  101 us (54%)
  Pallas kernels  52 us (28%)
  starting transfers between devices  31.1 us (17%)
    ppermute x8, waiting for transfers between devices, from_behind(): lax.ppermute(block, axis, [(i + 1, i) for i in devices if i + 1 in devices])  89.2 us
    pallas_call x8, Pallas kernels, fold(): pl.pallas_call(functools.partial(fold_body, pieces=pieces, tick=tick, sta...  39.8 us
    ppermute x26, starting transfers between devices, flip(): lax.ppermute(block, axis, [(i, i ^ bit) for i in range(lax.axis_size(axis...  20.6 us
    ppermute x26, waiting for transfers between devices, flip(): lax.ppermute(block, axis, [(i, i ^ bit) for i in range(lax.axis_size(axis...  11.4 us
    ppermute x8, starting transfers between devices, from_behind(): lax.ppermute(block, axis, [(i + 1, i) for i in devices if i + 1 in devices])  10.5 us
    pallas_call x2, Pallas kernels, masked_factor(): pl.pallas_call(functools.partial(mask_body, tick=tick), grid_spec=pltpu.P...  4.59 us
    pallas_call x4, Pallas kernels, cut_piece(): pl.pallas_call(functools.partial(cut_body, start=start), grid_spec=pltpu....  4.21 us
  transfers between devices with their start and end apart: 34, of which 13 were waited for; matrix products, arithmetic and copies ran while one was open for 0% of the time, Pallas kernels for 26%

profile of v3, /device:TPU:0, one launch (start us, length us, event | category | flops | bytes accessed | tf_op | source)
XLA Modules:
  0.0 185.4 jit_solution(14467772117867668734)
XLA Ops:
  1.3 2.3 %shard_map.78.refs_4_.refs_5_ = bf16[2,512,1024]{2,1,0:T(8,128)(2,1)S(1)} custom-call(s32[2,1,4,8]{3,2,1,0:T(4,128)S(1)} %copy-done.2, bf16[2,1,2,512,1024]{4,3,2,1,0:T(8,128)(2,1)} %coupling_ref.3), custom_call_target="tpu_custom_call" | custom-call | tf_op jit(solution)/shard_map/pallas_call | solution.py:63
  4.2 1.1 shard_map.82
  5.3 1.3 collective-permute-start.8
  6.6 1.1 shard_map.81
  7.7 1.3 collective-permute-start.6
  9.0 1.1 shard_map.80
  10.1 1.3 collective-permute-start.4
  11.4 16.8 %collective-permute-done.8.refs_7_ = bf16[2,512,384]{2,1,0:T(8,128)(2,1)S(1)} collective-permute-done((bf16[2,512,384]{2,1,0:T(8,128)(2,1)S(1)}, bf16[2,512,384]{2,1,0:T(8,128)(2,1)S(1)}, u32[]{:S(2)}, u32[]{:S(2)}) %collective-permute-start.8) | collective-permute-done | bytes 786464 | tf_op jit(solution)/shard_map/ppermute | solution.py:19
  28.2 1.0 shard_map.79
  29.2 1.3 collective-permute-start.2
  30.5 2.3 %shard_map.77.refs_4_.refs_5_ = bf16[2,512,1024]{2,1,0:T(8,128)(2,1)S(1)} custom-call(s32[2,1,4,8]{3,2,1,0:T(4,128)S(1)} %copy-done.3, bf16[2,1,2,512,1024]{4,3,2,1,0:T(8,128)(2,1)} %coupling_ref.3), custom_call_target="tpu_custom_call" | custom-call | tf_op jit(solution)/shard_map/pallas_call | solution.py:63
  32.8 23.3 %collective-permute-done.2.refs_7_ = bf16[2,512,128]{2,1,0:T(8,128)(2,1)S(1)} collective-permute-done((bf16[2,512,128]{2,1,0:T(8,128)(2,1)S(1)}, bf16[2,512,128]{2,1,0:T(8,128)(2,1)S(1)}, u32[]{:S(2)}, u32[]{:S(2)}) %collective-permute-start.2) | collective-permute-done | bytes 262176 | tf_op jit(solution)/shard_map/ppermute | solution.py:19
  57.1 7.5 %shard_map.83.refs_9_ = f32[2,512,1024]{2,1,0:T(8,128)S(1)} custom-call(s32[1]{0:T(128)} %bitcast.mine.refs_0_, s32[1,1,2]{2,1,0:T(1,128)S(1)} %bitcast.4, f32[2,16]{1,0:T(2,128)S(1)} %copy-done, s32[1]{0:T(128)} %bitcast.2.here.refs_3_, bf16[2,512,1024]{2,1,0:T(8,128)(2,1)S(1)} %shard_map.78.refs_4_.refs_5_, ...), custom_call_target="tpu_custom_call" | custom-call | tf_op jit(solution)/shard_map/pallas_call | solution.py:192
  64.6 5.4 %shard_map.84.refs_9_ = f32[2,512,1024]{2,1,0:T(8,128)S(1)} custom-call(s32[1]{0:T(128)} %bitcast.mine.refs_0_, s32[1,1,2]{2,1,0:T(1,128)S(1)} %bitcast.5, f32[2,16]{1,0:T(2,128)S(1)} %copy-done, s32[1]{0:T(128)} %bitcast.2.here.refs_3_, bf16[2,512,1024]{2,1,0:T(8,128)(2,1)S(1)} %shard_map.78.refs_4_.refs_5_, ...), custom_call_target="tpu_custom_call", output_to_operand_aliasing={{}: (9, {})} | custom-call | tf_op jit(solution)/shard_map/pallas_call | solution.py:192
  70.0 5.4 %shard_map.85.refs_9_ = f32[2,512,1024]{2,1,0:T(8,128)S(1)} custom-call(s32[1]{0:T(128)} %bitcast.mine.refs_0_, s32[1,1,2]{2,1,0:T(1,128)S(1)} %bitcast.6, f32[2,16]{1,0:T(2,128)S(1)} %copy-done, s32[1]{0:T(128)} %bitcast.2.here.refs_3_, bf16[2,512,1024]{2,1,0:T(8,128)(2,1)S(1)} %shard_map.78.refs_4_.refs_5_, ...), custom_call_target="tpu_custom_call", output_to_operand_aliasing={{}: (9, {})} | custom-call | tf_op jit(solution)/shard_map/pallas_call | solution.py:192
  75.5 3.8 %shard_map.86 = (bf16[2,512,384]{2,1,0:T(8,128)(2,1)S(1)}, bf16[2,512,256]{2,1,0:T(8,128)(2,1)S(1)}, bf16[2,512,256]{2,1,0:T(8,128)(2,1)S(1)}, bf16[2,512,128]{2,1,0:T(8,128)(2,1)S(1)}) custom-call(s32[1]{0:T(128)} %bitcast.mine.refs_0_, s32[1,1,2]{2,1,0:T(1,128)S(1)} %bitcast.7, f32[2,16]{1,0:T(2,128)S(1)} %copy-done, s32[1]{0:T(128)} %bitcast.2.here.refs_3_, ...), custom_call_target="tpu_custom_call" | custom-call | tf_op jit(solution)/shard_map/pallas_call | solution.py:192
  79.3 1.3 collective-permute-start.16
  80.6 1.3 collective-permute-start.14
  81.9 1.3 collective-permute-start.12
  83.2 18.4 %collective-permute-done.16.refs_7_ = bf16[2,512,384]{2,1,0:T(8,128)(2,1)S(1)} collective-permute-done((bf16[2,512,384]{2,1,0:T(8,128)(2,1)S(1)}, bf16[2,512,384]{2,1,0:T(8,128)(2,1)S(1)}, u32[]{:S(2)}, u32[]{:S(2)}) %collective-permute-start.16) | collective-permute-done | bytes 786464 | tf_op jit(solution)/shard_map/ppermute | solution.py:19
  101.6 11.2 %collective-permute-done.14.refs_7_ = bf16[2,512,256]{2,1,0:T(8,128)(2,1)S(1)} collective-permute-done((bf16[2,512,256]{2,1,0:T(8,128)(2,1)S(1)}, bf16[2,512,256]{2,1,0:T(8,128)(2,1)S(1)}, u32[]{:S(2)}, u32[]{:S(2)}) %collective-permute-start.14) | collective-permute-done | bytes 524320 | tf_op jit(solution)/shard_map/ppermute | solution.py:19
  112.8 10.3 %collective-permute-done.12.refs_7_ = bf16[2,512,256]{2,1,0:T(8,128)(2,1)S(1)} collective-permute-done((bf16[2,512,256]{2,1,0:T(8,128)(2,1)S(1)}, bf16[2,512,256]{2,1,0:T(8,128)(2,1)S(1)}, u32[]{:S(2)}, u32[]{:S(2)}) %collective-permute-start.12) | collective-permute-done | bytes 524320 | tf_op jit(solution)/shard_map/ppermute | solution.py:19
  123.2 1.5 collective-permute-start.10
  124.6 9.1 %collective-permute-done.10.refs_7_ = bf16[2,512,128]{2,1,0:T(8,128)(2,1)S(1)} collective-permute-done((bf16[2,512,128]{2,1,0:T(8,128)(2,1)S(1)}, bf16[2,512,128]{2,1,0:T(8,128)(2,1)S(1)}, u32[]{:S(2)}, u32[]{:S(2)}) %collective-permute-start.10) | collective-permute-done | bytes 262176 | tf_op jit(solution)/shard_map/ppermute | solution.py:19
  133.8 1.5 shard_map.91
  135.2 1.8 collective-permute-start.24
  137.0 1.5 collective-permute-start.25
  139.0 5.9 %shard_map.87.refs_9_ = f32[2,512,1024]{2,1,0:T(8,128)S(1)} custom-call(s32[1]{0:T(128)} %bitcast.mine.refs_0_, s32[1,1,2]{2,1,0:T(1,128)S(1)} %bitcast.9, f32[2,16]{1,0:T(2,128)S(1)} %copy-done, s32[1]{0:T(128)} %bitcast.2.here.refs_3_, bf16[2,512,1024]{2,1,0:T(8,128)(2,1)S(1)} %shard_map.77.refs_4_.refs_5_, ...), custom_call_target="tpu_custom_call" | custom-call | tf_op jit(solution)/shard_map/pallas_call | solution.py:192
  145.3 3.8 %shard_map.88.refs_9_ = f32[2,512,1024]{2,1,0:T(8,128)S(1)} custom-call(s32[1]{0:T(128)} %bitcast.mine.refs_0_, s32[1,1,2]{2,1,0:T(1,128)S(1)} %bitcast.10, f32[2,16]{1,0:T(2,128)S(1)} %copy-done, s32[1]{0:T(128)} %bitcast.2.here.refs_3_, bf16[2,512,1024]{2,1,0:T(8,128)(2,1)S(1)} %shard_map.77.refs_4_.refs_5_, ...), custom_call_target="tpu_custom_call", output_to_operand_aliasing={{}: (9, {})} | custom-call | tf_op jit(solution)/shard_map/pallas_call | solution.py:192
  149.2 3.8 %shard_map.89.refs_9_ = f32[2,512,1024]{2,1,0:T(8,128)S(1)} custom-call(s32[1]{0:T(128)} %bitcast.mine.refs_0_, s32[1,1,2]{2,1,0:T(1,128)S(1)} %bitcast.11, f32[2,16]{1,0:T(2,128)S(1)} %copy-done, s32[1]{0:T(128)} %bitcast.2.here.refs_3_, bf16[2,512,1024]{2,1,0:T(8,128)(2,1)S(1)} %shard_map.77.refs_4_.refs_5_, ...), custom_call_target="tpu_custom_call", output_to_operand_aliasing={{}: (9, {})} | custom-call | tf_op jit(solution)/shard_map/pallas_call | solution.py:192
  153.0 4.2 %shard_map.90 = (bf16[2,512,1024]{2,1,0:T(8,128)(2,1)}, bf16[256,512]{1,0:T(8,128)(2,1)S(1)}, bf16[256,512]{1,0:T(8,128)(2,1)S(1)}, bf16[256,512]{1,0:T(8,128)(2...) custom-call(s32[1]{0:T(128)} %bitcast.mine.refs_0_, ...), custom_call_target="tpu_custom_call" | custom-call | tf_op jit(solution)/shard_map/pallas_call | solution.py:192
  157.2 1.7 collective-permute-start.20
  158.9 1.5 collective-permute-start.21
  161.4 1.7 collective-permute-start.28
  163.2 3.2 %collective-permute-done.20.refs_5_.real_got = bf16[256,512]{1,0:T(8,128)(2,1)S(1)} collective-permute-done((bf16[256,512]{1,0:T(8,128)(2,1)S(1)}, bf16[256,512]{1,0:T(8,128)(2,1)S(1)}, u32[]{:S(2)}, u32[]{:S(2)}) %collective-permute-start.20) | collective-permute-done | bytes 262176 | tf_op jit(solution)/shard_map/ppermute | solution.py:23
  166.4 1.7 collective-permute-start.29
  168.1 1.5 collective-permute-start.26
  169.7 2.4 %collective-permute-done.18.refs_1_.real_got = bf16[256,512]{1,0:T(8,128)(2,1)S(1)} collective-permute-done((bf16[256,512]{1,0:T(8,128)(2,1)S(1)}, bf16[256,512]{1,0:T(8,128)(2,1)S(1)}, u32[]{:S(2)}, u32[]{:S(2)}) %collective-permute-start.18) | collective-permute-done | bytes 262176 | tf_op jit(solution)/shard_map/ppermute | solution.py:23
  172.0 1.7 collective-permute-start.27
  173.7 1.5 collective-permute-start.32
  175.3 1.2 collective-permute-done.28.refs_2_
  176.9 1.7 collective-permute-start.30
  178.5 0.8 collective-permute-done.26.refs_0_
  179.3 0.7 collective-permute-start.31
  180.5 1.2 collective-permute-done.32.refs_2_
  181.7 1.4 collective-permute-done.30.refs_0_
  183.1 1.2 collective-permute-done.31.refs_1_
  184.3 1.1 shard_map.99
  (51 shorter events, 5.4 us)
Async XLA Ops:
  0.6 0.7 copy-start.2
  3.6 53.5 %collective-permute-start.1 = (bf16[2,512,1024]{2,1,0:T(8,128)(2,1)S(1)}, bf16[2,512,1024]{2,1,0:T(8,128)(2,1)}, u32[]{:S(2)}, u32[]{:S(2)}) collective-permute-start(bf16[2,512,1024]{2,1,0:T(8,128)(2,1)S(1)} %shard_map.78.refs_4_.refs_5_), channel_id=1, source_target_pairs={{0,4},{4,0},{1,5},{5,1},{2,6},{6,2},{3,7},{7,3},{8,12},{12,8},{9,1... | collective-permute-start | bytes 6291464 | tf_op jit(solution)/shard_map/ppermute | solution.py:23
  5.3 25.2 %copy-start.3 = (s32[2,1,4,8]{3,2,1,0:T(4,128)S(1)}, s32[2,1,4,8]{3,2,1,0:T(4,128)}, u32[]{:S(2)}) copy-start(s32[2,1,4,8]{3,2,1,0:T(4,128)} %mask_ref.3) | copy-start | bytes 772
  5.3 22.9 %collective-permute-start.8 = (bf16[2,512,384]{2,1,0:T(8,128)(2,1)S(1)}, bf16[2,512,384]{2,1,0:T(8,128)(2,1)S(1)}, u32[]{:S(2)}, u32[]{:S(2)}) collective-permute-start(bf16[2,512,384]{2,1,0:T(8,128)(2,1)S(1)} %shard_map.82), channel_id=1, source_target_pairs={{8,0},{16,8},{24,16},{9,1},{17,9},{25,17},{10,2},{18,10},{26,18},{... | collective-permute-start | bytes 2359304 | tf_op jit(solution)/shard_map/ppermute | solution.py:19
  7.7 48.4 %collective-permute-start.6 = (bf16[2,512,256]{2,1,0:T(8,128)(2,1)S(1)}, bf16[2,512,256]{2,1,0:T(8,128)(2,1)S(1)}, u32[]{:S(2)}, u32[]{:S(2)}) collective-permute-start(bf16[2,512,256]{2,1,0:T(8,128)(2,1)S(1)} %shard_map.81), channel_id=1, source_target_pairs={{8,0},{16,8},{24,16},{9,1},{17,9},{25,17},{10,2},{18,10},{26,18},{... | collective-permute-start | bytes 1572872 | tf_op jit(solution)/shard_map/ppermute | solution.py:19
  10.1 47.1 %copy-start = (f32[2,16]{1,0:T(2,128)S(1)}, f32[2,16]{1,0:T(2,128)}, u32[]{:S(2)}) copy-start(f32[2,16]{1,0:T(2,128)} %pw.1) | copy-start | bytes 388
  10.1 47.1 %copy-start.1 = (s32[2,1,1]{0,2,1:T(1,128)S(1)}, s32[2,1,1]{0,2,1:T(1,128)}, u32[]{:S(2)}) copy-start(s32[2,1,1]{0,2,1:T(1,128)} %param.11) | copy-start | bytes 28
  10.1 46.5 %collective-permute-start.4 = (bf16[2,512,256]{2,1,0:T(8,128)(2,1)S(1)}, bf16[2,512,256]{2,1,0:T(8,128)(2,1)S(1)}, u32[]{:S(2)}, u32[]{:S(2)}) collective-permute-start(bf16[2,512,256]{2,1,0:T(8,128)(2,1)S(1)} %shard_map.80), channel_id=1, source_target_pairs={{8,0},{16,8},{24,16},{9,1},{17,9},{25,17},{10,2},{18,10},{26,18},{... | collective-permute-start | bytes 1572872 | tf_op jit(solution)/shard_map/ppermute | solution.py:19
  28.2 28.5 %collective-permute-start.9 = (bf16[2,512,384]{2,1,0:T(8,128)(2,1)S(1)}, bf16[2,512,384]{2,1,0:T(8,128)(2,1)S(1)}, u32[]{:S(2)}, u32[]{:S(2)}) collective-permute-start(bf16[2,512,384]{2,1,0:T(8,128)(2,1)S(1)} %collective-permute-done.8.refs_7_), channel_id=1, source_target_pairs={{0,4},{4,0},{1,5},{5,1},{2,6},{6,2},{3,7},{7,3},{8,12},{12,8},{9,1... | collective-permute-start | bytes 2359304 | tf_op jit(solution)/shard_map/ppermute | solution.py:23
  29.2 26.9 %collective-permute-start.2 = (bf16[2,512,128]{2,1,0:T(8,128)(2,1)S(1)}, bf16[2,512,128]{2,1,0:T(8,128)(2,1)S(1)}, u32[]{:S(2)}, u32[]{:S(2)}) collective-permute-start(bf16[2,512,128]{2,1,0:T(8,128)(2,1)S(1)} %shard_map.79), channel_id=1, source_target_pairs={{8,0},{16,8},{24,16},{9,1},{17,9},{25,17},{10,2},{18,10},{26,18},{... | collective-permute-start | bytes 786440 | tf_op jit(solution)/shard_map/ppermute | solution.py:19
  56.1 79.1 %collective-permute-start = (bf16[2,512,1024]{2,1,0:T(8,128)(2,1)S(1)}, bf16[2,512,1024]{2,1,0:T(8,128)(2,1)S(1)}, u32[]{:S(2)}, u32[]{:S(2)}) collective-permute-start(bf16[2,512,1024]{2,1,0:T(8,128)(2,1)S(1)} %shard_map.77.refs_4_.refs_5_), channel_id=1, source_target_pairs={{0,4},{4,0},{1,5},{5,1},{2,6},{6,2},{3,7},{7,3},{8,12},{12,8},{9,1... | collective-permute-start | bytes 6291464 | tf_op jit(solution)/shard_map/ppermute | solution.py:23
  56.1 8.5 %collective-permute-start.7 = (bf16[2,512,256]{2,1,0:T(8,128)(2,1)S(1)}, bf16[2,512,256]{2,1,0:T(8,128)(2,1)S(1)}, u32[]{:S(2)}, u32[]{:S(2)}) collective-permute-start(bf16[2,512,256]{2,1,0:T(8,128)(2,1)S(1)} %collective-permute-done.6.refs_7_), channel_id=1, source_target_pairs={{0,4},{4,0},{1,5},{5,1},{2,6},{6,2},{3,7},{7,3},{8,12},{12,8},{9,1... | collective-permute-start | bytes 1572872 | tf_op jit(solution)/shard_map/ppermute | solution.py:23
  56.6 13.4 %collective-permute-start.5 = (bf16[2,512,256]{2,1,0:T(8,128)(2,1)S(1)}, bf16[2,512,256]{2,1,0:T(8,128)(2,1)S(1)}, u32[]{:S(2)}, u32[]{:S(2)}) collective-permute-start(bf16[2,512,256]{2,1,0:T(8,128)(2,1)S(1)} %collective-permute-done.4.refs_7_), channel_id=1, source_target_pairs={{0,4},{4,0},{1,5},{5,1},{2,6},{6,2},{3,7},{7,3},{8,12},{12,8},{9,1... | collective-permute-start | bytes 1572872 | tf_op jit(solution)/shard_map/ppermute | solution.py:23
  56.7 18.8 %collective-permute-start.3 = (bf16[2,512,128]{2,1,0:T(8,128)(2,1)S(1)}, bf16[2,512,128]{2,1,0:T(8,128)(2,1)S(1)}, u32[]{:S(2)}, u32[]{:S(2)}) collective-permute-start(bf16[2,512,128]{2,1,0:T(8,128)(2,1)S(1)} %collective-permute-done.2.refs_7_), channel_id=1, source_target_pairs={{0,4},{4,0},{1,5},{5,1},{2,6},{6,2},{3,7},{7,3},{8,12},{12,8},{9,1... | collective-permute-start | bytes 786440 | tf_op jit(solution)/shard_map/ppermute | solution.py:23
  79.3 22.3 %collective-permute-start.16 = (bf16[2,512,384]{2,1,0:T(8,128)(2,1)S(1)}, bf16[2,512,384]{2,1,0:T(8,128)(2,1)S(1)}, u32[]{:S(2)}, u32[]{:S(2)}) collective-permute-start(bf16[2,512,384]{2,1,0:T(8,128)(2,1)S(1)} %get-tuple-element.34.refs_0_), channel_id=1, source_target_pairs={{8,0},{16,8},{24,16},{9,1},{17,9},{25,17},{10,2},{18,10},{26,18},{... | collective-permute-start | bytes 2359304 | tf_op jit(solution)/shard_map/ppermute | solution.py:19
  80.6 32.2 %collective-permute-start.14 = (bf16[2,512,256]{2,1,0:T(8,128)(2,1)S(1)}, bf16[2,512,256]{2,1,0:T(8,128)(2,1)S(1)}, u32[]{:S(2)}, u32[]{:S(2)}) collective-permute-start(bf16[2,512,256]{2,1,0:T(8,128)(2,1)S(1)} %get-tuple-element.33.refs_1_), channel_id=1, source_target_pairs={{8,0},{16,8},{24,16},{9,1},{17,9},{25,17},{10,2},{18,10},{26,18},{... | collective-permute-start | bytes 1572872 | tf_op jit(solution)/shard_map/ppermute | solution.py:19
  81.9 41.3 %collective-permute-start.12 = (bf16[2,512,256]{2,1,0:T(8,128)(2,1)S(1)}, bf16[2,512,256]{2,1,0:T(8,128)(2,1)S(1)}, u32[]{:S(2)}, u32[]{:S(2)}) collective-permute-start(bf16[2,512,256]{2,1,0:T(8,128)(2,1)S(1)} %get-tuple-element.32.refs_2_), channel_id=1, source_target_pairs={{8,0},{16,8},{24,16},{9,1},{17,9},{25,17},{10,2},{18,10},{26,18},{... | collective-permute-start | bytes 1572872 | tf_op jit(solution)/shard_map/ppermute | solution.py:19
  101.6 36.9 %collective-permute-start.17 = (bf16[2,512,384]{2,1,0:T(8,128)(2,1)S(1)}, bf16[2,512,384]{2,1,0:T(8,128)(2,1)S(1)}, u32[]{:S(2)}, u32[]{:S(2)}) collective-permute-start(bf16[2,512,384]{2,1,0:T(8,128)(2,1)S(1)} %collective-permute-done.16.refs_7_), channel_id=1, source_target_pairs={{0,4},{4,0},{1,5},{5,1},{2,6},{6,2},{3,7},{7,3},{8,12},{12,8},{9,1... | collective-permute-start | bytes 2359304 | tf_op jit(solution)/shard_map/ppermute | solution.py:23
  112.8 24.2 %collective-permute-start.15 = (bf16[2,512,256]{2,1,0:T(8,128)(2,1)S(1)}, bf16[2,512,256]{2,1,0:T(8,128)(2,1)S(1)}, u32[]{:S(2)}, u32[]{:S(2)}) collective-permute-start(bf16[2,512,256]{2,1,0:T(8,128)(2,1)S(1)} %collective-permute-done.14.refs_7_), channel_id=1, source_target_pairs={{0,4},{4,0},{1,5},{5,1},{2,6},{6,2},{3,7},{7,3},{8,12},{12,8},{9,1... | collective-permute-start | bytes 1572872 | tf_op jit(solution)/shard_map/ppermute | solution.py:23
  123.1 21.7 %collective-permute-start.13 = (bf16[2,512,256]{2,1,0:T(8,128)(2,1)S(1)}, bf16[2,512,256]{2,1,0:T(8,128)(2,1)S(1)}, u32[]{:S(2)}, u32[]{:S(2)}) collective-permute-start(bf16[2,512,256]{2,1,0:T(8,128)(2,1)S(1)} %collective-permute-done.12.refs_7_), channel_id=1, source_target_pairs={{0,4},{4,0},{1,5},{5,1},{2,6},{6,2},{3,7},{7,3},{8,12},{12,8},{9,1... | collective-permute-start | bytes 1572872 | tf_op jit(solution)/shard_map/ppermute | solution.py:23
  123.2 10.6 %collective-permute-start.10 = (bf16[2,512,128]{2,1,0:T(8,128)(2,1)S(1)}, bf16[2,512,128]{2,1,0:T(8,128)(2,1)S(1)}, u32[]{:S(2)}, u32[]{:S(2)}) collective-permute-start(bf16[2,512,128]{2,1,0:T(8,128)(2,1)S(1)} %get-tuple-element.31.refs_3_), channel_id=1, source_target_pairs={{8,0},{16,8},{24,16},{9,1},{17,9},{25,17},{10,2},{18,10},{26,18},{... | collective-permute-start | bytes 786440 | tf_op jit(solution)/shard_map/ppermute | solution.py:19
  133.8 19.2 %collective-permute-start.11 = (bf16[2,512,128]{2,1,0:T(8,128)(2,1)S(1)}, bf16[2,512,128]{2,1,0:T(8,128)(2,1)S(1)}, u32[]{:S(2)}, u32[]{:S(2)}) collective-permute-start(bf16[2,512,128]{2,1,0:T(8,128)(2,1)S(1)} %collective-permute-done.10.refs_7_), channel_id=1, source_target_pairs={{0,4},{4,0},{1,5},{5,1},{2,6},{6,2},{3,7},{7,3},{8,12},{12,8},{9,1... | collective-permute-start | bytes 786440 | tf_op jit(solution)/shard_map/ppermute | solution.py:23
  135.2 23.7 %collective-permute-start.24 = (bf16[256,512]{1,0:T(8,128)(2,1)S(1)}, bf16[256,512]{1,0:T(8,128)(2,1)S(1)}, u32[]{:S(2)}, u32[]{:S(2)}) collective-permute-start(bf16[256,512]{1,0:T(8,128)(2,1)S(1)} %get-tuple-element.49), channel_id=1, source_target_pairs={{0,2},{1,3},{2,0},{3,1},{4,6},{5,7},{6,4},{7,5},{8,10},{9,11},{10,... | collective-permute-start | bytes 786440 | tf_op jit(solution)/shard_map/ppermute | solution.py:23
  137.0 23.4 %collective-permute-start.25 = (bf16[256,512]{1,0:T(8,128)(2,1)S(1)}, bf16[256,512]{1,0:T(8,128)(2,1)S(1)}, u32[]{:S(2)}, u32[]{:S(2)}) collective-permute-start(bf16[256,512]{1,0:T(8,128)(2,1)S(1)} %get-tuple-element.51), channel_id=1, source_target_pairs={{0,1},{1,0},{2,3},{3,2},{4,5},{5,4},{6,7},{7,6},{8,9},{9,8},{10,11... | collective-permute-start | bytes 786440 | tf_op jit(solution)/shard_map/ppermute | solution.py:23
  138.5 22.5 %collective-permute-start.22 = (bf16[256,512]{1,0:T(8,128)(2,1)S(1)}, bf16[256,512]{1,0:T(8,128)(2,1)S(1)}, u32[]{:S(2)}, u32[]{:S(2)}) collective-permute-start(bf16[256,512]{1,0:T(8,128)(2,1)S(1)} %get-tuple-element.45), channel_id=1, source_target_pairs={{0,2},{1,3},{2,0},{3,1},{4,6},{5,7},{6,4},{7,5},{8,10},{9,11},{10,... | collective-permute-start | bytes 786440 | tf_op jit(solution)/shard_map/ppermute | solution.py:23
  144.9 16.5 %collective-permute-start.23 = (bf16[256,512]{1,0:T(8,128)(2,1)S(1)}, bf16[256,512]{1,0:T(8,128)(2,1)S(1)}, u32[]{:S(2)}, u32[]{:S(2)}) collective-permute-start(bf16[256,512]{1,0:T(8,128)(2,1)S(1)} %get-tuple-element.47), channel_id=1, source_target_pairs={{0,1},{1,0},{2,3},{3,2},{4,5},{5,4},{6,7},{7,6},{8,9},{9,8},{10,11... | collective-permute-start | bytes 786440 | tf_op jit(solution)/shard_map/ppermute | solution.py:23
  157.2 9.2 %collective-permute-start.20 = (bf16[256,512]{1,0:T(8,128)(2,1)S(1)}, bf16[256,512]{1,0:T(8,128)(2,1)S(1)}, u32[]{:S(2)}, u32[]{:S(2)}) collective-permute-start(bf16[256,512]{1,0:T(8,128)(2,1)S(1)} %get-tuple-element.41), channel_id=1, source_target_pairs={{0,2},{1,3},{2,0},{3,1},{4,6},{5,7},{6,4},{7,5},{8,10},{9,11},{10,... | collective-permute-start | bytes 786440 | tf_op jit(solution)/shard_map/ppermute | solution.py:23
  158.9 9.2 %collective-permute-start.21 = (bf16[256,512]{1,0:T(8,128)(2,1)S(1)}, bf16[256,512]{1,0:T(8,128)(2,1)S(1)}, u32[]{:S(2)}, u32[]{:S(2)}) collective-permute-start(bf16[256,512]{1,0:T(8,128)(2,1)S(1)} %get-tuple-element.43), channel_id=1, source_target_pairs={{0,1},{1,0},{2,3},{3,2},{4,5},{5,4},{6,7},{7,6},{8,9},{9,8},{10,11... | collective-permute-start | bytes 786440 | tf_op jit(solution)/shard_map/ppermute | solution.py:23
  160.4 11.6 %collective-permute-start.18 = (bf16[256,512]{1,0:T(8,128)(2,1)S(1)}, bf16[256,512]{1,0:T(8,128)(2,1)S(1)}, u32[]{:S(2)}, u32[]{:S(2)}) collective-permute-start(bf16[256,512]{1,0:T(8,128)(2,1)S(1)} %get-tuple-element.37), channel_id=1, source_target_pairs={{0,2},{1,3},{2,0},{3,1},{4,6},{5,7},{6,4},{7,5},{8,10},{9,11},{10,... | collective-permute-start | bytes 786440 | tf_op jit(solution)/shard_map/ppermute | solution.py:23
  160.9 12.8 %collective-permute-start.19 = (bf16[256,512]{1,0:T(8,128)(2,1)S(1)}, bf16[256,512]{1,0:T(8,128)(2,1)S(1)}, u32[]{:S(2)}, u32[]{:S(2)}) collective-permute-start(bf16[256,512]{1,0:T(8,128)(2,1)S(1)} %get-tuple-element.39), channel_id=1, source_target_pairs={{0,1},{1,0},{2,3},{3,2},{4,5},{5,4},{6,7},{7,6},{8,9},{9,8},{10,11... | collective-permute-start | bytes 786440 | tf_op jit(solution)/shard_map/ppermute | solution.py:23
  161.4 15.1 %collective-permute-start.28 = (bf16[256,256]{1,0:T(8,128)(2,1)S(1)}, bf16[256,256]{1,0:T(8,128)(2,1)S(1)}, u32[]{:S(2)}, u32[]{:S(2)}) collective-permute-start(bf16[256,256]{1,0:T(8,128)(2,1)S(1)} %get-tuple-element.54), channel_id=1, source_target_pairs={{0,1},{1,0},{2,3},{3,2},{4,5},{5,4},{6,7},{7,6},{8,9},{9,8},{10,11... | collective-permute-start | bytes 393224 | tf_op jit(solution)/shard_map/ppermute | solution.py:23
  166.4 10.5 %collective-permute-start.29 = (bf16[256,256]{1,0:T(8,128)(2,1)S(1)}, bf16[256,256]{1,0:T(8,128)(2,1)S(1)}, u32[]{:S(2)}, u32[]{:S(2)}) collective-permute-start(bf16[256,256]{1,0:T(8,128)(2,1)S(1)} %get-tuple-element.55), channel_id=1, source_target_pairs={{0,2},{1,3},{2,0},{3,1},{4,6},{5,7},{6,4},{7,5},{8,10},{9,11},{10,... | collective-permute-start | bytes 393224 | tf_op jit(solution)/shard_map/ppermute | solution.py:23
  168.1 11.2 %collective-permute-start.26 = (bf16[256,256]{1,0:T(8,128)(2,1)S(1)}, bf16[256,256]{1,0:T(8,128)(2,1)S(1)}, u32[]{:S(2)}, u32[]{:S(2)}) collective-permute-start(bf16[256,256]{1,0:T(8,128)(2,1)S(1)} %get-tuple-element.52), channel_id=1, source_target_pairs={{0,1},{1,0},{2,3},{3,2},{4,5},{5,4},{6,7},{7,6},{8,9},{9,8},{10,11... | collective-permute-start | bytes 393224 | tf_op jit(solution)/shard_map/ppermute | solution.py:23
  172.0 8.2 %collective-permute-start.27 = (bf16[256,256]{1,0:T(8,128)(2,1)S(1)}, bf16[256,256]{1,0:T(8,128)(2,1)S(1)}, u32[]{:S(2)}, u32[]{:S(2)}) collective-permute-start(bf16[256,256]{1,0:T(8,128)(2,1)S(1)} %get-tuple-element.53), channel_id=1, source_target_pairs={{0,2},{1,3},{2,0},{3,1},{4,6},{5,7},{6,4},{7,5},{8,10},{9,11},{10,... | collective-permute-start | bytes 393224 | tf_op jit(solution)/shard_map/ppermute | solution.py:23
  173.7 8.0 %collective-permute-start.32 = (bf16[256,256]{1,0:T(8,128)(2,1)S(1)}, bf16[256,256]{1,0:T(8,128)(2,1)S(1)}, u32[]{:S(2)}, u32[]{:S(2)}) collective-permute-start(bf16[256,256]{1,0:T(8,128)(2,1)S(1)} %get-tuple-element.58), channel_id=1, source_target_pairs={{0,1},{1,0},{2,3},{3,2},{4,5},{5,4},{6,7},{7,6},{8,9},{9,8},{10,11... | collective-permute-start | bytes 393224 | tf_op jit(solution)/shard_map/ppermute | solution.py:23
  176.5 5.2 %collective-permute-start.33 = (bf16[256,256]{1,0:T(8,128)(2,1)S(1)}, bf16[256,256]{1,0:T(8,128)(2,1)S(1)}, u32[]{:S(2)}, u32[]{:S(2)}) collective-permute-start(bf16[256,256]{1,0:T(8,128)(2,1)S(1)} %get-tuple-element.59), channel_id=1, source_target_pairs={{0,2},{1,3},{2,0},{3,1},{4,6},{5,7},{6,4},{7,5},{8,10},{9,11},{10,... | collective-permute-start | bytes 393224 | tf_op jit(solution)/shard_map/ppermute | solution.py:23
  176.9 6.2 %collective-permute-start.30 = (bf16[256,256]{1,0:T(8,128)(2,1)S(1)}, bf16[256,256]{1,0:T(8,128)(2,1)S(1)}, u32[]{:S(2)}, u32[]{:S(2)}) collective-permute-start(bf16[256,256]{1,0:T(8,128)(2,1)S(1)} %get-tuple-element.56), channel_id=1, source_target_pairs={{0,1},{1,0},{2,3},{3,2},{4,5},{5,4},{6,7},{7,6},{8,9},{9,8},{10,11... | collective-permute-start | bytes 393224 | tf_op jit(solution)/shard_map/ppermute | solution.py:23
  179.3 5.0 %collective-permute-start.31 = (bf16[256,256]{1,0:T(8,128)(2,1)S(1)}, bf16[256,256]{1,0:T(8,128)(2,1)S(1)}, u32[]{:S(2)}, u32[]{:S(2)}) collective-permute-start(bf16[256,256]{1,0:T(8,128)(2,1)S(1)} %get-tuple-element.57), channel_id=1, source_target_pairs={{0,2},{1,3},{2,0},{3,1},{4,6},{5,7},{6,4},{7,5},{8,10},{9,11},{10,... | collective-permute-start | bytes 393224 | tf_op jit(solution)/shard_map/ppermute | solution.py:23

commit v4 on v3

--- a/solution.py
+++ b/solution.py
@@ -14,23 +14,23 @@
 LIMIT = pltpu.CompilerParams(vmem_limit_bytes=20 << 20)
 
 
-def from_behind(block, axis):
+def shift(block, axis, step):
     devices = range(lax.axis_size(axis))
-    return lax.ppermute(block, axis, [(i + 1, i) for i in devices if i + 1 in devices])
+    return lax.ppermute(block, axis, [(i, i + step) for i in devices if i + step in devices])
 
 
 def flip(block, axis, bit):
     return lax.ppermute(block, axis, [(i, i ^ bit) for i in range(lax.axis_size(axis))])
 
 
-def row_pieces(block):
+def row_pieces(block, dim=1):
     count = lax.axis_size("row")
     if count == 1:
         return [block]
     if count == 2:
         there = flip(block, "row", 1)
         return [block, there]
-    return [lax.all_gather(block, "row", axis=1, tiled=True)]
+    return [lax.all_gather(block, "row", axis=dim, tiled=True)]
 
 
 VMEM = pl.BlockSpec(memory_space=pltpu.VMEM)
@@ -82,23 +82,114 @@
     return lax.dot_general(a, b, (((1,), (1,)), ((), ())), preferred_element_type=F32)
 
 
-def fold_body(*refs, pieces, tick, start, first, last, chunks):
-    mine, pidx, pw, here = refs[:4]
-    refs = refs[4:]
-    own = refs[0]
-    factor = refs[1 : 1 + pieces]
-    behind = refs[1 + pieces : 1 + 2 * pieces]
-    before = refs[1 + 2 * pieces]
+def plan_body(mine, *refs, tick):
+    out = refs[-1]
+    masks = refs[:-1]
+    blocks = masks[0].shape[3]
+    rows = []
+    for j in range(blocks):
+        bits = jnp.int32(0)
+        for c in range(blocks):
+            if len(masks) == 1:
+                value = masks[0][tick, 0, j, c]
+            else:
+                half = blocks // 2
+                a = masks[0][tick, 0, j % half, c]
+                b = masks[1][tick, 0, j % half, c]
+                value = jnp.where(mine[0] == j // half, a, b)
+            bits = bits + jnp.where(value != 0, jnp.int32(1 << c), jnp.int32(0))
+        rows.append(bits)
+    best = jnp.int32(-1)
+    pair = jnp.int32(0)
+    for c in range(1, blocks):
+        for d in range(c + 1, blocks):
+            count = jnp.int32(0)
+            for bits in rows:
+                count = count + jnp.where((bits & ((1 << c) | (1 << d))) == 0, jnp.int32(1), jnp.int32(0))
+            pair = jnp.where(count > best, jnp.int32((1 << c) | (1 << d)), pair)
+            best = jnp.maximum(best, count)
+    soon = jnp.int32(0)
+    late = jnp.int32(blocks - 2)
+    for c in range(blocks):
+        is_late = (pair & (1 << c)) != 0
+        out[jnp.where(is_late, late, soon)] = jnp.int32(c)
+        step = jnp.where(is_late, jnp.int32(1), jnp.int32(0))
+        late = late + step
+        soon = soon + 1 - step
+    lead = jnp.int32(0)
+    rest = jnp.int32(2)
+    for j in range(blocks):
+        leads = jnp.logical_and((rows[j] & pair) == 0, lead < 2)
+        at = jnp.where(leads, lead, jnp.minimum(rest, blocks - 1))
+        out[blocks + at] = jnp.int32(j)
+        step = jnp.where(leads, jnp.int32(1), jnp.int32(0))
+        lead = lead + step
+        rest = rest + 1 - step
+
+
+def make_plan(mine, masks, tick):
+    blocks = masks[0].shape[3]
+    smem = pl.BlockSpec(memory_space=pltpu.SMEM)
+    return pl.pallas_call(
+        functools.partial(plan_body, tick=tick),
+        grid_spec=pltpu.PrefetchScalarGridSpec(
+            num_scalar_prefetch=1, grid=(1,), in_specs=[smem] * len(masks), out_specs=smem
+        ),
+        out_shape=jax.ShapeDtypeStruct((2 * blocks,), jnp.int32),
+        compiler_params=LIMIT,
+        name="plan",
+    )(mine, *masks)
+
+
+def cut_body(mine, here, plan, src, out, sems, *, first, blocks):
+    wide = src.shape[3] // blocks
+    copies = []
+    for u in range(out.shape[2] // wide):
+        at = slice(0, wide) if first is None else pl.ds(pl.multiple_of(plan[first + u] * wide, wide), wide)
+        to = slice(u * wide, (u + 1) * wide)
+        copies.append(pltpu.make_async_copy(src.at[0, :, :, at], out.at[:, :, to], sems.at[u]))
+    for copy in copies:
+        copy.start()
+    for copy in copies:
+        copy.wait()
+
+
+def cut_piece(mine, here, plan, state, first, units, blocks):
+    rows, width = state.shape[2:]
+    return pl.pallas_call(
+        functools.partial(cut_body, first=first, blocks=blocks),
+        grid_spec=pltpu.PrefetchScalarGridSpec(
+            num_scalar_prefetch=3,
+            grid=(1,),
+            in_specs=[HBM],
+            out_specs=VMEM,
+            scratch_shapes=[pltpu.SemaphoreType.DMA((units,))],
+        ),
+        out_shape=jax.ShapeDtypeStruct((2, rows, units * width // blocks), BF16),
+        compiler_params=LIMIT,
+    )(mine, here, plan, state)
+
+
+def fold_body(*refs, pieces, tick, first, kind, base, top, count, blocks):
+    mine, pidx, pw, here, plan = refs[:5]
+    own = refs[5]
+    refs = refs[6:]
+    factor = refs[:pieces]
+    behind = refs[pieces : 2 * pieces]
+    before = refs[2 * pieces]
     right, low, high = refs[-3:]
-    outs = refs[2 + 2 * pieces : -3]
-    rows = own.shape[1]
+    outs = refs[1 + 2 * pieces : -3]
     span = behind[0].shape[2]
+    wide = own.shape[2] // blocks
+
+    def block_cols(index):
+        return pl.ds(pl.multiple_of(plan[index] * wide, wide), wide)
+
     if first:
         green, sem = outs[-2:]
         outs = outs[:-2]
         fetch = pltpu.make_async_copy(before.at[tick, 0], green, sem)
         fetch.start()
-    cols = slice(start, start + span)
     for k in range(pieces):
         size = behind[k].shape[1]
         at = slice(0, size)
@@ -106,13 +197,20 @@
             at = pl.ds(pl.multiple_of((mine[0] if k == 0 else 1 - mine[0]) * size, size), size)
         right[at, :span] = behind[k][0]
         right[at, span:] = behind[k][1]
-        low[at, :span] = factor[k][0, :, cols]
-        low[at, span:] = -factor[k][1, :, cols]
-        high[at, :span] = factor[k][1, :, cols]
-        high[at, span:] = factor[k][0, :, cols]
-    tile = min(rows, 256)
-    for step in range(rows // tile):
-        at = slice(step * tile, (step + 1) * tile)
+        for u in range(span // wide):
+            cols = block_cols(base + u)
+            real = factor[k][0, :, cols]
+            imag = factor[k][1, :, cols]
+            one = slice(u * wide, (u + 1) * wide)
+            two = slice(span + u * wide, span + (u + 1) * wide)
+            low[at, one] = real
+            low[at, two] = -imag
+            high[at, one] = imag
+            high[at, two] = real
+    tile = min(count, 256)
+    for step in range(count // tile):
+        at = slice(top + step * tile, top + (step + 1) * tile)
+        to = slice(step * tile, (step + 1) * tile)
         a = dot(own[0, at], right[...])
         b = dot(own[1, at], right[...])
         half = jnp.concatenate([a[:, :span] - b[:, span:], a[:, span:] + b[:, :span]], axis=1).astype(BF16)
@@ -126,19 +224,17 @@
         else:
             real = before[0, at] + real
             imag = before[1, at] + imag
-        if not last:
-            outs[0][0, at] = real
-            outs[0][1, at] = imag
+        outs[0][0, to] = real.astype(outs[0].dtype)
+        outs[0][1, to] = imag.astype(outs[0].dtype)
+        if kind == "final":
+            write_term(real.astype(BF16), imag.astype(BF16), pidx, pw, here, tick, outs[1:], step * tile)
             continue
-        real = real.astype(BF16)
-        imag = imag.astype(BF16)
-        left = 0
-        for out in outs[:chunks]:
-            out[0, at] = real[:, left : left + out.shape[2]]
-            out[1, at] = imag[:, left : left + out.shape[2]]
-            left += out.shape[2]
-        if len(outs) > chunks:
-            write_term(real, imag, pidx, pw, here, tick, outs[chunks:], step * tile)
+        index = blocks if kind == "lead" else blocks + 2
+        for out in outs[1:]:
+            for u in range(out.shape[2] // wide):
+                for part in range(2):
+                    out[part, to, u * wide : (u + 1) * wide] = outs[0][part, to, block_cols(index)].astype(BF16)
+                index += 1
 
 
 def write_term(real, imag, pidx, pw, here, tick, outs, row):
@@ -178,21 +274,24 @@
     return [jax.ShapeDtypeStruct((rows // parts, width // 2), BF16)] * (4 * parts)
 
 
-def fold(scalars, own, factor, behind, before, tick, start, first, last, widths, with_term):
+def fold(scalars, own, factor, behind, before, tick, first, kind, base, sends=(), part=None):
     rows, width = own.shape[1:]
+    blocks = scalars[4].shape[0] // 2
+    wide = width // blocks
     span = behind[0].shape[2]
     pieces = len(behind)
-    if last:
-        out_shape = [jax.ShapeDtypeStruct((2, rows, w), BF16) for w in widths]
-        if with_term:
-            out_shape += term_shapes(rows, width)
-    else:
-        out_shape = [jax.ShapeDtypeStruct((2, rows, width), F32)]
+    top, count = (0, rows) if part is None else (part[0] * (rows // part[1]), rows // part[1])
+    done = kind in ("final", "send")
+    out_shape = [jax.ShapeDtypeStruct((2, count, width), BF16 if done else F32)]
+    out_shape += [jax.ShapeDtypeStruct((2, rows, units * wide), BF16) for units in sends]
+    if kind == "final":
+        out_shape += term_shapes(rows, width)[: 4 if part[1] == 2 else None]
     scratch = [pltpu.VMEM((2, rows, width), BF16), pltpu.SemaphoreType.DMA] if first else []
-    return pl.pallas_call(
-        functools.partial(
-            fold_body, pieces=pieces, tick=tick, start=start, first=first, last=last, chunks=len(widths)
-        ),
+    body = functools.partial(
+        fold_body, pieces=pieces, tick=tick, first=first, kind=kind, base=base, top=top, count=count, blocks=blocks
+    )
+    return pl.pallas_call(
+        body,
         grid_spec=pltpu.PrefetchScalarGridSpec(
             num_scalar_prefetch=len(scalars),
             grid=(1,),
@@ -201,7 +300,7 @@
             scratch_shapes=scratch + [pltpu.VMEM((width, 2 * span), BF16)] * 3,
         ),
         out_shape=out_shape,
-        input_output_aliases={} if first or last else {len(scalars) + 1 + 2 * pieces: 0},
+        input_output_aliases={} if first or done else {len(scalars) + 1 + 2 * pieces: 0},
         compiler_params=LIMIT,
     )(*scalars, own, *factor, *behind, before)
 
@@ -230,25 +329,30 @@
     )(*scalars[1:], *state)
 
 
-def cut_body(mine, here, src, out, sem, *, start):
-    fetch = pltpu.make_async_copy(src.at[0, :, :, pl.ds(start, out.shape[2])], out, sem)
-    fetch.start()
-    fetch.wait()
-
-
-def cut_piece(mine, here, state, start, span):
-    return pl.pallas_call(
-        functools.partial(cut_body, start=start),
-        grid_spec=pltpu.PrefetchScalarGridSpec(
-            num_scalar_prefetch=2,
-            grid=(1,),
-            in_specs=[HBM],
-            out_specs=VMEM,
-            scratch_shapes=[pltpu.SemaphoreType.DMA],
-        ),
-        out_shape=jax.ShapeDtypeStruct((2, state.shape[2], span), BF16),
-        compiler_params=LIMIT,
-    )(mine, here, state)
+def emit_body(*refs):
+    out, sems = refs[-2:]
+    parts = refs[:-2]
+    high = parts[0].shape[1]
+    copies = [
+        pltpu.make_async_copy(ref, out.at[0, :, pl.ds(k * high, high), :], sems.at[k]) for k, ref in enumerate(parts)
+    ]
+    for copy in copies:
+        copy.start()
+    for copy in copies:
+        copy.wait()
+
+
+def emit(parts):
+    high, width = parts[0].shape[1:]
+    return pl.pallas_call(
+        emit_body,
+        in_specs=[VMEM] * len(parts),
+        out_specs=HBM,
+        out_shape=jax.ShapeDtypeStruct((1, 2, high * len(parts), width), BF16),
+        scratch_shapes=[pltpu.SemaphoreType.DMA((len(parts),))],
+        compiler_params=LIMIT,
+        name="emit",
+    )(*parts)
 
 
 def picked(ref, which):
@@ -318,9 +422,7 @@
         fields.append((real_keep, real_got, imag_keep, imag_got))
     lasts = []
     for k in range(parts):
-        sends = kernel_call(
-            pass_on_body, (here,), fields[k], [jax.ShapeDtypeStruct((high, quarter), BF16)] * 2
-        )
+        sends = kernel_call(pass_on_body, (here,), fields[k], [jax.ShapeDtypeStruct((high, quarter), BF16)] * 2)
         lasts.append(flip(sends[0], "pole", 1))
         lasts.append(flip(sends[1], "pole", 2))
     extra = [] if before is None else [before]
@@ -331,11 +433,8 @@
     return kernel_call(close_body, (), [base, *lasts], shape)
 
 
-def spans(width):
-    unit = width // 8
-    if unit % 128:
-        return [width]
-    return [3 * unit, 2 * unit, 2 * unit, unit]
+ARRIVE = (1, 3, 2, 2)
+LEAVE = (2, 3, 2, 1)
 
 
 def body(local_green, coupling, block_mask, state_in, pole_weight, pole_index):
@@ -343,41 +442,67 @@
         pltpu.with_memory_space_constraint(value, pltpu.HBM) for value in (local_green, coupling, state_in)
     )
     ticks = coupling.shape[0]
-    width = coupling.shape[4]
-    sizes = spans(width)
-    starts = [sum(sizes[:c]) for c in range(len(sizes))]
+    blocks = block_mask.shape[3]
     here = jnp.reshape(lax.axis_index("pole").astype(jnp.int32), (1,))
     mine = jnp.reshape(lax.axis_index("row").astype(jnp.int32), (1,))
-    scalars = (mine, jnp.transpose(pole_index, (1, 2, 0)), pole_weight, here)
-    state = []
-    for c, start in enumerate(starts):
-        state.append(cut_piece(mine, here, state_in, start, sizes[c]))
+    masks = row_pieces(block_mask, 2)
+    state = [cut_piece(mine, here, mine, state_in, None, 1, blocks)]
+    plan = make_plan(mine, masks, 0)
+    plan_up = shift(plan, "slab", 1)
+    plan_down = shift(plan, "slab", -1)
+    at = 1
+    for units in ARRIVE[1:]:
+        state.append(cut_piece(mine, here, plan_up, state_in, at, units, blocks))
+        at += units
     owns = []
     factors = []
-    density = None
     for tick in range(ticks):
         own = masked_factor(block_mask, coupling, tick)
         owns.append(own)
         factors.append(row_pieces(own))
+    weights = (mine, jnp.transpose(pole_index, (1, 2, 0)), pole_weight, here)
+    density = None
+    incoming = []
+    for piece in state:
+        incoming.append(shift(piece, "slab", -1))
     for tick in range(ticks):
-        incoming = []
-        for c in range(len(sizes)):
-            incoming.append(from_behind(state[c], "slab"))
         own, factor = owns[tick], factors[tick]
+        scalars = (*weights, plan_down if tick else plan)
+        base = blocks if tick else 0
         before = local_green
         last_tick = tick == ticks - 1
-        widths = [width] if last_tick else sizes
-        for c, start in enumerate(starts):
-            behind = row_pieces(incoming[c])
-            last = c == len(sizes) - 1
-            outs = fold(
-                scalars, own, factor, behind, before, tick, start, c == 0, last, widths if last else [], last_tick
-            )
+        leaving = []
+        for c, piece in enumerate(incoming):
+            behind = row_pieces(piece)
+            last = c == len(incoming) - 1
+            kind, sends = "sum", ()
+            if not last_tick and c == len(incoming) - 2:
+                kind, sends = "lead", LEAVE[:1]
+            if not last_tick and last:
+                kind, sends = "send", LEAVE[1:]
+            if last_tick and last:
+                break
+            outs = fold(scalars, own, factor, behind, before, tick, c == 0, kind, base, sends)
             before = outs[0]
-        state = outs[: len(widths)]
-        terms = outs[len(widths) :] or weigh(scalars, state, tick)
-        density = scatter_sum(terms, density, here)
-    return (state[0][None], density)
+            base += piece.shape[2] * blocks // own.shape[2]
+            for block in outs[1:]:
+                leaving.append(shift(block, "slab", -1))
+        if last_tick:
+            shapes = len(term_shapes(*own.shape[1:]))
+            parts = 2 if shapes == 8 else 1
+            finals = []
+            terms = []
+            for k in range(parts):
+                outs = fold(scalars, own, factor, behind, before, tick, False, "final", base, (), (k, parts))
+                finals.append(outs[0])
+                terms += outs[1:]
+            density = scatter_sum(terms, density, here)
+            state_out = emit(finals)
+        else:
+            terms = weigh(scalars[:4], [before], tick)
+            density = scatter_sum(terms, density, here)
+        incoming = leaving
+    return (state_out, density)
 
 
 def solution(mesh):

time: 186 us -> 199 us (1.070)
  starting transfers between devices: 31.1 us -> 37.4 us
  Pallas kernels: 52 us -> 58.1 us
    ppermute x8 -> x10, starting transfers between devices: 10.5 us -> 16.6 us  [shift(): lax.ppermute(block, axis, [(i, i + step) for i in devices if i + step in...]
    pallas_call x12 -> x15, Pallas kernels: 44 us -> 50 us  [the longest x9 40.9 us: fold(): pl.pallas_call(body, grid_spec=pltpu.PrefetchScalarGridSpec(num_scalar_pr...]
    ppermute x8 -> x10, waiting for transfers between devices: 89.2 us -> 90.2 us  [shift(): lax.ppermute(block, axis, [(i, i + step) for i in devices if i + step in...]
    ppermute x26 -> x27, starting transfers between devices: 20.6 us -> 20.7 us  [flip(): lax.ppermute(block, axis, [(i, i ^ bit) for i in range(lax.axis_size(axis...]
    ppermute x26 -> x27, waiting for transfers between devices: 11.4 us -> 11.4 us  [flip(): lax.ppermute(block, axis, [(i, i ^ bit) for i in range(lax.axis_size(axis...]
  transfers between devices with their start and end apart: 34 -> 37, of which waited for: 13 -> 16; matrix products, arithmetic and copies ran while one was open for 0% -> 0% of each run, Pallas kernels for 26% -> 28%
where the time goes in v4:
time: 199 us; the launch traced here: 198 us
  waiting for transfers between devices  102 us (51%)
  Pallas kernels  58.1 us (29%)
  starting transfers between devices  37.4 us (19%)
    ppermute x10, waiting for transfers between devices, shift(): lax.ppermute(block, axis, [(i, i + step) for i in devices if i + step in...  90.2 us
    pallas_call x9, Pallas kernels, fold(): pl.pallas_call(body, grid_spec=pltpu.PrefetchScalarGridSpec(num_scalar_pr...  40.9 us
    ppermute x27, starting transfers between devices, flip(): lax.ppermute(block, axis, [(i, i ^ bit) for i in range(lax.axis_size(axis...  20.7 us
    ppermute x10, starting transfers between devices, shift(): lax.ppermute(block, axis, [(i, i + step) for i in devices if i + step in...  16.6 us
    ppermute x27, waiting for transfers between devices, flip(): lax.ppermute(block, axis, [(i, i ^ bit) for i in range(lax.axis_size(axis...  11.4 us
    pallas_call x4, Pallas kernels, cut_piece(): pl.pallas_call(functools.partial(cut_body, first=first, blocks=blocks), g...  6.01 us
    pallas_call x2, Pallas kernels, masked_factor(): pl.pallas_call(functools.partial(mask_body, tick=tick), grid_spec=pltpu.P...  4.84 us
  transfers between devices with their start and end apart: 37, of which 16 were waited for; matrix products, arithmetic and copies ran while one was open for 0% of the time, Pallas kernels for 28%

profile of v4, /device:TPU:0, one launch (start us, length us, event | category | flops | bytes accessed | tf_op | source)
XLA Modules:
  0.0 198.1 jit_solution(3180521275230529531)
XLA Ops:
  0.6 2.4 %shard_map.78.refs_5_.refs_6_ = bf16[2,512,1024]{2,1,0:T(8,128)(2,1)S(1)} custom-call(s32[2,1,4,8]{3,2,1,0:T(4,128)} %mask_ref.3, bf16[2,1,2,512,1024]{4,3,2,1,0:T(8,128)(2,1)} %coupling_ref.3), custom_call_target="tpu_custom_call" | custom-call | tf_op jit(solution)/shard_map/pallas_call | solution.py:63
  3.7 3.8 %collective-permute-done.refs_1_ = s32[2,1,4,8]{3,2,1,0:T(4,128)S(1)} collective-permute-done((s32[2,1,4,8]{3,2,1,0:T(4,128)}, s32[2,1,4,8]{3,2,1,0:T(4,128)S(1)}, u32[]{:S(2)}, u32[]{:S(2)}) %collective-permute-start) | collective-permute-done | bytes 288 | tf_op jit(solution)/shard_map/ppermute | solution.py:23
  7.5 1.8 plan.1.refs_4_
  9.3 4.8 %collective-permute-start.4 = (s32[16]{0:T(128)S(1)}, s32[16]{0:T(128)S(1)}, u32[]{:S(2)}, u32[]{:S(2)}) collective-permute-start(s32[16]{0:T(128)S(1)} %plan.1.refs_4_), channel_id=1, source_target_pairs={{0,8},{8,16},{16,24},{1,9},{9,17},{17,25},{2,10},{10,18},{18,26},{... | collective-permute-start | bytes 200 | tf_op jit(solution)/shard_map/ppermute | solution.py:19
  14.2 1.3 collective-permute-done.4.plan
  15.4 1.8 shard_map.81
  17.3 1.3 collective-permute-start.9
  19.6 1.3 collective-permute-start.11
  20.9 1.6 shard_map.80
  22.5 1.3 collective-permute-start.7
  23.8 1.6 shard_map.79
  25.4 1.3 collective-permute-start.5
  26.7 18.6 %collective-permute-done.11.refs_8_ = bf16[2,512,128]{2,1,0:T(8,128)(2,1)S(1)} collective-permute-done((bf16[2,512,128]{2,1,0:T(8,128)(2,1)S(1)}, bf16[2,512,128]{2,1,0:T(8,128)(2,1)S(1)}, u32[]{:S(2)}, u32[]{:S(2)}) %collective-permute-start.11) | collective-permute-done | bytes 262176 | tf_op jit(solution)/shard_map/ppermute | solution.py:19
  45.8 2.4 %shard_map.77.refs_5_.refs_6_ = bf16[2,512,1024]{2,1,0:T(8,128)(2,1)S(1)} custom-call(s32[2,1,4,8]{3,2,1,0:T(4,128)} %mask_ref.3, bf16[2,1,2,512,1024]{4,3,2,1,0:T(8,128)(2,1)} %coupling_ref.3), custom_call_target="tpu_custom_call" | custom-call | tf_op jit(solution)/shard_map/pallas_call | solution.py:63
  48.4 8.2 %collective-permute-done.7.refs_8_ = bf16[2,512,256]{2,1,0:T(8,128)(2,1)S(1)} collective-permute-done((bf16[2,512,256]{2,1,0:T(8,128)(2,1)S(1)}, bf16[2,512,256]{2,1,0:T(8,128)(2,1)S(1)}, u32[]{:S(2)}, u32[]{:S(2)}) %collective-permute-start.7) | collective-permute-done | bytes 524320 | tf_op jit(solution)/shard_map/ppermute | solution.py:19
  56.6 9.5 %collective-permute-done.5.refs_8_ = bf16[2,512,256]{2,1,0:T(8,128)(2,1)S(1)} collective-permute-done((bf16[2,512,256]{2,1,0:T(8,128)(2,1)S(1)}, bf16[2,512,256]{2,1,0:T(8,128)(2,1)S(1)}, u32[]{:S(2)}, u32[]{:S(2)}) %collective-permute-start.5) | collective-permute-done | bytes 524320 | tf_op jit(solution)/shard_map/ppermute | solution.py:19
  66.1 5.2 %shard_map.83.refs_10_ = f32[2,512,1024]{2,1,0:T(8,128)S(1)} custom-call(s32[1]{0:T(128)} %bitcast.mine.plan.refs_0_, s32[1,1,2]{2,1,0:T(1,128)S(1)} %bitcast.3, f32[2,16]{1,0:T(2,128)S(1)} %copy-done, s32[1]{0:T(128)} %bitcast.2.here.refs_3_, s32[16]{0:T(128)S(1)} %plan.1.refs_4_, bf16[2,512,1024]{2,1,0:T(8,128)(2,1)S(1)} %shard_map.78.refs_5_.refs_6_, ...), custom_call_target="tpu_custom_call" | custom-call | tf_op jit(solution)/shard_map/pallas_call | solution.py:293
  71.3 6.8 %shard_map.84.refs_10_ = f32[2,512,1024]{2,1,0:T(8,128)S(1)} custom-call(s32[1]{0:T(128)} %bitcast.mine.plan.refs_0_, s32[1,1,2]{2,1,0:T(1,128)S(1)} %bitcast.4, f32[2,16]{1,0:T(2,128)S(1)} %copy-done, s32[1]{0:T(128)} %bitcast.2.here.refs_3_, s32[16]{0:T(128)S(1)} %plan.1.refs_4_, ...), custom_call_target="tpu_custom_call", output_to_operand_aliasing={{}: (10, {})} | custom-call | tf_op jit(solution)/shard_map/pallas_call | solution.py:293
  78.2 5.6 %shard_map.85 = (f32[2,512,1024]{2,1,0:T(8,128)S(1)}, bf16[2,512,256]{2,1,0:T(8,128)(2,1)S(1)}) custom-call(s32[1]{0:T(128)} %bitcast.mine.plan.refs_0_, s32[1,1,2]{2,1,0:T(1,128)S(1)} %bitcast.5, f32[2,16]{1,0:T(2,128)S(1)} %copy-done, s32[1]{0:T(128)} %bitcast.2.here.refs_3_, s32[16]{0:T(128)S(1)} %plan.1.refs_4_, ...), custom_call_target="tpu_custom_call", output_to_operand_aliasing={{0}: (10, {})} | custom-call | tf_op jit(solution)/shard_map/pallas_call | solution.py:293
  83.8 5.5 %shard_map.86 = (bf16[2,512,1024]{2,1,0:T(8,128)(2,1)S(1)}, bf16[2,512,384]{2,1,0:T(8,128)(2,1)S(1)}, bf16[2,512,256]{2,1,0:T(8,128)(2,1)S(1)}, bf16[2,512,128]{2,1,0:T(8,128)(2,1)S(1)}) custom-call(s32[1]{0:T(128)} %bitcast.mine.plan.refs_0_, s32[1,1,2]{2,1,0:T(1,128)S(1)} %bitcast.6, f32[2,16]{1,0:T(2,128)S(1)} %copy-done, s32[1]{0:T(128)} %bitcast.2.here.refs_3_, ...), custom_call_target="tpu_custom_call" | custom-call | tf_op jit(solution)/shard_map/pallas_call | solution.py:293
  89.3 1.3 collective-permute-start.17
  90.6 1.3 collective-permute-start.15
  91.9 1.3 collective-permute-start.19
  93.2 18.4 %collective-permute-done.17.refs_8_ = bf16[2,512,384]{2,1,0:T(8,128)(2,1)S(1)} collective-permute-done((bf16[2,512,384]{2,1,0:T(8,128)(2,1)S(1)}, bf16[2,512,384]{2,1,0:T(8,128)(2,1)S(1)}, u32[]{:S(2)}, u32[]{:S(2)}) %collective-permute-start.17) | collective-permute-done | bytes 786464 | tf_op jit(solution)/shard_map/ppermute | solution.py:19
  111.7 11.2 %collective-permute-done.15.refs_8_ = bf16[2,512,256]{2,1,0:T(8,128)(2,1)S(1)} collective-permute-done((bf16[2,512,256]{2,1,0:T(8,128)(2,1)S(1)}, bf16[2,512,256]{2,1,0:T(8,128)(2,1)S(1)}, u32[]{:S(2)}, u32[]{:S(2)}) %collective-permute-start.15) | collective-permute-done | bytes 524320 | tf_op jit(solution)/shard_map/ppermute | solution.py:19
  122.9 10.8 %collective-permute-done.19.refs_8_ = bf16[2,512,256]{2,1,0:T(8,128)(2,1)S(1)} collective-permute-done((bf16[2,512,256]{2,1,0:T(8,128)(2,1)S(1)}, bf16[2,512,256]{2,1,0:T(8,128)(2,1)S(1)}, u32[]{:S(2)}, u32[]{:S(2)}) %collective-permute-start.19) | collective-permute-done | bytes 524320 | tf_op jit(solution)/shard_map/ppermute | solution.py:19
  133.7 1.3 collective-permute-start.1
  134.9 4.2 %collective-permute-done.1.refs_4_ = s32[16]{0:T(128)S(1)} collective-permute-done((s32[16]{0:T(128)S(1)}, s32[16]{0:T(128)S(1)}, u32[]{:S(2)}, u32[]{:S(2)}) %collective-permute-start.1) | collective-permute-done | bytes 96 | tf_op jit(solution)/shard_map/ppermute | solution.py:19
  139.1 1.5 collective-permute-start.13
  140.6 8.0 %collective-permute-done.13.refs_8_ = bf16[2,512,128]{2,1,0:T(8,128)(2,1)S(1)} collective-permute-done((bf16[2,512,128]{2,1,0:T(8,128)(2,1)S(1)}, bf16[2,512,128]{2,1,0:T(8,128)(2,1)S(1)}, u32[]{:S(2)}, u32[]{:S(2)}) %collective-permute-start.13) | collective-permute-done | bytes 262176 | tf_op jit(solution)/shard_map/ppermute | solution.py:19
  148.6 1.4 shard_map.92
  150.0 1.6 collective-permute-start.25
  151.6 1.5 collective-permute-start.26
  153.6 4.7 %shard_map.87.refs_10_ = f32[2,512,1024]{2,1,0:T(8,128)S(1)} custom-call(s32[1]{0:T(128)} %bitcast.mine.plan.refs_0_, s32[1,1,2]{2,1,0:T(1,128)S(1)} %bitcast.8, f32[2,16]{1,0:T(2,128)S(1)} %copy-done, s32[1]{0:T(128)} %bitcast.2.here.refs_3_, s32[16]{0:T(128)S(1)} %collective-permute-done.1.refs_4_, bf16[2,512,1024]{2,1,0:T(8,128)(2,1)S(1)} %shard_map.77.refs_5_.refs_6_, ...), custom_call_target="tpu_custom_call" | custom-call | tf_op jit(solution)/shard_map/pallas_call | solution.py:293
  159.0 5.3 %shard_map.88.refs_10_ = f32[2,512,1024]{2,1,0:T(8,128)S(1)} custom-call(s32[1]{0:T(128)} %bitcast.mine.plan.refs_0_, s32[1,1,2]{2,1,0:T(1,128)S(1)} %bitcast.9, f32[2,16]{1,0:T(2,128)S(1)} %copy-done, s32[1]{0:T(128)} %bitcast.2.here.refs_3_, s32[16]{0:T(128)S(1)} %collective-permute-done.1.refs_4_, ...), custom_call_target="tpu_custom_call", output_to_operand_aliasing={{}: (10, {})} | custom-call | tf_op jit(solution)/shard_map/pallas_call | solution.py:293
  164.2 3.9 %shard_map.89.refs_10_ = f32[2,512,1024]{2,1,0:T(8,128)S(1)} custom-call(s32[1]{0:T(128)} %bitcast.mine.plan.refs_0_, s32[1,1,2]{2,1,0:T(1,128)S(1)} %bitcast.10, f32[2,16]{1,0:T(2,128)S(1)} %copy-done, s32[1]{0:T(128)} %bitcast.2.here.refs_3_, s32[16]{0:T(128)S(1)} %collective-permute-done.1.refs_4_, ...), custom_call_target="tpu_custom_call", output_to_operand_aliasing={{}: (10, {})} | custom-call | tf_op jit(solution)/shard_map/pallas_call | solution.py:293
  168.2 1.9 shard_map.91
  170.1 1.6 collective-permute-start.23
  171.7 1.5 collective-permute-start.24
  173.2 1.9 shard_map.90
  176.3 1.6 collective-permute-start.29
  178.9 1.9 collective-permute-start.30
  180.9 1.5 collective-permute-start.31
  182.4 2.1 %collective-permute-done.21.refs_1_.real_got = bf16[256,512]{1,0:T(8,128)(2,1)S(1)} collective-permute-done((bf16[256,512]{1,0:T(8,128)(2,1)S(1)}, bf16[256,512]{1,0:T(8,128)(2,1)S(1)}, u32[]{:S(2)}, u32[]{:S(2)}) %collective-permute-start.21) | collective-permute-done | bytes 262176 | tf_op jit(solution)/shard_map/ppermute | solution.py:23
  184.5 1.9 collective-permute-start.32
  186.5 1.5 collective-permute-start.35
  189.3 2.0 %collective-permute-start.33 = (bf16[256,256]{1,0:T(8,128)(2,1)S(1)}, bf16[256,256]{1,0:T(8,128)(2,1)S(1)}, u32[]{:S(2)}, u32[]{:S(2)}) collective-permute-start(bf16[256,256]{1,0:T(8,128)(2,1)S(1)} %get-tuple-element.62), channel_id=1, source_target_pairs={{0,1},{1,0},{2,3},{3,2},{4,5},{5,4},{6,7},{7,6},{8,9},{9,8},{10,11... | collective-permute-start | bytes 393224 | tf_op jit(solution)/shard_map/ppermute | solution.py:23
  193.1 1.3 emit.1
  (56 shorter events, 12.5 us)
Async XLA Ops:
  3.1 63.0 %collective-permute-start.3 = (bf16[2,512,1024]{2,1,0:T(8,128)(2,1)S(1)}, bf16[2,512,1024]{2,1,0:T(8,128)(2,1)}, u32[]{:S(2)}, u32[]{:S(2)}) collective-permute-start(bf16[2,512,1024]{2,1,0:T(8,128)(2,1)S(1)} %shard_map.78.refs_5_.refs_6_), channel_id=1, source_target_pairs={{0,4},{4,0},{1,5},{5,1},{2,6},{6,2},{3,7},{7,3},{8,12},{12,8},{9,1... | collective-permute-start | bytes 6291464 | tf_op jit(solution)/shard_map/ppermute | solution.py:23
  3.6 3.9 %collective-permute-start = (s32[2,1,4,8]{3,2,1,0:T(4,128)}, s32[2,1,4,8]{3,2,1,0:T(4,128)S(1)}, u32[]{:S(2)}, u32[]{:S(2)}) collective-permute-start(s32[2,1,4,8]{3,2,1,0:T(4,128)} %mask_ref.3), channel_id=1, source_target_pairs={{0,4},{4,0},{1,5},{5,1},{2,6},{6,2},{3,7},{7,3},{8,12},{12,8},{9,1... | collective-permute-start | bytes 776 | tf_op jit(solution)/shard_map/ppermute | solution.py:23
  9.3 6.1 %collective-permute-start.4 = (s32[16]{0:T(128)S(1)}, s32[16]{0:T(128)S(1)}, u32[]{:S(2)}, u32[]{:S(2)}) collective-permute-start(s32[16]{0:T(128)S(1)} %plan.1.refs_4_), channel_id=1, source_target_pairs={{0,8},{8,16},{16,24},{1,9},{9,17},{17,25},{2,10},{10,18},{18,26},{... | collective-permute-start | bytes 200 | tf_op jit(solution)/shard_map/ppermute | solution.py:19
  17.3 28.0 %collective-permute-start.9 = (bf16[2,512,384]{2,1,0:T(8,128)(2,1)S(1)}, bf16[2,512,384]{2,1,0:T(8,128)(2,1)S(1)}, u32[]{:S(2)}, u32[]{:S(2)}) collective-permute-start(bf16[2,512,384]{2,1,0:T(8,128)(2,1)S(1)} %shard_map.81), channel_id=1, source_target_pairs={{8,0},{16,8},{24,16},{9,1},{17,9},{25,17},{10,2},{18,10},{26,18},{... | collective-permute-start | bytes 2359304 | tf_op jit(solution)/shard_map/ppermute | solution.py:19
  19.6 25.8 %collective-permute-start.11 = (bf16[2,512,128]{2,1,0:T(8,128)(2,1)S(1)}, bf16[2,512,128]{2,1,0:T(8,128)(2,1)S(1)}, u32[]{:S(2)}, u32[]{:S(2)}) collective-permute-start(bf16[2,512,128]{2,1,0:T(8,128)(2,1)S(1)} %shard_map.82), channel_id=1, source_target_pairs={{8,0},{16,8},{24,16},{9,1},{17,9},{25,17},{10,2},{18,10},{26,18},{... | collective-permute-start | bytes 786440 | tf_op jit(solution)/shard_map/ppermute | solution.py:19
  22.5 43.6 %copy-start = (f32[2,16]{1,0:T(2,128)S(1)}, f32[2,16]{1,0:T(2,128)}, u32[]{:S(2)}) copy-start(f32[2,16]{1,0:T(2,128)} %pw.1) | copy-start | bytes 388
  22.5 43.6 %copy-start.1 = (s32[2,1,1]{0,2,1:T(1,128)S(1)}, s32[2,1,1]{0,2,1:T(1,128)}, u32[]{:S(2)}) copy-start(s32[2,1,1]{0,2,1:T(1,128)} %param.11) | copy-start | bytes 28
  22.5 34.1 %collective-permute-start.7 = (bf16[2,512,256]{2,1,0:T(8,128)(2,1)S(1)}, bf16[2,512,256]{2,1,0:T(8,128)(2,1)S(1)}, u32[]{:S(2)}, u32[]{:S(2)}) collective-permute-start(bf16[2,512,256]{2,1,0:T(8,128)(2,1)S(1)} %shard_map.80), channel_id=1, source_target_pairs={{8,0},{16,8},{24,16},{9,1},{17,9},{25,17},{10,2},{18,10},{26,18},{... | collective-permute-start | bytes 1572872 | tf_op jit(solution)/shard_map/ppermute | solution.py:19
  25.4 40.7 %collective-permute-start.5 = (bf16[2,512,256]{2,1,0:T(8,128)(2,1)S(1)}, bf16[2,512,256]{2,1,0:T(8,128)(2,1)S(1)}, u32[]{:S(2)}, u32[]{:S(2)}) collective-permute-start(bf16[2,512,256]{2,1,0:T(8,128)(2,1)S(1)} %shard_map.79), channel_id=1, source_target_pairs={{8,0},{16,8},{24,16},{9,1},{17,9},{25,17},{10,2},{18,10},{26,18},{... | collective-permute-start | bytes 1572872 | tf_op jit(solution)/shard_map/ppermute | solution.py:19
  45.3 2.9 %collective-permute-start.12 = (bf16[2,512,128]{2,1,0:T(8,128)(2,1)S(1)}, bf16[2,512,128]{2,1,0:T(8,128)(2,1)S(1)}, u32[]{:S(2)}, u32[]{:S(2)}) collective-permute-start(bf16[2,512,128]{2,1,0:T(8,128)(2,1)S(1)} %collective-permute-done.11.refs_8_), channel_id=1, source_target_pairs={{0,4},{4,0},{1,5},{5,1},{2,6},{6,2},{3,7},{7,3},{8,12},{12,8},{9,1... | collective-permute-start | bytes 786440 | tf_op jit(solution)/shard_map/ppermute | solution.py:23
  45.3 26.0 %collective-permute-start.10 = (bf16[2,512,384]{2,1,0:T(8,128)(2,1)S(1)}, bf16[2,512,384]{2,1,0:T(8,128)(2,1)S(1)}, u32[]{:S(2)}, u32[]{:S(2)}) collective-permute-start(bf16[2,512,384]{2,1,0:T(8,128)(2,1)S(1)} %collective-permute-done.9.refs_8_), channel_id=1, source_target_pairs={{0,4},{4,0},{1,5},{5,1},{2,6},{6,2},{3,7},{7,3},{8,12},{12,8},{9,1... | collective-permute-start | bytes 2359304 | tf_op jit(solution)/shard_map/ppermute | solution.py:23
  48.3 101.7 %collective-permute-start.2 = (bf16[2,512,1024]{2,1,0:T(8,128)(2,1)S(1)}, bf16[2,512,1024]{2,1,0:T(8,128)(2,1)S(1)}, u32[]{:S(2)}, u32[]{:S(2)}) collective-permute-start(bf16[2,512,1024]{2,1,0:T(8,128)(2,1)S(1)} %shard_map.77.refs_5_.refs_6_), channel_id=1, source_target_pairs={{0,4},{4,0},{1,5},{5,1},{2,6},{6,2},{3,7},{7,3},{8,12},{12,8},{9,1... | collective-permute-start | bytes 6291464 | tf_op jit(solution)/shard_map/ppermute | solution.py:23
  56.6 21.6 %collective-permute-start.8 = (bf16[2,512,256]{2,1,0:T(8,128)(2,1)S(1)}, bf16[2,512,256]{2,1,0:T(8,128)(2,1)S(1)}, u32[]{:S(2)}, u32[]{:S(2)}) collective-permute-start(bf16[2,512,256]{2,1,0:T(8,128)(2,1)S(1)} %collective-permute-done.7.refs_8_), channel_id=1, source_target_pairs={{0,4},{4,0},{1,5},{5,1},{2,6},{6,2},{3,7},{7,3},{8,12},{12,8},{9,1... | collective-permute-start | bytes 1572872 | tf_op jit(solution)/shard_map/ppermute | solution.py:23
  66.1 17.7 %collective-permute-start.6 = (bf16[2,512,256]{2,1,0:T(8,128)(2,1)S(1)}, bf16[2,512,256]{2,1,0:T(8,128)(2,1)S(1)}, u32[]{:S(2)}, u32[]{:S(2)}) collective-permute-start(bf16[2,512,256]{2,1,0:T(8,128)(2,1)S(1)} %collective-permute-done.5.refs_8_), channel_id=1, source_target_pairs={{0,4},{4,0},{1,5},{5,1},{2,6},{6,2},{3,7},{7,3},{8,12},{12,8},{9,1... | collective-permute-start | bytes 1572872 | tf_op jit(solution)/shard_map/ppermute | solution.py:23
  89.3 22.3 %collective-permute-start.17 = (bf16[2,512,384]{2,1,0:T(8,128)(2,1)S(1)}, bf16[2,512,384]{2,1,0:T(8,128)(2,1)S(1)}, u32[]{:S(2)}, u32[]{:S(2)}) collective-permute-start(bf16[2,512,384]{2,1,0:T(8,128)(2,1)S(1)} %get-tuple-element.37), channel_id=1, source_target_pairs={{8,0},{16,8},{24,16},{9,1},{17,9},{25,17},{10,2},{18,10},{26,18},{... | collective-permute-start | bytes 2359304 | tf_op jit(solution)/shard_map/ppermute | solution.py:19
  90.6 32.2 %collective-permute-start.15 = (bf16[2,512,256]{2,1,0:T(8,128)(2,1)S(1)}, bf16[2,512,256]{2,1,0:T(8,128)(2,1)S(1)}, u32[]{:S(2)}, u32[]{:S(2)}) collective-permute-start(bf16[2,512,256]{2,1,0:T(8,128)(2,1)S(1)} %get-tuple-element.36), channel_id=1, source_target_pairs={{8,0},{16,8},{24,16},{9,1},{17,9},{25,17},{10,2},{18,10},{26,18},{... | collective-permute-start | bytes 1572872 | tf_op jit(solution)/shard_map/ppermute | solution.py:19
  91.9 41.7 %collective-permute-start.19 = (bf16[2,512,256]{2,1,0:T(8,128)(2,1)S(1)}, bf16[2,512,256]{2,1,0:T(8,128)(2,1)S(1)}, u32[]{:S(2)}, u32[]{:S(2)}) collective-permute-start(bf16[2,512,256]{2,1,0:T(8,128)(2,1)S(1)} %get-tuple-element.38), channel_id=1, source_target_pairs={{8,0},{16,8},{24,16},{9,1},{17,9},{25,17},{10,2},{18,10},{26,18},{... | collective-permute-start | bytes 1572872 | tf_op jit(solution)/shard_map/ppermute | solution.py:19
  111.7 46.7 %collective-permute-start.18 = (bf16[2,512,384]{2,1,0:T(8,128)(2,1)S(1)}, bf16[2,512,384]{2,1,0:T(8,128)(2,1)S(1)}, u32[]{:S(2)}, u32[]{:S(2)}) collective-permute-start(bf16[2,512,384]{2,1,0:T(8,128)(2,1)S(1)} %collective-permute-done.17.refs_8_), channel_id=1, source_target_pairs={{0,4},{4,0},{1,5},{5,1},{2,6},{6,2},{3,7},{7,3},{8,12},{12,8},{9,1... | collective-permute-start | bytes 2359304 | tf_op jit(solution)/shard_map/ppermute | solution.py:23
  122.9 28.7 %collective-permute-start.16 = (bf16[2,512,256]{2,1,0:T(8,128)(2,1)S(1)}, bf16[2,512,256]{2,1,0:T(8,128)(2,1)S(1)}, u32[]{:S(2)}, u32[]{:S(2)}) collective-permute-start(bf16[2,512,256]{2,1,0:T(8,128)(2,1)S(1)} %collective-permute-done.15.refs_8_), channel_id=1, source_target_pairs={{0,4},{4,0},{1,5},{5,1},{2,6},{6,2},{3,7},{7,3},{8,12},{12,8},{9,1... | collective-permute-start | bytes 1572872 | tf_op jit(solution)/shard_map/ppermute | solution.py:23
  133.6 19.5 %collective-permute-start.20 = (bf16[2,512,256]{2,1,0:T(8,128)(2,1)S(1)}, bf16[2,512,256]{2,1,0:T(8,128)(2,1)S(1)}, u32[]{:S(2)}, u32[]{:S(2)}) collective-permute-start(bf16[2,512,256]{2,1,0:T(8,128)(2,1)S(1)} %collective-permute-done.19.refs_8_), channel_id=1, source_target_pairs={{0,4},{4,0},{1,5},{5,1},{2,6},{6,2},{3,7},{7,3},{8,12},{12,8},{9,1... | collective-permute-start | bytes 1572872 | tf_op jit(solution)/shard_map/ppermute | solution.py:23
  133.7 5.5 %collective-permute-start.1 = (s32[16]{0:T(128)S(1)}, s32[16]{0:T(128)S(1)}, u32[]{:S(2)}, u32[]{:S(2)}) collective-permute-start(s32[16]{0:T(128)S(1)} %plan.1.refs_4_), channel_id=1, source_target_pairs={{8,0},{16,8},{24,16},{9,1},{17,9},{25,17},{10,2},{18,10},{26,18},{... | collective-permute-start | bytes 200 | tf_op jit(solution)/shard_map/ppermute | solution.py:19
  139.1 9.4 %collective-permute-start.13 = (bf16[2,512,128]{2,1,0:T(8,128)(2,1)S(1)}, bf16[2,512,128]{2,1,0:T(8,128)(2,1)S(1)}, u32[]{:S(2)}, u32[]{:S(2)}) collective-permute-start(bf16[2,512,128]{2,1,0:T(8,128)(2,1)S(1)} %get-tuple-element.35), channel_id=1, source_target_pairs={{8,0},{16,8},{24,16},{9,1},{17,9},{25,17},{10,2},{18,10},{26,18},{... | collective-permute-start | bytes 786440 | tf_op jit(solution)/shard_map/ppermute | solution.py:19
  148.6 19.6 %collective-permute-start.14 = (bf16[2,512,128]{2,1,0:T(8,128)(2,1)S(1)}, bf16[2,512,128]{2,1,0:T(8,128)(2,1)S(1)}, u32[]{:S(2)}, u32[]{:S(2)}) collective-permute-start(bf16[2,512,128]{2,1,0:T(8,128)(2,1)S(1)} %collective-permute-done.13.refs_8_), channel_id=1, source_target_pairs={{0,4},{4,0},{1,5},{5,1},{2,6},{6,2},{3,7},{7,3},{8,12},{12,8},{9,1... | collective-permute-start | bytes 786440 | tf_op jit(solution)/shard_map/ppermute | solution.py:23
  150.0 21.7 %collective-permute-start.25 = (bf16[256,512]{1,0:T(8,128)(2,1)S(1)}, bf16[256,512]{1,0:T(8,128)(2,1)S(1)}, u32[]{:S(2)}, u32[]{:S(2)}) collective-permute-start(bf16[256,512]{1,0:T(8,128)(2,1)S(1)} %get-tuple-element.51), channel_id=1, source_target_pairs={{0,2},{1,3},{2,0},{3,1},{4,6},{5,7},{6,4},{7,5},{8,10},{9,11},{10,... | collective-permute-start | bytes 786440 | tf_op jit(solution)/shard_map/ppermute | solution.py:23
  151.6 23.5 %collective-permute-start.26 = (bf16[256,512]{1,0:T(8,128)(2,1)S(1)}, bf16[256,512]{1,0:T(8,128)(2,1)S(1)}, u32[]{:S(2)}, u32[]{:S(2)}) collective-permute-start(bf16[256,512]{1,0:T(8,128)(2,1)S(1)} %get-tuple-element.53), channel_id=1, source_target_pairs={{0,1},{1,0},{2,3},{3,2},{4,5},{5,4},{6,7},{7,6},{8,9},{9,8},{10,11... | collective-permute-start | bytes 786440 | tf_op jit(solution)/shard_map/ppermute | solution.py:23
  153.1 22.6 %collective-permute-start.27 = (bf16[256,512]{1,0:T(8,128)(2,1)S(1)}, bf16[256,512]{1,0:T(8,128)(2,1)S(1)}, u32[]{:S(2)}, u32[]{:S(2)}) collective-permute-start(bf16[256,512]{1,0:T(8,128)(2,1)S(1)} %get-tuple-element.55), channel_id=1, source_target_pairs={{0,2},{1,3},{2,0},{3,1},{4,6},{5,7},{6,4},{7,5},{8,10},{9,11},{10,... | collective-permute-start | bytes 786440 | tf_op jit(solution)/shard_map/ppermute | solution.py:23
  158.4 18.0 %collective-permute-start.28 = (bf16[256,512]{1,0:T(8,128)(2,1)S(1)}, bf16[256,512]{1,0:T(8,128)(2,1)S(1)}, u32[]{:S(2)}, u32[]{:S(2)}) collective-permute-start(bf16[256,512]{1,0:T(8,128)(2,1)S(1)} %get-tuple-element.57), channel_id=1, source_target_pairs={{0,1},{1,0},{2,3},{3,2},{4,5},{5,4},{6,7},{7,6},{8,9},{9,8},{10,11... | collective-permute-start | bytes 786440 | tf_op jit(solution)/shard_map/ppermute | solution.py:23
  170.1 8.8 %collective-permute-start.23 = (bf16[256,512]{1,0:T(8,128)(2,1)S(1)}, bf16[256,512]{1,0:T(8,128)(2,1)S(1)}, u32[]{:S(2)}, u32[]{:S(2)}) collective-permute-start(bf16[256,512]{1,0:T(8,128)(2,1)S(1)} %get-tuple-element.46), channel_id=1, source_target_pairs={{0,2},{1,3},{2,0},{3,1},{4,6},{5,7},{6,4},{7,5},{8,10},{9,11},{10,... | collective-permute-start | bytes 786440 | tf_op jit(solution)/shard_map/ppermute | solution.py:23
  171.7 9.2 %collective-permute-start.24 = (bf16[256,512]{1,0:T(8,128)(2,1)S(1)}, bf16[256,512]{1,0:T(8,128)(2,1)S(1)}, u32[]{:S(2)}, u32[]{:S(2)}) collective-permute-start(bf16[256,512]{1,0:T(8,128)(2,1)S(1)} %get-tuple-element.48), channel_id=1, source_target_pairs={{0,1},{1,0},{2,3},{3,2},{4,5},{5,4},{6,7},{7,6},{8,9},{9,8},{10,11... | collective-permute-start | bytes 786440 | tf_op jit(solution)/shard_map/ppermute | solution.py:23
  175.1 9.4 %collective-permute-start.21 = (bf16[256,512]{1,0:T(8,128)(2,1)S(1)}, bf16[256,512]{1,0:T(8,128)(2,1)S(1)}, u32[]{:S(2)}, u32[]{:S(2)}) collective-permute-start(bf16[256,512]{1,0:T(8,128)(2,1)S(1)} %get-tuple-element.42), channel_id=1, source_target_pairs={{0,2},{1,3},{2,0},{3,1},{4,6},{5,7},{6,4},{7,5},{8,10},{9,11},{10,... | collective-permute-start | bytes 786440 | tf_op jit(solution)/shard_map/ppermute | solution.py:23
  175.7 10.8 %collective-permute-start.22 = (bf16[256,512]{1,0:T(8,128)(2,1)S(1)}, bf16[256,512]{1,0:T(8,128)(2,1)S(1)}, u32[]{:S(2)}, u32[]{:S(2)}) collective-permute-start(bf16[256,512]{1,0:T(8,128)(2,1)S(1)} %get-tuple-element.44), channel_id=1, source_target_pairs={{0,1},{1,0},{2,3},{3,2},{4,5},{5,4},{6,7},{7,6},{8,9},{9,8},{10,11... | collective-permute-start | bytes 786440 | tf_op jit(solution)/shard_map/ppermute | solution.py:23
  176.3 13.0 %collective-permute-start.29 = (bf16[256,256]{1,0:T(8,128)(2,1)S(1)}, bf16[256,256]{1,0:T(8,128)(2,1)S(1)}, u32[]{:S(2)}, u32[]{:S(2)}) collective-permute-start(bf16[256,256]{1,0:T(8,128)(2,1)S(1)} %get-tuple-element.58), channel_id=1, source_target_pairs={{0,1},{1,0},{2,3},{3,2},{4,5},{5,4},{6,7},{7,6},{8,9},{9,8},{10,11... | collective-permute-start | bytes 393224 | tf_op jit(solution)/shard_map/ppermute | solution.py:23
  178.9 10.4 %collective-permute-start.30 = (bf16[256,256]{1,0:T(8,128)(2,1)S(1)}, bf16[256,256]{1,0:T(8,128)(2,1)S(1)}, u32[]{:S(2)}, u32[]{:S(2)}) collective-permute-start(bf16[256,256]{1,0:T(8,128)(2,1)S(1)} %get-tuple-element.59), channel_id=1, source_target_pairs={{0,2},{1,3},{2,0},{3,1},{4,6},{5,7},{6,4},{7,5},{8,10},{9,11},{10,... | collective-permute-start | bytes 393224 | tf_op jit(solution)/shard_map/ppermute | solution.py:23
  180.9 11.2 %collective-permute-start.31 = (bf16[256,256]{1,0:T(8,128)(2,1)S(1)}, bf16[256,256]{1,0:T(8,128)(2,1)S(1)}, u32[]{:S(2)}, u32[]{:S(2)}) collective-permute-start(bf16[256,256]{1,0:T(8,128)(2,1)S(1)} %get-tuple-element.60), channel_id=1, source_target_pairs={{0,1},{1,0},{2,3},{3,2},{4,5},{5,4},{6,7},{7,6},{8,9},{9,8},{10,11... | collective-permute-start | bytes 393224 | tf_op jit(solution)/shard_map/ppermute | solution.py:23
  184.5 8.4 %collective-permute-start.32 = (bf16[256,256]{1,0:T(8,128)(2,1)S(1)}, bf16[256,256]{1,0:T(8,128)(2,1)S(1)}, u32[]{:S(2)}, u32[]{:S(2)}) collective-permute-start(bf16[256,256]{1,0:T(8,128)(2,1)S(1)} %get-tuple-element.61), channel_id=1, source_target_pairs={{0,2},{1,3},{2,0},{3,1},{4,6},{5,7},{6,4},{7,5},{8,10},{9,11},{10,... | collective-permute-start | bytes 393224 | tf_op jit(solution)/shard_map/ppermute | solution.py:23
  186.5 8.1 %collective-permute-start.35 = (bf16[256,256]{1,0:T(8,128)(2,1)S(1)}, bf16[256,256]{1,0:T(8,128)(2,1)S(1)}, u32[]{:S(2)}, u32[]{:S(2)}) collective-permute-start(bf16[256,256]{1,0:T(8,128)(2,1)S(1)} %get-tuple-element.64), channel_id=1, source_target_pairs={{0,1},{1,0},{2,3},{3,2},{4,5},{5,4},{6,7},{7,6},{8,9},{9,8},{10,11... | collective-permute-start | bytes 393224 | tf_op jit(solution)/shard_map/ppermute | solution.py:23
  189.3 5.3 %collective-permute-start.36 = (bf16[256,256]{1,0:T(8,128)(2,1)S(1)}, bf16[256,256]{1,0:T(8,128)(2,1)S(1)}, u32[]{:S(2)}, u32[]{:S(2)}) collective-permute-start(bf16[256,256]{1,0:T(8,128)(2,1)S(1)} %get-tuple-element.65), channel_id=1, source_target_pairs={{0,2},{1,3},{2,0},{3,1},{4,6},{5,7},{6,4},{7,5},{8,10},{9,11},{10,... | collective-permute-start | bytes 393224 | tf_op jit(solution)/shard_map/ppermute | solution.py:23
  189.3 6.6 %collective-permute-start.33 = (bf16[256,256]{1,0:T(8,128)(2,1)S(1)}, bf16[256,256]{1,0:T(8,128)(2,1)S(1)}, u32[]{:S(2)}, u32[]{:S(2)}) collective-permute-start(bf16[256,256]{1,0:T(8,128)(2,1)S(1)} %get-tuple-element.62), channel_id=1, source_target_pairs={{0,1},{1,0},{2,3},{3,2},{4,5},{5,4},{6,7},{7,6},{8,9},{9,8},{10,11... | collective-permute-start | bytes 393224 | tf_op jit(solution)/shard_map/ppermute | solution.py:23
  192.1 5.0 %collective-permute-start.34 = (bf16[256,256]{1,0:T(8,128)(2,1)S(1)}, bf16[256,256]{1,0:T(8,128)(2,1)S(1)}, u32[]{:S(2)}, u32[]{:S(2)}) collective-permute-start(bf16[256,256]{1,0:T(8,128)(2,1)S(1)} %get-tuple-element.63), channel_id=1, source_target_pairs={{0,2},{1,3},{2,0},{3,1},{4,6},{5,7},{6,4},{7,5},{8,10},{9,11},{10,... | collective-permute-start | bytes 393224 | tf_op jit(solution)/shard_map/ppermute | solution.py:23

commit v5 on v4

--- a/solution.py
+++ b/solution.py
@@ -86,9 +86,10 @@
     out = refs[-1]
     masks = refs[:-1]
     blocks = masks[0].shape[3]
+    one, none = jnp.int32(1), jnp.int32(0)
     rows = []
     for j in range(blocks):
-        bits = jnp.int32(0)
+        bits = none
         for c in range(blocks):
             if len(masks) == 1:
                 value = masks[0][tick, 0, j, c]
@@ -97,34 +98,40 @@
                 a = masks[0][tick, 0, j % half, c]
                 b = masks[1][tick, 0, j % half, c]
                 value = jnp.where(mine[0] == j // half, a, b)
-            bits = bits + jnp.where(value != 0, jnp.int32(1 << c), jnp.int32(0))
+            bits = bits + jnp.where(value != 0, jnp.int32(1 << c), none)
         rows.append(bits)
-    best = jnp.int32(-1)
-    pair = jnp.int32(0)
-    for c in range(1, blocks):
-        for d in range(c + 1, blocks):
-            count = jnp.int32(0)
+
+    def widest(start):
+        best, found = jnp.int32(-1), none
+        for c in range(2, blocks):
+            both = start | (1 << c)
+            count = none
             for bits in rows:
-                count = count + jnp.where((bits & ((1 << c) | (1 << d))) == 0, jnp.int32(1), jnp.int32(0))
-            pair = jnp.where(count > best, jnp.int32((1 << c) | (1 << d)), pair)
+                count = count + jnp.where((bits & both) == 0, one, none)
+            count = jnp.where((start & (1 << c)) != 0, jnp.int32(-1), count)
+            found = jnp.where(count > best, jnp.int32(1 << c), found)
             best = jnp.maximum(best, count)
-    soon = jnp.int32(0)
-    late = jnp.int32(blocks - 2)
+        return found
+
+    last = widest(none)
+    near = widest(last)
+    soon = none
     for c in range(blocks):
-        is_late = (pair & (1 << c)) != 0
-        out[jnp.where(is_late, late, soon)] = jnp.int32(c)
-        step = jnp.where(is_late, jnp.int32(1), jnp.int32(0))
-        late = late + step
-        soon = soon + 1 - step
-    lead = jnp.int32(0)
-    rest = jnp.int32(2)
+        is_last = (last & (1 << c)) != 0
+        is_near = (near & (1 << c)) != 0
+        at = jnp.where(is_last, jnp.int32(blocks - 1), jnp.where(is_near, jnp.int32(blocks - 2), soon))
+        out[at] = jnp.int32(c)
+        soon = soon + jnp.where(jnp.logical_or(is_last, is_near), none, one)
+    lead, next_two, rest = none, one, jnp.int32(3)
     for j in range(blocks):
-        leads = jnp.logical_and((rows[j] & pair) == 0, lead < 2)
-        at = jnp.where(leads, lead, jnp.minimum(rest, blocks - 1))
+        leads = jnp.logical_and((rows[j] & (last | near)) == 0, lead == 0)
+        follows = jnp.logical_and((rows[j] & last) == 0, next_two < 3)
+        follows = jnp.logical_and(follows, jnp.logical_not(leads))
+        at = jnp.where(leads, none, jnp.where(follows, next_two, jnp.minimum(rest, blocks - 1)))
         out[blocks + at] = jnp.int32(j)
-        step = jnp.where(leads, jnp.int32(1), jnp.int32(0))
-        lead = lead + step
-        rest = rest + 1 - step
+        lead = lead + jnp.where(leads, one, none)
+        next_two = next_two + jnp.where(follows, one, none)
+        rest = rest + jnp.where(jnp.logical_or(leads, follows), none, one)
 
 
 def make_plan(mine, masks, tick):
@@ -142,10 +149,10 @@
 
 
 def cut_body(mine, here, plan, src, out, sems, *, first, blocks):
-    wide = src.shape[3] // blocks
+    wide = src.shape[3] // blocks if first else out.shape[2]
     copies = []
     for u in range(out.shape[2] // wide):
-        at = slice(0, wide) if first is None else pl.ds(pl.multiple_of(plan[first + u] * wide, wide), wide)
+        at = pl.ds(pl.multiple_of(plan[first + u] * wide, wide) if first else 0, wide)
         to = slice(u * wide, (u + 1) * wide)
         copies.append(pltpu.make_async_copy(src.at[0, :, :, at], out.at[:, :, to], sems.at[u]))
     for copy in copies:
@@ -170,7 +177,7 @@
     )(mine, here, plan, state)
 
 
-def fold_body(*refs, pieces, tick, first, kind, base, top, count, blocks):
+def fold_body(*refs, pieces, tick, first, kind, base, index, top, count, blocks):
     mine, pidx, pw, here, plan = refs[:5]
     own = refs[5]
     refs = refs[6:]
@@ -229,12 +236,12 @@
         if kind == "final":
             write_term(real.astype(BF16), imag.astype(BF16), pidx, pw, here, tick, outs[1:], step * tile)
             continue
-        index = blocks if kind == "lead" else blocks + 2
+        at_block = blocks + index
         for out in outs[1:]:
             for u in range(out.shape[2] // wide):
                 for part in range(2):
-                    out[part, to, u * wide : (u + 1) * wide] = outs[0][part, to, block_cols(index)].astype(BF16)
-                index += 1
+                    out[part, to, u * wide : (u + 1) * wide] = outs[0][part, to, block_cols(at_block)].astype(BF16)
+                at_block += 1
 
 
 def write_term(real, imag, pidx, pw, here, tick, outs, row):
@@ -274,7 +281,7 @@
     return [jax.ShapeDtypeStruct((rows // parts, width // 2), BF16)] * (4 * parts)
 
 
-def fold(scalars, own, factor, behind, before, tick, first, kind, base, sends=(), part=None):
+def fold(scalars, own, factor, behind, before, tick, first, kind, base, sends=(), index=0, part=None):
     rows, width = own.shape[1:]
     blocks = scalars[4].shape[0] // 2
     wide = width // blocks
@@ -288,7 +295,7 @@
         out_shape += term_shapes(rows, width)[: 4 if part[1] == 2 else None]
     scratch = [pltpu.VMEM((2, rows, width), BF16), pltpu.SemaphoreType.DMA] if first else []
     body = functools.partial(
-        fold_body, pieces=pieces, tick=tick, first=first, kind=kind, base=base, top=top, count=count, blocks=blocks
+        fold_body, pieces=pieces, tick=tick, first=first, kind=kind, base=base, index=index, top=top, count=count, blocks=blocks
     )
     return pl.pallas_call(
         body,
@@ -433,8 +440,8 @@
     return kernel_call(close_body, (), [base, *lasts], shape)
 
 
-ARRIVE = (1, 3, 2, 2)
-LEAVE = (2, 3, 2, 1)
+ARRIVE = (2, 2, 2, 1, 1)
+LEAVE = (1, 2, 2, 2, 1)
 
 
 def body(local_green, coupling, block_mask, state_in, pole_weight, pole_index):
@@ -446,11 +453,11 @@
     here = jnp.reshape(lax.axis_index("pole").astype(jnp.int32), (1,))
     mine = jnp.reshape(lax.axis_index("row").astype(jnp.int32), (1,))
     masks = row_pieces(block_mask, 2)
-    state = [cut_piece(mine, here, mine, state_in, None, 1, blocks)]
+    state = [cut_piece(mine, here, mine, state_in, 0, ARRIVE[0], blocks)]
     plan = make_plan(mine, masks, 0)
     plan_up = shift(plan, "slab", 1)
     plan_down = shift(plan, "slab", -1)
-    at = 1
+    at = ARRIVE[0]
     for units in ARRIVE[1:]:
         state.append(cut_piece(mine, here, plan_up, state_in, at, units, blocks))
         at += units
@@ -475,14 +482,14 @@
         for c, piece in enumerate(incoming):
             behind = row_pieces(piece)
             last = c == len(incoming) - 1
-            kind, sends = "sum", ()
-            if not last_tick and c == len(incoming) - 2:
-                kind, sends = "lead", LEAVE[:1]
-            if not last_tick and last:
-                kind, sends = "send", LEAVE[1:]
+            kind, sends, index = "sum", (), 0
+            if not last_tick and len(incoming) - c <= 3:
+                kind = "send" if last else "sum"
+                index = sum(LEAVE[: len(leaving)])
+                sends = LEAVE[len(leaving) :] if last else LEAVE[len(leaving) : len(leaving) + 1]
             if last_tick and last:
                 break
-            outs = fold(scalars, own, factor, behind, before, tick, c == 0, kind, base, sends)
+            outs = fold(scalars, own, factor, behind, before, tick, c == 0, kind, base, sends, index)
             before = outs[0]
             base += piece.shape[2] * blocks // own.shape[2]
             for block in outs[1:]:
@@ -493,7 +500,7 @@
             finals = []
             terms = []
             for k in range(parts):
-                outs = fold(scalars, own, factor, behind, before, tick, False, "final", base, (), (k, parts))
+                outs = fold(scalars, own, factor, behind, before, tick, False, "final", base, part=(k, parts))
                 finals.append(outs[0])
                 terms += outs[1:]
             density = scatter_sum(terms, density, here)

time: 199 us -> 216 us (1.085)
  Pallas kernels: 58.1 us -> 79.9 us
  waiting for transfers between devices: 102 us -> 95.7 us
    pallas_call x9 -> x11, Pallas kernels: 40.9 us -> 60.2 us  [fold(): pl.pallas_call(body, grid_spec=pltpu.PrefetchScalarGridSpec(num_scalar_pr...]
    ppermute x10 -> x12, waiting for transfers between devices: 90.2 us -> 83 us  [shift(): lax.ppermute(block, axis, [(i, i + step) for i in devices if i + step in...]
    ppermute x10 -> x12, starting transfers between devices: 16.6 us -> 19.4 us  [shift(): lax.ppermute(block, axis, [(i, i + step) for i in devices if i + step in...]
    ppermute x27 -> x29, starting transfers between devices: 20.7 us -> 19.3 us  [flip(): lax.ppermute(block, axis, [(i, i ^ bit) for i in range(lax.axis_size(axis...]
    ppermute x27 -> x29, waiting for transfers between devices: 11.4 us -> 12.7 us  [flip(): lax.ppermute(block, axis, [(i, i ^ bit) for i in range(lax.axis_size(axis...]
    pallas_call x4 -> x5, Pallas kernels: 6.01 us -> 7.27 us  [cut_piece(): pl.pallas_call(functools.partial(cut_body, first=first, blocks=blocks), g...]
  transfers between devices with their start and end apart: 37 -> 41, of which waited for: 16 -> 15; matrix products, arithmetic and copies ran while one was open for 0% -> 0% of each run, Pallas kernels for 28% -> 35%
where the time goes in v5:
time: 216 us; the launch traced here: 215 us
  waiting for transfers between devices  95.7 us (44%)
  Pallas kernels  79.9 us (37%)
  starting transfers between devices  38.7 us (18%)
    ppermute x12, waiting for transfers between devices, shift(): lax.ppermute(block, axis, [(i, i + step) for i in devices if i + step in...  83 us
    pallas_call x11, Pallas kernels, fold(): pl.pallas_call(body, grid_spec=pltpu.PrefetchScalarGridSpec(num_scalar_pr...  60.2 us
    ppermute x12, starting transfers between devices, shift(): lax.ppermute(block, axis, [(i, i + step) for i in devices if i + step in...  19.4 us
    ppermute x29, starting transfers between devices, flip(): lax.ppermute(block, axis, [(i, i ^ bit) for i in range(lax.axis_size(axis...  19.3 us
    ppermute x29, waiting for transfers between devices, flip(): lax.ppermute(block, axis, [(i, i ^ bit) for i in range(lax.axis_size(axis...  12.7 us
    pallas_call x5, Pallas kernels, cut_piece(): pl.pallas_call(functools.partial(cut_body, first=first, blocks=blocks), g...  7.27 us
    pallas_call x2, Pallas kernels, masked_factor(): pl.pallas_call(functools.partial(mask_body, tick=tick), grid_spec=pltpu.P...  6.17 us
  transfers between devices with their start and end apart: 41, of which 15 were waited for; matrix products, arithmetic and copies ran while one was open for 0% of the time, Pallas kernels for 35%

profile of v5, /device:TPU:0, one launch (start us, length us, event | category | flops | bytes accessed | tf_op | source)
XLA Modules:
  0.0 215.4 jit_solution(1089131103971874591)
XLA Ops:
  0.6 3.7 %shard_map.78.refs_5_.refs_6_ = bf16[2,512,1024]{2,1,0:T(8,128)(2,1)} custom-call(s32[2,1,4,8]{3,2,1,0:T(4,128)} %mask_ref.3, bf16[2,1,2,512,1024]{4,3,2,1,0:T(8,128)(2,1)} %coupling_ref.3), custom_call_target="tpu_custom_call" | custom-call | tf_op jit(solution)/shard_map/pallas_call | solution.py:63
  4.9 2.4 %shard_map.77.refs_5_.refs_6_ = bf16[2,512,1024]{2,1,0:T(8,128)(2,1)S(1)} custom-call(s32[2,1,4,8]{3,2,1,0:T(4,128)} %mask_ref.3, bf16[2,1,2,512,1024]{4,3,2,1,0:T(8,128)(2,1)} %coupling_ref.3), custom_call_target="tpu_custom_call" | custom-call | tf_op jit(solution)/shard_map/pallas_call | solution.py:63
  8.0 4.1 %collective-permute-done.refs_1_ = s32[2,1,4,8]{3,2,1,0:T(4,128)S(1)} collective-permute-done((s32[2,1,4,8]{3,2,1,0:T(4,128)}, s32[2,1,4,8]{3,2,1,0:T(4,128)S(1)}, u32[]{:S(2)}, u32[]{:S(2)}) %collective-permute-start) | collective-permute-done | bytes 288 | tf_op jit(solution)/shard_map/ppermute | solution.py:23
  12.1 1.7 plan.1.refs_4_
  13.8 4.8 %collective-permute-start.4 = (s32[16]{0:T(128)S(1)}, s32[16]{0:T(128)S(1)}, u32[]{:S(2)}, u32[]{:S(2)}) collective-permute-start(s32[16]{0:T(128)S(1)} %plan.1.refs_4_), channel_id=1, source_target_pairs={{0,8},{8,16},{16,24},{1,9},{9,17},{17,25},{2,10},{10,18},{18,26},{... | collective-permute-start | bytes 200 | tf_op jit(solution)/shard_map/ppermute | solution.py:19
  19.9 1.5 shard_map.79
  21.4 1.3 collective-permute-start.5
  22.7 1.5 shard_map.80
  24.2 1.3 collective-permute-start.7
  26.6 1.3 collective-permute-start.13
  27.9 1.6 shard_map.82
  29.5 1.6 shard_map.81
  31.1 1.6 collective-permute-done.5.refs_8_
  34.0 4.3 %collective-permute-done.7.refs_8_ = bf16[2,512,128]{2,1,0:T(8,128)(2,1)S(1)} collective-permute-done((bf16[2,512,128]{2,1,0:T(8,128)(2,1)S(1)}, bf16[2,512,128]{2,1,0:T(8,128)(2,1)S(1)}, u32[]{:S(2)}, u32[]{:S(2)}) %collective-permute-start.7) | collective-permute-done | bytes 262176 | tf_op jit(solution)/shard_map/ppermute | solution.py:19
  38.4 1.5 collective-permute-start.9
  39.8 9.8 %collective-permute-done.13.refs_8_ = bf16[2,512,256]{2,1,0:T(8,128)(2,1)S(1)} collective-permute-done((bf16[2,512,256]{2,1,0:T(8,128)(2,1)S(1)}, bf16[2,512,256]{2,1,0:T(8,128)(2,1)S(1)}, u32[]{:S(2)}, u32[]{:S(2)}) %collective-permute-start.13) | collective-permute-done | bytes 524320 | tf_op jit(solution)/shard_map/ppermute | solution.py:19
  49.6 11.2 %collective-permute-done.11.refs_8_ = bf16[2,512,256]{2,1,0:T(8,128)(2,1)S(1)} collective-permute-done((bf16[2,512,256]{2,1,0:T(8,128)(2,1)S(1)}, bf16[2,512,256]{2,1,0:T(8,128)(2,1)S(1)}, u32[]{:S(2)}, u32[]{:S(2)}) %collective-permute-start.11) | collective-permute-done | bytes 524320 | tf_op jit(solution)/shard_map/ppermute | solution.py:19
  60.8 9.5 %collective-permute-done.9.refs_8_ = bf16[2,512,256]{2,1,0:T(8,128)(2,1)S(1)} collective-permute-done((bf16[2,512,256]{2,1,0:T(8,128)(2,1)S(1)}, bf16[2,512,256]{2,1,0:T(8,128)(2,1)S(1)}, u32[]{:S(2)}, u32[]{:S(2)}) %collective-permute-start.9) | collective-permute-done | bytes 524320 | tf_op jit(solution)/shard_map/ppermute | solution.py:19
  71.0 6.7 %shard_map.84.refs_10_ = f32[2,512,1024]{2,1,0:T(8,128)S(1)} custom-call(s32[1]{0:T(128)} %bitcast.mine.plan.refs_0_, s32[1,1,2]{2,1,0:T(1,128)S(1)} %bitcast.3, f32[2,16]{1,0:T(2,128)S(1)} %copy-done, s32[1]{0:T(128)} %bitcast.2.here.refs_3_, s32[16]{0:T(128)S(1)} %plan.1.refs_4_, bf16[2,512,1024]{2,1,0:T(8,128)(2,1)} %shard_map.78.refs_5_.refs_6_, ...), custom_call_target="tpu_custom_call" | custom-call | tf_op jit(solution)/shard_map/pallas_call | solution.py:300
  77.7 6.8 %shard_map.85.refs_10_ = f32[2,512,1024]{2,1,0:T(8,128)S(1)} custom-call(s32[1]{0:T(128)} %bitcast.mine.plan.refs_0_, s32[1,1,2]{2,1,0:T(1,128)S(1)} %bitcast.4, f32[2,16]{1,0:T(2,128)S(1)} %copy-done, s32[1]{0:T(128)} %bitcast.2.here.refs_3_, s32[16]{0:T(128)S(1)} %plan.1.refs_4_, ...), custom_call_target="tpu_custom_call", output_to_operand_aliasing={{}: (10, {})} | custom-call | tf_op jit(solution)/shard_map/pallas_call | solution.py:300
  84.4 6.8 %shard_map.86 = (f32[2,512,1024]{2,1,0:T(8,128)S(1)}, bf16[2,512,128]{2,1,0:T(8,128)(2,1)S(1)}) custom-call(s32[1]{0:T(128)} %bitcast.mine.plan.refs_0_, s32[1,1,2]{2,1,0:T(1,128)S(1)} %bitcast.5, f32[2,16]{1,0:T(2,128)S(1)} %copy-done, s32[1]{0:T(128)} %bitcast.2.here.refs_3_, s32[16]{0:T(128)S(1)} %plan.1.refs_4_, ...), custom_call_target="tpu_custom_call", output_to_operand_aliasing={{0}: (10, {})} | custom-call | tf_op jit(solution)/shard_map/pallas_call | solution.py:300
  91.3 5.5 %shard_map.87 = (f32[2,512,1024]{2,1,0:T(8,128)S(1)}, bf16[2,512,256]{2,1,0:T(8,128)(2,1)S(1)}) custom-call(s32[1]{0:T(128)} %bitcast.mine.plan.refs_0_, s32[1,1,2]{2,1,0:T(1,128)S(1)} %bitcast.6, f32[2,16]{1,0:T(2,128)S(1)} %copy-done, s32[1]{0:T(128)} %bitcast.2.here.refs_3_, s32[16]{0:T(128)S(1)} %plan.1.refs_4_, ...), custom_call_target="tpu_custom_call", output_to_operand_aliasing={{0}: (10, {})} | custom-call | tf_op jit(solution)/shard_map/pallas_call | solution.py:300
  96.8 5.4 %shard_map.88 = (bf16[2,512,1024]{2,1,0:T(8,128)(2,1)S(1)}, bf16[2,512,256]{2,1,0:T(8,128)(2,1)S(1)}, bf16[2,512,256]{2,1,0:T(8,128)(2,1)S(1)}, bf16[2,512,128]{2,1,0:T(8,128)(2,1)S(1)}) custom-call(s32[1]{0:T(128)} %bitcast.mine.plan.refs_0_, s32[1,1,2]{2,1,0:T(1,128)S(1)} %bitcast.7, f32[2,16]{1,0:T(2,128)S(1)} %copy-done, s32[1]{0:T(128)} %bitcast.2.here.refs_3_, ...), custom_call_target="tpu_custom_call" | custom-call | tf_op jit(solution)/shard_map/pallas_call | solution.py:300
  102.2 1.3 collective-permute-start.17
  103.5 1.3 collective-permute-start.21
  107.4 33.5 %collective-permute-done.1.refs_4_ = s32[16]{0:T(128)S(1)} collective-permute-done((s32[16]{0:T(128)S(1)}, s32[16]{0:T(128)S(1)}, u32[]{:S(2)}, u32[]{:S(2)}) %collective-permute-start.1) | collective-permute-done | bytes 96 | tf_op jit(solution)/shard_map/ppermute | solution.py:19
  142.9 1.5 collective-permute-start.15
  144.4 7.6 %collective-permute-done.23.refs_8_ = bf16[2,512,128]{2,1,0:T(8,128)(2,1)S(1)} collective-permute-done((bf16[2,512,128]{2,1,0:T(8,128)(2,1)S(1)}, bf16[2,512,128]{2,1,0:T(8,128)(2,1)S(1)}, u32[]{:S(2)}, u32[]{:S(2)}) %collective-permute-start.23) | collective-permute-done | bytes 262176 | tf_op jit(solution)/shard_map/ppermute | solution.py:19
  152.0 4.1 %collective-permute-done.15.refs_8_ = bf16[2,512,128]{2,1,0:T(8,128)(2,1)S(1)} collective-permute-done((bf16[2,512,128]{2,1,0:T(8,128)(2,1)S(1)}, bf16[2,512,128]{2,1,0:T(8,128)(2,1)S(1)}, u32[]{:S(2)}, u32[]{:S(2)}) %collective-permute-start.15) | collective-permute-done | bytes 262176 | tf_op jit(solution)/shard_map/ppermute | solution.py:19
  156.1 1.4 shard_map.95
  157.6 1.6 collective-permute-start.29
  159.2 1.5 collective-permute-start.30
  161.2 5.3 %shard_map.89.refs_10_ = f32[2,512,1024]{2,1,0:T(8,128)S(1)} custom-call(s32[1]{0:T(128)} %bitcast.mine.plan.refs_0_, s32[1,1,2]{2,1,0:T(1,128)S(1)} %bitcast.9, f32[2,16]{1,0:T(2,128)S(1)} %copy-done, s32[1]{0:T(128)} %bitcast.2.here.refs_3_, s32[16]{0:T(128)S(1)} %collective-permute-done.1.refs_4_, bf16[2,512,1024]{2,1,0:T(8,128)(2,1)S(1)} %shard_map.77.refs_5_.refs_6_, ...), custom_call_target="tpu_custom_call" | custom-call | tf_op jit(solution)/shard_map/pallas_call | solution.py:300
  166.6 5.5 %shard_map.90.refs_10_ = f32[2,512,1024]{2,1,0:T(8,128)S(1)} custom-call(s32[1]{0:T(128)} %bitcast.mine.plan.refs_0_, s32[1,1,2]{2,1,0:T(1,128)S(1)} %bitcast.10, f32[2,16]{1,0:T(2,128)S(1)} %copy-done, s32[1]{0:T(128)} %bitcast.2.here.refs_3_, s32[16]{0:T(128)S(1)} %collective-permute-done.1.refs_4_, ...), custom_call_target="tpu_custom_call", output_to_operand_aliasing={{}: (10, {})} | custom-call | tf_op jit(solution)/shard_map/pallas_call | solution.py:300
  172.6 5.5 %shard_map.91.refs_10_ = f32[2,512,1024]{2,1,0:T(8,128)S(1)} custom-call(s32[1]{0:T(128)} %bitcast.mine.plan.refs_0_, s32[1,1,2]{2,1,0:T(1,128)S(1)} %bitcast.11, f32[2,16]{1,0:T(2,128)S(1)} %copy-done, s32[1]{0:T(128)} %bitcast.2.here.refs_3_, s32[16]{0:T(128)S(1)} %collective-permute-done.1.refs_4_, ...), custom_call_target="tpu_custom_call", output_to_operand_aliasing={{}: (10, {})} | custom-call | tf_op jit(solution)/shard_map/pallas_call | solution.py:300
  178.1 5.5 %shard_map.92.refs_10_ = f32[2,512,1024]{2,1,0:T(8,128)S(1)} custom-call(s32[1]{0:T(128)} %bitcast.mine.plan.refs_0_, s32[1,1,2]{2,1,0:T(1,128)S(1)} %bitcast.12, f32[2,16]{1,0:T(2,128)S(1)} %copy-done, s32[1]{0:T(128)} %bitcast.2.here.refs_3_, s32[16]{0:T(128)S(1)} %collective-permute-done.1.refs_4_, ...), custom_call_target="tpu_custom_call", output_to_operand_aliasing={{}: (10, {})} | custom-call | tf_op jit(solution)/shard_map/pallas_call | solution.py:300
  183.6 3.5 %shard_map.94 = (bf16[2,256,1024]{2,1,0:T(8,128)(2,1)S(1)}, bf16[256,512]{1,0:T(8,128)(2,1)S(1)}, bf16[256,512]{1,0:T(8,128)(2,1)S(1)}, bf16[256,512]{1,0:T(8,128)(2,1)S(1)}, bf16[256,512]{1,0:T(8,128)(2,1)S(1)}) custom-call(s32[1]{0:T(128)} %bitcast.mine.plan.refs_0_, s32[1,1,2]{2,1,0:T(1,128)S(1)} %bitcast.13, f32[2,16]{1,0:T(2,128)S(1)} %copy-done, ...), custom_call_target="tpu_custom_call" | custom-call | tf_op jit(solution)/shard_map/pallas_call | solution.py:300
  187.1 1.6 collective-permute-start.27
  188.7 1.5 collective-permute-start.28
  190.2 3.8 %shard_map.93 = (bf16[2,256,1024]{2,1,0:T(8,128)(2,1)S(1)}, bf16[256,512]{1,0:T(8,128)(2,1)S(1)}, bf16[256,512]{1,0:T(8,128)(2,1)S(1)}, bf16[256,512]{1,0:T(8,128)(2,1)S(1)}, bf16[256,512]{1,0:T(8,128)(2,1)S(1)}) custom-call(s32[1]{0:T(128)} %bitcast.mine.plan.refs_0_, s32[1,1,2]{2,1,0:T(1,128)S(1)} %bitcast.14, f32[2,16]{1,0:T(2,128)S(1)} %copy-done, ...), custom_call_target="tpu_custom_call" | custom-call | tf_op jit(solution)/shard_map/pallas_call | solution.py:300
  195.2 1.6 collective-permute-start.33
  196.9 1.5 collective-permute-start.34
  199.1 4.1 %collective-permute-done.25.refs_1_.real_got = bf16[256,512]{1,0:T(8,128)(2,1)S(1)} collective-permute-done((bf16[256,512]{1,0:T(8,128)(2,1)S(1)}, bf16[256,512]{1,0:T(8,128)(2,1)S(1)}, u32[]{:S(2)}, u32[]{:S(2)}) %collective-permute-start.25) | collective-permute-done | bytes 262176 | tf_op jit(solution)/shard_map/ppermute | solution.py:23
  204.7 1.9 collective-permute-done.33.refs_0_
  206.6 1.4 collective-permute-start.40
  209.4 1.4 collective-permute-start.38
  211.1 1.3 emit.1
  213.0 1.4 collective-permute-done.38.refs_1_
  (67 shorter events, 17.7 us)
Async XLA Ops:
  4.4 66.5 %collective-permute-start.3 = (bf16[2,512,1024]{2,1,0:T(8,128)(2,1)}, bf16[2,512,1024]{2,1,0:T(8,128)(2,1)}, u32[]{:S(2)}, u32[]{:S(2)}) collective-permute-start(bf16[2,512,1024]{2,1,0:T(8,128)(2,1)} %shard_map.78.refs_5_.refs_6_), channel_id=1, source_target_pairs={{0,4},{4,0},{1,5},{5,1},{2,6},{6,2},{3,7},{7,3},{8,12},{12,8},{9,1... | collective-permute-start | bytes 6291464 | tf_op jit(solution)/shard_map/ppermute | solution.py:23
  7.4 135.5 %collective-permute-start.2 = (bf16[2,512,1024]{2,1,0:T(8,128)(2,1)S(1)}, bf16[2,512,1024]{2,1,0:T(8,128)(2,1)}, u32[]{:S(2)}, u32[]{:S(2)}) collective-permute-start(bf16[2,512,1024]{2,1,0:T(8,128)(2,1)S(1)} %shard_map.77.refs_5_.refs_6_), channel_id=1, source_target_pairs={{0,4},{4,0},{1,5},{5,1},{2,6},{6,2},{3,7},{7,3},{8,12},{12,8},{9,1... | collective-permute-start | bytes 6291464 | tf_op jit(solution)/shard_map/ppermute | solution.py:23
  7.5 4.6 %collective-permute-start = (s32[2,1,4,8]{3,2,1,0:T(4,128)}, s32[2,1,4,8]{3,2,1,0:T(4,128)S(1)}, u32[]{:S(2)}, u32[]{:S(2)}) collective-permute-start(s32[2,1,4,8]{3,2,1,0:T(4,128)} %mask_ref.3), channel_id=1, source_target_pairs={{0,4},{4,0},{1,5},{5,1},{2,6},{6,2},{3,7},{7,3},{8,12},{12,8},{9,1... | collective-permute-start | bytes 776 | tf_op jit(solution)/shard_map/ppermute | solution.py:23
  13.8 6.1 %collective-permute-start.4 = (s32[16]{0:T(128)S(1)}, s32[16]{0:T(128)S(1)}, u32[]{:S(2)}, u32[]{:S(2)}) collective-permute-start(s32[16]{0:T(128)S(1)} %plan.1.refs_4_), channel_id=1, source_target_pairs={{0,8},{8,16},{16,24},{1,9},{9,17},{17,25},{2,10},{10,18},{18,26},{... | collective-permute-start | bytes 200 | tf_op jit(solution)/shard_map/ppermute | solution.py:19
  21.4 11.3 %collective-permute-start.5 = (bf16[2,512,128]{2,1,0:T(8,128)(2,1)S(1)}, bf16[2,512,128]{2,1,0:T(8,128)(2,1)S(1)}, u32[]{:S(2)}, u32[]{:S(2)}) collective-permute-start(bf16[2,512,128]{2,1,0:T(8,128)(2,1)S(1)} %shard_map.79), channel_id=1, source_target_pairs={{8,0},{16,8},{24,16},{9,1},{17,9},{25,17},{10,2},{18,10},{26,18},{... | collective-permute-start | bytes 786440 | tf_op jit(solution)/shard_map/ppermute | solution.py:19
  24.2 46.7 %copy-start = (f32[2,16]{1,0:T(2,128)S(1)}, f32[2,16]{1,0:T(2,128)}, u32[]{:S(2)}) copy-start(f32[2,16]{1,0:T(2,128)} %pw.1) | copy-start | bytes 388
  24.2 46.7 %copy-start.1 = (s32[2,1,1]{0,2,1:T(1,128)S(1)}, s32[2,1,1]{0,2,1:T(1,128)}, u32[]{:S(2)}) copy-start(s32[2,1,1]{0,2,1:T(1,128)} %param.11) | copy-start | bytes 28
  24.2 14.1 %collective-permute-start.7 = (bf16[2,512,128]{2,1,0:T(8,128)(2,1)S(1)}, bf16[2,512,128]{2,1,0:T(8,128)(2,1)S(1)}, u32[]{:S(2)}, u32[]{:S(2)}) collective-permute-start(bf16[2,512,128]{2,1,0:T(8,128)(2,1)S(1)} %shard_map.80), channel_id=1, source_target_pairs={{8,0},{16,8},{24,16},{9,1},{17,9},{25,17},{10,2},{18,10},{26,18},{... | collective-permute-start | bytes 786440 | tf_op jit(solution)/shard_map/ppermute | solution.py:19
  26.6 23.0 %collective-permute-start.13 = (bf16[2,512,256]{2,1,0:T(8,128)(2,1)S(1)}, bf16[2,512,256]{2,1,0:T(8,128)(2,1)S(1)}, u32[]{:S(2)}, u32[]{:S(2)}) collective-permute-start(bf16[2,512,256]{2,1,0:T(8,128)(2,1)S(1)} %shard_map.83), channel_id=1, source_target_pairs={{8,0},{16,8},{24,16},{9,1},{17,9},{25,17},{10,2},{18,10},{26,18},{... | collective-permute-start | bytes 1572872 | tf_op jit(solution)/shard_map/ppermute | solution.py:19
  32.7 28.1 %collective-permute-start.11 = (bf16[2,512,256]{2,1,0:T(8,128)(2,1)S(1)}, bf16[2,512,256]{2,1,0:T(8,128)(2,1)S(1)}, u32[]{:S(2)}, u32[]{:S(2)}) collective-permute-start(bf16[2,512,256]{2,1,0:T(8,128)(2,1)S(1)} %shard_map.82), channel_id=1, source_target_pairs={{8,0},{16,8},{24,16},{9,1},{17,9},{25,17},{10,2},{18,10},{26,18},{... | collective-permute-start | bytes 1572872 | tf_op jit(solution)/shard_map/ppermute | solution.py:19
  38.4 32.0 %collective-permute-start.9 = (bf16[2,512,256]{2,1,0:T(8,128)(2,1)S(1)}, bf16[2,512,256]{2,1,0:T(8,128)(2,1)S(1)}, u32[]{:S(2)}, u32[]{:S(2)}) collective-permute-start(bf16[2,512,256]{2,1,0:T(8,128)(2,1)S(1)} %shard_map.81), channel_id=1, source_target_pairs={{8,0},{16,8},{24,16},{9,1},{17,9},{25,17},{10,2},{18,10},{26,18},{... | collective-permute-start | bytes 1572872 | tf_op jit(solution)/shard_map/ppermute | solution.py:19
  49.6 20.8 %collective-permute-start.14 = (bf16[2,512,256]{2,1,0:T(8,128)(2,1)S(1)}, bf16[2,512,256]{2,1,0:T(8,128)(2,1)S(1)}, u32[]{:S(2)}, u32[]{:S(2)}) collective-permute-start(bf16[2,512,256]{2,1,0:T(8,128)(2,1)S(1)} %collective-permute-done.13.refs_8_), channel_id=1, source_target_pairs={{0,4},{4,0},{1,5},{5,1},{2,6},{6,2},{3,7},{7,3},{8,12},{12,8},{9,1... | collective-permute-start | bytes 1572872 | tf_op jit(solution)/shard_map/ppermute | solution.py:23
  60.8 16.8 %collective-permute-start.12 = (bf16[2,512,256]{2,1,0:T(8,128)(2,1)S(1)}, bf16[2,512,256]{2,1,0:T(8,128)(2,1)S(1)}, u32[]{:S(2)}, u32[]{:S(2)}) collective-permute-start(bf16[2,512,256]{2,1,0:T(8,128)(2,1)S(1)} %collective-permute-done.11.refs_8_), channel_id=1, source_target_pairs={{0,4},{4,0},{1,5},{5,1},{2,6},{6,2},{3,7},{7,3},{8,12},{12,8},{9,1... | collective-permute-start | bytes 1572872 | tf_op jit(solution)/shard_map/ppermute | solution.py:23
  70.4 14.1 %collective-permute-start.10 = (bf16[2,512,256]{2,1,0:T(8,128)(2,1)S(1)}, bf16[2,512,256]{2,1,0:T(8,128)(2,1)S(1)}, u32[]{:S(2)}, u32[]{:S(2)}) collective-permute-start(bf16[2,512,256]{2,1,0:T(8,128)(2,1)S(1)} %collective-permute-done.9.refs_8_), channel_id=1, source_target_pairs={{0,4},{4,0},{1,5},{5,1},{2,6},{6,2},{3,7},{7,3},{8,12},{12,8},{9,1... | collective-permute-start | bytes 1572872 | tf_op jit(solution)/shard_map/ppermute | solution.py:23
  70.4 20.9 %collective-permute-start.8 = (bf16[2,512,128]{2,1,0:T(8,128)(2,1)S(1)}, bf16[2,512,128]{2,1,0:T(8,128)(2,1)S(1)}, u32[]{:S(2)}, u32[]{:S(2)}) collective-permute-start(bf16[2,512,128]{2,1,0:T(8,128)(2,1)S(1)} %collective-permute-done.7.refs_8_), channel_id=1, source_target_pairs={{0,4},{4,0},{1,5},{5,1},{2,6},{6,2},{3,7},{7,3},{8,12},{12,8},{9,1... | collective-permute-start | bytes 786440 | tf_op jit(solution)/shard_map/ppermute | solution.py:23
  70.9 25.9 %collective-permute-start.6 = (bf16[2,512,128]{2,1,0:T(8,128)(2,1)S(1)}, bf16[2,512,128]{2,1,0:T(8,128)(2,1)S(1)}, u32[]{:S(2)}, u32[]{:S(2)}) collective-permute-start(bf16[2,512,128]{2,1,0:T(8,128)(2,1)S(1)} %collective-permute-done.5.refs_8_), channel_id=1, source_target_pairs={{0,4},{4,0},{1,5},{5,1},{2,6},{6,2},{3,7},{7,3},{8,12},{12,8},{9,1... | collective-permute-start | bytes 786440 | tf_op jit(solution)/shard_map/ppermute | solution.py:23
  102.2 40.0 %collective-permute-start.17 = (bf16[2,512,256]{2,1,0:T(8,128)(2,1)S(1)}, bf16[2,512,256]{2,1,0:T(8,128)(2,1)S(1)}, u32[]{:S(2)}, u32[]{:S(2)}) collective-permute-start(bf16[2,512,256]{2,1,0:T(8,128)(2,1)S(1)} %get-tuple-element.39), channel_id=1, source_target_pairs={{8,0},{16,8},{24,16},{9,1},{17,9},{25,17},{10,2},{18,10},{26,18},{... | collective-permute-start | bytes 1572872 | tf_op jit(solution)/shard_map/ppermute | solution.py:19
  103.5 38.8 %collective-permute-start.21 = (bf16[2,512,256]{2,1,0:T(8,128)(2,1)S(1)}, bf16[2,512,256]{2,1,0:T(8,128)(2,1)S(1)}, u32[]{:S(2)}, u32[]{:S(2)}) collective-permute-start(bf16[2,512,256]{2,1,0:T(8,128)(2,1)S(1)} %get-tuple-element.41), channel_id=1, source_target_pairs={{8,0},{16,8},{24,16},{9,1},{17,9},{25,17},{10,2},{18,10},{26,18},{... | collective-permute-start | bytes 1572872 | tf_op jit(solution)/shard_map/ppermute | solution.py:19
  104.8 38.0 %collective-permute-start.19 = (bf16[2,512,256]{2,1,0:T(8,128)(2,1)S(1)}, bf16[2,512,256]{2,1,0:T(8,128)(2,1)S(1)}, u32[]{:S(2)}, u32[]{:S(2)}) collective-permute-start(bf16[2,512,256]{2,1,0:T(8,128)(2,1)S(1)} %get-tuple-element.40), channel_id=1, source_target_pairs={{8,0},{16,8},{24,16},{9,1},{17,9},{25,17},{10,2},{18,10},{26,18},{... | collective-permute-start | bytes 1572872 | tf_op jit(solution)/shard_map/ppermute | solution.py:19
  106.1 34.8 %collective-permute-start.1 = (s32[16]{0:T(128)S(1)}, s32[16]{0:T(128)S(1)}, u32[]{:S(2)}, u32[]{:S(2)}) collective-permute-start(s32[16]{0:T(128)S(1)} %plan.1.refs_4_), channel_id=1, source_target_pairs={{8,0},{16,8},{24,16},{9,1},{17,9},{25,17},{10,2},{18,10},{26,18},{... | collective-permute-start | bytes 200 | tf_op jit(solution)/shard_map/ppermute | solution.py:19
  140.9 11.1 %collective-permute-start.23 = (bf16[2,512,128]{2,1,0:T(8,128)(2,1)S(1)}, bf16[2,512,128]{2,1,0:T(8,128)(2,1)S(1)}, u32[]{:S(2)}, u32[]{:S(2)}) collective-permute-start(bf16[2,512,128]{2,1,0:T(8,128)(2,1)S(1)} %get-tuple-element.42), channel_id=1, source_target_pairs={{8,0},{16,8},{24,16},{9,1},{17,9},{25,17},{10,2},{18,10},{26,18},{... | collective-permute-start | bytes 786440 | tf_op jit(solution)/shard_map/ppermute | solution.py:19
  142.2 17.0 %collective-permute-start.18 = (bf16[2,512,256]{2,1,0:T(8,128)(2,1)S(1)}, bf16[2,512,256]{2,1,0:T(8,128)(2,1)S(1)}, u32[]{:S(2)}, u32[]{:S(2)}) collective-permute-start(bf16[2,512,256]{2,1,0:T(8,128)(2,1)S(1)} %collective-permute-done.17.refs_8_), channel_id=1, source_target_pairs={{0,4},{4,0},{1,5},{5,1},{2,6},{6,2},{3,7},{7,3},{8,12},{12,8},{9,1... | collective-permute-start | bytes 1572872 | tf_op jit(solution)/shard_map/ppermute | solution.py:23
  142.3 18.4 %collective-permute-start.22 = (bf16[2,512,256]{2,1,0:T(8,128)(2,1)S(1)}, bf16[2,512,256]{2,1,0:T(8,128)(2,1)S(1)}, u32[]{:S(2)}, u32[]{:S(2)}) collective-permute-start(bf16[2,512,256]{2,1,0:T(8,128)(2,1)S(1)} %collective-permute-done.21.refs_8_), channel_id=1, source_target_pairs={{0,4},{4,0},{1,5},{5,1},{2,6},{6,2},{3,7},{7,3},{8,12},{12,8},{9,1... | collective-permute-start | bytes 1572872 | tf_op jit(solution)/shard_map/ppermute | solution.py:23
  142.8 29.3 %collective-permute-start.20 = (bf16[2,512,256]{2,1,0:T(8,128)(2,1)S(1)}, bf16[2,512,256]{2,1,0:T(8,128)(2,1)S(1)}, u32[]{:S(2)}, u32[]{:S(2)}) collective-permute-start(bf16[2,512,256]{2,1,0:T(8,128)(2,1)S(1)} %collective-permute-done.19.refs_8_), channel_id=1, source_target_pairs={{0,4},{4,0},{1,5},{5,1},{2,6},{6,2},{3,7},{7,3},{8,12},{12,8},{9,1... | collective-permute-start | bytes 1572872 | tf_op jit(solution)/shard_map/ppermute | solution.py:23
  142.9 13.2 %collective-permute-start.15 = (bf16[2,512,128]{2,1,0:T(8,128)(2,1)S(1)}, bf16[2,512,128]{2,1,0:T(8,128)(2,1)S(1)}, u32[]{:S(2)}, u32[]{:S(2)}) collective-permute-start(bf16[2,512,128]{2,1,0:T(8,128)(2,1)S(1)} %get-tuple-element.38), channel_id=1, source_target_pairs={{8,0},{16,8},{24,16},{9,1},{17,9},{25,17},{10,2},{18,10},{26,18},{... | collective-permute-start | bytes 786440 | tf_op jit(solution)/shard_map/ppermute | solution.py:19
  152.0 5.6 %collective-permute-start.24 = (bf16[2,512,128]{2,1,0:T(8,128)(2,1)S(1)}, bf16[2,512,128]{2,1,0:T(8,128)(2,1)S(1)}, u32[]{:S(2)}, u32[]{:S(2)}) collective-permute-start(bf16[2,512,128]{2,1,0:T(8,128)(2,1)S(1)} %collective-permute-done.23.refs_8_), channel_id=1, source_target_pairs={{0,4},{4,0},{1,5},{5,1},{2,6},{6,2},{3,7},{7,3},{8,12},{12,8},{9,1... | collective-permute-start | bytes 786440 | tf_op jit(solution)/shard_map/ppermute | solution.py:23
  156.1 27.4 %collective-permute-start.16 = (bf16[2,512,128]{2,1,0:T(8,128)(2,1)S(1)}, bf16[2,512,128]{2,1,0:T(8,128)(2,1)S(1)}, u32[]{:S(2)}, u32[]{:S(2)}) collective-permute-start(bf16[2,512,128]{2,1,0:T(8,128)(2,1)S(1)} %collective-permute-done.15.refs_8_), channel_id=1, source_target_pairs={{0,4},{4,0},{1,5},{5,1},{2,6},{6,2},{3,7},{7,3},{8,12},{12,8},{9,1... | collective-permute-start | bytes 786440 | tf_op jit(solution)/shard_map/ppermute | solution.py:23
  157.6 31.1 %collective-permute-start.29 = (bf16[256,512]{1,0:T(8,128)(2,1)S(1)}, bf16[256,512]{1,0:T(8,128)(2,1)S(1)}, u32[]{:S(2)}, u32[]{:S(2)}) collective-permute-start(bf16[256,512]{1,0:T(8,128)(2,1)S(1)} %get-tuple-element.55), channel_id=1, source_target_pairs={{0,2},{1,3},{2,0},{3,1},{4,6},{5,7},{6,4},{7,5},{8,10},{9,11},{10,... | collective-permute-start | bytes 786440 | tf_op jit(solution)/shard_map/ppermute | solution.py:23
  159.2 34.8 %collective-permute-start.30 = (bf16[256,512]{1,0:T(8,128)(2,1)S(1)}, bf16[256,512]{1,0:T(8,128)(2,1)S(1)}, u32[]{:S(2)}, u32[]{:S(2)}) collective-permute-start(bf16[256,512]{1,0:T(8,128)(2,1)S(1)} %get-tuple-element.57), channel_id=1, source_target_pairs={{0,1},{1,0},{2,3},{3,2},{4,5},{5,4},{6,7},{7,6},{8,9},{9,8},{10,11... | collective-permute-start | bytes 786440 | tf_op jit(solution)/shard_map/ppermute | solution.py:23
  160.7 33.9 %collective-permute-start.31 = (bf16[256,512]{1,0:T(8,128)(2,1)S(1)}, bf16[256,512]{1,0:T(8,128)(2,1)S(1)}, u32[]{:S(2)}, u32[]{:S(2)}) collective-permute-start(bf16[256,512]{1,0:T(8,128)(2,1)S(1)} %get-tuple-element.59), channel_id=1, source_target_pairs={{0,2},{1,3},{2,0},{3,1},{4,6},{5,7},{6,4},{7,5},{8,10},{9,11},{10,... | collective-permute-start | bytes 786440 | tf_op jit(solution)/shard_map/ppermute | solution.py:23
  172.1 23.1 %collective-permute-start.32 = (bf16[256,512]{1,0:T(8,128)(2,1)S(1)}, bf16[256,512]{1,0:T(8,128)(2,1)S(1)}, u32[]{:S(2)}, u32[]{:S(2)}) collective-permute-start(bf16[256,512]{1,0:T(8,128)(2,1)S(1)} %get-tuple-element.61), channel_id=1, source_target_pairs={{0,1},{1,0},{2,3},{3,2},{4,5},{5,4},{6,7},{7,6},{8,9},{9,8},{10,11... | collective-permute-start | bytes 786440 | tf_op jit(solution)/shard_map/ppermute | solution.py:23
  187.1 9.8 %collective-permute-start.27 = (bf16[256,512]{1,0:T(8,128)(2,1)S(1)}, bf16[256,512]{1,0:T(8,128)(2,1)S(1)}, u32[]{:S(2)}, u32[]{:S(2)}) collective-permute-start(bf16[256,512]{1,0:T(8,128)(2,1)S(1)} %get-tuple-element.50), channel_id=1, source_target_pairs={{0,2},{1,3},{2,0},{3,1},{4,6},{5,7},{6,4},{7,5},{8,10},{9,11},{10,... | collective-permute-start | bytes 786440 | tf_op jit(solution)/shard_map/ppermute | solution.py:23
  188.7 9.8 %collective-permute-start.28 = (bf16[256,512]{1,0:T(8,128)(2,1)S(1)}, bf16[256,512]{1,0:T(8,128)(2,1)S(1)}, u32[]{:S(2)}, u32[]{:S(2)}) collective-permute-start(bf16[256,512]{1,0:T(8,128)(2,1)S(1)} %get-tuple-element.52), channel_id=1, source_target_pairs={{0,1},{1,0},{2,3},{3,2},{4,5},{5,4},{6,7},{7,6},{8,9},{9,8},{10,11... | collective-permute-start | bytes 786440 | tf_op jit(solution)/shard_map/ppermute | solution.py:23
  194.0 9.2 %collective-permute-start.25 = (bf16[256,512]{1,0:T(8,128)(2,1)S(1)}, bf16[256,512]{1,0:T(8,128)(2,1)S(1)}, u32[]{:S(2)}, u32[]{:S(2)}) collective-permute-start(bf16[256,512]{1,0:T(8,128)(2,1)S(1)} %get-tuple-element.46), channel_id=1, source_target_pairs={{0,2},{1,3},{2,0},{3,1},{4,6},{5,7},{6,4},{7,5},{8,10},{9,11},{10,... | collective-permute-start | bytes 786440 | tf_op jit(solution)/shard_map/ppermute | solution.py:23
  194.6 9.2 %collective-permute-start.26 = (bf16[256,512]{1,0:T(8,128)(2,1)S(1)}, bf16[256,512]{1,0:T(8,128)(2,1)S(1)}, u32[]{:S(2)}, u32[]{:S(2)}) collective-permute-start(bf16[256,512]{1,0:T(8,128)(2,1)S(1)} %get-tuple-element.48), channel_id=1, source_target_pairs={{0,1},{1,0},{2,3},{3,2},{4,5},{5,4},{6,7},{7,6},{8,9},{9,8},{10,11... | collective-permute-start | bytes 786440 | tf_op jit(solution)/shard_map/ppermute | solution.py:23
  195.2 11.4 %collective-permute-start.33 = (bf16[256,256]{1,0:T(8,128)(2,1)S(1)}, bf16[256,256]{1,0:T(8,128)(2,1)S(1)}, u32[]{:S(2)}, u32[]{:S(2)}) collective-permute-start(bf16[256,256]{1,0:T(8,128)(2,1)S(1)} %get-tuple-element.62), channel_id=1, source_target_pairs={{0,1},{1,0},{2,3},{3,2},{4,5},{5,4},{6,7},{7,6},{8,9},{9,8},{10,11... | collective-permute-start | bytes 393224 | tf_op jit(solution)/shard_map/ppermute | solution.py:23
  196.9 11.2 %collective-permute-start.34 = (bf16[256,256]{1,0:T(8,128)(2,1)S(1)}, bf16[256,256]{1,0:T(8,128)(2,1)S(1)}, u32[]{:S(2)}, u32[]{:S(2)}) collective-permute-start(bf16[256,256]{1,0:T(8,128)(2,1)S(1)} %get-tuple-element.63), channel_id=1, source_target_pairs={{0,2},{1,3},{2,0},{3,1},{4,6},{5,7},{6,4},{7,5},{8,10},{9,11},{10,... | collective-permute-start | bytes 393224 | tf_op jit(solution)/shard_map/ppermute | solution.py:23
  198.4 11.0 %collective-permute-start.35 = (bf16[256,256]{1,0:T(8,128)(2,1)S(1)}, bf16[256,256]{1,0:T(8,128)(2,1)S(1)}, u32[]{:S(2)}, u32[]{:S(2)}) collective-permute-start(bf16[256,256]{1,0:T(8,128)(2,1)S(1)} %get-tuple-element.64), channel_id=1, source_target_pairs={{0,1},{1,0},{2,3},{3,2},{4,5},{5,4},{6,7},{7,6},{8,9},{9,8},{10,11... | collective-permute-start | bytes 393224 | tf_op jit(solution)/shard_map/ppermute | solution.py:23
  203.2 7.8 %collective-permute-start.36 = (bf16[256,256]{1,0:T(8,128)(2,1)S(1)}, bf16[256,256]{1,0:T(8,128)(2,1)S(1)}, u32[]{:S(2)}, u32[]{:S(2)}) collective-permute-start(bf16[256,256]{1,0:T(8,128)(2,1)S(1)} %get-tuple-element.65), channel_id=1, source_target_pairs={{0,2},{1,3},{2,0},{3,1},{4,6},{5,7},{6,4},{7,5},{8,10},{9,11},{10,... | collective-permute-start | bytes 393224 | tf_op jit(solution)/shard_map/ppermute | solution.py:23
  203.8 8.9 %collective-permute-start.39 = (bf16[256,256]{1,0:T(8,128)(2,1)S(1)}, bf16[256,256]{1,0:T(8,128)(2,1)S(1)}, u32[]{:S(2)}, u32[]{:S(2)}) collective-permute-start(bf16[256,256]{1,0:T(8,128)(2,1)S(1)} %get-tuple-element.68), channel_id=1, source_target_pairs={{0,1},{1,0},{2,3},{3,2},{4,5},{5,4},{6,7},{7,6},{8,9},{9,8},{10,11... | collective-permute-start | bytes 393224 | tf_op jit(solution)/shard_map/ppermute | solution.py:23
  206.6 6.1 %collective-permute-start.40 = (bf16[256,256]{1,0:T(8,128)(2,1)S(1)}, bf16[256,256]{1,0:T(8,128)(2,1)S(1)}, u32[]{:S(2)}, u32[]{:S(2)}) collective-permute-start(bf16[256,256]{1,0:T(8,128)(2,1)S(1)} %get-tuple-element.69), channel_id=1, source_target_pairs={{0,2},{1,3},{2,0},{3,1},{4,6},{5,7},{6,4},{7,5},{8,10},{9,11},{10,... | collective-permute-start | bytes 393224 | tf_op jit(solution)/shard_map/ppermute | solution.py:23
  208.0 5.0 %collective-permute-start.37 = (bf16[256,256]{1,0:T(8,128)(2,1)S(1)}, bf16[256,256]{1,0:T(8,128)(2,1)S(1)}, u32[]{:S(2)}, u32[]{:S(2)}) collective-permute-start(bf16[256,256]{1,0:T(8,128)(2,1)S(1)} %get-tuple-element.66), channel_id=1, source_target_pairs={{0,1},{1,0},{2,3},{3,2},{4,5},{5,4},{6,7},{7,6},{8,9},{9,8},{10,11... | collective-permute-start | bytes 393224 | tf_op jit(solution)/shard_map/ppermute | solution.py:23
  209.4 5.0 %collective-permute-start.38 = (bf16[256,256]{1,0:T(8,128)(2,1)S(1)}, bf16[256,256]{1,0:T(8,128)(2,1)S(1)}, u32[]{:S(2)}, u32[]{:S(2)}) collective-permute-start(bf16[256,256]{1,0:T(8,128)(2,1)S(1)} %get-tuple-element.67), channel_id=1, source_target_pairs={{0,2},{1,3},{2,0},{3,1},{4,6},{5,7},{6,4},{7,5},{8,10},{9,11},{10,... | collective-permute-start | bytes 393224 | tf_op jit(solution)/shard_map/ppermute | solution.py:23

commit v6 on v5

--- a/solution.py
+++ b/solution.py
@@ -148,20 +148,23 @@
     )(mine, *masks)
 
 
-def cut_body(mine, here, plan, src, out, sems, *, first, blocks):
-    wide = src.shape[3] // blocks if first else out.shape[2]
+def cut_body(mine, here, plan, src, *refs, first, blocks):
+    outs, sems = refs[:-1], refs[-1]
+    wide = src.shape[3] // blocks if first else outs[0].shape[2]
     copies = []
-    for u in range(out.shape[2] // wide):
-        at = pl.ds(pl.multiple_of(plan[first + u] * wide, wide) if first else 0, wide)
-        to = slice(u * wide, (u + 1) * wide)
-        copies.append(pltpu.make_async_copy(src.at[0, :, :, at], out.at[:, :, to], sems.at[u]))
+    for out in outs:
+        for u in range(out.shape[2] // wide):
+            unit = len(copies)
+            at = pl.ds(pl.multiple_of(plan[first + unit] * wide, wide) if first else 0, wide)
+            to = slice(u * wide, (u + 1) * wide)
+            copies.append(pltpu.make_async_copy(src.at[0, :, :, at], out.at[:, :, to], sems.at[unit]))
     for copy in copies:
         copy.start()
     for copy in copies:
         copy.wait()
 
 
-def cut_piece(mine, here, plan, state, first, units, blocks):
+def cut_pieces(mine, here, plan, state, first, sizes, blocks):
     rows, width = state.shape[2:]
     return pl.pallas_call(
         functools.partial(cut_body, first=first, blocks=blocks),
@@ -169,10 +172,10 @@
             num_scalar_prefetch=3,
             grid=(1,),
             in_specs=[HBM],
-            out_specs=VMEM,
-            scratch_shapes=[pltpu.SemaphoreType.DMA((units,))],
+            out_specs=[VMEM] * len(sizes),
+            scratch_shapes=[pltpu.SemaphoreType.DMA((sum(sizes),))],
         ),
-        out_shape=jax.ShapeDtypeStruct((2, rows, units * width // blocks), BF16),
+        out_shape=[jax.ShapeDtypeStruct((2, rows, units * width // blocks), BF16) for units in sizes],
         compiler_params=LIMIT,
     )(mine, here, plan, state)
 
@@ -453,14 +456,12 @@
     here = jnp.reshape(lax.axis_index("pole").astype(jnp.int32), (1,))
     mine = jnp.reshape(lax.axis_index("row").astype(jnp.int32), (1,))
     masks = row_pieces(block_mask, 2)
-    state = [cut_piece(mine, here, mine, state_in, 0, ARRIVE[0], blocks)]
+    state = cut_pieces(mine, here, mine, state_in, 0, ARRIVE[:1], blocks)
     plan = make_plan(mine, masks, 0)
     plan_up = shift(plan, "slab", 1)
     plan_down = shift(plan, "slab", -1)
-    at = ARRIVE[0]
-    for units in ARRIVE[1:]:
-        state.append(cut_piece(mine, here, plan_up, state_in, at, units, blocks))
-        at += units
+    state += cut_pieces(mine, here, plan_up, state_in, ARRIVE[0], ARRIVE[1:2], blocks)
+    state += cut_pieces(mine, here, plan_up, state_in, sum(ARRIVE[:2]), ARRIVE[2:], blocks)
     owns = []
     factors = []
     for tick in range(ticks):

time: 216 us -> 217 us (level)
  waiting for transfers between devices: 95.7 us -> 98.3 us
  Pallas kernels: 79.9 us -> 77.4 us
    ppermute x12, waiting for transfers between devices: 83 us -> 85.9 us  [shift(): lax.ppermute(block, axis, [(i, i + step) for i in devices if i + step in...]
    pallas_call x5 -> x3, Pallas kernels: 7.27 us -> 4.74 us  [cut_pieces(): pl.pallas_call(functools.partial(cut_body, first=first, blocks=blocks), g...]
  transfers between devices with their start and end apart: 41 -> 41, of which waited for: 15 -> 15; matrix products, arithmetic and copies ran while one was open for 0% -> 0% of each run, Pallas kernels for 35% -> 34%
where the time goes in v6:
time: 217 us; the launch traced here: 216 us
  waiting for transfers between devices  98.3 us (45%)
  Pallas kernels  77.4 us (36%)
  starting transfers between devices  38.9 us (18%)
    ppermute x12, waiting for transfers between devices, shift(): lax.ppermute(block, axis, [(i, i + step) for i in devices if i + step in...  85.9 us
    pallas_call x11, Pallas kernels, fold(): pl.pallas_call(body, grid_spec=pltpu.PrefetchScalarGridSpec(num_scalar_pr...  60.2 us
    ppermute x29, starting transfers between devices, flip(): lax.ppermute(block, axis, [(i, i ^ bit) for i in range(lax.axis_size(axis...  19.4 us
    ppermute x12, starting transfers between devices, shift(): lax.ppermute(block, axis, [(i, i + step) for i in devices if i + step in...  19.4 us
    ppermute x29, waiting for transfers between devices, flip(): lax.ppermute(block, axis, [(i, i ^ bit) for i in range(lax.axis_size(axis...  12.4 us
    pallas_call x2, Pallas kernels, masked_factor(): pl.pallas_call(functools.partial(mask_body, tick=tick), grid_spec=pltpu.P...  6.17 us
    pallas_call x3, Pallas kernels, cut_pieces(): pl.pallas_call(functools.partial(cut_body, first=first, blocks=blocks), g...  4.74 us
  transfers between devices with their start and end apart: 41, of which 15 were waited for; matrix products, arithmetic and copies ran while one was open for 0% of the time, Pallas kernels for 34%

profile of v6, /device:TPU:0, one launch (start us, length us, event | category | flops | bytes accessed | tf_op | source)
XLA Modules:
  0.0 215.7 jit_solution(13975282309491174561)
XLA Ops:
  0.6 3.7 %shard_map.78.refs_5_.refs_6_ = bf16[2,512,1024]{2,1,0:T(8,128)(2,1)} custom-call(s32[2,1,4,8]{3,2,1,0:T(4,128)} %mask_ref.3, bf16[2,1,2,512,1024]{4,3,2,1,0:T(8,128)(2,1)} %coupling_ref.3), custom_call_target="tpu_custom_call" | custom-call | tf_op jit(solution)/shard_map/pallas_call | solution.py:63
  4.9 2.4 %shard_map.77.refs_5_.refs_6_ = bf16[2,512,1024]{2,1,0:T(8,128)(2,1)S(1)} custom-call(s32[2,1,4,8]{3,2,1,0:T(4,128)} %mask_ref.3, bf16[2,1,2,512,1024]{4,3,2,1,0:T(8,128)(2,1)} %coupling_ref.3), custom_call_target="tpu_custom_call" | custom-call | tf_op jit(solution)/shard_map/pallas_call | solution.py:63
  8.0 4.1 %collective-permute-done.refs_1_ = s32[2,1,4,8]{3,2,1,0:T(4,128)S(1)} collective-permute-done((s32[2,1,4,8]{3,2,1,0:T(4,128)}, s32[2,1,4,8]{3,2,1,0:T(4,128)S(1)}, u32[]{:S(2)}, u32[]{:S(2)}) %collective-permute-start) | collective-permute-done | bytes 288 | tf_op jit(solution)/shard_map/ppermute | solution.py:23
  12.1 1.7 plan.1.refs_4_
  13.8 4.8 %collective-permute-start.4 = (s32[16]{0:T(128)S(1)}, s32[16]{0:T(128)S(1)}, u32[]{:S(2)}, u32[]{:S(2)}) collective-permute-start(s32[16]{0:T(128)S(1)} %plan.1.refs_4_), channel_id=1, source_target_pairs={{0,8},{8,16},{16,24},{1,9},{9,17},{17,25},{2,10},{10,18},{18,26},{... | collective-permute-start | bytes 200 | tf_op jit(solution)/shard_map/ppermute | solution.py:19
  19.9 2.1 shard_map.79
  22.0 1.3 collective-permute-start.5
  23.3 1.3 collective-permute-start.7
  25.7 1.3 collective-permute-start.13
  27.0 1.6 shard_map.80
  28.6 4.5 %collective-permute-done.5.refs_8_ = bf16[2,512,128]{2,1,0:T(8,128)(2,1)S(1)} collective-permute-done((bf16[2,512,128]{2,1,0:T(8,128)(2,1)S(1)}, bf16[2,512,128]{2,1,0:T(8,128)(2,1)S(1)}, u32[]{:S(2)}, u32[]{:S(2)}) %collective-permute-start.5) | collective-permute-done | bytes 262176 | tf_op jit(solution)/shard_map/ppermute | solution.py:19
  33.1 1.3 collective-permute-start.11
  34.4 4.3 %collective-permute-done.7.refs_8_ = bf16[2,512,128]{2,1,0:T(8,128)(2,1)S(1)} collective-permute-done((bf16[2,512,128]{2,1,0:T(8,128)(2,1)S(1)}, bf16[2,512,128]{2,1,0:T(8,128)(2,1)S(1)}, u32[]{:S(2)}, u32[]{:S(2)}) %collective-permute-start.7) | collective-permute-done | bytes 262176 | tf_op jit(solution)/shard_map/ppermute | solution.py:19
  38.7 1.5 collective-permute-start.9
  40.1 9.8 %collective-permute-done.13.refs_8_ = bf16[2,512,256]{2,1,0:T(8,128)(2,1)S(1)} collective-permute-done((bf16[2,512,256]{2,1,0:T(8,128)(2,1)S(1)}, bf16[2,512,256]{2,1,0:T(8,128)(2,1)S(1)}, u32[]{:S(2)}, u32[]{:S(2)}) %collective-permute-start.13) | collective-permute-done | bytes 524320 | tf_op jit(solution)/shard_map/ppermute | solution.py:19
  49.9 11.2 %collective-permute-done.11.refs_8_ = bf16[2,512,256]{2,1,0:T(8,128)(2,1)S(1)} collective-permute-done((bf16[2,512,256]{2,1,0:T(8,128)(2,1)S(1)}, bf16[2,512,256]{2,1,0:T(8,128)(2,1)S(1)}, u32[]{:S(2)}, u32[]{:S(2)}) %collective-permute-start.11) | collective-permute-done | bytes 524320 | tf_op jit(solution)/shard_map/ppermute | solution.py:19
  61.2 9.5 %collective-permute-done.9.refs_8_ = bf16[2,512,256]{2,1,0:T(8,128)(2,1)S(1)} collective-permute-done((bf16[2,512,256]{2,1,0:T(8,128)(2,1)S(1)}, bf16[2,512,256]{2,1,0:T(8,128)(2,1)S(1)}, u32[]{:S(2)}, u32[]{:S(2)}) %collective-permute-start.9) | collective-permute-done | bytes 524320 | tf_op jit(solution)/shard_map/ppermute | solution.py:19
  71.3 6.7 %shard_map.82.refs_10_ = f32[2,512,1024]{2,1,0:T(8,128)S(1)} custom-call(s32[1]{0:T(128)} %bitcast.mine.plan.refs_0_, s32[1,1,2]{2,1,0:T(1,128)S(1)} %bitcast.3, f32[2,16]{1,0:T(2,128)S(1)} %copy-done, s32[1]{0:T(128)} %bitcast.2.here.refs_3_, s32[16]{0:T(128)S(1)} %plan.1.refs_4_, bf16[2,512,1024]{2,1,0:T(8,128)(2,1)} %shard_map.78.refs_5_.refs_6_, ...), custom_call_target="tpu_custom_call" | custom-call | tf_op jit(solution)/shard_map/pallas_call | solution.py:303
  78.0 6.8 %shard_map.83.refs_10_ = f32[2,512,1024]{2,1,0:T(8,128)S(1)} custom-call(s32[1]{0:T(128)} %bitcast.mine.plan.refs_0_, s32[1,1,2]{2,1,0:T(1,128)S(1)} %bitcast.4, f32[2,16]{1,0:T(2,128)S(1)} %copy-done, s32[1]{0:T(128)} %bitcast.2.here.refs_3_, s32[16]{0:T(128)S(1)} %plan.1.refs_4_, ...), custom_call_target="tpu_custom_call", output_to_operand_aliasing={{}: (10, {})} | custom-call | tf_op jit(solution)/shard_map/pallas_call | solution.py:303
  84.8 6.8 %shard_map.84 = (f32[2,512,1024]{2,1,0:T(8,128)S(1)}, bf16[2,512,128]{2,1,0:T(8,128)(2,1)S(1)}) custom-call(s32[1]{0:T(128)} %bitcast.mine.plan.refs_0_, s32[1,1,2]{2,1,0:T(1,128)S(1)} %bitcast.5, f32[2,16]{1,0:T(2,128)S(1)} %copy-done, s32[1]{0:T(128)} %bitcast.2.here.refs_3_, s32[16]{0:T(128)S(1)} %plan.1.refs_4_, ...), custom_call_target="tpu_custom_call", output_to_operand_aliasing={{0}: (10, {})} | custom-call | tf_op jit(solution)/shard_map/pallas_call | solution.py:303
  91.6 5.5 %shard_map.85 = (f32[2,512,1024]{2,1,0:T(8,128)S(1)}, bf16[2,512,256]{2,1,0:T(8,128)(2,1)S(1)}) custom-call(s32[1]{0:T(128)} %bitcast.mine.plan.refs_0_, s32[1,1,2]{2,1,0:T(1,128)S(1)} %bitcast.6, f32[2,16]{1,0:T(2,128)S(1)} %copy-done, s32[1]{0:T(128)} %bitcast.2.here.refs_3_, s32[16]{0:T(128)S(1)} %plan.1.refs_4_, ...), custom_call_target="tpu_custom_call", output_to_operand_aliasing={{0}: (10, {})} | custom-call | tf_op jit(solution)/shard_map/pallas_call | solution.py:303
  97.1 5.4 %shard_map.86 = (bf16[2,512,1024]{2,1,0:T(8,128)(2,1)S(1)}, bf16[2,512,256]{2,1,0:T(8,128)(2,1)S(1)}, bf16[2,512,256]{2,1,0:T(8,128)(2,1)S(1)}, bf16[2,512,128]{2,1,0:T(8,128)(2,1)S(1)}) custom-call(s32[1]{0:T(128)} %bitcast.mine.plan.refs_0_, s32[1,1,2]{2,1,0:T(1,128)S(1)} %bitcast.7, f32[2,16]{1,0:T(2,128)S(1)} %copy-done, s32[1]{0:T(128)} %bitcast.2.here.refs_3_, ...), custom_call_target="tpu_custom_call" | custom-call | tf_op jit(solution)/shard_map/pallas_call | solution.py:303
  102.5 1.3 collective-permute-start.17
  103.8 1.3 collective-permute-start.21
  105.1 1.3 collective-permute-start.19
  106.4 1.3 collective-permute-start.1
  107.7 33.5 %collective-permute-done.1.refs_4_ = s32[16]{0:T(128)S(1)} collective-permute-done((s32[16]{0:T(128)S(1)}, s32[16]{0:T(128)S(1)}, u32[]{:S(2)}, u32[]{:S(2)}) %collective-permute-start.1) | collective-permute-done | bytes 96 | tf_op jit(solution)/shard_map/ppermute | solution.py:19
  143.2 1.5 collective-permute-start.15
  144.7 7.6 %collective-permute-done.23.refs_8_ = bf16[2,512,128]{2,1,0:T(8,128)(2,1)S(1)} collective-permute-done((bf16[2,512,128]{2,1,0:T(8,128)(2,1)S(1)}, bf16[2,512,128]{2,1,0:T(8,128)(2,1)S(1)}, u32[]{:S(2)}, u32[]{:S(2)}) %collective-permute-start.23) | collective-permute-done | bytes 262176 | tf_op jit(solution)/shard_map/ppermute | solution.py:19
  152.3 4.1 %collective-permute-done.15.refs_8_ = bf16[2,512,128]{2,1,0:T(8,128)(2,1)S(1)} collective-permute-done((bf16[2,512,128]{2,1,0:T(8,128)(2,1)S(1)}, bf16[2,512,128]{2,1,0:T(8,128)(2,1)S(1)}, u32[]{:S(2)}, u32[]{:S(2)}) %collective-permute-start.15) | collective-permute-done | bytes 262176 | tf_op jit(solution)/shard_map/ppermute | solution.py:19
  156.5 1.4 shard_map.93
  157.9 1.6 collective-permute-start.29
  159.5 1.5 collective-permute-start.30
  161.5 5.3 %shard_map.87.refs_10_ = f32[2,512,1024]{2,1,0:T(8,128)S(1)} custom-call(s32[1]{0:T(128)} %bitcast.mine.plan.refs_0_, s32[1,1,2]{2,1,0:T(1,128)S(1)} %bitcast.9, f32[2,16]{1,0:T(2,128)S(1)} %copy-done, s32[1]{0:T(128)} %bitcast.2.here.refs_3_, s32[16]{0:T(128)S(1)} %collective-permute-done.1.refs_4_, bf16[2,512,1024]{2,1,0:T(8,128)(2,1)S(1)} %shard_map.77.refs_5_.refs_6_, ...), custom_call_target="tpu_custom_call" | custom-call | tf_op jit(solution)/shard_map/pallas_call | solution.py:303
  166.8 5.5 %shard_map.88.refs_10_ = f32[2,512,1024]{2,1,0:T(8,128)S(1)} custom-call(s32[1]{0:T(128)} %bitcast.mine.plan.refs_0_, s32[1,1,2]{2,1,0:T(1,128)S(1)} %bitcast.10, f32[2,16]{1,0:T(2,128)S(1)} %copy-done, s32[1]{0:T(128)} %bitcast.2.here.refs_3_, s32[16]{0:T(128)S(1)} %collective-permute-done.1.refs_4_, ...), custom_call_target="tpu_custom_call", output_to_operand_aliasing={{}: (10, {})} | custom-call | tf_op jit(solution)/shard_map/pallas_call | solution.py:303
  172.9 5.5 %shard_map.89.refs_10_ = f32[2,512,1024]{2,1,0:T(8,128)S(1)} custom-call(s32[1]{0:T(128)} %bitcast.mine.plan.refs_0_, s32[1,1,2]{2,1,0:T(1,128)S(1)} %bitcast.11, f32[2,16]{1,0:T(2,128)S(1)} %copy-done, s32[1]{0:T(128)} %bitcast.2.here.refs_3_, s32[16]{0:T(128)S(1)} %collective-permute-done.1.refs_4_, ...), custom_call_target="tpu_custom_call", output_to_operand_aliasing={{}: (10, {})} | custom-call | tf_op jit(solution)/shard_map/pallas_call | solution.py:303
  178.4 5.5 %shard_map.90.refs_10_ = f32[2,512,1024]{2,1,0:T(8,128)S(1)} custom-call(s32[1]{0:T(128)} %bitcast.mine.plan.refs_0_, s32[1,1,2]{2,1,0:T(1,128)S(1)} %bitcast.12, f32[2,16]{1,0:T(2,128)S(1)} %copy-done, s32[1]{0:T(128)} %bitcast.2.here.refs_3_, s32[16]{0:T(128)S(1)} %collective-permute-done.1.refs_4_, ...), custom_call_target="tpu_custom_call", output_to_operand_aliasing={{}: (10, {})} | custom-call | tf_op jit(solution)/shard_map/pallas_call | solution.py:303
  183.9 3.5 %shard_map.92 = (bf16[2,256,1024]{2,1,0:T(8,128)(2,1)S(1)}, bf16[256,512]{1,0:T(8,128)(2,1)S(1)}, bf16[256,512]{1,0:T(8,128)(2,1)S(1)}, bf16[256,512]{1,0:T(8,128)(2,1)S(1)}, bf16[256,512]{1,0:T(8,128)(2,1)S(1)}) custom-call(s32[1]{0:T(128)} %bitcast.mine.plan.refs_0_, s32[1,1,2]{2,1,0:T(1,128)S(1)} %bitcast.13, f32[2,16]{1,0:T(2,128)S(1)} %copy-done, ...), custom_call_target="tpu_custom_call" | custom-call | tf_op jit(solution)/shard_map/pallas_call | solution.py:303
  187.4 1.6 collective-permute-start.27
  189.0 1.5 collective-permute-start.28
  190.5 3.8 %shard_map.91 = (bf16[2,256,1024]{2,1,0:T(8,128)(2,1)S(1)}, bf16[256,512]{1,0:T(8,128)(2,1)S(1)}, bf16[256,512]{1,0:T(8,128)(2,1)S(1)}, bf16[256,512]{1,0:T(8,128)(2,1)S(1)}, bf16[256,512]{1,0:T(8,128)(2,1)S(1)}) custom-call(s32[1]{0:T(128)} %bitcast.mine.plan.refs_0_, s32[1,1,2]{2,1,0:T(1,128)S(1)} %bitcast.14, f32[2,16]{1,0:T(2,128)S(1)} %copy-done, ...), custom_call_target="tpu_custom_call" | custom-call | tf_op jit(solution)/shard_map/pallas_call | solution.py:303
  195.5 1.5 collective-permute-start.33
  197.1 1.6 collective-permute-start.34
  199.4 4.1 %collective-permute-done.25.refs_1_.real_got = bf16[256,512]{1,0:T(8,128)(2,1)S(1)} collective-permute-done((bf16[256,512]{1,0:T(8,128)(2,1)S(1)}, bf16[256,512]{1,0:T(8,128)(2,1)S(1)}, u32[]{:S(2)}, u32[]{:S(2)}) %collective-permute-start.25) | collective-permute-done | bytes 262176 | tf_op jit(solution)/shard_map/ppermute | solution.py:23
  205.0 1.8 collective-permute-done.33.refs_0_
  206.8 1.5 collective-permute-start.40
  209.6 1.5 collective-permute-start.38
  211.4 1.3 emit.1
  (65 shorter events, 15.0 us)
Async XLA Ops:
  4.4 66.8 %collective-permute-start.3 = (bf16[2,512,1024]{2,1,0:T(8,128)(2,1)}, bf16[2,512,1024]{2,1,0:T(8,128)(2,1)}, u32[]{:S(2)}, u32[]{:S(2)}) collective-permute-start(bf16[2,512,1024]{2,1,0:T(8,128)(2,1)} %shard_map.78.refs_5_.refs_6_), channel_id=1, source_target_pairs={{0,4},{4,0},{1,5},{5,1},{2,6},{6,2},{3,7},{7,3},{8,12},{12,8},{9,1... | collective-permute-start | bytes 6291464 | tf_op jit(solution)/shard_map/ppermute | solution.py:23
  7.4 63.9 %copy-start = (f32[2,16]{1,0:T(2,128)S(1)}, f32[2,16]{1,0:T(2,128)}, u32[]{:S(2)}) copy-start(f32[2,16]{1,0:T(2,128)} %pw.1) | copy-start | bytes 388
  7.4 63.9 %copy-start.1 = (s32[2,1,1]{0,2,1:T(1,128)S(1)}, s32[2,1,1]{0,2,1:T(1,128)}, u32[]{:S(2)}) copy-start(s32[2,1,1]{0,2,1:T(1,128)} %param.11) | copy-start | bytes 28
  7.4 135.8 %collective-permute-start.2 = (bf16[2,512,1024]{2,1,0:T(8,128)(2,1)S(1)}, bf16[2,512,1024]{2,1,0:T(8,128)(2,1)}, u32[]{:S(2)}, u32[]{:S(2)}) collective-permute-start(bf16[2,512,1024]{2,1,0:T(8,128)(2,1)S(1)} %shard_map.77.refs_5_.refs_6_), channel_id=1, source_target_pairs={{0,4},{4,0},{1,5},{5,1},{2,6},{6,2},{3,7},{7,3},{8,12},{12,8},{9,1... | collective-permute-start | bytes 6291464 | tf_op jit(solution)/shard_map/ppermute | solution.py:23
  7.5 4.6 %collective-permute-start = (s32[2,1,4,8]{3,2,1,0:T(4,128)}, s32[2,1,4,8]{3,2,1,0:T(4,128)S(1)}, u32[]{:S(2)}, u32[]{:S(2)}) collective-permute-start(s32[2,1,4,8]{3,2,1,0:T(4,128)} %mask_ref.3), channel_id=1, source_target_pairs={{0,4},{4,0},{1,5},{5,1},{2,6},{6,2},{3,7},{7,3},{8,12},{12,8},{9,1... | collective-permute-start | bytes 776 | tf_op jit(solution)/shard_map/ppermute | solution.py:23
  13.8 6.1 %collective-permute-start.4 = (s32[16]{0:T(128)S(1)}, s32[16]{0:T(128)S(1)}, u32[]{:S(2)}, u32[]{:S(2)}) collective-permute-start(s32[16]{0:T(128)S(1)} %plan.1.refs_4_), channel_id=1, source_target_pairs={{0,8},{8,16},{16,24},{1,9},{9,17},{17,25},{2,10},{10,18},{18,26},{... | collective-permute-start | bytes 200 | tf_op jit(solution)/shard_map/ppermute | solution.py:19
  22.0 11.1 %collective-permute-start.5 = (bf16[2,512,128]{2,1,0:T(8,128)(2,1)S(1)}, bf16[2,512,128]{2,1,0:T(8,128)(2,1)S(1)}, u32[]{:S(2)}, u32[]{:S(2)}) collective-permute-start(bf16[2,512,128]{2,1,0:T(8,128)(2,1)S(1)} %get-tuple-element.39), channel_id=1, source_target_pairs={{8,0},{16,8},{24,16},{9,1},{17,9},{25,17},{10,2},{18,10},{26,18},{... | collective-permute-start | bytes 786440 | tf_op jit(solution)/shard_map/ppermute | solution.py:19
  23.3 15.4 %collective-permute-start.7 = (bf16[2,512,128]{2,1,0:T(8,128)(2,1)S(1)}, bf16[2,512,128]{2,1,0:T(8,128)(2,1)S(1)}, u32[]{:S(2)}, u32[]{:S(2)}) collective-permute-start(bf16[2,512,128]{2,1,0:T(8,128)(2,1)S(1)} %get-tuple-element.40), channel_id=1, source_target_pairs={{8,0},{16,8},{24,16},{9,1},{17,9},{25,17},{10,2},{18,10},{26,18},{... | collective-permute-start | bytes 786440 | tf_op jit(solution)/shard_map/ppermute | solution.py:19
  25.7 24.3 %collective-permute-start.13 = (bf16[2,512,256]{2,1,0:T(8,128)(2,1)S(1)}, bf16[2,512,256]{2,1,0:T(8,128)(2,1)S(1)}, u32[]{:S(2)}, u32[]{:S(2)}) collective-permute-start(bf16[2,512,256]{2,1,0:T(8,128)(2,1)S(1)} %shard_map.81), channel_id=1, source_target_pairs={{8,0},{16,8},{24,16},{9,1},{17,9},{25,17},{10,2},{18,10},{26,18},{... | collective-permute-start | bytes 1572872 | tf_op jit(solution)/shard_map/ppermute | solution.py:19
  33.1 28.1 %collective-permute-start.11 = (bf16[2,512,256]{2,1,0:T(8,128)(2,1)S(1)}, bf16[2,512,256]{2,1,0:T(8,128)(2,1)S(1)}, u32[]{:S(2)}, u32[]{:S(2)}) collective-permute-start(bf16[2,512,256]{2,1,0:T(8,128)(2,1)S(1)} %shard_map.80), channel_id=1, source_target_pairs={{8,0},{16,8},{24,16},{9,1},{17,9},{25,17},{10,2},{18,10},{26,18},{... | collective-permute-start | bytes 1572872 | tf_op jit(solution)/shard_map/ppermute | solution.py:19
  38.7 32.0 %collective-permute-start.9 = (bf16[2,512,256]{2,1,0:T(8,128)(2,1)S(1)}, bf16[2,512,256]{2,1,0:T(8,128)(2,1)S(1)}, u32[]{:S(2)}, u32[]{:S(2)}) collective-permute-start(bf16[2,512,256]{2,1,0:T(8,128)(2,1)S(1)} %get-tuple-element.41), channel_id=1, source_target_pairs={{8,0},{16,8},{24,16},{9,1},{17,9},{25,17},{10,2},{18,10},{26,18},{... | collective-permute-start | bytes 1572872 | tf_op jit(solution)/shard_map/ppermute | solution.py:19
  49.9 20.8 %collective-permute-start.14 = (bf16[2,512,256]{2,1,0:T(8,128)(2,1)S(1)}, bf16[2,512,256]{2,1,0:T(8,128)(2,1)S(1)}, u32[]{:S(2)}, u32[]{:S(2)}) collective-permute-start(bf16[2,512,256]{2,1,0:T(8,128)(2,1)S(1)} %collective-permute-done.13.refs_8_), channel_id=1, source_target_pairs={{0,4},{4,0},{1,5},{5,1},{2,6},{6,2},{3,7},{7,3},{8,12},{12,8},{9,1... | collective-permute-start | bytes 1572872 | tf_op jit(solution)/shard_map/ppermute | solution.py:23
  61.2 16.8 %collective-permute-start.12 = (bf16[2,512,256]{2,1,0:T(8,128)(2,1)S(1)}, bf16[2,512,256]{2,1,0:T(8,128)(2,1)S(1)}, u32[]{:S(2)}, u32[]{:S(2)}) collective-permute-start(bf16[2,512,256]{2,1,0:T(8,128)(2,1)S(1)} %collective-permute-done.11.refs_8_), channel_id=1, source_target_pairs={{0,4},{4,0},{1,5},{5,1},{2,6},{6,2},{3,7},{7,3},{8,12},{12,8},{9,1... | collective-permute-start | bytes 1572872 | tf_op jit(solution)/shard_map/ppermute | solution.py:23
  70.7 14.1 %collective-permute-start.10 = (bf16[2,512,256]{2,1,0:T(8,128)(2,1)S(1)}, bf16[2,512,256]{2,1,0:T(8,128)(2,1)S(1)}, u32[]{:S(2)}, u32[]{:S(2)}) collective-permute-start(bf16[2,512,256]{2,1,0:T(8,128)(2,1)S(1)} %collective-permute-done.9.refs_8_), channel_id=1, source_target_pairs={{0,4},{4,0},{1,5},{5,1},{2,6},{6,2},{3,7},{7,3},{8,12},{12,8},{9,1... | collective-permute-start | bytes 1572872 | tf_op jit(solution)/shard_map/ppermute | solution.py:23
  70.7 20.9 %collective-permute-start.8 = (bf16[2,512,128]{2,1,0:T(8,128)(2,1)S(1)}, bf16[2,512,128]{2,1,0:T(8,128)(2,1)S(1)}, u32[]{:S(2)}, u32[]{:S(2)}) collective-permute-start(bf16[2,512,128]{2,1,0:T(8,128)(2,1)S(1)} %collective-permute-done.7.refs_8_), channel_id=1, source_target_pairs={{0,4},{4,0},{1,5},{5,1},{2,6},{6,2},{3,7},{7,3},{8,12},{12,8},{9,1... | collective-permute-start | bytes 786440 | tf_op jit(solution)/shard_map/ppermute | solution.py:23
  71.2 25.9 %collective-permute-start.6 = (bf16[2,512,128]{2,1,0:T(8,128)(2,1)S(1)}, bf16[2,512,128]{2,1,0:T(8,128)(2,1)S(1)}, u32[]{:S(2)}, u32[]{:S(2)}) collective-permute-start(bf16[2,512,128]{2,1,0:T(8,128)(2,1)S(1)} %collective-permute-done.5.refs_8_), channel_id=1, source_target_pairs={{0,4},{4,0},{1,5},{5,1},{2,6},{6,2},{3,7},{7,3},{8,12},{12,8},{9,1... | collective-permute-start | bytes 786440 | tf_op jit(solution)/shard_map/ppermute | solution.py:23
  102.5 40.0 %collective-permute-start.17 = (bf16[2,512,256]{2,1,0:T(8,128)(2,1)S(1)}, bf16[2,512,256]{2,1,0:T(8,128)(2,1)S(1)}, u32[]{:S(2)}, u32[]{:S(2)}) collective-permute-start(bf16[2,512,256]{2,1,0:T(8,128)(2,1)S(1)} %get-tuple-element.45), channel_id=1, source_target_pairs={{8,0},{16,8},{24,16},{9,1},{17,9},{25,17},{10,2},{18,10},{26,18},{... | collective-permute-start | bytes 1572872 | tf_op jit(solution)/shard_map/ppermute | solution.py:19
  103.8 38.8 %collective-permute-start.21 = (bf16[2,512,256]{2,1,0:T(8,128)(2,1)S(1)}, bf16[2,512,256]{2,1,0:T(8,128)(2,1)S(1)}, u32[]{:S(2)}, u32[]{:S(2)}) collective-permute-start(bf16[2,512,256]{2,1,0:T(8,128)(2,1)S(1)} %get-tuple-element.47), channel_id=1, source_target_pairs={{8,0},{16,8},{24,16},{9,1},{17,9},{25,17},{10,2},{18,10},{26,18},{... | collective-permute-start | bytes 1572872 | tf_op jit(solution)/shard_map/ppermute | solution.py:19
  105.1 38.0 %collective-permute-start.19 = (bf16[2,512,256]{2,1,0:T(8,128)(2,1)S(1)}, bf16[2,512,256]{2,1,0:T(8,128)(2,1)S(1)}, u32[]{:S(2)}, u32[]{:S(2)}) collective-permute-start(bf16[2,512,256]{2,1,0:T(8,128)(2,1)S(1)} %get-tuple-element.46), channel_id=1, source_target_pairs={{8,0},{16,8},{24,16},{9,1},{17,9},{25,17},{10,2},{18,10},{26,18},{... | collective-permute-start | bytes 1572872 | tf_op jit(solution)/shard_map/ppermute | solution.py:19
  106.4 34.8 %collective-permute-start.1 = (s32[16]{0:T(128)S(1)}, s32[16]{0:T(128)S(1)}, u32[]{:S(2)}, u32[]{:S(2)}) collective-permute-start(s32[16]{0:T(128)S(1)} %plan.1.refs_4_), channel_id=1, source_target_pairs={{8,0},{16,8},{24,16},{9,1},{17,9},{25,17},{10,2},{18,10},{26,18},{... | collective-permute-start | bytes 200 | tf_op jit(solution)/shard_map/ppermute | solution.py:19
  141.3 11.1 %collective-permute-start.23 = (bf16[2,512,128]{2,1,0:T(8,128)(2,1)S(1)}, bf16[2,512,128]{2,1,0:T(8,128)(2,1)S(1)}, u32[]{:S(2)}, u32[]{:S(2)}) collective-permute-start(bf16[2,512,128]{2,1,0:T(8,128)(2,1)S(1)} %get-tuple-element.48), channel_id=1, source_target_pairs={{8,0},{16,8},{24,16},{9,1},{17,9},{25,17},{10,2},{18,10},{26,18},{... | collective-permute-start | bytes 786440 | tf_op jit(solution)/shard_map/ppermute | solution.py:19
  142.6 16.9 %collective-permute-start.18 = (bf16[2,512,256]{2,1,0:T(8,128)(2,1)S(1)}, bf16[2,512,256]{2,1,0:T(8,128)(2,1)S(1)}, u32[]{:S(2)}, u32[]{:S(2)}) collective-permute-start(bf16[2,512,256]{2,1,0:T(8,128)(2,1)S(1)} %collective-permute-done.17.refs_8_), channel_id=1, source_target_pairs={{0,4},{4,0},{1,5},{5,1},{2,6},{6,2},{3,7},{7,3},{8,12},{12,8},{9,1... | collective-permute-start | bytes 1572872 | tf_op jit(solution)/shard_map/ppermute | solution.py:23
  142.6 18.4 %collective-permute-start.22 = (bf16[2,512,256]{2,1,0:T(8,128)(2,1)S(1)}, bf16[2,512,256]{2,1,0:T(8,128)(2,1)S(1)}, u32[]{:S(2)}, u32[]{:S(2)}) collective-permute-start(bf16[2,512,256]{2,1,0:T(8,128)(2,1)S(1)} %collective-permute-done.21.refs_8_), channel_id=1, source_target_pairs={{0,4},{4,0},{1,5},{5,1},{2,6},{6,2},{3,7},{7,3},{8,12},{12,8},{9,1... | collective-permute-start | bytes 1572872 | tf_op jit(solution)/shard_map/ppermute | solution.py:23
  143.1 29.2 %collective-permute-start.20 = (bf16[2,512,256]{2,1,0:T(8,128)(2,1)S(1)}, bf16[2,512,256]{2,1,0:T(8,128)(2,1)S(1)}, u32[]{:S(2)}, u32[]{:S(2)}) collective-permute-start(bf16[2,512,256]{2,1,0:T(8,128)(2,1)S(1)} %collective-permute-done.19.refs_8_), channel_id=1, source_target_pairs={{0,4},{4,0},{1,5},{5,1},{2,6},{6,2},{3,7},{7,3},{8,12},{12,8},{9,1... | collective-permute-start | bytes 1572872 | tf_op jit(solution)/shard_map/ppermute | solution.py:23
  143.2 13.2 %collective-permute-start.15 = (bf16[2,512,128]{2,1,0:T(8,128)(2,1)S(1)}, bf16[2,512,128]{2,1,0:T(8,128)(2,1)S(1)}, u32[]{:S(2)}, u32[]{:S(2)}) collective-permute-start(bf16[2,512,128]{2,1,0:T(8,128)(2,1)S(1)} %get-tuple-element.44), channel_id=1, source_target_pairs={{8,0},{16,8},{24,16},{9,1},{17,9},{25,17},{10,2},{18,10},{26,18},{... | collective-permute-start | bytes 786440 | tf_op jit(solution)/shard_map/ppermute | solution.py:19
  152.3 5.6 %collective-permute-start.24 = (bf16[2,512,128]{2,1,0:T(8,128)(2,1)S(1)}, bf16[2,512,128]{2,1,0:T(8,128)(2,1)S(1)}, u32[]{:S(2)}, u32[]{:S(2)}) collective-permute-start(bf16[2,512,128]{2,1,0:T(8,128)(2,1)S(1)} %collective-permute-done.23.refs_8_), channel_id=1, source_target_pairs={{0,4},{4,0},{1,5},{5,1},{2,6},{6,2},{3,7},{7,3},{8,12},{12,8},{9,1... | collective-permute-start | bytes 786440 | tf_op jit(solution)/shard_map/ppermute | solution.py:23
  156.5 27.4 %collective-permute-start.16 = (bf16[2,512,128]{2,1,0:T(8,128)(2,1)S(1)}, bf16[2,512,128]{2,1,0:T(8,128)(2,1)S(1)}, u32[]{:S(2)}, u32[]{:S(2)}) collective-permute-start(bf16[2,512,128]{2,1,0:T(8,128)(2,1)S(1)} %collective-permute-done.15.refs_8_), channel_id=1, source_target_pairs={{0,4},{4,0},{1,5},{5,1},{2,6},{6,2},{3,7},{7,3},{8,12},{12,8},{9,1... | collective-permute-start | bytes 786440 | tf_op jit(solution)/shard_map/ppermute | solution.py:23
  157.9 31.1 %collective-permute-start.29 = (bf16[256,512]{1,0:T(8,128)(2,1)S(1)}, bf16[256,512]{1,0:T(8,128)(2,1)S(1)}, u32[]{:S(2)}, u32[]{:S(2)}) collective-permute-start(bf16[256,512]{1,0:T(8,128)(2,1)S(1)} %get-tuple-element.61), channel_id=1, source_target_pairs={{0,2},{1,3},{2,0},{3,1},{4,6},{5,7},{6,4},{7,5},{8,10},{9,11},{10,... | collective-permute-start | bytes 786440 | tf_op jit(solution)/shard_map/ppermute | solution.py:23
  159.5 34.8 %collective-permute-start.30 = (bf16[256,512]{1,0:T(8,128)(2,1)S(1)}, bf16[256,512]{1,0:T(8,128)(2,1)S(1)}, u32[]{:S(2)}, u32[]{:S(2)}) collective-permute-start(bf16[256,512]{1,0:T(8,128)(2,1)S(1)} %get-tuple-element.63), channel_id=1, source_target_pairs={{0,1},{1,0},{2,3},{3,2},{4,5},{5,4},{6,7},{7,6},{8,9},{9,8},{10,11... | collective-permute-start | bytes 786440 | tf_op jit(solution)/shard_map/ppermute | solution.py:23
  161.0 33.9 %collective-permute-start.31 = (bf16[256,512]{1,0:T(8,128)(2,1)S(1)}, bf16[256,512]{1,0:T(8,128)(2,1)S(1)}, u32[]{:S(2)}, u32[]{:S(2)}) collective-permute-start(bf16[256,512]{1,0:T(8,128)(2,1)S(1)} %get-tuple-element.65), channel_id=1, source_target_pairs={{0,2},{1,3},{2,0},{3,1},{4,6},{5,7},{6,4},{7,5},{8,10},{9,11},{10,... | collective-permute-start | bytes 786440 | tf_op jit(solution)/shard_map/ppermute | solution.py:23
  172.3 23.2 %collective-permute-start.32 = (bf16[256,512]{1,0:T(8,128)(2,1)S(1)}, bf16[256,512]{1,0:T(8,128)(2,1)S(1)}, u32[]{:S(2)}, u32[]{:S(2)}) collective-permute-start(bf16[256,512]{1,0:T(8,128)(2,1)S(1)} %get-tuple-element.67), channel_id=1, source_target_pairs={{0,1},{1,0},{2,3},{3,2},{4,5},{5,4},{6,7},{7,6},{8,9},{9,8},{10,11... | collective-permute-start | bytes 786440 | tf_op jit(solution)/shard_map/ppermute | solution.py:23
  187.4 9.7 %collective-permute-start.27 = (bf16[256,512]{1,0:T(8,128)(2,1)S(1)}, bf16[256,512]{1,0:T(8,128)(2,1)S(1)}, u32[]{:S(2)}, u32[]{:S(2)}) collective-permute-start(bf16[256,512]{1,0:T(8,128)(2,1)S(1)} %get-tuple-element.56), channel_id=1, source_target_pairs={{0,2},{1,3},{2,0},{3,1},{4,6},{5,7},{6,4},{7,5},{8,10},{9,11},{10,... | collective-permute-start | bytes 786440 | tf_op jit(solution)/shard_map/ppermute | solution.py:23
  189.0 9.8 %collective-permute-start.28 = (bf16[256,512]{1,0:T(8,128)(2,1)S(1)}, bf16[256,512]{1,0:T(8,128)(2,1)S(1)}, u32[]{:S(2)}, u32[]{:S(2)}) collective-permute-start(bf16[256,512]{1,0:T(8,128)(2,1)S(1)} %get-tuple-element.58), channel_id=1, source_target_pairs={{0,1},{1,0},{2,3},{3,2},{4,5},{5,4},{6,7},{7,6},{8,9},{9,8},{10,11... | collective-permute-start | bytes 786440 | tf_op jit(solution)/shard_map/ppermute | solution.py:23
  194.3 9.2 %collective-permute-start.25 = (bf16[256,512]{1,0:T(8,128)(2,1)S(1)}, bf16[256,512]{1,0:T(8,128)(2,1)S(1)}, u32[]{:S(2)}, u32[]{:S(2)}) collective-permute-start(bf16[256,512]{1,0:T(8,128)(2,1)S(1)} %get-tuple-element.52), channel_id=1, source_target_pairs={{0,2},{1,3},{2,0},{3,1},{4,6},{5,7},{6,4},{7,5},{8,10},{9,11},{10,... | collective-permute-start | bytes 786440 | tf_op jit(solution)/shard_map/ppermute | solution.py:23
  194.8 9.2 %collective-permute-start.26 = (bf16[256,512]{1,0:T(8,128)(2,1)S(1)}, bf16[256,512]{1,0:T(8,128)(2,1)S(1)}, u32[]{:S(2)}, u32[]{:S(2)}) collective-permute-start(bf16[256,512]{1,0:T(8,128)(2,1)S(1)} %get-tuple-element.54), channel_id=1, source_target_pairs={{0,1},{1,0},{2,3},{3,2},{4,5},{5,4},{6,7},{7,6},{8,9},{9,8},{10,11... | collective-permute-start | bytes 786440 | tf_op jit(solution)/shard_map/ppermute | solution.py:23
  195.5 11.3 %collective-permute-start.33 = (bf16[256,256]{1,0:T(8,128)(2,1)S(1)}, bf16[256,256]{1,0:T(8,128)(2,1)S(1)}, u32[]{:S(2)}, u32[]{:S(2)}) collective-permute-start(bf16[256,256]{1,0:T(8,128)(2,1)S(1)} %get-tuple-element.68), channel_id=1, source_target_pairs={{0,1},{1,0},{2,3},{3,2},{4,5},{5,4},{6,7},{7,6},{8,9},{9,8},{10,11... | collective-permute-start | bytes 393224 | tf_op jit(solution)/shard_map/ppermute | solution.py:23
  197.1 11.2 %collective-permute-start.34 = (bf16[256,256]{1,0:T(8,128)(2,1)S(1)}, bf16[256,256]{1,0:T(8,128)(2,1)S(1)}, u32[]{:S(2)}, u32[]{:S(2)}) collective-permute-start(bf16[256,256]{1,0:T(8,128)(2,1)S(1)} %get-tuple-element.69), channel_id=1, source_target_pairs={{0,2},{1,3},{2,0},{3,1},{4,6},{5,7},{6,4},{7,5},{8,10},{9,11},{10,... | collective-permute-start | bytes 393224 | tf_op jit(solution)/shard_map/ppermute | solution.py:23
  198.8 10.9 %collective-permute-start.35 = (bf16[256,256]{1,0:T(8,128)(2,1)S(1)}, bf16[256,256]{1,0:T(8,128)(2,1)S(1)}, u32[]{:S(2)}, u32[]{:S(2)}) collective-permute-start(bf16[256,256]{1,0:T(8,128)(2,1)S(1)} %get-tuple-element.70), channel_id=1, source_target_pairs={{0,1},{1,0},{2,3},{3,2},{4,5},{5,4},{6,7},{7,6},{8,9},{9,8},{10,11... | collective-permute-start | bytes 393224 | tf_op jit(solution)/shard_map/ppermute | solution.py:23
  203.5 7.8 %collective-permute-start.36 = (bf16[256,256]{1,0:T(8,128)(2,1)S(1)}, bf16[256,256]{1,0:T(8,128)(2,1)S(1)}, u32[]{:S(2)}, u32[]{:S(2)}) collective-permute-start(bf16[256,256]{1,0:T(8,128)(2,1)S(1)} %get-tuple-element.71), channel_id=1, source_target_pairs={{0,2},{1,3},{2,0},{3,1},{4,6},{5,7},{6,4},{7,5},{8,10},{9,11},{10,... | collective-permute-start | bytes 393224 | tf_op jit(solution)/shard_map/ppermute | solution.py:23
  204.0 9.0 %collective-permute-start.39 = (bf16[256,256]{1,0:T(8,128)(2,1)S(1)}, bf16[256,256]{1,0:T(8,128)(2,1)S(1)}, u32[]{:S(2)}, u32[]{:S(2)}) collective-permute-start(bf16[256,256]{1,0:T(8,128)(2,1)S(1)} %get-tuple-element.74), channel_id=1, source_target_pairs={{0,1},{1,0},{2,3},{3,2},{4,5},{5,4},{6,7},{7,6},{8,9},{9,8},{10,11... | collective-permute-start | bytes 393224 | tf_op jit(solution)/shard_map/ppermute | solution.py:23
  206.8 6.2 %collective-permute-start.40 = (bf16[256,256]{1,0:T(8,128)(2,1)S(1)}, bf16[256,256]{1,0:T(8,128)(2,1)S(1)}, u32[]{:S(2)}, u32[]{:S(2)}) collective-permute-start(bf16[256,256]{1,0:T(8,128)(2,1)S(1)} %get-tuple-element.75), channel_id=1, source_target_pairs={{0,2},{1,3},{2,0},{3,1},{4,6},{5,7},{6,4},{7,5},{8,10},{9,11},{10,... | collective-permute-start | bytes 393224 | tf_op jit(solution)/shard_map/ppermute | solution.py:23
  208.4 5.0 %collective-permute-start.37 = (bf16[256,256]{1,0:T(8,128)(2,1)S(1)}, bf16[256,256]{1,0:T(8,128)(2,1)S(1)}, u32[]{:S(2)}, u32[]{:S(2)}) collective-permute-start(bf16[256,256]{1,0:T(8,128)(2,1)S(1)} %get-tuple-element.72), channel_id=1, source_target_pairs={{0,1},{1,0},{2,3},{3,2},{4,5},{5,4},{6,7},{7,6},{8,9},{9,8},{10,11... | collective-permute-start | bytes 393224 | tf_op jit(solution)/shard_map/ppermute | solution.py:23
  209.6 5.0 %collective-permute-start.38 = (bf16[256,256]{1,0:T(8,128)(2,1)S(1)}, bf16[256,256]{1,0:T(8,128)(2,1)S(1)}, u32[]{:S(2)}, u32[]{:S(2)}) collective-permute-start(bf16[256,256]{1,0:T(8,128)(2,1)S(1)} %get-tuple-element.73), channel_id=1, source_target_pairs={{0,2},{1,3},{2,0},{3,1},{4,6},{5,7},{6,4},{7,5},{8,10},{9,11},{10,... | collective-permute-start | bytes 393224 | tf_op jit(solution)/shard_map/ppermute | solution.py:23

commit v7 on v6

--- a/solution.py
+++ b/solution.py
@@ -187,57 +187,69 @@
     factor = refs[:pieces]
     behind = refs[pieces : 2 * pieces]
     before = refs[2 * pieces]
-    right, low, high = refs[-3:]
-    outs = refs[1 + 2 * pieces : -3]
+    outs = refs[1 + 2 * pieces :]
     span = behind[0].shape[2]
     wide = own.shape[2] // blocks
 
-    def block_cols(index):
-        return pl.ds(pl.multiple_of(plan[index] * wide, wide), wide)
+    def block_cols(at_block):
+        return pl.ds(pl.multiple_of(plan[at_block] * wide, wide), wide)
+
+    def offset(k):
+        size = behind[k].shape[1]
+        return 0 if pieces == 1 else pl.multiple_of((mine[0] if k == 0 else 1 - mine[0]) * size, size)
 
     if first:
         green, sem = outs[-2:]
         outs = outs[:-2]
         fetch = pltpu.make_async_copy(before.at[tick, 0], green, sem)
         fetch.start()
-    for k in range(pieces):
-        size = behind[k].shape[1]
-        at = slice(0, size)
-        if pieces == 2:
-            at = pl.ds(pl.multiple_of((mine[0] if k == 0 else 1 - mine[0]) * size, size), size)
-        right[at, :span] = behind[k][0]
-        right[at, span:] = behind[k][1]
-        for u in range(span // wide):
-            cols = block_cols(base + u)
-            real = factor[k][0, :, cols]
-            imag = factor[k][1, :, cols]
-            one = slice(u * wide, (u + 1) * wide)
-            two = slice(span + u * wide, span + (u + 1) * wide)
-            low[at, one] = real
-            low[at, two] = -imag
-            high[at, one] = imag
-            high[at, two] = real
+    if kind == "final":
+        term = outs[-1]
+        outs = outs[:-1]
+    units = [block_cols(base + u) for u in range(span // wide)]
     tile = min(count, 256)
     for step in range(count // tile):
         at = slice(top + step * tile, top + (step + 1) * tile)
         to = slice(step * tile, (step + 1) * tile)
-        a = dot(own[0, at], right[...])
-        b = dot(own[1, at], right[...])
-        half = jnp.concatenate([a[:, :span] - b[:, span:], a[:, span:] + b[:, :span]], axis=1).astype(BF16)
-        real = dot_t(half, low[...])
-        imag = dot_t(half, high[...])
-        if first:
-            if step == 0:
-                fetch.wait()
-            real = green[0, at].astype(F32) + real
-            imag = green[1, at].astype(F32) + imag
-        else:
-            real = before[0, at] + real
-            imag = before[1, at] + imag
-        outs[0][0, to] = real.astype(outs[0].dtype)
-        outs[0][1, to] = imag.astype(outs[0].dtype)
+        both = None
+        for k in range(pieces):
+            inner = pl.ds(offset(k), behind[k].shape[1])
+            left = jnp.concatenate([own[0, at, inner], own[1, at, inner]], axis=0)
+            share = dot(left, jnp.concatenate([behind[k][0], behind[k][1]], axis=1))
+            both = share if both is None else both + share
+        real = both[:tile, :span] - both[tile:, span:]
+        imag = both[:tile, span:] + both[tile:, :span]
+        left = jnp.concatenate(
+            [jnp.concatenate([real, -imag], axis=1), jnp.concatenate([imag, real], axis=1)], axis=0
+        ).astype(BF16)
+        if first and step == 0:
+            fetch.wait()
+        for k in range(pieces):
+            size = behind[k].shape[1]
+            group = min(size, 256)
+            for start in range(0, size, group):
+                rows = slice(start, start + group)
+                right = jnp.concatenate([factor[k][part, rows, cols] for part in range(2) for cols in units], axis=1)
+                pair = dot_t(left, right)
+                cols = pl.ds(offset(k) + start, group)
+                if pieces == 2:
+                    cols = pl.ds(pl.multiple_of(offset(k) + start, group), group)
+                values = []
+                for part in range(2):
+                    value = pair[part * tile : (part + 1) * tile]
+                    if first:
+                        value = green[part, at, cols].astype(F32) + value
+                    else:
+                        value = before[part, at, cols] + value
+                    value = value.astype(outs[0].dtype)
+                    outs[0][part, to, cols] = value
+                    values.append(value)
+                if kind == "final":
+                    weighted = weigh_pair(values, pidx, pw, tick)
+                    term[0, to, cols] = weighted[0]
+                    term[1, to, cols] = weighted[1]
         if kind == "final":
-            write_term(real.astype(BF16), imag.astype(BF16), pidx, pw, here, tick, outs[1:], step * tile)
+            deal_term(term, here, outs[1:], to)
             continue
         at_block = blocks + index
         for out in outs[1:]:
@@ -247,56 +259,58 @@
                 at_block += 1
 
 
-def write_term(real, imag, pidx, pw, here, tick, outs, row):
-    real = real.astype(F32)
-    imag = imag.astype(F32)
+def weigh_pair(values, pidx, pw, tick):
+    real, imag = (value.astype(F32) for value in values)
     w0 = pw[0, pidx[0, 0, tick]]
     w1 = pw[1, pidx[0, 0, tick]]
-    term_real = (w0 * real - w1 * imag).astype(BF16)
-    term_imag = (w0 * imag + w1 * real).astype(BF16)
-    high, width = real.shape
+    return (w0 * real - w1 * imag).astype(BF16), (w0 * imag + w1 * real).astype(BF16)
+
+
+def deal_term(term, here, outs, at):
     if len(outs) == 1:
-        outs[0][0, row : row + high] = term_real
-        outs[0][1, row : row + high] = term_imag
+        outs[0][:, at] = term[:, at]
         return
-    part = row // outs[0].shape[0]
-    row -= part * outs[0].shape[0]
-    at = slice(row, row + high)
-    real_send, real_keep, imag_send, imag_keep = outs[4 * part : 4 * part + 4]
-    quarter = width // 4
-    first_major = here[0] // 2 == 0
-    first_minor = here[0] % 2 == 0
-    lower, upper = term_real[:, : 2 * quarter], term_real[:, 2 * quarter :]
-    real_send[at] = jnp.where(first_major, upper, lower)
-    real_keep[at] = jnp.where(first_major, lower, upper)
+    real_send, real_keep, imag_send, imag_keep = outs
+    quarter = term.shape[2] // 4
+    major, minor = here[0] // 2, here[0] % 2
+
+    def cut(part, start, size):
+        return term[part, at, pl.ds(pl.multiple_of(start * quarter, quarter), size * quarter)]
+
+    real_send[at] = cut(0, 2 * (1 - major), 2)
+    real_keep[at] = cut(0, 2 * major, 2)
     for pair in range(2):
         cols = slice(pair * quarter, (pair + 1) * quarter)
-        even = term_imag[:, 2 * pair * quarter : (2 * pair + 1) * quarter]
-        odd = term_imag[:, (2 * pair + 1) * quarter : (2 * pair + 2) * quarter]
-        imag_send[at, cols] = jnp.where(first_minor, odd, even)
-        imag_keep[at, cols] = jnp.where(first_minor, even, odd)
+        imag_send[at, cols] = cut(1, 2 * pair + 1 - minor, 1)
+        imag_keep[at, cols] = cut(1, 2 * pair + minor, 1)
 
 
 def term_shapes(rows, width):
     if lax.axis_size("pole") != 4:
         return [jax.ShapeDtypeStruct((2, rows, width), BF16)]
-    parts = 2 if rows % 512 == 0 else 1
-    return [jax.ShapeDtypeStruct((rows // parts, width // 2), BF16)] * (4 * parts)
+    return [jax.ShapeDtypeStruct((rows, width // 2), BF16)] * 4
+
+
+def row_parts(rows):
+    if rows % 512 or lax.axis_size("pole") != 4:
+        return [(0, rows)]
+    unit = rows // 4
+    return [(0, unit), (unit, 2 * unit), (3 * unit, unit)]
 
 
 def fold(scalars, own, factor, behind, before, tick, first, kind, base, sends=(), index=0, part=None):
     rows, width = own.shape[1:]
     blocks = scalars[4].shape[0] // 2
     wide = width // blocks
-    span = behind[0].shape[2]
     pieces = len(behind)
-    top, count = (0, rows) if part is None else (part[0] * (rows // part[1]), rows // part[1])
+    top, count = part or (0, rows)
     done = kind in ("final", "send")
     out_shape = [jax.ShapeDtypeStruct((2, count, width), BF16 if done else F32)]
     out_shape += [jax.ShapeDtypeStruct((2, rows, units * wide), BF16) for units in sends]
+    scratch = [pltpu.VMEM((2, rows, width), BF16), pltpu.SemaphoreType.DMA] if first else []
     if kind == "final":
-        out_shape += term_shapes(rows, width)[: 4 if part[1] == 2 else None]
-    scratch = [pltpu.VMEM((2, rows, width), BF16), pltpu.SemaphoreType.DMA] if first else []
+        out_shape += term_shapes(count, width)
+        scratch = [pltpu.VMEM((2, count, width), BF16)]
     body = functools.partial(
         fold_body, pieces=pieces, tick=tick, first=first, kind=kind, base=base, index=index, top=top, count=count, blocks=blocks
     )
@@ -307,7 +321,7 @@
             grid=(1,),
             in_specs=[VMEM] * (1 + 2 * pieces) + [HBM if first else VMEM],
             out_specs=[VMEM] * len(out_shape),
-            scratch_shapes=scratch + [pltpu.VMEM((width, 2 * span), BF16)] * 3,
+            scratch_shapes=scratch,
         ),
         out_shape=out_shape,
         input_output_aliases={} if first or done else {len(scalars) + 1 + 2 * pieces: 0},
@@ -315,37 +329,45 @@
     )(*scalars, own, *factor, *behind, before)
 
 
-def term_body(pidx, pw, here, *refs, tick, count):
-    rows = refs[0].shape[1]
-    tile = min(rows, 256)
+def term_body(pidx, pw, here, state, *refs, tick):
+    outs, term = refs[:-1], refs[-1]
+    rows, width = state.shape[1:]
+    tile = min(rows, 128)
+    group = min(width, 256)
     for row in range(0, rows, tile):
-        real = jnp.concatenate([ref[0, row : row + tile] for ref in refs[:count]], axis=1)
-        imag = jnp.concatenate([ref[1, row : row + tile] for ref in refs[:count]], axis=1)
-        write_term(real, imag, pidx, pw, here, tick, refs[count:], row)
+        at = slice(row, row + tile)
+        for col in range(0, width, group):
+            cols = slice(col, col + group)
+            weighted = weigh_pair([state[part, at, cols] for part in range(2)], pidx, pw, tick)
+            term[0, at, cols] = weighted[0]
+            term[1, at, cols] = weighted[1]
+        deal_term(term, here, outs, at)
 
 
 def weigh(scalars, state, tick):
-    out_shape = term_shapes(state[0].shape[1], sum(piece.shape[2] for piece in state))
-    return pl.pallas_call(
-        functools.partial(term_body, tick=tick, count=len(state)),
+    out_shape = term_shapes(*state.shape[1:])
+    return pl.pallas_call(
+        functools.partial(term_body, tick=tick),
         grid_spec=pltpu.PrefetchScalarGridSpec(
             num_scalar_prefetch=3,
             grid=(1,),
-            in_specs=[VMEM] * len(state),
+            in_specs=[VMEM],
             out_specs=[VMEM] * len(out_shape),
+            scratch_shapes=[pltpu.VMEM(state.shape, BF16)],
         ),
         out_shape=out_shape,
         compiler_params=LIMIT,
-    )(*scalars[1:], *state)
+    )(*scalars[1:], state)
 
 
 def emit_body(*refs):
     out, sems = refs[-2:]
-    parts = refs[:-2]
-    high = parts[0].shape[1]
-    copies = [
-        pltpu.make_async_copy(ref, out.at[0, :, pl.ds(k * high, high), :], sems.at[k]) for k, ref in enumerate(parts)
-    ]
+    copies = []
+    row = 0
+    for k, ref in enumerate(refs[:-2]):
+        high = ref.shape[1]
+        copies.append(pltpu.make_async_copy(ref, out.at[0, :, pl.ds(row, high), :], sems.at[k]))
+        row += high
     for copy in copies:
         copy.start()
     for copy in copies:
@@ -353,12 +375,12 @@
 
 
 def emit(parts):
-    high, width = parts[0].shape[1:]
+    rows, width = sum(part.shape[1] for part in parts), parts[0].shape[2]
     return pl.pallas_call(
         emit_body,
         in_specs=[VMEM] * len(parts),
         out_specs=HBM,
-        out_shape=jax.ShapeDtypeStruct((1, 2, high * len(parts), width), BF16),
+        out_shape=jax.ShapeDtypeStruct((1, 2, rows, width), BF16),
         scratch_shapes=[pltpu.SemaphoreType.DMA((len(parts),))],
         compiler_params=LIMIT,
         name="emit",
@@ -379,10 +401,11 @@
 def retain_body(here, *refs, parts, extra):
     major, minor = here[0] // 2, here[0] % 2
     out = refs[-1]
-    high = refs[0].shape[0]
+    row = 0
     for k in range(parts):
         real_keep, real_got, imag_keep, imag_got = refs[4 * k : 4 * k + 4]
-        at = slice(k * high, (k + 1) * high)
+        at = slice(row, row + real_keep.shape[0])
+        row = at.stop
         real = picked(real_keep, minor) + picked(real_got, minor)
         imag = picked(imag_keep, major) + picked(imag_got, major)
         if extra:
@@ -392,14 +415,40 @@
         out[1, at] = imag
 
 
-def close_body(base, *refs):
-    out = refs[-1]
-    parts = len(refs) // 2
-    high = refs[0].shape[0]
-    for k in range(parts):
-        at = slice(k * high, (k + 1) * high)
-        out[0, at] = base[0, at] + refs[2 * k][...].astype(F32)
-        out[1, at] = base[1, at] + refs[2 * k + 1][...].astype(F32)
+def close_body(base, *refs, top, write):
+    if write:
+        out, total, sem = refs[-3:]
+        lasts = refs[:-4] if top else refs[:-3]
+        row = top
+    else:
+        total = refs[-1]
+        lasts = refs[:-1]
+        row = 0
+    first = row
+    for k in range(len(lasts) // 2):
+        at = slice(row, row + lasts[2 * k].shape[0])
+        to = slice(row - first, at.stop - first)
+        row = at.stop
+        total[0, to] = base[0, at] + lasts[2 * k][...].astype(F32)
+        total[1, to] = base[1, at] + lasts[2 * k + 1][...].astype(F32)
+    if write:
+        copy = pltpu.make_async_copy(total, out.at[:, pl.ds(first, row - first), :], sem)
+        copy.start()
+        copy.wait()
+
+
+def close_out(base, lasts, top, whole):
+    high = sum(last.shape[0] for last in lasts[::2])
+    args = [base, *lasts] + ([whole] if top else [])
+    return pl.pallas_call(
+        functools.partial(close_body, top=top, write=True),
+        in_specs=[VMEM] * (1 + len(lasts)) + ([HBM] if top else []),
+        out_specs=HBM,
+        out_shape=jax.ShapeDtypeStruct(base.shape, F32),
+        scratch_shapes=[pltpu.VMEM((2, high, base.shape[2]), F32), pltpu.SemaphoreType.DMA],
+        input_output_aliases={len(args) - 1: 0} if top else {},
+        compiler_params=LIMIT,
+    )(*args)
 
 
 def kernel_call(fn, scalars, args, out_shape):
@@ -417,30 +466,40 @@
     )(*scalars, *args)
 
 
-def scatter_sum(terms, before, here):
-    if len(terms) == 1:
-        share = lax.psum_scatter(terms[0], "pole", scatter_dimension=2, tiled=True).astype(F32)
+def scatter_sum(terms, before, here, last):
+    if len(terms[0]) == 1:
+        share = lax.psum_scatter(terms[0][0], "pole", scatter_dimension=2, tiled=True).astype(F32)
         return share if before is None else before + share
-    parts = len(terms) // 4
-    high, half = terms[0].shape
-    quarter = half // 2
     fields = []
-    for k in range(parts):
-        real_out, real_keep, imag_out, imag_keep = terms[4 * k : 4 * k + 4]
+    for real_out, real_keep, imag_out, imag_keep in terms:
         real_got = flip(real_out, "pole", 2)
         imag_got = flip(imag_out, "pole", 1)
         fields.append((real_keep, real_got, imag_keep, imag_got))
     lasts = []
-    for k in range(parts):
-        sends = kernel_call(pass_on_body, (here,), fields[k], [jax.ShapeDtypeStruct((high, quarter), BF16)] * 2)
-        lasts.append(flip(sends[0], "pole", 1))
-        lasts.append(flip(sends[1], "pole", 2))
+    for field in fields:
+        high, half = field[0].shape
+        send = jax.ShapeDtypeStruct((high, half // 2), BF16)
+        sends = kernel_call(pass_on_body, (here,), field, [send] * 2)
+        real_last = flip(sends[0], "pole", 1)
+        imag_last = flip(sends[1], "pole", 2)
+        lasts.append((real_last, imag_last))
     extra = [] if before is None else [before]
-    shape = jax.ShapeDtypeStruct((2, parts * high, quarter), F32)
+    rows = sum(field[0].shape[0] for field in fields)
+    shape = jax.ShapeDtypeStruct((2, rows, half // 2), F32)
     flat = [value for field in fields for value in field]
-    retain = functools.partial(retain_body, parts=parts, extra=len(extra))
+    retain = functools.partial(retain_body, parts=len(fields), extra=len(extra))
     base = kernel_call(retain, (here,), flat + extra, shape)
-    return kernel_call(close_body, (), [base, *lasts], shape)
+    if not last:
+        close = functools.partial(close_body, top=0, write=False)
+        return kernel_call(close, (), [base, *(v for pair in lasts for v in pair)], shape)
+    whole = None
+    top = 0
+    groups = [lasts[:-1], lasts[-1:]] if len(lasts) > 1 else [lasts]
+    for group in groups:
+        flat = [value for pair in group for value in pair]
+        whole = close_out(base, flat, top, whole)
+        top += sum(pair[0].shape[0] for pair in group)
+    return whole
 
 
 ARRIVE = (2, 2, 2, 1, 1)
@@ -496,19 +555,17 @@
             for block in outs[1:]:
                 leaving.append(shift(block, "slab", -1))
         if last_tick:
-            shapes = len(term_shapes(*own.shape[1:]))
-            parts = 2 if shapes == 8 else 1
             finals = []
             terms = []
-            for k in range(parts):
-                outs = fold(scalars, own, factor, behind, before, tick, False, "final", base, part=(k, parts))
+            for part in row_parts(own.shape[1]):
+                outs = fold(scalars, own, factor, behind, before, tick, False, "final", base, part=part)
                 finals.append(outs[0])
-                terms += outs[1:]
-            density = scatter_sum(terms, density, here)
+                terms.append(outs[1:])
+            density = scatter_sum(terms, density, here, True)
             state_out = emit(finals)
         else:
-            terms = weigh(scalars[:4], [before], tick)
-            density = scatter_sum(terms, density, here)
+            terms = weigh(scalars[:4], before, tick)
+            density = scatter_sum([terms], density, here, False)
         incoming = leaving
     return (state_out, density)
 

time: 217 us -> 217 us (level)
  Pallas kernels: 77.4 us -> 82.7 us
  starting transfers between devices: 38.9 us -> 36.3 us
  waiting for transfers between devices: 98.3 us -> 96 us
    ppermute x12, waiting for transfers between devices: 85.9 us -> 78.5 us  [shift(): lax.ppermute(block, axis, [(i, i + step) for i in devices if i + step in...]
    ppermute x29, waiting for transfers between devices: 12.4 us -> 17.5 us  [flip(): lax.ppermute(block, axis, [(i, i ^ bit) for i in range(lax.axis_size(axis...]
    pallas_call x11 -> x12, Pallas kernels: 60.2 us -> 64.5 us  [fold(): pl.pallas_call(body, grid_spec=pltpu.PrefetchScalarGridSpec(num_scalar_pr...]
    ppermute x29, starting transfers between devices: 19.4 us -> 16.9 us  [flip(): lax.ppermute(block, axis, [(i, i ^ bit) for i in range(lax.axis_size(axis...]
  transfers between devices with their start and end apart: 41 -> 41, of which waited for: 15 -> 16; matrix products, arithmetic and copies ran while one was open for 0% -> 0% of each run, Pallas kernels for 34% -> 36%
where the time goes in v7:
time: 217 us; the launch traced here: 216 us
  waiting for transfers between devices  96 us (44%)
  Pallas kernels  82.7 us (38%)
  starting transfers between devices  36.3 us (17%)
    ppermute x12, waiting for transfers between devices, shift(): lax.ppermute(block, axis, [(i, i + step) for i in devices if i + step in...  78.5 us
    pallas_call x12, Pallas kernels, fold(): pl.pallas_call(body, grid_spec=pltpu.PrefetchScalarGridSpec(num_scalar_pr...  64.5 us
    ppermute x12, starting transfers between devices, shift(): lax.ppermute(block, axis, [(i, i + step) for i in devices if i + step in...  19.4 us
    ppermute x29, waiting for transfers between devices, flip(): lax.ppermute(block, axis, [(i, i ^ bit) for i in range(lax.axis_size(axis...  17.5 us
    ppermute x29, starting transfers between devices, flip(): lax.ppermute(block, axis, [(i, i ^ bit) for i in range(lax.axis_size(axis...  16.9 us
    pallas_call x2, Pallas kernels, masked_factor(): pl.pallas_call(functools.partial(mask_body, tick=tick), grid_spec=pltpu.P...  6.17 us
    pallas_call x3, Pallas kernels, cut_pieces(): pl.pallas_call(functools.partial(cut_body, first=first, blocks=blocks), g...  4.74 us
  transfers between devices with their start and end apart: 41, of which 16 were waited for; matrix products, arithmetic and copies ran while one was open for 0% of the time, Pallas kernels for 36%

profile of v7, /device:TPU:0, one launch (start us, length us, event | category | flops | bytes accessed | tf_op | source)
XLA Modules:
  0.0 216.4 jit_solution(5411342628336937908)
XLA Ops:
  0.6 3.7 %shard_map.78.refs_5_.refs_6_ = bf16[2,512,1024]{2,1,0:T(8,128)(2,1)} custom-call(s32[2,1,4,8]{3,2,1,0:T(4,128)} %mask_ref.3, bf16[2,1,2,512,1024]{4,3,2,1,0:T(8,128)(2,1)} %coupling_ref.3), custom_call_target="tpu_custom_call" | custom-call | tf_op jit(solution)/shard_map/pallas_call | solution.py:63
  4.9 2.4 %shard_map.77.refs_5_.refs_6_ = bf16[2,512,1024]{2,1,0:T(8,128)(2,1)S(1)} custom-call(s32[2,1,4,8]{3,2,1,0:T(4,128)} %mask_ref.3, bf16[2,1,2,512,1024]{4,3,2,1,0:T(8,128)(2,1)} %coupling_ref.3), custom_call_target="tpu_custom_call" | custom-call | tf_op jit(solution)/shard_map/pallas_call | solution.py:63
  8.0 4.1 %collective-permute-done.refs_1_ = s32[2,1,4,8]{3,2,1,0:T(4,128)S(1)} collective-permute-done((s32[2,1,4,8]{3,2,1,0:T(4,128)}, s32[2,1,4,8]{3,2,1,0:T(4,128)S(1)}, u32[]{:S(2)}, u32[]{:S(2)}) %collective-permute-start) | collective-permute-done | bytes 288 | tf_op jit(solution)/shard_map/ppermute | solution.py:23
  12.1 1.7 plan.1.refs_4_
  13.8 4.8 %collective-permute-start.4 = (s32[16]{0:T(128)S(1)}, s32[16]{0:T(128)S(1)}, u32[]{:S(2)}, u32[]{:S(2)}) collective-permute-start(s32[16]{0:T(128)S(1)} %plan.1.refs_4_), channel_id=1, source_target_pairs={{0,8},{8,16},{16,24},{1,9},{9,17},{17,25},{2,10},{10,18},{18,26},{... | collective-permute-start | bytes 200 | tf_op jit(solution)/shard_map/ppermute | solution.py:19
  19.9 2.1 shard_map.79
  22.0 1.3 collective-permute-start.5
  23.3 1.3 collective-permute-start.7
  27.0 1.6 shard_map.80
  28.6 4.5 %collective-permute-done.5.refs_8_ = bf16[2,512,128]{2,1,0:T(8,128)(2,1)S(1)} collective-permute-done((bf16[2,512,128]{2,1,0:T(8,128)(2,1)S(1)}, bf16[2,512,128]{2,1,0:T(8,128)(2,1)S(1)}, u32[]{:S(2)}, u32[]{:S(2)}) %collective-permute-start.5) | collective-permute-done | bytes 262176 | tf_op jit(solution)/shard_map/ppermute | solution.py:19
  34.4 4.3 %collective-permute-done.7.refs_8_ = bf16[2,512,128]{2,1,0:T(8,128)(2,1)S(1)} collective-permute-done((bf16[2,512,128]{2,1,0:T(8,128)(2,1)S(1)}, bf16[2,512,128]{2,1,0:T(8,128)(2,1)S(1)}, u32[]{:S(2)}, u32[]{:S(2)}) %collective-permute-start.7) | collective-permute-done | bytes 262176 | tf_op jit(solution)/shard_map/ppermute | solution.py:19
  38.7 1.5 collective-permute-start.9
  40.1 9.8 %collective-permute-done.13.refs_8_ = bf16[2,512,256]{2,1,0:T(8,128)(2,1)S(1)} collective-permute-done((bf16[2,512,256]{2,1,0:T(8,128)(2,1)S(1)}, bf16[2,512,256]{2,1,0:T(8,128)(2,1)S(1)}, u32[]{:S(2)}, u32[]{:S(2)}) %collective-permute-start.13) | collective-permute-done | bytes 524320 | tf_op jit(solution)/shard_map/ppermute | solution.py:19
  49.9 11.2 %collective-permute-done.11.refs_8_ = bf16[2,512,256]{2,1,0:T(8,128)(2,1)S(1)} collective-permute-done((bf16[2,512,256]{2,1,0:T(8,128)(2,1)S(1)}, bf16[2,512,256]{2,1,0:T(8,128)(2,1)S(1)}, u32[]{:S(2)}, u32[]{:S(2)}) %collective-permute-start.11) | collective-permute-done | bytes 524320 | tf_op jit(solution)/shard_map/ppermute | solution.py:19
  61.2 9.5 %collective-permute-done.9.refs_8_ = bf16[2,512,256]{2,1,0:T(8,128)(2,1)S(1)} collective-permute-done((bf16[2,512,256]{2,1,0:T(8,128)(2,1)S(1)}, bf16[2,512,256]{2,1,0:T(8,128)(2,1)S(1)}, u32[]{:S(2)}, u32[]{:S(2)}) %collective-permute-start.9) | collective-permute-done | bytes 524320 | tf_op jit(solution)/shard_map/ppermute | solution.py:19
  71.3 7.4 %shard_map.82.refs_10_ = f32[2,512,1024]{2,1,0:T(8,128)S(1)} custom-call(s32[1]{0:T(128)} %bitcast.mine.plan.refs_0_, s32[1,1,2]{2,1,0:T(1,128)S(1)} %bitcast.3, f32[2,16]{1,0:T(2,128)S(1)} %copy-done, s32[1]{0:T(128)} %bitcast.2.here.refs_3_, s32[16]{0:T(128)S(1)} %plan.1.refs_4_, bf16[2,512,1024]{2,1,0:T(8,128)(2,1)} %shard_map.78.refs_5_.refs_6_, ...), custom_call_target="tpu_custom_call" | custom-call | tf_op jit(solution)/shard_map/pallas_call | solution.py:317
  78.7 7.0 %shard_map.83.refs_10_ = f32[2,512,1024]{2,1,0:T(8,128)S(1)} custom-call(s32[1]{0:T(128)} %bitcast.mine.plan.refs_0_, s32[1,1,2]{2,1,0:T(1,128)S(1)} %bitcast.4, f32[2,16]{1,0:T(2,128)S(1)} %copy-done, s32[1]{0:T(128)} %bitcast.2.here.refs_3_, s32[16]{0:T(128)S(1)} %plan.1.refs_4_, ...), custom_call_target="tpu_custom_call", output_to_operand_aliasing={{}: (10, {})} | custom-call | tf_op jit(solution)/shard_map/pallas_call | solution.py:317
  85.7 7.0 %shard_map.84 = (f32[2,512,1024]{2,1,0:T(8,128)S(1)}, bf16[2,512,128]{2,1,0:T(8,128)(2,1)S(1)}) custom-call(s32[1]{0:T(128)} %bitcast.mine.plan.refs_0_, s32[1,1,2]{2,1,0:T(1,128)S(1)} %bitcast.5, f32[2,16]{1,0:T(2,128)S(1)} %copy-done, s32[1]{0:T(128)} %bitcast.2.here.refs_3_, s32[16]{0:T(128)S(1)} %plan.1.refs_4_, ...), custom_call_target="tpu_custom_call", output_to_operand_aliasing={{0}: (10, {})} | custom-call | tf_op jit(solution)/shard_map/pallas_call | solution.py:317
  92.8 5.5 %shard_map.85 = (f32[2,512,1024]{2,1,0:T(8,128)S(1)}, bf16[2,512,256]{2,1,0:T(8,128)(2,1)S(1)}) custom-call(s32[1]{0:T(128)} %bitcast.mine.plan.refs_0_, s32[1,1,2]{2,1,0:T(1,128)S(1)} %bitcast.6, f32[2,16]{1,0:T(2,128)S(1)} %copy-done, s32[1]{0:T(128)} %bitcast.2.here.refs_3_, s32[16]{0:T(128)S(1)} %plan.1.refs_4_, ...), custom_call_target="tpu_custom_call", output_to_operand_aliasing={{0}: (10, {})} | custom-call | tf_op jit(solution)/shard_map/pallas_call | solution.py:317
  98.3 1.3 collective-permute-start.21
  99.6 5.6 %shard_map.86 = (bf16[2,512,1024]{2,1,0:T(8,128)(2,1)S(1)}, bf16[2,512,256]{2,1,0:T(8,128)(2,1)S(1)}, bf16[2,512,256]{2,1,0:T(8,128)(2,1)S(1)}, bf16[2,512,128]{2,1,0:T(8,128)(2,1)S(1)}) custom-call(s32[1]{0:T(128)} %bitcast.mine.plan.refs_0_, s32[1,1,2]{2,1,0:T(1,128)S(1)} %bitcast.7, f32[2,16]{1,0:T(2,128)S(1)} %copy-done, s32[1]{0:T(128)} %bitcast.2.here.refs_3_, ...), custom_call_target="tpu_custom_call" | custom-call | tf_op jit(solution)/shard_map/pallas_call | solution.py:317
  105.2 1.3 collective-permute-start.19
  106.5 1.3 collective-permute-start.17
  107.8 1.3 collective-permute-start.1
  109.1 27.9 %collective-permute-done.1.refs_4_ = s32[16]{0:T(128)S(1)} collective-permute-done((s32[16]{0:T(128)S(1)}, s32[16]{0:T(128)S(1)}, u32[]{:S(2)}, u32[]{:S(2)}) %collective-permute-start.1) | collective-permute-done | bytes 96 | tf_op jit(solution)/shard_map/ppermute | solution.py:19
  138.4 1.5 collective-permute-start.15
  139.9 8.2 %collective-permute-done.23.refs_8_ = bf16[2,512,128]{2,1,0:T(8,128)(2,1)S(1)} collective-permute-done((bf16[2,512,128]{2,1,0:T(8,128)(2,1)S(1)}, bf16[2,512,128]{2,1,0:T(8,128)(2,1)S(1)}, u32[]{:S(2)}, u32[]{:S(2)}) %collective-permute-start.23) | collective-permute-done | bytes 262176 | tf_op jit(solution)/shard_map/ppermute | solution.py:19
  148.7 1.8 shard_map.94
  150.4 1.8 collective-permute-done.15.refs_8_
  152.2 1.5 collective-permute-start.31
  153.8 1.5 collective-permute-start.32
  155.3 5.1 %shard_map.87.refs_10_ = f32[2,512,1024]{2,1,0:T(8,128)S(1)} custom-call(s32[1]{0:T(128)} %bitcast.mine.plan.refs_0_, s32[1,1,2]{2,1,0:T(1,128)S(1)} %bitcast.9, f32[2,16]{1,0:T(2,128)S(1)} %copy-done, s32[1]{0:T(128)} %bitcast.2.here.refs_3_, s32[16]{0:T(128)S(1)} %collective-permute-done.1.refs_4_, bf16[2,512,1024]{2,1,0:T(8,128)(2,1)S(1)} %shard_map.77.refs_5_.refs_6_, ...), custom_call_target="tpu_custom_call" | custom-call | tf_op jit(solution)/shard_map/pallas_call | solution.py:317
  160.3 5.7 %shard_map.88.refs_10_ = f32[2,512,1024]{2,1,0:T(8,128)S(1)} custom-call(s32[1]{0:T(128)} %bitcast.mine.plan.refs_0_, s32[1,1,2]{2,1,0:T(1,128)S(1)} %bitcast.10, f32[2,16]{1,0:T(2,128)S(1)} %copy-done, s32[1]{0:T(128)} %bitcast.2.here.refs_3_, s32[16]{0:T(128)S(1)} %collective-permute-done.1.refs_4_, ...), custom_call_target="tpu_custom_call", output_to_operand_aliasing={{}: (10, {})} | custom-call | tf_op jit(solution)/shard_map/pallas_call | solution.py:317
  166.0 5.7 %shard_map.89.refs_10_ = f32[2,512,1024]{2,1,0:T(8,128)S(1)} custom-call(s32[1]{0:T(128)} %bitcast.mine.plan.refs_0_, s32[1,1,2]{2,1,0:T(1,128)S(1)} %bitcast.11, f32[2,16]{1,0:T(2,128)S(1)} %copy-done, s32[1]{0:T(128)} %bitcast.2.here.refs_3_, s32[16]{0:T(128)S(1)} %collective-permute-done.1.refs_4_, ...), custom_call_target="tpu_custom_call", output_to_operand_aliasing={{}: (10, {})} | custom-call | tf_op jit(solution)/shard_map/pallas_call | solution.py:317
  171.8 5.7 %shard_map.90.refs_10_ = f32[2,512,1024]{2,1,0:T(8,128)S(1)} custom-call(s32[1]{0:T(128)} %bitcast.mine.plan.refs_0_, s32[1,1,2]{2,1,0:T(1,128)S(1)} %bitcast.12, f32[2,16]{1,0:T(2,128)S(1)} %copy-done, s32[1]{0:T(128)} %bitcast.2.here.refs_3_, s32[16]{0:T(128)S(1)} %collective-permute-done.1.refs_4_, ...), custom_call_target="tpu_custom_call", output_to_operand_aliasing={{}: (10, {})} | custom-call | tf_op jit(solution)/shard_map/pallas_call | solution.py:317
  177.5 3.8 %shard_map.92 = (bf16[2,256,1024]{2,1,0:T(8,128)(2,1)S(1)}, bf16[256,512]{1,0:T(8,128)(2,1)S(1)}, bf16[256,512]{1,0:T(8,128)(2,1)S(1)}, bf16[256,512]{1,0:T(8,128)(2,1)S(1)}, bf16[256,512]{1,0:T(8,128)(2,1)S(1)}) custom-call(s32[1]{0:T(128)} %bitcast.mine.plan.refs_0_, s32[1,1,2]{2,1,0:T(1,128)S(1)} %bitcast.13, f32[2,16]{1,0:T(2,128)S(1)} %copy-done, ...), custom_call_target="tpu_custom_call" | custom-call | tf_op jit(solution)/shard_map/pallas_call | solution.py:317
  181.9 3.0 %shard_map.91 = (bf16[2,128,1024]{2,1,0:T(8,128)(2,1)S(1)}, bf16[128,512]{1,0:T(8,128)(2,1)S(1)}, bf16[128,512]{1,0:T(8,128)(2,1)S(1)}, bf16[128,512]{1,0:T(8,128)(2,1)S(1)}, bf16[128,512]{1,0:T(8,128)(2,1)S(1)}) custom-call(s32[1]{0:T(128)} %bitcast.mine.plan.refs_0_, s32[1,1,2]{2,1,0:T(1,128)S(1)} %bitcast.14, f32[2,16]{1,0:T(2,128)S(1)} %copy-done, ...), custom_call_target="tpu_custom_call" | custom-call | tf_op jit(solution)/shard_map/pallas_call | solution.py:317
  184.9 1.6 collective-permute-start.25
  187.0 1.5 collective-permute-start.26
  189.3 3.6 %collective-permute-done.25.refs_1_.real_got = bf16[128,512]{1,0:T(8,128)(2,1)S(1)} collective-permute-done((bf16[128,512]{1,0:T(8,128)(2,1)S(1)}, bf16[128,512]{1,0:T(8,128)(2,1)S(1)}, u32[]{:S(2)}, u32[]{:S(2)}) %collective-permute-start.25) | collective-permute-done | bytes 131104 | tf_op jit(solution)/shard_map/ppermute | solution.py:23
  193.4 3.0 %shard_map.93 = (bf16[2,128,1024]{2,1,0:T(8,128)(2,1)S(1)}, bf16[128,512]{1,0:T(8,128)(2,1)S(1)}, bf16[128,512]{1,0:T(8,128)(2,1)S(1)}, bf16[128,512]{1,0:T(8,128)(2,1)S(1)}, bf16[128,512]{1,0:T(8,128)(2,1)S(1)}) custom-call(s32[1]{0:T(128)} %bitcast.mine.plan.refs_0_, s32[1,1,2]{2,1,0:T(1,128)S(1)} %bitcast.15, f32[2,16]{1,0:T(2,128)S(1)} %copy-done, ...), custom_call_target="tpu_custom_call" | custom-call | tf_op jit(solution)/shard_map/pallas_call | solution.py:317
  196.4 2.0 collective-permute-done.26.refs_3_.imag_got
  199.7 1.6 collective-permute-start.39
  201.2 2.3 %collective-permute-done.29.refs_9_.real_got = bf16[128,512]{1,0:T(8,128)(2,1)S(1)} collective-permute-done((bf16[128,512]{1,0:T(8,128)(2,1)S(1)}, bf16[128,512]{1,0:T(8,128)(2,1)S(1)}, u32[]{:S(2)}, u32[]{:S(2)}) %collective-permute-start.29) | collective-permute-done | bytes 131104 | tf_op jit(solution)/shard_map/ppermute | solution.py:23
  204.1 2.8 %collective-permute-done.30.refs_11_.imag_got = bf16[128,512]{1,0:T(8,128)(2,1)S(1)} collective-permute-done((bf16[128,512]{1,0:T(8,128)(2,1)S(1)}, bf16[128,512]{1,0:T(8,128)(2,1)S(1)}, u32[]{:S(2)}, u32[]{:S(2)}) %collective-permute-start.30) | collective-permute-done | bytes 131104 | tf_op jit(solution)/shard_map/ppermute | solution.py:23
  208.1 1.5 collective-permute-start.35
  209.6 1.6 collective-permute-done.37.refs_0_
  211.9 1.3 emit.1
  (67 shorter events, 17.5 us)
Async XLA Ops:
  4.4 66.8 %collective-permute-start.3 = (bf16[2,512,1024]{2,1,0:T(8,128)(2,1)}, bf16[2,512,1024]{2,1,0:T(8,128)(2,1)}, u32[]{:S(2)}, u32[]{:S(2)}) collective-permute-start(bf16[2,512,1024]{2,1,0:T(8,128)(2,1)} %shard_map.78.refs_5_.refs_6_), channel_id=1, source_target_pairs={{0,4},{4,0},{1,5},{5,1},{2,6},{6,2},{3,7},{7,3},{8,12},{12,8},{9,1... | collective-permute-start | bytes 6291464 | tf_op jit(solution)/shard_map/ppermute | solution.py:23
  7.4 63.9 %copy-start = (f32[2,16]{1,0:T(2,128)S(1)}, f32[2,16]{1,0:T(2,128)}, u32[]{:S(2)}) copy-start(f32[2,16]{1,0:T(2,128)} %pw.1) | copy-start | bytes 388
  7.4 63.9 %copy-start.1 = (s32[2,1,1]{0,2,1:T(1,128)S(1)}, s32[2,1,1]{0,2,1:T(1,128)}, u32[]{:S(2)}) copy-start(s32[2,1,1]{0,2,1:T(1,128)} %param.11) | copy-start | bytes 28
  7.4 131.0 %collective-permute-start.2 = (bf16[2,512,1024]{2,1,0:T(8,128)(2,1)S(1)}, bf16[2,512,1024]{2,1,0:T(8,128)(2,1)}, u32[]{:S(2)}, u32[]{:S(2)}) collective-permute-start(bf16[2,512,1024]{2,1,0:T(8,128)(2,1)S(1)} %shard_map.77.refs_5_.refs_6_), channel_id=1, source_target_pairs={{0,4},{4,0},{1,5},{5,1},{2,6},{6,2},{3,7},{7,3},{8,12},{12,8},{9,1... | collective-permute-start | bytes 6291464 | tf_op jit(solution)/shard_map/ppermute | solution.py:23
  7.5 4.6 %collective-permute-start = (s32[2,1,4,8]{3,2,1,0:T(4,128)}, s32[2,1,4,8]{3,2,1,0:T(4,128)S(1)}, u32[]{:S(2)}, u32[]{:S(2)}) collective-permute-start(s32[2,1,4,8]{3,2,1,0:T(4,128)} %mask_ref.3), channel_id=1, source_target_pairs={{0,4},{4,0},{1,5},{5,1},{2,6},{6,2},{3,7},{7,3},{8,12},{12,8},{9,1... | collective-permute-start | bytes 776 | tf_op jit(solution)/shard_map/ppermute | solution.py:23
  13.8 6.1 %collective-permute-start.4 = (s32[16]{0:T(128)S(1)}, s32[16]{0:T(128)S(1)}, u32[]{:S(2)}, u32[]{:S(2)}) collective-permute-start(s32[16]{0:T(128)S(1)} %plan.1.refs_4_), channel_id=1, source_target_pairs={{0,8},{8,16},{16,24},{1,9},{9,17},{17,25},{2,10},{10,18},{18,26},{... | collective-permute-start | bytes 200 | tf_op jit(solution)/shard_map/ppermute | solution.py:19
  22.0 11.1 %collective-permute-start.5 = (bf16[2,512,128]{2,1,0:T(8,128)(2,1)S(1)}, bf16[2,512,128]{2,1,0:T(8,128)(2,1)S(1)}, u32[]{:S(2)}, u32[]{:S(2)}) collective-permute-start(bf16[2,512,128]{2,1,0:T(8,128)(2,1)S(1)} %get-tuple-element.40), channel_id=1, source_target_pairs={{8,0},{16,8},{24,16},{9,1},{17,9},{25,17},{10,2},{18,10},{26,18},{... | collective-permute-start | bytes 786440 | tf_op jit(solution)/shard_map/ppermute | solution.py:19
  23.3 15.4 %collective-permute-start.7 = (bf16[2,512,128]{2,1,0:T(8,128)(2,1)S(1)}, bf16[2,512,128]{2,1,0:T(8,128)(2,1)S(1)}, u32[]{:S(2)}, u32[]{:S(2)}) collective-permute-start(bf16[2,512,128]{2,1,0:T(8,128)(2,1)S(1)} %get-tuple-element.41), channel_id=1, source_target_pairs={{8,0},{16,8},{24,16},{9,1},{17,9},{25,17},{10,2},{18,10},{26,18},{... | collective-permute-start | bytes 786440 | tf_op jit(solution)/shard_map/ppermute | solution.py:19
  25.7 24.3 %collective-permute-start.13 = (bf16[2,512,256]{2,1,0:T(8,128)(2,1)S(1)}, bf16[2,512,256]{2,1,0:T(8,128)(2,1)S(1)}, u32[]{:S(2)}, u32[]{:S(2)}) collective-permute-start(bf16[2,512,256]{2,1,0:T(8,128)(2,1)S(1)} %shard_map.81), channel_id=1, source_target_pairs={{8,0},{16,8},{24,16},{9,1},{17,9},{25,17},{10,2},{18,10},{26,18},{... | collective-permute-start | bytes 1572872 | tf_op jit(solution)/shard_map/ppermute | solution.py:19
  33.1 28.1 %collective-permute-start.11 = (bf16[2,512,256]{2,1,0:T(8,128)(2,1)S(1)}, bf16[2,512,256]{2,1,0:T(8,128)(2,1)S(1)}, u32[]{:S(2)}, u32[]{:S(2)}) collective-permute-start(bf16[2,512,256]{2,1,0:T(8,128)(2,1)S(1)} %shard_map.80), channel_id=1, source_target_pairs={{8,0},{16,8},{24,16},{9,1},{17,9},{25,17},{10,2},{18,10},{26,18},{... | collective-permute-start | bytes 1572872 | tf_op jit(solution)/shard_map/ppermute | solution.py:19
  38.7 32.0 %collective-permute-start.9 = (bf16[2,512,256]{2,1,0:T(8,128)(2,1)S(1)}, bf16[2,512,256]{2,1,0:T(8,128)(2,1)S(1)}, u32[]{:S(2)}, u32[]{:S(2)}) collective-permute-start(bf16[2,512,256]{2,1,0:T(8,128)(2,1)S(1)} %get-tuple-element.42), channel_id=1, source_target_pairs={{8,0},{16,8},{24,16},{9,1},{17,9},{25,17},{10,2},{18,10},{26,18},{... | collective-permute-start | bytes 1572872 | tf_op jit(solution)/shard_map/ppermute | solution.py:19
  49.9 20.8 %collective-permute-start.14 = (bf16[2,512,256]{2,1,0:T(8,128)(2,1)S(1)}, bf16[2,512,256]{2,1,0:T(8,128)(2,1)S(1)}, u32[]{:S(2)}, u32[]{:S(2)}) collective-permute-start(bf16[2,512,256]{2,1,0:T(8,128)(2,1)S(1)} %collective-permute-done.13.refs_8_), channel_id=1, source_target_pairs={{0,4},{4,0},{1,5},{5,1},{2,6},{6,2},{3,7},{7,3},{8,12},{12,8},{9,1... | collective-permute-start | bytes 1572872 | tf_op jit(solution)/shard_map/ppermute | solution.py:23
  61.2 17.6 %collective-permute-start.12 = (bf16[2,512,256]{2,1,0:T(8,128)(2,1)S(1)}, bf16[2,512,256]{2,1,0:T(8,128)(2,1)S(1)}, u32[]{:S(2)}, u32[]{:S(2)}) collective-permute-start(bf16[2,512,256]{2,1,0:T(8,128)(2,1)S(1)} %collective-permute-done.11.refs_8_), channel_id=1, source_target_pairs={{0,4},{4,0},{1,5},{5,1},{2,6},{6,2},{3,7},{7,3},{8,12},{12,8},{9,1... | collective-permute-start | bytes 1572872 | tf_op jit(solution)/shard_map/ppermute | solution.py:23
  70.7 15.0 %collective-permute-start.10 = (bf16[2,512,256]{2,1,0:T(8,128)(2,1)S(1)}, bf16[2,512,256]{2,1,0:T(8,128)(2,1)S(1)}, u32[]{:S(2)}, u32[]{:S(2)}) collective-permute-start(bf16[2,512,256]{2,1,0:T(8,128)(2,1)S(1)} %collective-permute-done.9.refs_8_), channel_id=1, source_target_pairs={{0,4},{4,0},{1,5},{5,1},{2,6},{6,2},{3,7},{7,3},{8,12},{12,8},{9,1... | collective-permute-start | bytes 1572872 | tf_op jit(solution)/shard_map/ppermute | solution.py:23
  70.7 22.1 %collective-permute-start.8 = (bf16[2,512,128]{2,1,0:T(8,128)(2,1)S(1)}, bf16[2,512,128]{2,1,0:T(8,128)(2,1)S(1)}, u32[]{:S(2)}, u32[]{:S(2)}) collective-permute-start(bf16[2,512,128]{2,1,0:T(8,128)(2,1)S(1)} %collective-permute-done.7.refs_8_), channel_id=1, source_target_pairs={{0,4},{4,0},{1,5},{5,1},{2,6},{6,2},{3,7},{7,3},{8,12},{12,8},{9,1... | collective-permute-start | bytes 786440 | tf_op jit(solution)/shard_map/ppermute | solution.py:23
  71.2 28.4 %collective-permute-start.6 = (bf16[2,512,128]{2,1,0:T(8,128)(2,1)S(1)}, bf16[2,512,128]{2,1,0:T(8,128)(2,1)S(1)}, u32[]{:S(2)}, u32[]{:S(2)}) collective-permute-start(bf16[2,512,128]{2,1,0:T(8,128)(2,1)S(1)} %collective-permute-done.5.refs_8_), channel_id=1, source_target_pairs={{0,4},{4,0},{1,5},{5,1},{2,6},{6,2},{3,7},{7,3},{8,12},{12,8},{9,1... | collective-permute-start | bytes 786440 | tf_op jit(solution)/shard_map/ppermute | solution.py:23
  98.3 40.0 %collective-permute-start.21 = (bf16[2,512,256]{2,1,0:T(8,128)(2,1)S(1)}, bf16[2,512,256]{2,1,0:T(8,128)(2,1)S(1)}, u32[]{:S(2)}, u32[]{:S(2)}) collective-permute-start(bf16[2,512,256]{2,1,0:T(8,128)(2,1)S(1)} %get-tuple-element.48), channel_id=1, source_target_pairs={{8,0},{16,8},{24,16},{9,1},{17,9},{25,17},{10,2},{18,10},{26,18},{... | collective-permute-start | bytes 1572872 | tf_op jit(solution)/shard_map/ppermute | solution.py:19
  105.2 42.9 %collective-permute-start.19 = (bf16[2,512,256]{2,1,0:T(8,128)(2,1)S(1)}, bf16[2,512,256]{2,1,0:T(8,128)(2,1)S(1)}, u32[]{:S(2)}, u32[]{:S(2)}) collective-permute-start(bf16[2,512,256]{2,1,0:T(8,128)(2,1)S(1)} %get-tuple-element.47), channel_id=1, source_target_pairs={{8,0},{16,8},{24,16},{9,1},{17,9},{25,17},{10,2},{18,10},{26,18},{... | collective-permute-start | bytes 1572872 | tf_op jit(solution)/shard_map/ppermute | solution.py:19
  106.5 42.1 %collective-permute-start.17 = (bf16[2,512,256]{2,1,0:T(8,128)(2,1)S(1)}, bf16[2,512,256]{2,1,0:T(8,128)(2,1)S(1)}, u32[]{:S(2)}, u32[]{:S(2)}) collective-permute-start(bf16[2,512,256]{2,1,0:T(8,128)(2,1)S(1)} %get-tuple-element.46), channel_id=1, source_target_pairs={{8,0},{16,8},{24,16},{9,1},{17,9},{25,17},{10,2},{18,10},{26,18},{... | collective-permute-start | bytes 1572872 | tf_op jit(solution)/shard_map/ppermute | solution.py:19
  107.8 29.2 %collective-permute-start.1 = (s32[16]{0:T(128)S(1)}, s32[16]{0:T(128)S(1)}, u32[]{:S(2)}, u32[]{:S(2)}) collective-permute-start(s32[16]{0:T(128)S(1)} %plan.1.refs_4_), channel_id=1, source_target_pairs={{8,0},{16,8},{24,16},{9,1},{17,9},{25,17},{10,2},{18,10},{26,18},{... | collective-permute-start | bytes 200 | tf_op jit(solution)/shard_map/ppermute | solution.py:19
  137.0 11.1 %collective-permute-start.23 = (bf16[2,512,128]{2,1,0:T(8,128)(2,1)S(1)}, bf16[2,512,128]{2,1,0:T(8,128)(2,1)S(1)}, u32[]{:S(2)}, u32[]{:S(2)}) collective-permute-start(bf16[2,512,128]{2,1,0:T(8,128)(2,1)S(1)} %get-tuple-element.49), channel_id=1, source_target_pairs={{8,0},{16,8},{24,16},{9,1},{17,9},{25,17},{10,2},{18,10},{26,18},{... | collective-permute-start | bytes 786440 | tf_op jit(solution)/shard_map/ppermute | solution.py:19
  138.3 16.9 %collective-permute-start.22 = (bf16[2,512,256]{2,1,0:T(8,128)(2,1)S(1)}, bf16[2,512,256]{2,1,0:T(8,128)(2,1)S(1)}, u32[]{:S(2)}, u32[]{:S(2)}) collective-permute-start(bf16[2,512,256]{2,1,0:T(8,128)(2,1)S(1)} %collective-permute-done.21.refs_8_), channel_id=1, source_target_pairs={{0,4},{4,0},{1,5},{5,1},{2,6},{6,2},{3,7},{7,3},{8,12},{12,8},{9,1... | collective-permute-start | bytes 1572872 | tf_op jit(solution)/shard_map/ppermute | solution.py:23
  138.4 13.8 %collective-permute-start.15 = (bf16[2,512,128]{2,1,0:T(8,128)(2,1)S(1)}, bf16[2,512,128]{2,1,0:T(8,128)(2,1)S(1)}, u32[]{:S(2)}, u32[]{:S(2)}) collective-permute-start(bf16[2,512,128]{2,1,0:T(8,128)(2,1)S(1)} %get-tuple-element.45), channel_id=1, source_target_pairs={{8,0},{16,8},{24,16},{9,1},{17,9},{25,17},{10,2},{18,10},{26,18},{... | collective-permute-start | bytes 786440 | tf_op jit(solution)/shard_map/ppermute | solution.py:19
  148.1 5.7 %collective-permute-start.24 = (bf16[2,512,128]{2,1,0:T(8,128)(2,1)S(1)}, bf16[2,512,128]{2,1,0:T(8,128)(2,1)S(1)}, u32[]{:S(2)}, u32[]{:S(2)}) collective-permute-start(bf16[2,512,128]{2,1,0:T(8,128)(2,1)S(1)} %collective-permute-done.23.refs_8_), channel_id=1, source_target_pairs={{0,4},{4,0},{1,5},{5,1},{2,6},{6,2},{3,7},{7,3},{8,12},{12,8},{9,1... | collective-permute-start | bytes 786440 | tf_op jit(solution)/shard_map/ppermute | solution.py:23
  148.1 17.9 %collective-permute-start.20 = (bf16[2,512,256]{2,1,0:T(8,128)(2,1)S(1)}, bf16[2,512,256]{2,1,0:T(8,128)(2,1)S(1)}, u32[]{:S(2)}, u32[]{:S(2)}) collective-permute-start(bf16[2,512,256]{2,1,0:T(8,128)(2,1)S(1)} %collective-permute-done.19.refs_8_), channel_id=1, source_target_pairs={{0,4},{4,0},{1,5},{5,1},{2,6},{6,2},{3,7},{7,3},{8,12},{12,8},{9,1... | collective-permute-start | bytes 1572872 | tf_op jit(solution)/shard_map/ppermute | solution.py:23
  148.6 23.1 %collective-permute-start.18 = (bf16[2,512,256]{2,1,0:T(8,128)(2,1)S(1)}, bf16[2,512,256]{2,1,0:T(8,128)(2,1)S(1)}, u32[]{:S(2)}, u32[]{:S(2)}) collective-permute-start(bf16[2,512,256]{2,1,0:T(8,128)(2,1)S(1)} %collective-permute-done.17.refs_8_), channel_id=1, source_target_pairs={{0,4},{4,0},{1,5},{5,1},{2,6},{6,2},{3,7},{7,3},{8,12},{12,8},{9,1... | collective-permute-start | bytes 1572872 | tf_op jit(solution)/shard_map/ppermute | solution.py:23
  152.2 34.8 %collective-permute-start.31 = (bf16[512,512]{1,0:T(8,128)(2,1)S(1)}, bf16[512,512]{1,0:T(8,128)(2,1)S(1)}, u32[]{:S(2)}, u32[]{:S(2)}) collective-permute-start(bf16[512,512]{1,0:T(8,128)(2,1)S(1)} %get-tuple-element.67), channel_id=1, source_target_pairs={{0,2},{1,3},{2,0},{3,1},{4,6},{5,7},{6,4},{7,5},{8,10},{9,11},{10,... | collective-permute-start | bytes 1572872 | tf_op jit(solution)/shard_map/ppermute | solution.py:23
  153.8 34.8 %collective-permute-start.32 = (bf16[512,512]{1,0:T(8,128)(2,1)S(1)}, bf16[512,512]{1,0:T(8,128)(2,1)S(1)}, u32[]{:S(2)}, u32[]{:S(2)}) collective-permute-start(bf16[512,512]{1,0:T(8,128)(2,1)S(1)} %get-tuple-element.69), channel_id=1, source_target_pairs={{0,1},{1,0},{2,3},{3,2},{4,5},{5,4},{6,7},{7,6},{8,9},{9,8},{10,11... | collective-permute-start | bytes 1572872 | tf_op jit(solution)/shard_map/ppermute | solution.py:23
  155.2 22.2 %collective-permute-start.16 = (bf16[2,512,128]{2,1,0:T(8,128)(2,1)S(1)}, bf16[2,512,128]{2,1,0:T(8,128)(2,1)S(1)}, u32[]{:S(2)}, u32[]{:S(2)}) collective-permute-start(bf16[2,512,128]{2,1,0:T(8,128)(2,1)S(1)} %collective-permute-done.15.refs_8_), channel_id=1, source_target_pairs={{0,4},{4,0},{1,5},{5,1},{2,6},{6,2},{3,7},{7,3},{8,12},{12,8},{9,1... | collective-permute-start | bytes 786440 | tf_op jit(solution)/shard_map/ppermute | solution.py:23
  181.3 17.7 %collective-permute-start.27 = (bf16[256,512]{1,0:T(8,128)(2,1)S(1)}, bf16[256,512]{1,0:T(8,128)(2,1)S(1)}, u32[]{:S(2)}, u32[]{:S(2)}) collective-permute-start(bf16[256,512]{1,0:T(8,128)(2,1)S(1)} %get-tuple-element.58), channel_id=1, source_target_pairs={{0,2},{1,3},{2,0},{3,1},{4,6},{5,7},{6,4},{7,5},{8,10},{9,11},{10,... | collective-permute-start | bytes 786440 | tf_op jit(solution)/shard_map/ppermute | solution.py:23
  184.9 8.0 %collective-permute-start.25 = (bf16[128,512]{1,0:T(8,128)(2,1)S(1)}, bf16[128,512]{1,0:T(8,128)(2,1)S(1)}, u32[]{:S(2)}, u32[]{:S(2)}) collective-permute-start(bf16[128,512]{1,0:T(8,128)(2,1)S(1)} %get-tuple-element.54), channel_id=1, source_target_pairs={{0,2},{1,3},{2,0},{3,1},{4,6},{5,7},{6,4},{7,5},{8,10},{9,11},{10,... | collective-permute-start | bytes 393224 | tf_op jit(solution)/shard_map/ppermute | solution.py:23
  186.5 13.1 %collective-permute-start.28 = (bf16[256,512]{1,0:T(8,128)(2,1)S(1)}, bf16[256,512]{1,0:T(8,128)(2,1)S(1)}, u32[]{:S(2)}, u32[]{:S(2)}) collective-permute-start(bf16[256,512]{1,0:T(8,128)(2,1)S(1)} %get-tuple-element.60), channel_id=1, source_target_pairs={{0,1},{1,0},{2,3},{3,2},{4,5},{5,4},{6,7},{7,6},{8,9},{9,8},{10,11... | collective-permute-start | bytes 786440 | tf_op jit(solution)/shard_map/ppermute | solution.py:23
  187.0 11.4 %collective-permute-start.26 = (bf16[128,512]{1,0:T(8,128)(2,1)S(1)}, bf16[128,512]{1,0:T(8,128)(2,1)S(1)}, u32[]{:S(2)}, u32[]{:S(2)}) collective-permute-start(bf16[128,512]{1,0:T(8,128)(2,1)S(1)} %get-tuple-element.56), channel_id=1, source_target_pairs={{0,1},{1,0},{2,3},{3,2},{4,5},{5,4},{6,7},{7,6},{8,9},{9,8},{10,11... | collective-permute-start | bytes 393224 | tf_op jit(solution)/shard_map/ppermute | solution.py:23
  188.7 18.8 %collective-permute-start.33 = (bf16[512,256]{1,0:T(8,128)(2,1)S(1)}, bf16[512,256]{1,0:T(8,128)(2,1)S(1)}, u32[]{:S(2)}, u32[]{:S(2)}) collective-permute-start(bf16[512,256]{1,0:T(8,128)(2,1)S(1)} %get-tuple-element.70), channel_id=1, source_target_pairs={{0,1},{1,0},{2,3},{3,2},{4,5},{5,4},{6,7},{7,6},{8,9},{9,8},{10,11... | collective-permute-start | bytes 786440 | tf_op jit(solution)/shard_map/ppermute | solution.py:23
  192.9 15.2 %collective-permute-start.34 = (bf16[512,256]{1,0:T(8,128)(2,1)S(1)}, bf16[512,256]{1,0:T(8,128)(2,1)S(1)}, u32[]{:S(2)}, u32[]{:S(2)}) collective-permute-start(bf16[512,256]{1,0:T(8,128)(2,1)S(1)} %get-tuple-element.71), channel_id=1, source_target_pairs={{0,2},{1,3},{2,0},{3,1},{4,6},{5,7},{6,4},{7,5},{8,10},{9,11},{10,... | collective-permute-start | bytes 786440 | tf_op jit(solution)/shard_map/ppermute | solution.py:23
  198.5 5.1 %collective-permute-start.29 = (bf16[128,512]{1,0:T(8,128)(2,1)S(1)}, bf16[128,512]{1,0:T(8,128)(2,1)S(1)}, u32[]{:S(2)}, u32[]{:S(2)}) collective-permute-start(bf16[128,512]{1,0:T(8,128)(2,1)S(1)} %get-tuple-element.62), channel_id=1, source_target_pairs={{0,2},{1,3},{2,0},{3,1},{4,6},{5,7},{6,4},{7,5},{8,10},{9,11},{10,... | collective-permute-start | bytes 393224 | tf_op jit(solution)/shard_map/ppermute | solution.py:23
  199.0 7.9 %collective-permute-start.30 = (bf16[128,512]{1,0:T(8,128)(2,1)S(1)}, bf16[128,512]{1,0:T(8,128)(2,1)S(1)}, u32[]{:S(2)}, u32[]{:S(2)}) collective-permute-start(bf16[128,512]{1,0:T(8,128)(2,1)S(1)} %get-tuple-element.64), channel_id=1, source_target_pairs={{0,1},{1,0},{2,3},{3,2},{4,5},{5,4},{6,7},{7,6},{8,9},{9,8},{10,11... | collective-permute-start | bytes 393224 | tf_op jit(solution)/shard_map/ppermute | solution.py:23
  199.7 13.8 %collective-permute-start.39 = (bf16[256,256]{1,0:T(8,128)(2,1)S(1)}, bf16[256,256]{1,0:T(8,128)(2,1)S(1)}, u32[]{:S(2)}, u32[]{:S(2)}) collective-permute-start(bf16[256,256]{1,0:T(8,128)(2,1)S(1)} %get-tuple-element.76), channel_id=1, source_target_pairs={{0,1},{1,0},{2,3},{3,2},{4,5},{5,4},{6,7},{7,6},{8,9},{9,8},{10,11... | collective-permute-start | bytes 393224 | tf_op jit(solution)/shard_map/ppermute | solution.py:23
  203.6 9.9 %collective-permute-start.40 = (bf16[256,256]{1,0:T(8,128)(2,1)S(1)}, bf16[256,256]{1,0:T(8,128)(2,1)S(1)}, u32[]{:S(2)}, u32[]{:S(2)}) collective-permute-start(bf16[256,256]{1,0:T(8,128)(2,1)S(1)} %get-tuple-element.77), channel_id=1, source_target_pairs={{0,2},{1,3},{2,0},{3,1},{4,6},{5,7},{6,4},{7,5},{8,10},{9,11},{10,... | collective-permute-start | bytes 393224 | tf_op jit(solution)/shard_map/ppermute | solution.py:23
  206.9 4.3 %collective-permute-start.37 = (bf16[128,256]{1,0:T(8,128)(2,1)S(1)}, bf16[128,256]{1,0:T(8,128)(2,1)S(1)}, u32[]{:S(2)}, u32[]{:S(2)}) collective-permute-start(bf16[128,256]{1,0:T(8,128)(2,1)S(1)} %get-tuple-element.74), channel_id=1, source_target_pairs={{0,1},{1,0},{2,3},{3,2},{4,5},{5,4},{6,7},{7,6},{8,9},{9,8},{10,11... | collective-permute-start | bytes 196616 | tf_op jit(solution)/shard_map/ppermute | solution.py:23
  207.5 6.0 %collective-permute-start.38 = (bf16[128,256]{1,0:T(8,128)(2,1)S(1)}, bf16[128,256]{1,0:T(8,128)(2,1)S(1)}, u32[]{:S(2)}, u32[]{:S(2)}) collective-permute-start(bf16[128,256]{1,0:T(8,128)(2,1)S(1)} %get-tuple-element.75), channel_id=1, source_target_pairs={{0,2},{1,3},{2,0},{3,1},{4,6},{5,7},{6,4},{7,5},{8,10},{9,11},{10,... | collective-permute-start | bytes 196616 | tf_op jit(solution)/shard_map/ppermute | solution.py:23
  208.1 6.4 %collective-permute-start.35 = (bf16[128,256]{1,0:T(8,128)(2,1)S(1)}, bf16[128,256]{1,0:T(8,128)(2,1)S(1)}, u32[]{:S(2)}, u32[]{:S(2)}) collective-permute-start(bf16[128,256]{1,0:T(8,128)(2,1)S(1)} %get-tuple-element.72), channel_id=1, source_target_pairs={{0,1},{1,0},{2,3},{3,2},{4,5},{5,4},{6,7},{7,6},{8,9},{9,8},{10,11... | collective-permute-start | bytes 196616 | tf_op jit(solution)/shard_map/ppermute | solution.py:23
  211.2 4.3 %collective-permute-start.36 = (bf16[128,256]{1,0:T(8,128)(2,1)S(1)}, bf16[128,256]{1,0:T(8,128)(2,1)S(1)}, u32[]{:S(2)}, u32[]{:S(2)}) collective-permute-start(bf16[128,256]{1,0:T(8,128)(2,1)S(1)} %get-tuple-element.73), channel_id=1, source_target_pairs={{0,2},{1,3},{2,0},{3,1},{4,6},{5,7},{6,4},{7,5},{8,10},{9,11},{10,... | collective-permute-start | bytes 196616 | tf_op jit(solution)/shard_map/ppermute | solution.py:23

commit v8 on v7

--- a/solution.py
+++ b/solution.py
@@ -148,16 +148,23 @@
     )(mine, *masks)
 
 
+SPLIT = 4
+
+
 def cut_body(mine, here, plan, src, *refs, first, blocks):
     outs, sems = refs[:-1], refs[-1]
     wide = src.shape[3] // blocks if first else outs[0].shape[2]
     copies = []
     for out in outs:
         for u in range(out.shape[2] // wide):
-            unit = len(copies)
+            unit = len(copies) // SPLIT
             at = pl.ds(pl.multiple_of(plan[first + unit] * wide, wide) if first else 0, wide)
             to = slice(u * wide, (u + 1) * wide)
-            copies.append(pltpu.make_async_copy(src.at[0, :, :, at], out.at[:, :, to], sems.at[unit]))
+            high = out.shape[1] // SPLIT
+            for k in range(SPLIT):
+                rows = pl.ds(k * high, high)
+                sem = sems.at[SPLIT * unit + k]
+                copies.append(pltpu.make_async_copy(src.at[0, :, rows, at], out.at[:, rows, to], sem))
     for copy in copies:
         copy.start()
     for copy in copies:
@@ -173,7 +180,7 @@
             grid=(1,),
             in_specs=[HBM],
             out_specs=[VMEM] * len(sizes),
-            scratch_shapes=[pltpu.SemaphoreType.DMA((sum(sizes),))],
+            scratch_shapes=[pltpu.SemaphoreType.DMA((SPLIT * sum(sizes),))],
         ),
         out_shape=[jax.ShapeDtypeStruct((2, rows, units * width // blocks), BF16) for units in sizes],
         compiler_params=LIMIT,
@@ -502,7 +509,7 @@
     return whole
 
 
-ARRIVE = (2, 2, 2, 1, 1)
+ARRIVE = (2, 2, 1, 1, 1, 1)
 LEAVE = (1, 2, 2, 2, 1)
 
 

time: 217 us -> 227 us (1.046)
  Pallas kernels: 82.7 us -> 86.8 us
  waiting for transfers between devices: 96 us -> 98.6 us
  starting transfers between devices: 36.3 us -> 38.7 us
    pallas_call x12 -> x13, Pallas kernels: 64.5 us -> 68.2 us  [fold(): pl.pallas_call(body, grid_spec=pltpu.PrefetchScalarGridSpec(num_scalar_pr...]
    ppermute x12 -> x13, waiting for transfers between devices: 78.5 us -> 81.2 us  [shift(): lax.ppermute(block, axis, [(i, i + step) for i in devices if i + step in...]
    ppermute x12 -> x13, starting transfers between devices: 19.4 us -> 20.7 us  [shift(): lax.ppermute(block, axis, [(i, i + step) for i in devices if i + step in...]
    ppermute x29 -> x30, starting transfers between devices: 16.9 us -> 18.1 us  [flip(): lax.ppermute(block, axis, [(i, i ^ bit) for i in range(lax.axis_size(axis...]
    ppermute x29 -> x30, waiting for transfers between devices: 17.5 us -> 17.4 us  [flip(): lax.ppermute(block, axis, [(i, i ^ bit) for i in range(lax.axis_size(axis...]
  transfers between devices with their start and end apart: 41 -> 43, of which waited for: 16 -> 15; matrix products, arithmetic and copies ran while one was open for 0% -> 0% of each run, Pallas kernels for 36% -> 36%
where the time goes in v8:
time: 227 us; the launch traced here: 225 us
  waiting for transfers between devices  98.6 us (43%)
  Pallas kernels  86.8 us (38%)
  starting transfers between devices  38.7 us (17%)
    ppermute x13, waiting for transfers between devices, shift(): lax.ppermute(block, axis, [(i, i + step) for i in devices if i + step in...  81.2 us
    pallas_call x13, Pallas kernels, fold(): pl.pallas_call(body, grid_spec=pltpu.PrefetchScalarGridSpec(num_scalar_pr...  68.2 us
    ppermute x13, starting transfers between devices, shift(): lax.ppermute(block, axis, [(i, i + step) for i in devices if i + step in...  20.7 us
    ppermute x30, starting transfers between devices, flip(): lax.ppermute(block, axis, [(i, i ^ bit) for i in range(lax.axis_size(axis...  18.1 us
    ppermute x30, waiting for transfers between devices, flip(): lax.ppermute(block, axis, [(i, i ^ bit) for i in range(lax.axis_size(axis...  17.4 us
    pallas_call x2, Pallas kernels, masked_factor(): pl.pallas_call(functools.partial(mask_body, tick=tick), grid_spec=pltpu.P...  6.17 us
    pallas_call x3, Pallas kernels, cut_pieces(): pl.pallas_call(functools.partial(cut_body, first=first, blocks=blocks), g...  5.08 us
  transfers between devices with their start and end apart: 43, of which 15 were waited for; matrix products, arithmetic and copies ran while one was open for 0% of the time, Pallas kernels for 36%

profile of v8, /device:TPU:0, one launch (start us, length us, event | category | flops | bytes accessed | tf_op | source)
XLA Modules:
  0.0 225.5 jit_solution(8236871195930832274)
XLA Ops:
  0.6 3.7 %shard_map.78.refs_5_.refs_6_ = bf16[2,512,1024]{2,1,0:T(8,128)(2,1)} custom-call(s32[2,1,4,8]{3,2,1,0:T(4,128)} %mask_ref.3, bf16[2,1,2,512,1024]{4,3,2,1,0:T(8,128)(2,1)} %coupling_ref.3), custom_call_target="tpu_custom_call" | custom-call | tf_op jit(solution)/shard_map/pallas_call | solution.py:63
  4.9 2.4 %shard_map.77.refs_5_.refs_6_ = bf16[2,512,1024]{2,1,0:T(8,128)(2,1)S(1)} custom-call(s32[2,1,4,8]{3,2,1,0:T(4,128)} %mask_ref.3, bf16[2,1,2,512,1024]{4,3,2,1,0:T(8,128)(2,1)} %coupling_ref.3), custom_call_target="tpu_custom_call" | custom-call | tf_op jit(solution)/shard_map/pallas_call | solution.py:63
  8.0 4.1 %collective-permute-done.refs_1_ = s32[2,1,4,8]{3,2,1,0:T(4,128)S(1)} collective-permute-done((s32[2,1,4,8]{3,2,1,0:T(4,128)}, s32[2,1,4,8]{3,2,1,0:T(4,128)S(1)}, u32[]{:S(2)}, u32[]{:S(2)}) %collective-permute-start) | collective-permute-done | bytes 288 | tf_op jit(solution)/shard_map/ppermute | solution.py:23
  12.1 1.7 plan.1.refs_4_
  13.8 4.8 %collective-permute-start.4 = (s32[16]{0:T(128)S(1)}, s32[16]{0:T(128)S(1)}, u32[]{:S(2)}, u32[]{:S(2)}) collective-permute-start(s32[16]{0:T(128)S(1)} %plan.1.refs_4_), channel_id=1, source_target_pairs={{0,8},{8,16},{16,24},{1,9},{9,17},{17,25},{2,10},{10,18},{18,26},{... | collective-permute-start | bytes 200 | tf_op jit(solution)/shard_map/ppermute | solution.py:19
  19.9 2.2 shard_map.79
  22.1 1.3 collective-permute-start.5
  24.6 1.3 collective-permute-start.15
  25.9 1.7 shard_map.80
  27.6 1.3 collective-permute-start.13
  28.9 4.3 %collective-permute-done.5.refs_8_ = bf16[2,512,128]{2,1,0:T(8,128)(2,1)S(1)} collective-permute-done((bf16[2,512,128]{2,1,0:T(8,128)(2,1)S(1)}, bf16[2,512,128]{2,1,0:T(8,128)(2,1)S(1)}, u32[]{:S(2)}, u32[]{:S(2)}) %collective-permute-start.5) | collective-permute-done | bytes 262176 | tf_op jit(solution)/shard_map/ppermute | solution.py:19
  34.5 25.1 %collective-permute-done.7.refs_8_ = bf16[2,512,128]{2,1,0:T(8,128)(2,1)S(1)} collective-permute-done((bf16[2,512,128]{2,1,0:T(8,128)(2,1)S(1)}, bf16[2,512,128]{2,1,0:T(8,128)(2,1)S(1)}, u32[]{:S(2)}, u32[]{:S(2)}) %collective-permute-start.7) | collective-permute-done | bytes 262176 | tf_op jit(solution)/shard_map/ppermute | solution.py:19
  61.5 6.6 %collective-permute-done.9.refs_8_ = bf16[2,512,128]{2,1,0:T(8,128)(2,1)S(1)} collective-permute-done((bf16[2,512,128]{2,1,0:T(8,128)(2,1)S(1)}, bf16[2,512,128]{2,1,0:T(8,128)(2,1)S(1)}, u32[]{:S(2)}, u32[]{:S(2)}) %collective-permute-start.9) | collective-permute-done | bytes 262176 | tf_op jit(solution)/shard_map/ppermute | solution.py:19
  68.1 1.5 collective-permute-start.11
  69.6 6.8 %collective-permute-done.11.refs_8_ = bf16[2,512,128]{2,1,0:T(8,128)(2,1)S(1)} collective-permute-done((bf16[2,512,128]{2,1,0:T(8,128)(2,1)S(1)}, bf16[2,512,128]{2,1,0:T(8,128)(2,1)S(1)}, u32[]{:S(2)}, u32[]{:S(2)}) %collective-permute-start.11) | collective-permute-done | bytes 262176 | tf_op jit(solution)/shard_map/ppermute | solution.py:19
  76.9 7.4 %shard_map.82.refs_10_ = f32[2,512,1024]{2,1,0:T(8,128)S(1)} custom-call(s32[1]{0:T(128)} %bitcast.mine.plan.refs_0_, s32[1,1,2]{2,1,0:T(1,128)S(1)} %bitcast.3, f32[2,16]{1,0:T(2,128)S(1)} %copy-done, s32[1]{0:T(128)} %bitcast.2.here.refs_3_, s32[16]{0:T(128)S(1)} %plan.1.refs_4_, bf16[2,512,1024]{2,1,0:T(8,128)(2,1)} %shard_map.78.refs_5_.refs_6_, ...), custom_call_target="tpu_custom_call" | custom-call | tf_op jit(solution)/shard_map/pallas_call | solution.py:324
  84.9 7.0 %shard_map.83.refs_10_ = f32[2,512,1024]{2,1,0:T(8,128)S(1)} custom-call(s32[1]{0:T(128)} %bitcast.mine.plan.refs_0_, s32[1,1,2]{2,1,0:T(1,128)S(1)} %bitcast.4, f32[2,16]{1,0:T(2,128)S(1)} %copy-done, s32[1]{0:T(128)} %bitcast.2.here.refs_3_, s32[16]{0:T(128)S(1)} %plan.1.refs_4_, ...), custom_call_target="tpu_custom_call", output_to_operand_aliasing={{}: (10, {})} | custom-call | tf_op jit(solution)/shard_map/pallas_call | solution.py:324
  91.9 5.3 %shard_map.84.refs_10_ = f32[2,512,1024]{2,1,0:T(8,128)S(1)} custom-call(s32[1]{0:T(128)} %bitcast.mine.plan.refs_0_, s32[1,1,2]{2,1,0:T(1,128)S(1)} %bitcast.5, f32[2,16]{1,0:T(2,128)S(1)} %copy-done, s32[1]{0:T(128)} %bitcast.2.here.refs_3_, s32[16]{0:T(128)S(1)} %plan.1.refs_4_, ...), custom_call_target="tpu_custom_call", output_to_operand_aliasing={{}: (10, {})} | custom-call | tf_op jit(solution)/shard_map/pallas_call | solution.py:324
  97.3 5.4 %shard_map.85 = (f32[2,512,1024]{2,1,0:T(8,128)S(1)}, bf16[2,512,128]{2,1,0:T(8,128)(2,1)S(1)}) custom-call(s32[1]{0:T(128)} %bitcast.mine.plan.refs_0_, s32[1,1,2]{2,1,0:T(1,128)S(1)} %bitcast.6, f32[2,16]{1,0:T(2,128)S(1)} %copy-done, s32[1]{0:T(128)} %bitcast.2.here.refs_3_, s32[16]{0:T(128)S(1)} %plan.1.refs_4_, ...), custom_call_target="tpu_custom_call", output_to_operand_aliasing={{0}: (10, {})} | custom-call | tf_op jit(solution)/shard_map/pallas_call | solution.py:324
  102.7 5.5 %shard_map.86 = (f32[2,512,1024]{2,1,0:T(8,128)S(1)}, bf16[2,512,256]{2,1,0:T(8,128)(2,1)S(1)}) custom-call(s32[1]{0:T(128)} %bitcast.mine.plan.refs_0_, s32[1,1,2]{2,1,0:T(1,128)S(1)} %bitcast.7, f32[2,16]{1,0:T(2,128)S(1)} %copy-done, s32[1]{0:T(128)} %bitcast.2.here.refs_3_, s32[16]{0:T(128)S(1)} %plan.1.refs_4_, ...), custom_call_target="tpu_custom_call", output_to_operand_aliasing={{0}: (10, {})} | custom-call | tf_op jit(solution)/shard_map/pallas_call | solution.py:324
  108.2 1.3 collective-permute-start.23
  109.5 5.6 %shard_map.87 = (bf16[2,512,1024]{2,1,0:T(8,128)(2,1)S(1)}, bf16[2,512,256]{2,1,0:T(8,128)(2,1)S(1)}, bf16[2,512,256]{2,1,0:T(8,128)(2,1)S(1)}, bf16[2,512,128]{2,1,0:T(8,128)(2,1)S(1)}) custom-call(s32[1]{0:T(128)} %bitcast.mine.plan.refs_0_, s32[1,1,2]{2,1,0:T(1,128)S(1)} %bitcast.8, f32[2,16]{1,0:T(2,128)S(1)} %copy-done, s32[1]{0:T(128)} %bitcast.2.here.refs_3_, ...), custom_call_target="tpu_custom_call" | custom-call | tf_op jit(solution)/shard_map/pallas_call | solution.py:324
  115.1 1.3 collective-permute-start.21
  116.4 1.3 collective-permute-start.19
  119.0 27.5 %collective-permute-done.1.refs_4_ = s32[16]{0:T(128)S(1)} collective-permute-done((s32[16]{0:T(128)S(1)}, s32[16]{0:T(128)S(1)}, u32[]{:S(2)}, u32[]{:S(2)}) %collective-permute-start.1) | collective-permute-done | bytes 96 | tf_op jit(solution)/shard_map/ppermute | solution.py:19
  147.9 1.5 collective-permute-start.17
  149.4 8.2 %collective-permute-done.25.refs_8_ = bf16[2,512,128]{2,1,0:T(8,128)(2,1)S(1)} collective-permute-done((bf16[2,512,128]{2,1,0:T(8,128)(2,1)S(1)}, bf16[2,512,128]{2,1,0:T(8,128)(2,1)S(1)}, u32[]{:S(2)}, u32[]{:S(2)}) %collective-permute-start.25) | collective-permute-done | bytes 262176 | tf_op jit(solution)/shard_map/ppermute | solution.py:19
  158.2 1.8 shard_map.95
  159.9 1.4 collective-permute-done.17.refs_8_
  161.4 1.5 collective-permute-start.33
  162.9 1.5 collective-permute-start.34
  164.4 5.1 %shard_map.88.refs_10_ = f32[2,512,1024]{2,1,0:T(8,128)S(1)} custom-call(s32[1]{0:T(128)} %bitcast.mine.plan.refs_0_, s32[1,1,2]{2,1,0:T(1,128)S(1)} %bitcast.10, f32[2,16]{1,0:T(2,128)S(1)} %copy-done, s32[1]{0:T(128)} %bitcast.2.here.refs_3_, s32[16]{0:T(128)S(1)} %collective-permute-done.1.refs_4_, bf16[2,512,1024]{2,1,0:T(8,128)(2,1)S(1)} %shard_map.77.refs_5_.refs_6_, ...), custom_call_target="tpu_custom_call" | custom-call | tf_op jit(solution)/shard_map/pallas_call | solution.py:324
  169.4 5.7 %shard_map.89.refs_10_ = f32[2,512,1024]{2,1,0:T(8,128)S(1)} custom-call(s32[1]{0:T(128)} %bitcast.mine.plan.refs_0_, s32[1,1,2]{2,1,0:T(1,128)S(1)} %bitcast.11, f32[2,16]{1,0:T(2,128)S(1)} %copy-done, s32[1]{0:T(128)} %bitcast.2.here.refs_3_, s32[16]{0:T(128)S(1)} %collective-permute-done.1.refs_4_, ...), custom_call_target="tpu_custom_call", output_to_operand_aliasing={{}: (10, {})} | custom-call | tf_op jit(solution)/shard_map/pallas_call | solution.py:324
  175.1 5.7 %shard_map.90.refs_10_ = f32[2,512,1024]{2,1,0:T(8,128)S(1)} custom-call(s32[1]{0:T(128)} %bitcast.mine.plan.refs_0_, s32[1,1,2]{2,1,0:T(1,128)S(1)} %bitcast.12, f32[2,16]{1,0:T(2,128)S(1)} %copy-done, s32[1]{0:T(128)} %bitcast.2.here.refs_3_, s32[16]{0:T(128)S(1)} %collective-permute-done.1.refs_4_, ...), custom_call_target="tpu_custom_call", output_to_operand_aliasing={{}: (10, {})} | custom-call | tf_op jit(solution)/shard_map/pallas_call | solution.py:324
  180.9 5.7 %shard_map.91.refs_10_ = f32[2,512,1024]{2,1,0:T(8,128)S(1)} custom-call(s32[1]{0:T(128)} %bitcast.mine.plan.refs_0_, s32[1,1,2]{2,1,0:T(1,128)S(1)} %bitcast.13, f32[2,16]{1,0:T(2,128)S(1)} %copy-done, s32[1]{0:T(128)} %bitcast.2.here.refs_3_, s32[16]{0:T(128)S(1)} %collective-permute-done.1.refs_4_, ...), custom_call_target="tpu_custom_call", output_to_operand_aliasing={{}: (10, {})} | custom-call | tf_op jit(solution)/shard_map/pallas_call | solution.py:324
  186.6 3.8 %shard_map.93 = (bf16[2,256,1024]{2,1,0:T(8,128)(2,1)S(1)}, bf16[256,512]{1,0:T(8,128)(2,1)S(1)}, bf16[256,512]{1,0:T(8,128)(2,1)S(1)}, bf16[256,512]{1,0:T(8,128)(2,1)S(1)}, bf16[256,512]{1,0:T(8,128)(2,1)S(1)}) custom-call(s32[1]{0:T(128)} %bitcast.mine.plan.refs_0_, s32[1,1,2]{2,1,0:T(1,128)S(1)} %bitcast.14, f32[2,16]{1,0:T(2,128)S(1)} %copy-done, ...), custom_call_target="tpu_custom_call" | custom-call | tf_op jit(solution)/shard_map/pallas_call | solution.py:324
  191.0 3.0 %shard_map.92 = (bf16[2,128,1024]{2,1,0:T(8,128)(2,1)S(1)}, bf16[128,512]{1,0:T(8,128)(2,1)S(1)}, bf16[128,512]{1,0:T(8,128)(2,1)S(1)}, bf16[128,512]{1,0:T(8,128)(2,1)S(1)}, bf16[128,512]{1,0:T(8,128)(2,1)S(1)}) custom-call(s32[1]{0:T(128)} %bitcast.mine.plan.refs_0_, s32[1,1,2]{2,1,0:T(1,128)S(1)} %bitcast.15, f32[2,16]{1,0:T(2,128)S(1)} %copy-done, ...), custom_call_target="tpu_custom_call" | custom-call | tf_op jit(solution)/shard_map/pallas_call | solution.py:324
  194.0 1.6 collective-permute-start.27
  196.2 1.5 collective-permute-start.28
  198.4 3.6 %collective-permute-done.27.refs_1_.real_got = bf16[128,512]{1,0:T(8,128)(2,1)S(1)} collective-permute-done((bf16[128,512]{1,0:T(8,128)(2,1)S(1)}, bf16[128,512]{1,0:T(8,128)(2,1)S(1)}, u32[]{:S(2)}, u32[]{:S(2)}) %collective-permute-start.27) | collective-permute-done | bytes 131104 | tf_op jit(solution)/shard_map/ppermute | solution.py:23
  202.6 3.0 %shard_map.94 = (bf16[2,128,1024]{2,1,0:T(8,128)(2,1)S(1)}, bf16[128,512]{1,0:T(8,128)(2,1)S(1)}, bf16[128,512]{1,0:T(8,128)(2,1)S(1)}, bf16[128,512]{1,0:T(8,128)(2,1)S(1)}, bf16[128,512]{1,0:T(8,128)(2,1)S(1)}) custom-call(s32[1]{0:T(128)} %bitcast.mine.plan.refs_0_, s32[1,1,2]{2,1,0:T(1,128)S(1)} %bitcast.16, f32[2,16]{1,0:T(2,128)S(1)} %copy-done, ...), custom_call_target="tpu_custom_call" | custom-call | tf_op jit(solution)/shard_map/pallas_call | solution.py:324
  205.6 2.0 collective-permute-done.28.refs_3_.imag_got
  208.8 1.6 collective-permute-start.41
  210.4 2.3 %collective-permute-done.31.refs_9_.real_got = bf16[128,512]{1,0:T(8,128)(2,1)S(1)} collective-permute-done((bf16[128,512]{1,0:T(8,128)(2,1)S(1)}, bf16[128,512]{1,0:T(8,128)(2,1)S(1)}, u32[]{:S(2)}, u32[]{:S(2)}) %collective-permute-start.31) | collective-permute-done | bytes 131104 | tf_op jit(solution)/shard_map/ppermute | solution.py:23
  213.2 2.8 %collective-permute-done.32.refs_11_.imag_got = bf16[128,512]{1,0:T(8,128)(2,1)S(1)} collective-permute-done((bf16[128,512]{1,0:T(8,128)(2,1)S(1)}, bf16[128,512]{1,0:T(8,128)(2,1)S(1)}, u32[]{:S(2)}, u32[]{:S(2)}) %collective-permute-start.32) | collective-permute-done | bytes 131104 | tf_op jit(solution)/shard_map/ppermute | solution.py:23
  217.2 1.5 collective-permute-start.37
  218.7 1.6 collective-permute-done.39.refs_0_
  221.1 1.3 emit.1
  (72 shorter events, 20.0 us)
Async XLA Ops:
  4.4 72.5 %collective-permute-start.3 = (bf16[2,512,1024]{2,1,0:T(8,128)(2,1)}, bf16[2,512,1024]{2,1,0:T(8,128)(2,1)}, u32[]{:S(2)}, u32[]{:S(2)}) collective-permute-start(bf16[2,512,1024]{2,1,0:T(8,128)(2,1)} %shard_map.78.refs_5_.refs_6_), channel_id=1, source_target_pairs={{0,4},{4,0},{1,5},{5,1},{2,6},{6,2},{3,7},{7,3},{8,12},{12,8},{9,1... | collective-permute-start | bytes 6291464 | tf_op jit(solution)/shard_map/ppermute | solution.py:23
  7.4 69.6 %copy-start = (f32[2,16]{1,0:T(2,128)S(1)}, f32[2,16]{1,0:T(2,128)}, u32[]{:S(2)}) copy-start(f32[2,16]{1,0:T(2,128)} %pw.1) | copy-start | bytes 388
  7.4 69.6 %copy-start.1 = (s32[2,1,1]{0,2,1:T(1,128)S(1)}, s32[2,1,1]{0,2,1:T(1,128)}, u32[]{:S(2)}) copy-start(s32[2,1,1]{0,2,1:T(1,128)} %param.11) | copy-start | bytes 28
  7.4 140.5 %collective-permute-start.2 = (bf16[2,512,1024]{2,1,0:T(8,128)(2,1)S(1)}, bf16[2,512,1024]{2,1,0:T(8,128)(2,1)}, u32[]{:S(2)}, u32[]{:S(2)}) collective-permute-start(bf16[2,512,1024]{2,1,0:T(8,128)(2,1)S(1)} %shard_map.77.refs_5_.refs_6_), channel_id=1, source_target_pairs={{0,4},{4,0},{1,5},{5,1},{2,6},{6,2},{3,7},{7,3},{8,12},{12,8},{9,1... | collective-permute-start | bytes 6291464 | tf_op jit(solution)/shard_map/ppermute | solution.py:23
  7.5 4.6 %collective-permute-start = (s32[2,1,4,8]{3,2,1,0:T(4,128)}, s32[2,1,4,8]{3,2,1,0:T(4,128)S(1)}, u32[]{:S(2)}, u32[]{:S(2)}) collective-permute-start(s32[2,1,4,8]{3,2,1,0:T(4,128)} %mask_ref.3), channel_id=1, source_target_pairs={{0,4},{4,0},{1,5},{5,1},{2,6},{6,2},{3,7},{7,3},{8,12},{12,8},{9,1... | collective-permute-start | bytes 776 | tf_op jit(solution)/shard_map/ppermute | solution.py:23
  13.8 6.1 %collective-permute-start.4 = (s32[16]{0:T(128)S(1)}, s32[16]{0:T(128)S(1)}, u32[]{:S(2)}, u32[]{:S(2)}) collective-permute-start(s32[16]{0:T(128)S(1)} %plan.1.refs_4_), channel_id=1, source_target_pairs={{0,8},{8,16},{16,24},{1,9},{9,17},{17,25},{2,10},{10,18},{18,26},{... | collective-permute-start | bytes 200 | tf_op jit(solution)/shard_map/ppermute | solution.py:19
  22.1 11.1 %collective-permute-start.5 = (bf16[2,512,128]{2,1,0:T(8,128)(2,1)S(1)}, bf16[2,512,128]{2,1,0:T(8,128)(2,1)S(1)}, u32[]{:S(2)}, u32[]{:S(2)}) collective-permute-start(bf16[2,512,128]{2,1,0:T(8,128)(2,1)S(1)} %get-tuple-element.41), channel_id=1, source_target_pairs={{8,0},{16,8},{24,16},{9,1},{17,9},{25,17},{10,2},{18,10},{26,18},{... | collective-permute-start | bytes 786440 | tf_op jit(solution)/shard_map/ppermute | solution.py:19
  24.6 36.3 %collective-permute-start.15 = (bf16[2,512,256]{2,1,0:T(8,128)(2,1)S(1)}, bf16[2,512,256]{2,1,0:T(8,128)(2,1)S(1)}, u32[]{:S(2)}, u32[]{:S(2)}) collective-permute-start(bf16[2,512,256]{2,1,0:T(8,128)(2,1)S(1)} %shard_map.81), channel_id=1, source_target_pairs={{8,0},{16,8},{24,16},{9,1},{17,9},{25,17},{10,2},{18,10},{26,18},{... | collective-permute-start | bytes 1572872 | tf_op jit(solution)/shard_map/ppermute | solution.py:19
  27.6 33.4 %collective-permute-start.13 = (bf16[2,512,256]{2,1,0:T(8,128)(2,1)S(1)}, bf16[2,512,256]{2,1,0:T(8,128)(2,1)S(1)}, u32[]{:S(2)}, u32[]{:S(2)}) collective-permute-start(bf16[2,512,256]{2,1,0:T(8,128)(2,1)S(1)} %shard_map.80), channel_id=1, source_target_pairs={{8,0},{16,8},{24,16},{9,1},{17,9},{25,17},{10,2},{18,10},{26,18},{... | collective-permute-start | bytes 1572872 | tf_op jit(solution)/shard_map/ppermute | solution.py:19
  33.2 26.4 %collective-permute-start.7 = (bf16[2,512,128]{2,1,0:T(8,128)(2,1)S(1)}, bf16[2,512,128]{2,1,0:T(8,128)(2,1)S(1)}, u32[]{:S(2)}, u32[]{:S(2)}) collective-permute-start(bf16[2,512,128]{2,1,0:T(8,128)(2,1)S(1)} %get-tuple-element.42), channel_id=1, source_target_pairs={{8,0},{16,8},{24,16},{9,1},{17,9},{25,17},{10,2},{18,10},{26,18},{... | collective-permute-start | bytes 786440 | tf_op jit(solution)/shard_map/ppermute | solution.py:19
  59.6 8.5 %collective-permute-start.9 = (bf16[2,512,128]{2,1,0:T(8,128)(2,1)S(1)}, bf16[2,512,128]{2,1,0:T(8,128)(2,1)S(1)}, u32[]{:S(2)}, u32[]{:S(2)}) collective-permute-start(bf16[2,512,128]{2,1,0:T(8,128)(2,1)S(1)} %get-tuple-element.43), channel_id=1, source_target_pairs={{8,0},{16,8},{24,16},{9,1},{17,9},{25,17},{10,2},{18,10},{26,18},{... | collective-permute-start | bytes 786440 | tf_op jit(solution)/shard_map/ppermute | solution.py:19
  60.9 15.5 %collective-permute-start.16 = (bf16[2,512,256]{2,1,0:T(8,128)(2,1)S(1)}, bf16[2,512,256]{2,1,0:T(8,128)(2,1)S(1)}, u32[]{:S(2)}, u32[]{:S(2)}) collective-permute-start(bf16[2,512,256]{2,1,0:T(8,128)(2,1)S(1)} %collective-permute-done.15.refs_8_), channel_id=1, source_target_pairs={{0,4},{4,0},{1,5},{5,1},{2,6},{6,2},{3,7},{7,3},{8,12},{12,8},{9,1... | collective-permute-start | bytes 1572872 | tf_op jit(solution)/shard_map/ppermute | solution.py:23
  61.0 23.4 %collective-permute-start.14 = (bf16[2,512,256]{2,1,0:T(8,128)(2,1)S(1)}, bf16[2,512,256]{2,1,0:T(8,128)(2,1)S(1)}, u32[]{:S(2)}, u32[]{:S(2)}) collective-permute-start(bf16[2,512,256]{2,1,0:T(8,128)(2,1)S(1)} %collective-permute-done.13.refs_8_), channel_id=1, source_target_pairs={{0,4},{4,0},{1,5},{5,1},{2,6},{6,2},{3,7},{7,3},{8,12},{12,8},{9,1... | collective-permute-start | bytes 1572872 | tf_op jit(solution)/shard_map/ppermute | solution.py:23
  68.1 8.3 %collective-permute-start.11 = (bf16[2,512,128]{2,1,0:T(8,128)(2,1)S(1)}, bf16[2,512,128]{2,1,0:T(8,128)(2,1)S(1)}, u32[]{:S(2)}, u32[]{:S(2)}) collective-permute-start(bf16[2,512,128]{2,1,0:T(8,128)(2,1)S(1)} %get-tuple-element.44), channel_id=1, source_target_pairs={{8,0},{16,8},{24,16},{9,1},{17,9},{25,17},{10,2},{18,10},{26,18},{... | collective-permute-start | bytes 786440 | tf_op jit(solution)/shard_map/ppermute | solution.py:19
  76.4 15.5 %collective-permute-start.12 = (bf16[2,512,128]{2,1,0:T(8,128)(2,1)S(1)}, bf16[2,512,128]{2,1,0:T(8,128)(2,1)S(1)}, u32[]{:S(2)}, u32[]{:S(2)}) collective-permute-start(bf16[2,512,128]{2,1,0:T(8,128)(2,1)S(1)} %collective-permute-done.11.refs_8_), channel_id=1, source_target_pairs={{0,4},{4,0},{1,5},{5,1},{2,6},{6,2},{3,7},{7,3},{8,12},{12,8},{9,1... | collective-permute-start | bytes 786440 | tf_op jit(solution)/shard_map/ppermute | solution.py:23
  76.4 20.9 %collective-permute-start.10 = (bf16[2,512,128]{2,1,0:T(8,128)(2,1)S(1)}, bf16[2,512,128]{2,1,0:T(8,128)(2,1)S(1)}, u32[]{:S(2)}, u32[]{:S(2)}) collective-permute-start(bf16[2,512,128]{2,1,0:T(8,128)(2,1)S(1)} %collective-permute-done.9.refs_8_), channel_id=1, source_target_pairs={{0,4},{4,0},{1,5},{5,1},{2,6},{6,2},{3,7},{7,3},{8,12},{12,8},{9,1... | collective-permute-start | bytes 786440 | tf_op jit(solution)/shard_map/ppermute | solution.py:23
  76.9 25.8 %collective-permute-start.8 = (bf16[2,512,128]{2,1,0:T(8,128)(2,1)S(1)}, bf16[2,512,128]{2,1,0:T(8,128)(2,1)S(1)}, u32[]{:S(2)}, u32[]{:S(2)}) collective-permute-start(bf16[2,512,128]{2,1,0:T(8,128)(2,1)S(1)} %collective-permute-done.7.refs_8_), channel_id=1, source_target_pairs={{0,4},{4,0},{1,5},{5,1},{2,6},{6,2},{3,7},{7,3},{8,12},{12,8},{9,1... | collective-permute-start | bytes 786440 | tf_op jit(solution)/shard_map/ppermute | solution.py:23
  84.4 25.1 %collective-permute-start.6 = (bf16[2,512,128]{2,1,0:T(8,128)(2,1)S(1)}, bf16[2,512,128]{2,1,0:T(8,128)(2,1)S(1)}, u32[]{:S(2)}, u32[]{:S(2)}) collective-permute-start(bf16[2,512,128]{2,1,0:T(8,128)(2,1)S(1)} %collective-permute-done.5.refs_8_), channel_id=1, source_target_pairs={{0,4},{4,0},{1,5},{5,1},{2,6},{6,2},{3,7},{7,3},{8,12},{12,8},{9,1... | collective-permute-start | bytes 786440 | tf_op jit(solution)/shard_map/ppermute | solution.py:23
  108.2 39.6 %collective-permute-start.23 = (bf16[2,512,256]{2,1,0:T(8,128)(2,1)S(1)}, bf16[2,512,256]{2,1,0:T(8,128)(2,1)S(1)}, u32[]{:S(2)}, u32[]{:S(2)}) collective-permute-start(bf16[2,512,256]{2,1,0:T(8,128)(2,1)S(1)} %get-tuple-element.50), channel_id=1, source_target_pairs={{8,0},{16,8},{24,16},{9,1},{17,9},{25,17},{10,2},{18,10},{26,18},{... | collective-permute-start | bytes 1572872 | tf_op jit(solution)/shard_map/ppermute | solution.py:19
  115.1 42.5 %collective-permute-start.21 = (bf16[2,512,256]{2,1,0:T(8,128)(2,1)S(1)}, bf16[2,512,256]{2,1,0:T(8,128)(2,1)S(1)}, u32[]{:S(2)}, u32[]{:S(2)}) collective-permute-start(bf16[2,512,256]{2,1,0:T(8,128)(2,1)S(1)} %get-tuple-element.49), channel_id=1, source_target_pairs={{8,0},{16,8},{24,16},{9,1},{17,9},{25,17},{10,2},{18,10},{26,18},{... | collective-permute-start | bytes 1572872 | tf_op jit(solution)/shard_map/ppermute | solution.py:19
  116.4 41.7 %collective-permute-start.19 = (bf16[2,512,256]{2,1,0:T(8,128)(2,1)S(1)}, bf16[2,512,256]{2,1,0:T(8,128)(2,1)S(1)}, u32[]{:S(2)}, u32[]{:S(2)}) collective-permute-start(bf16[2,512,256]{2,1,0:T(8,128)(2,1)S(1)} %get-tuple-element.48), channel_id=1, source_target_pairs={{8,0},{16,8},{24,16},{9,1},{17,9},{25,17},{10,2},{18,10},{26,18},{... | collective-permute-start | bytes 1572872 | tf_op jit(solution)/shard_map/ppermute | solution.py:19
  117.7 28.8 %collective-permute-start.1 = (s32[16]{0:T(128)S(1)}, s32[16]{0:T(128)S(1)}, u32[]{:S(2)}, u32[]{:S(2)}) collective-permute-start(s32[16]{0:T(128)S(1)} %plan.1.refs_4_), channel_id=1, source_target_pairs={{8,0},{16,8},{24,16},{9,1},{17,9},{25,17},{10,2},{18,10},{26,18},{... | collective-permute-start | bytes 200 | tf_op jit(solution)/shard_map/ppermute | solution.py:19
  146.5 11.1 %collective-permute-start.25 = (bf16[2,512,128]{2,1,0:T(8,128)(2,1)S(1)}, bf16[2,512,128]{2,1,0:T(8,128)(2,1)S(1)}, u32[]{:S(2)}, u32[]{:S(2)}) collective-permute-start(bf16[2,512,128]{2,1,0:T(8,128)(2,1)S(1)} %get-tuple-element.51), channel_id=1, source_target_pairs={{8,0},{16,8},{24,16},{9,1},{17,9},{25,17},{10,2},{18,10},{26,18},{... | collective-permute-start | bytes 786440 | tf_op jit(solution)/shard_map/ppermute | solution.py:19
  147.8 16.6 %collective-permute-start.24 = (bf16[2,512,256]{2,1,0:T(8,128)(2,1)S(1)}, bf16[2,512,256]{2,1,0:T(8,128)(2,1)S(1)}, u32[]{:S(2)}, u32[]{:S(2)}) collective-permute-start(bf16[2,512,256]{2,1,0:T(8,128)(2,1)S(1)} %collective-permute-done.23.refs_8_), channel_id=1, source_target_pairs={{0,4},{4,0},{1,5},{5,1},{2,6},{6,2},{3,7},{7,3},{8,12},{12,8},{9,1... | collective-permute-start | bytes 1572872 | tf_op jit(solution)/shard_map/ppermute | solution.py:23
  147.9 13.4 %collective-permute-start.17 = (bf16[2,512,128]{2,1,0:T(8,128)(2,1)S(1)}, bf16[2,512,128]{2,1,0:T(8,128)(2,1)S(1)}, u32[]{:S(2)}, u32[]{:S(2)}) collective-permute-start(bf16[2,512,128]{2,1,0:T(8,128)(2,1)S(1)} %get-tuple-element.47), channel_id=1, source_target_pairs={{8,0},{16,8},{24,16},{9,1},{17,9},{25,17},{10,2},{18,10},{26,18},{... | collective-permute-start | bytes 786440 | tf_op jit(solution)/shard_map/ppermute | solution.py:19
  157.6 5.3 %collective-permute-start.26 = (bf16[2,512,128]{2,1,0:T(8,128)(2,1)S(1)}, bf16[2,512,128]{2,1,0:T(8,128)(2,1)S(1)}, u32[]{:S(2)}, u32[]{:S(2)}) collective-permute-start(bf16[2,512,128]{2,1,0:T(8,128)(2,1)S(1)} %collective-permute-done.25.refs_8_), channel_id=1, source_target_pairs={{0,4},{4,0},{1,5},{5,1},{2,6},{6,2},{3,7},{7,3},{8,12},{12,8},{9,1... | collective-permute-start | bytes 786440 | tf_op jit(solution)/shard_map/ppermute | solution.py:23
  157.6 17.5 %collective-permute-start.22 = (bf16[2,512,256]{2,1,0:T(8,128)(2,1)S(1)}, bf16[2,512,256]{2,1,0:T(8,128)(2,1)S(1)}, u32[]{:S(2)}, u32[]{:S(2)}) collective-permute-start(bf16[2,512,256]{2,1,0:T(8,128)(2,1)S(1)} %collective-permute-done.21.refs_8_), channel_id=1, source_target_pairs={{0,4},{4,0},{1,5},{5,1},{2,6},{6,2},{3,7},{7,3},{8,12},{12,8},{9,1... | collective-permute-start | bytes 1572872 | tf_op jit(solution)/shard_map/ppermute | solution.py:23
  158.1 22.8 %collective-permute-start.20 = (bf16[2,512,256]{2,1,0:T(8,128)(2,1)S(1)}, bf16[2,512,256]{2,1,0:T(8,128)(2,1)S(1)}, u32[]{:S(2)}, u32[]{:S(2)}) collective-permute-start(bf16[2,512,256]{2,1,0:T(8,128)(2,1)S(1)} %collective-permute-done.19.refs_8_), channel_id=1, source_target_pairs={{0,4},{4,0},{1,5},{5,1},{2,6},{6,2},{3,7},{7,3},{8,12},{12,8},{9,1... | collective-permute-start | bytes 1572872 | tf_op jit(solution)/shard_map/ppermute | solution.py:23
  161.4 34.8 %collective-permute-start.33 = (bf16[512,512]{1,0:T(8,128)(2,1)S(1)}, bf16[512,512]{1,0:T(8,128)(2,1)S(1)}, u32[]{:S(2)}, u32[]{:S(2)}) collective-permute-start(bf16[512,512]{1,0:T(8,128)(2,1)S(1)} %get-tuple-element.69), channel_id=1, source_target_pairs={{0,2},{1,3},{2,0},{3,1},{4,6},{5,7},{6,4},{7,5},{8,10},{9,11},{10,... | collective-permute-start | bytes 1572872 | tf_op jit(solution)/shard_map/ppermute | solution.py:23
  162.9 34.7 %collective-permute-start.34 = (bf16[512,512]{1,0:T(8,128)(2,1)S(1)}, bf16[512,512]{1,0:T(8,128)(2,1)S(1)}, u32[]{:S(2)}, u32[]{:S(2)}) collective-permute-start(bf16[512,512]{1,0:T(8,128)(2,1)S(1)} %get-tuple-element.71), channel_id=1, source_target_pairs={{0,1},{1,0},{2,3},{3,2},{4,5},{5,4},{6,7},{7,6},{8,9},{9,8},{10,11... | collective-permute-start | bytes 1572872 | tf_op jit(solution)/shard_map/ppermute | solution.py:23
  164.4 22.2 %collective-permute-start.18 = (bf16[2,512,128]{2,1,0:T(8,128)(2,1)S(1)}, bf16[2,512,128]{2,1,0:T(8,128)(2,1)S(1)}, u32[]{:S(2)}, u32[]{:S(2)}) collective-permute-start(bf16[2,512,128]{2,1,0:T(8,128)(2,1)S(1)} %collective-permute-done.17.refs_8_), channel_id=1, source_target_pairs={{0,4},{4,0},{1,5},{5,1},{2,6},{6,2},{3,7},{7,3},{8,12},{12,8},{9,1... | collective-permute-start | bytes 786440 | tf_op jit(solution)/shard_map/ppermute | solution.py:23
  190.5 17.7 %collective-permute-start.29 = (bf16[256,512]{1,0:T(8,128)(2,1)S(1)}, bf16[256,512]{1,0:T(8,128)(2,1)S(1)}, u32[]{:S(2)}, u32[]{:S(2)}) collective-permute-start(bf16[256,512]{1,0:T(8,128)(2,1)S(1)} %get-tuple-element.60), channel_id=1, source_target_pairs={{0,2},{1,3},{2,0},{3,1},{4,6},{5,7},{6,4},{7,5},{8,10},{9,11},{10,... | collective-permute-start | bytes 786440 | tf_op jit(solution)/shard_map/ppermute | solution.py:23
  194.0 8.0 %collective-permute-start.27 = (bf16[128,512]{1,0:T(8,128)(2,1)S(1)}, bf16[128,512]{1,0:T(8,128)(2,1)S(1)}, u32[]{:S(2)}, u32[]{:S(2)}) collective-permute-start(bf16[128,512]{1,0:T(8,128)(2,1)S(1)} %get-tuple-element.56), channel_id=1, source_target_pairs={{0,2},{1,3},{2,0},{3,1},{4,6},{5,7},{6,4},{7,5},{8,10},{9,11},{10,... | collective-permute-start | bytes 393224 | tf_op jit(solution)/shard_map/ppermute | solution.py:23
  195.6 13.1 %collective-permute-start.30 = (bf16[256,512]{1,0:T(8,128)(2,1)S(1)}, bf16[256,512]{1,0:T(8,128)(2,1)S(1)}, u32[]{:S(2)}, u32[]{:S(2)}) collective-permute-start(bf16[256,512]{1,0:T(8,128)(2,1)S(1)} %get-tuple-element.62), channel_id=1, source_target_pairs={{0,1},{1,0},{2,3},{3,2},{4,5},{5,4},{6,7},{7,6},{8,9},{9,8},{10,11... | collective-permute-start | bytes 786440 | tf_op jit(solution)/shard_map/ppermute | solution.py:23
  196.2 11.4 %collective-permute-start.28 = (bf16[128,512]{1,0:T(8,128)(2,1)S(1)}, bf16[128,512]{1,0:T(8,128)(2,1)S(1)}, u32[]{:S(2)}, u32[]{:S(2)}) collective-permute-start(bf16[128,512]{1,0:T(8,128)(2,1)S(1)} %get-tuple-element.58), channel_id=1, source_target_pairs={{0,1},{1,0},{2,3},{3,2},{4,5},{5,4},{6,7},{7,6},{8,9},{9,8},{10,11... | collective-permute-start | bytes 393224 | tf_op jit(solution)/shard_map/ppermute | solution.py:23
  197.8 18.8 %collective-permute-start.35 = (bf16[512,256]{1,0:T(8,128)(2,1)S(1)}, bf16[512,256]{1,0:T(8,128)(2,1)S(1)}, u32[]{:S(2)}, u32[]{:S(2)}) collective-permute-start(bf16[512,256]{1,0:T(8,128)(2,1)S(1)} %get-tuple-element.72), channel_id=1, source_target_pairs={{0,1},{1,0},{2,3},{3,2},{4,5},{5,4},{6,7},{7,6},{8,9},{9,8},{10,11... | collective-permute-start | bytes 786440 | tf_op jit(solution)/shard_map/ppermute | solution.py:23
  202.0 15.2 %collective-permute-start.36 = (bf16[512,256]{1,0:T(8,128)(2,1)S(1)}, bf16[512,256]{1,0:T(8,128)(2,1)S(1)}, u32[]{:S(2)}, u32[]{:S(2)}) collective-permute-start(bf16[512,256]{1,0:T(8,128)(2,1)S(1)} %get-tuple-element.73), channel_id=1, source_target_pairs={{0,2},{1,3},{2,0},{3,1},{4,6},{5,7},{6,4},{7,5},{8,10},{9,11},{10,... | collective-permute-start | bytes 786440 | tf_op jit(solution)/shard_map/ppermute | solution.py:23
  207.6 5.1 %collective-permute-start.31 = (bf16[128,512]{1,0:T(8,128)(2,1)S(1)}, bf16[128,512]{1,0:T(8,128)(2,1)S(1)}, u32[]{:S(2)}, u32[]{:S(2)}) collective-permute-start(bf16[128,512]{1,0:T(8,128)(2,1)S(1)} %get-tuple-element.64), channel_id=1, source_target_pairs={{0,2},{1,3},{2,0},{3,1},{4,6},{5,7},{6,4},{7,5},{8,10},{9,11},{10,... | collective-permute-start | bytes 393224 | tf_op jit(solution)/shard_map/ppermute | solution.py:23
  208.1 7.9 %collective-permute-start.32 = (bf16[128,512]{1,0:T(8,128)(2,1)S(1)}, bf16[128,512]{1,0:T(8,128)(2,1)S(1)}, u32[]{:S(2)}, u32[]{:S(2)}) collective-permute-start(bf16[128,512]{1,0:T(8,128)(2,1)S(1)} %get-tuple-element.66), channel_id=1, source_target_pairs={{0,1},{1,0},{2,3},{3,2},{4,5},{5,4},{6,7},{7,6},{8,9},{9,8},{10,11... | collective-permute-start | bytes 393224 | tf_op jit(solution)/shard_map/ppermute | solution.py:23
  208.8 13.8 %collective-permute-start.41 = (bf16[256,256]{1,0:T(8,128)(2,1)S(1)}, bf16[256,256]{1,0:T(8,128)(2,1)S(1)}, u32[]{:S(2)}, u32[]{:S(2)}) collective-permute-start(bf16[256,256]{1,0:T(8,128)(2,1)S(1)} %get-tuple-element.78), channel_id=1, source_target_pairs={{0,1},{1,0},{2,3},{3,2},{4,5},{5,4},{6,7},{7,6},{8,9},{9,8},{10,11... | collective-permute-start | bytes 393224 | tf_op jit(solution)/shard_map/ppermute | solution.py:23
  212.7 9.9 %collective-permute-start.42 = (bf16[256,256]{1,0:T(8,128)(2,1)S(1)}, bf16[256,256]{1,0:T(8,128)(2,1)S(1)}, u32[]{:S(2)}, u32[]{:S(2)}) collective-permute-start(bf16[256,256]{1,0:T(8,128)(2,1)S(1)} %get-tuple-element.79), channel_id=1, source_target_pairs={{0,2},{1,3},{2,0},{3,1},{4,6},{5,7},{6,4},{7,5},{8,10},{9,11},{10,... | collective-permute-start | bytes 393224 | tf_op jit(solution)/shard_map/ppermute | solution.py:23
  216.0 4.3 %collective-permute-start.39 = (bf16[128,256]{1,0:T(8,128)(2,1)S(1)}, bf16[128,256]{1,0:T(8,128)(2,1)S(1)}, u32[]{:S(2)}, u32[]{:S(2)}) collective-permute-start(bf16[128,256]{1,0:T(8,128)(2,1)S(1)} %get-tuple-element.76), channel_id=1, source_target_pairs={{0,1},{1,0},{2,3},{3,2},{4,5},{5,4},{6,7},{7,6},{8,9},{9,8},{10,11... | collective-permute-start | bytes 196616 | tf_op jit(solution)/shard_map/ppermute | solution.py:23
  216.6 6.0 %collective-permute-start.40 = (bf16[128,256]{1,0:T(8,128)(2,1)S(1)}, bf16[128,256]{1,0:T(8,128)(2,1)S(1)}, u32[]{:S(2)}, u32[]{:S(2)}) collective-permute-start(bf16[128,256]{1,0:T(8,128)(2,1)S(1)} %get-tuple-element.77), channel_id=1, source_target_pairs={{0,2},{1,3},{2,0},{3,1},{4,6},{5,7},{6,4},{7,5},{8,10},{9,11},{10,... | collective-permute-start | bytes 196616 | tf_op jit(solution)/shard_map/ppermute | solution.py:23
  217.2 6.4 %collective-permute-start.37 = (bf16[128,256]{1,0:T(8,128)(2,1)S(1)}, bf16[128,256]{1,0:T(8,128)(2,1)S(1)}, u32[]{:S(2)}, u32[]{:S(2)}) collective-permute-start(bf16[128,256]{1,0:T(8,128)(2,1)S(1)} %get-tuple-element.74), channel_id=1, source_target_pairs={{0,1},{1,0},{2,3},{3,2},{4,5},{5,4},{6,7},{7,6},{8,9},{9,8},{10,11... | collective-permute-start | bytes 196616 | tf_op jit(solution)/shard_map/ppermute | solution.py:23
  220.3 4.3 %collective-permute-start.38 = (bf16[128,256]{1,0:T(8,128)(2,1)S(1)}, bf16[128,256]{1,0:T(8,128)(2,1)S(1)}, u32[]{:S(2)}, u32[]{:S(2)}) collective-permute-start(bf16[128,256]{1,0:T(8,128)(2,1)S(1)} %get-tuple-element.75), channel_id=1, source_target_pairs={{0,2},{1,3},{2,0},{3,1},{4,6},{5,7},{6,4},{7,5},{8,10},{9,11},{10,... | collective-permute-start | bytes 196616 | tf_op jit(solution)/shard_map/ppermute | solution.py:23

commit v9 on v8

--- a/solution.py
+++ b/solution.py
@@ -148,7 +148,7 @@
     )(mine, *masks)
 
 
-SPLIT = 4
+SPLIT = 1
 
 
 def cut_body(mine, here, plan, src, *refs, first, blocks):
@@ -214,7 +214,7 @@
         term = outs[-1]
         outs = outs[:-1]
     units = [block_cols(base + u) for u in range(span // wide)]
-    tile = min(count, 256)
+    tile = min(count, 512)
     for step in range(count // tile):
         at = slice(top + step * tile, top + (step + 1) * tile)
         to = slice(step * tile, (step + 1) * tile)
@@ -301,8 +301,7 @@
 def row_parts(rows):
     if rows % 512 or lax.axis_size("pole") != 4:
         return [(0, rows)]
-    unit = rows // 4
-    return [(0, unit), (unit, 2 * unit), (3 * unit, unit)]
+    return [(0, rows // 2), (rows // 2, rows // 2)]
 
 
 def fold(scalars, own, factor, behind, before, tick, first, kind, base, sends=(), index=0, part=None):
@@ -510,7 +509,7 @@
 
 
 ARRIVE = (2, 2, 1, 1, 1, 1)
-LEAVE = (1, 2, 2, 2, 1)
+LEAVE = (1, 2, 2, 1, 1, 1)
 
 
 def body(local_green, coupling, block_mask, state_in, pole_weight, pole_index):

time: 227 us -> 236 us (1.040)
  Pallas kernels: 86.8 us -> 95.2 us
    pallas_call x13, Pallas kernels: 68.2 us -> 77 us  [fold(): pl.pallas_call(body, grid_spec=pltpu.PrefetchScalarGridSpec(num_scalar_pr...]
    ppermute x13 -> x14, waiting for transfers between devices: 81.2 us -> 84.5 us  [shift(): lax.ppermute(block, axis, [(i, i + step) for i in devices if i + step in...]
    ppermute x30 -> x27, waiting for transfers between devices: 17.4 us -> 15.2 us  [flip(): lax.ppermute(block, axis, [(i, i ^ bit) for i in range(lax.axis_size(axis...]
    ppermute x30 -> x27, starting transfers between devices: 18.1 us -> 16.8 us  [flip(): lax.ppermute(block, axis, [(i, i ^ bit) for i in range(lax.axis_size(axis...]
    ppermute x13 -> x14, starting transfers between devices: 20.7 us -> 21.8 us  [shift(): lax.ppermute(block, axis, [(i, i + step) for i in devices if i + step in...]
  transfers between devices with their start and end apart: 43 -> 41, of which waited for: 15 -> 15; matrix products, arithmetic and copies ran while one was open for 0% -> 0% of each run, Pallas kernels for 36% -> 39%
where the time goes in v9:
time: 236 us; the launch traced here: 235 us
  waiting for transfers between devices  99.8 us (42%)
  Pallas kernels  95.2 us (40%)
  starting transfers between devices  38.6 us (16%)
    ppermute x14, waiting for transfers between devices, shift(): lax.ppermute(block, axis, [(i, i + step) for i in devices if i + step in...  84.5 us
    pallas_call x13, Pallas kernels, fold(): pl.pallas_call(body, grid_spec=pltpu.PrefetchScalarGridSpec(num_scalar_pr...  77 us
    ppermute x14, starting transfers between devices, shift(): lax.ppermute(block, axis, [(i, i + step) for i in devices if i + step in...  21.8 us
    ppermute x27, starting transfers between devices, flip(): lax.ppermute(block, axis, [(i, i ^ bit) for i in range(lax.axis_size(axis...  16.8 us
    ppermute x27, waiting for transfers between devices, flip(): lax.ppermute(block, axis, [(i, i ^ bit) for i in range(lax.axis_size(axis...  15.2 us
    pallas_call x2, Pallas kernels, masked_factor(): pl.pallas_call(functools.partial(mask_body, tick=tick), grid_spec=pltpu.P...  6.17 us
    pallas_call x3, Pallas kernels, cut_pieces(): pl.pallas_call(functools.partial(cut_body, first=first, blocks=blocks), g...  4.74 us
  transfers between devices with their start and end apart: 41, of which 15 were waited for; matrix products, arithmetic and copies ran while one was open for 0% of the time, Pallas kernels for 39%

profile of v9, /device:TPU:0, one launch (start us, length us, event | category | flops | bytes accessed | tf_op | source)
XLA Modules:
  0.0 234.9 jit_solution(14681021929535738459)
XLA Ops:
  0.6 3.7 %shard_map.78.refs_5_.refs_6_ = bf16[2,512,1024]{2,1,0:T(8,128)(2,1)} custom-call(s32[2,1,4,8]{3,2,1,0:T(4,128)} %mask_ref.3, bf16[2,1,2,512,1024]{4,3,2,1,0:T(8,128)(2,1)} %coupling_ref.3), custom_call_target="tpu_custom_call" | custom-call | tf_op jit(solution)/shard_map/pallas_call | solution.py:63
  4.9 2.4 %shard_map.77.refs_5_.refs_6_ = bf16[2,512,1024]{2,1,0:T(8,128)(2,1)S(1)} custom-call(s32[2,1,4,8]{3,2,1,0:T(4,128)} %mask_ref.3, bf16[2,1,2,512,1024]{4,3,2,1,0:T(8,128)(2,1)} %coupling_ref.3), custom_call_target="tpu_custom_call" | custom-call | tf_op jit(solution)/shard_map/pallas_call | solution.py:63
  8.0 4.1 %collective-permute-done.refs_1_ = s32[2,1,4,8]{3,2,1,0:T(4,128)S(1)} collective-permute-done((s32[2,1,4,8]{3,2,1,0:T(4,128)}, s32[2,1,4,8]{3,2,1,0:T(4,128)S(1)}, u32[]{:S(2)}, u32[]{:S(2)}) %collective-permute-start) | collective-permute-done | bytes 288 | tf_op jit(solution)/shard_map/ppermute | solution.py:23
  12.1 1.7 plan.1.refs_4_
  13.8 4.8 %collective-permute-start.4 = (s32[16]{0:T(128)S(1)}, s32[16]{0:T(128)S(1)}, u32[]{:S(2)}, u32[]{:S(2)}) collective-permute-start(s32[16]{0:T(128)S(1)} %plan.1.refs_4_), channel_id=1, source_target_pairs={{0,8},{8,16},{16,24},{1,9},{9,17},{17,25},{2,10},{10,18},{18,26},{... | collective-permute-start | bytes 200 | tf_op jit(solution)/shard_map/ppermute | solution.py:19
  19.9 2.1 shard_map.79
  22.0 1.3 collective-permute-start.5
  24.4 1.3 collective-permute-start.15
  25.7 1.6 shard_map.80
  27.3 1.3 collective-permute-start.13
  28.6 4.5 %collective-permute-done.5.refs_8_ = bf16[2,512,128]{2,1,0:T(8,128)(2,1)S(1)} collective-permute-done((bf16[2,512,128]{2,1,0:T(8,128)(2,1)S(1)}, bf16[2,512,128]{2,1,0:T(8,128)(2,1)S(1)}, u32[]{:S(2)}, u32[]{:S(2)}) %collective-permute-start.5) | collective-permute-done | bytes 262176 | tf_op jit(solution)/shard_map/ppermute | solution.py:19
  34.4 25.1 %collective-permute-done.7.refs_8_ = bf16[2,512,128]{2,1,0:T(8,128)(2,1)S(1)} collective-permute-done((bf16[2,512,128]{2,1,0:T(8,128)(2,1)S(1)}, bf16[2,512,128]{2,1,0:T(8,128)(2,1)S(1)}, u32[]{:S(2)}, u32[]{:S(2)}) %collective-permute-start.7) | collective-permute-done | bytes 262176 | tf_op jit(solution)/shard_map/ppermute | solution.py:19
  61.3 6.6 %collective-permute-done.9.refs_8_ = bf16[2,512,128]{2,1,0:T(8,128)(2,1)S(1)} collective-permute-done((bf16[2,512,128]{2,1,0:T(8,128)(2,1)S(1)}, bf16[2,512,128]{2,1,0:T(8,128)(2,1)S(1)}, u32[]{:S(2)}, u32[]{:S(2)}) %collective-permute-start.9) | collective-permute-done | bytes 262176 | tf_op jit(solution)/shard_map/ppermute | solution.py:19
  68.0 1.5 collective-permute-start.11
  69.5 6.8 %collective-permute-done.11.refs_8_ = bf16[2,512,128]{2,1,0:T(8,128)(2,1)S(1)} collective-permute-done((bf16[2,512,128]{2,1,0:T(8,128)(2,1)S(1)}, bf16[2,512,128]{2,1,0:T(8,128)(2,1)S(1)}, u32[]{:S(2)}, u32[]{:S(2)}) %collective-permute-start.11) | collective-permute-done | bytes 262176 | tf_op jit(solution)/shard_map/ppermute | solution.py:19
  77.3 9.1 %shard_map.82.refs_10_ = f32[2,512,1024]{2,1,0:T(8,128)S(1)} custom-call(s32[1]{0:T(128)} %bitcast.mine.plan.refs_0_, s32[1,1,2]{2,1,0:T(1,128)S(1)} %bitcast.3, f32[2,16]{1,0:T(2,128)S(1)} %copy-done, s32[1]{0:T(128)} %bitcast.2.here.refs_3_, s32[16]{0:T(128)S(1)} %plan.1.refs_4_, bf16[2,512,1024]{2,1,0:T(8,128)(2,1)} %shard_map.78.refs_5_.refs_6_, ...), custom_call_target="tpu_custom_call" | custom-call | tf_op jit(solution)/shard_map/pallas_call | solution.py:323
  86.4 7.9 %shard_map.83.refs_10_ = f32[2,512,1024]{2,1,0:T(8,128)S(1)} custom-call(s32[1]{0:T(128)} %bitcast.mine.plan.refs_0_, s32[1,1,2]{2,1,0:T(1,128)S(1)} %bitcast.4, f32[2,16]{1,0:T(2,128)S(1)} %copy-done, s32[1]{0:T(128)} %bitcast.2.here.refs_3_, s32[16]{0:T(128)S(1)} %plan.1.refs_4_, ...), custom_call_target="tpu_custom_call", output_to_operand_aliasing={{}: (10, {})} | custom-call | tf_op jit(solution)/shard_map/pallas_call | solution.py:323
  94.4 5.8 %shard_map.84.refs_10_ = f32[2,512,1024]{2,1,0:T(8,128)S(1)} custom-call(s32[1]{0:T(128)} %bitcast.mine.plan.refs_0_, s32[1,1,2]{2,1,0:T(1,128)S(1)} %bitcast.5, f32[2,16]{1,0:T(2,128)S(1)} %copy-done, s32[1]{0:T(128)} %bitcast.2.here.refs_3_, s32[16]{0:T(128)S(1)} %plan.1.refs_4_, ...), custom_call_target="tpu_custom_call", output_to_operand_aliasing={{}: (10, {})} | custom-call | tf_op jit(solution)/shard_map/pallas_call | solution.py:323
  100.2 5.9 %shard_map.85 = (f32[2,512,1024]{2,1,0:T(8,128)S(1)}, bf16[2,512,128]{2,1,0:T(8,128)(2,1)S(1)}) custom-call(s32[1]{0:T(128)} %bitcast.mine.plan.refs_0_, s32[1,1,2]{2,1,0:T(1,128)S(1)} %bitcast.6, f32[2,16]{1,0:T(2,128)S(1)} %copy-done, s32[1]{0:T(128)} %bitcast.2.here.refs_3_, s32[16]{0:T(128)S(1)} %plan.1.refs_4_, ...), custom_call_target="tpu_custom_call", output_to_operand_aliasing={{0}: (10, {})} | custom-call | tf_op jit(solution)/shard_map/pallas_call | solution.py:323
  106.1 6.0 %shard_map.86 = (f32[2,512,1024]{2,1,0:T(8,128)S(1)}, bf16[2,512,256]{2,1,0:T(8,128)(2,1)S(1)}) custom-call(s32[1]{0:T(128)} %bitcast.mine.plan.refs_0_, s32[1,1,2]{2,1,0:T(1,128)S(1)} %bitcast.7, f32[2,16]{1,0:T(2,128)S(1)} %copy-done, s32[1]{0:T(128)} %bitcast.2.here.refs_3_, s32[16]{0:T(128)S(1)} %plan.1.refs_4_, ...), custom_call_target="tpu_custom_call", output_to_operand_aliasing={{0}: (10, {})} | custom-call | tf_op jit(solution)/shard_map/pallas_call | solution.py:323
  112.1 6.3 %shard_map.87 = (bf16[2,512,1024]{2,1,0:T(8,128)(2,1)S(1)}, bf16[2,512,256]{2,1,0:T(8,128)(2,1)S(1)}, bf16[2,512,128]{2,1,0:T(8,128)(2,1)S(1)}, bf16[2,512,128]{2,1,0:T(8,128)(2,1)S(1)}, bf16[2,512,128]{2,1,0:T(8,128)(2,1)S(1)}) custom-call(s32[1]{0:T(128)} %bitcast.mine.plan.refs_0_, s32[1,1,2]{2,1,0:T(1,128)S(1)} %bitcast.8, f32[2,16]{1,0:T(2,128)S(1)} %copy-done, ...), custom_call_target="tpu_custom_call" | custom-call | tf_op jit(solution)/shard_map/pallas_call | solution.py:323
  118.4 1.3 collective-permute-start.23
  119.7 1.3 collective-permute-start.25
  121.0 1.3 collective-permute-start.17
  122.3 1.3 collective-permute-start.1
  123.6 27.5 %collective-permute-done.1.refs_4_ = s32[16]{0:T(128)S(1)} collective-permute-done((s32[16]{0:T(128)S(1)}, s32[16]{0:T(128)S(1)}, u32[]{:S(2)}, u32[]{:S(2)}) %collective-permute-start.1) | collective-permute-done | bytes 96 | tf_op jit(solution)/shard_map/ppermute | solution.py:19
  155.6 6.6 %collective-permute-done.27.refs_8_ = bf16[2,512,128]{2,1,0:T(8,128)(2,1)S(1)} collective-permute-done((bf16[2,512,128]{2,1,0:T(8,128)(2,1)S(1)}, bf16[2,512,128]{2,1,0:T(8,128)(2,1)S(1)}, u32[]{:S(2)}, u32[]{:S(2)}) %collective-permute-start.27) | collective-permute-done | bytes 262176 | tf_op jit(solution)/shard_map/ppermute | solution.py:19
  162.2 1.8 shard_map.95
  164.0 3.8 %collective-permute-done.19.refs_8_ = bf16[2,512,128]{2,1,0:T(8,128)(2,1)S(1)} collective-permute-done((bf16[2,512,128]{2,1,0:T(8,128)(2,1)S(1)}, bf16[2,512,128]{2,1,0:T(8,128)(2,1)S(1)}, u32[]{:S(2)}, u32[]{:S(2)}) %collective-permute-start.19) | collective-permute-done | bytes 262176 | tf_op jit(solution)/shard_map/ppermute | solution.py:19
  167.8 1.5 collective-permute-start.33
  169.3 2.2 collective-permute-done.21.refs_8_
  171.6 1.5 collective-permute-start.34
  173.7 6.1 %shard_map.88.refs_10_ = f32[2,512,1024]{2,1,0:T(8,128)S(1)} custom-call(s32[1]{0:T(128)} %bitcast.mine.plan.refs_0_, s32[1,1,2]{2,1,0:T(1,128)S(1)} %bitcast.10, f32[2,16]{1,0:T(2,128)S(1)} %copy-done, s32[1]{0:T(128)} %bitcast.2.here.refs_3_, s32[16]{0:T(128)S(1)} %collective-permute-done.1.refs_4_, bf16[2,512,1024]{2,1,0:T(8,128)(2,1)S(1)} %shard_map.77.refs_5_.refs_6_, ...), custom_call_target="tpu_custom_call" | custom-call | tf_op jit(solution)/shard_map/pallas_call | solution.py:323
  179.8 6.7 %shard_map.89.refs_10_ = f32[2,512,1024]{2,1,0:T(8,128)S(1)} custom-call(s32[1]{0:T(128)} %bitcast.mine.plan.refs_0_, s32[1,1,2]{2,1,0:T(1,128)S(1)} %bitcast.11, f32[2,16]{1,0:T(2,128)S(1)} %copy-done, s32[1]{0:T(128)} %bitcast.2.here.refs_3_, s32[16]{0:T(128)S(1)} %collective-permute-done.1.refs_4_, ...), custom_call_target="tpu_custom_call", output_to_operand_aliasing={{}: (10, {})} | custom-call | tf_op jit(solution)/shard_map/pallas_call | solution.py:323
  186.5 6.7 %shard_map.90.refs_10_ = f32[2,512,1024]{2,1,0:T(8,128)S(1)} custom-call(s32[1]{0:T(128)} %bitcast.mine.plan.refs_0_, s32[1,1,2]{2,1,0:T(1,128)S(1)} %bitcast.12, f32[2,16]{1,0:T(2,128)S(1)} %copy-done, s32[1]{0:T(128)} %bitcast.2.here.refs_3_, s32[16]{0:T(128)S(1)} %collective-permute-done.1.refs_4_, ...), custom_call_target="tpu_custom_call", output_to_operand_aliasing={{}: (10, {})} | custom-call | tf_op jit(solution)/shard_map/pallas_call | solution.py:323
  193.1 4.5 %shard_map.91.refs_10_ = f32[2,512,1024]{2,1,0:T(8,128)S(1)} custom-call(s32[1]{0:T(128)} %bitcast.mine.plan.refs_0_, s32[1,1,2]{2,1,0:T(1,128)S(1)} %bitcast.13, f32[2,16]{1,0:T(2,128)S(1)} %copy-done, s32[1]{0:T(128)} %bitcast.2.here.refs_3_, s32[16]{0:T(128)S(1)} %collective-permute-done.1.refs_4_, ...), custom_call_target="tpu_custom_call", output_to_operand_aliasing={{}: (10, {})} | custom-call | tf_op jit(solution)/shard_map/pallas_call | solution.py:323
  197.7 4.8 %shard_map.92.refs_10_ = f32[2,512,1024]{2,1,0:T(8,128)S(1)} custom-call(s32[1]{0:T(128)} %bitcast.mine.plan.refs_0_, s32[1,1,2]{2,1,0:T(1,128)S(1)} %bitcast.14, f32[2,16]{1,0:T(2,128)S(1)} %copy-done, s32[1]{0:T(128)} %bitcast.2.here.refs_3_, s32[16]{0:T(128)S(1)} %collective-permute-done.1.refs_4_, ...), custom_call_target="tpu_custom_call", output_to_operand_aliasing={{}: (10, {})} | custom-call | tf_op jit(solution)/shard_map/pallas_call | solution.py:323
  202.5 3.6 %shard_map.94 = (bf16[2,256,1024]{2,1,0:T(8,128)(2,1)S(1)}, bf16[256,512]{1,0:T(8,128)(2,1)S(1)}, bf16[256,512]{1,0:T(8,128)(2,1)S(1)}, bf16[256,512]{1,0:T(8,128)(2,1)S(1)}, bf16[256,512]{1,0:T(8,128)(2,1)S(1)}) custom-call(s32[1]{0:T(128)} %bitcast.mine.plan.refs_0_, s32[1,1,2]{2,1,0:T(1,128)S(1)} %bitcast.15, f32[2,16]{1,0:T(2,128)S(1)} %copy-done, ...), custom_call_target="tpu_custom_call" | custom-call | tf_op jit(solution)/shard_map/pallas_call | solution.py:323
  206.1 1.6 collective-permute-start.31
  208.2 3.6 %shard_map.93 = (bf16[2,256,1024]{2,1,0:T(8,128)(2,1)S(1)}, bf16[256,512]{1,0:T(8,128)(2,1)S(1)}, bf16[256,512]{1,0:T(8,128)(2,1)S(1)}, bf16[256,512]{1,0:T(8,128)(2,1)S(1)}, bf16[256,512]{1,0:T(8,128)(2,1)S(1)}) custom-call(s32[1]{0:T(128)} %bitcast.mine.plan.refs_0_, s32[1,1,2]{2,1,0:T(1,128)S(1)} %bitcast.16, f32[2,16]{1,0:T(2,128)S(1)} %copy-done, ...), custom_call_target="tpu_custom_call" | custom-call | tf_op jit(solution)/shard_map/pallas_call | solution.py:323
  212.4 1.5 collective-permute-start.30
  215.3 1.6 collective-permute-start.36
  217.8 3.2 %collective-permute-done.29.refs_1_.real_got = bf16[256,512]{1,0:T(8,128)(2,1)S(1)} collective-permute-done((bf16[256,512]{1,0:T(8,128)(2,1)S(1)}, bf16[256,512]{1,0:T(8,128)(2,1)S(1)}, u32[]{:S(2)}, u32[]{:S(2)}) %collective-permute-start.29) | collective-permute-done | bytes 262176 | tf_op jit(solution)/shard_map/ppermute | solution.py:23
  221.1 1.4 collective-permute-done.30.refs_3_.imag_got
  223.2 1.5 collective-permute-start.40
  224.7 3.4 %collective-permute-done.35.refs_0_ = bf16[512,256]{1,0:T(8,128)(2,1)S(1)} collective-permute-done((bf16[512,256]{1,0:T(8,128)(2,1)S(1)}, bf16[512,256]{1,0:T(8,128)(2,1)S(1)}, u32[]{:S(2)}, u32[]{:S(2)}) %collective-permute-start.35) | collective-permute-done | bytes 262176 | tf_op jit(solution)/shard_map/ppermute | solution.py:23
  229.0 1.3 emit.1
  230.5 2.4 %collective-permute-done.39.refs_0_ = bf16[256,256]{1,0:T(8,128)(2,1)S(1)} collective-permute-done((bf16[256,256]{1,0:T(8,128)(2,1)S(1)}, bf16[256,256]{1,0:T(8,128)(2,1)S(1)}, u32[]{:S(2)}, u32[]{:S(2)}) %collective-permute-start.39) | collective-permute-done | bytes 131104 | tf_op jit(solution)/shard_map/ppermute | solution.py:23
  (67 shorter events, 19.6 us)
Async XLA Ops:
  4.4 72.5 %collective-permute-start.3 = (bf16[2,512,1024]{2,1,0:T(8,128)(2,1)}, bf16[2,512,1024]{2,1,0:T(8,128)(2,1)}, u32[]{:S(2)}, u32[]{:S(2)}) collective-permute-start(bf16[2,512,1024]{2,1,0:T(8,128)(2,1)} %shard_map.78.refs_5_.refs_6_), channel_id=1, source_target_pairs={{0,4},{4,0},{1,5},{5,1},{2,6},{6,2},{3,7},{7,3},{8,12},{12,8},{9,1... | collective-permute-start | bytes 6291464 | tf_op jit(solution)/shard_map/ppermute | solution.py:23
  7.4 69.9 %copy-start = (f32[2,16]{1,0:T(2,128)S(1)}, f32[2,16]{1,0:T(2,128)}, u32[]{:S(2)}) copy-start(f32[2,16]{1,0:T(2,128)} %pw.1) | copy-start | bytes 388
  7.4 69.9 %copy-start.1 = (s32[2,1,1]{0,2,1:T(1,128)S(1)}, s32[2,1,1]{0,2,1:T(1,128)}, u32[]{:S(2)}) copy-start(s32[2,1,1]{0,2,1:T(1,128)} %param.11) | copy-start | bytes 28
  7.4 145.6 %collective-permute-start.2 = (bf16[2,512,1024]{2,1,0:T(8,128)(2,1)S(1)}, bf16[2,512,1024]{2,1,0:T(8,128)(2,1)}, u32[]{:S(2)}, u32[]{:S(2)}) collective-permute-start(bf16[2,512,1024]{2,1,0:T(8,128)(2,1)S(1)} %shard_map.77.refs_5_.refs_6_), channel_id=1, source_target_pairs={{0,4},{4,0},{1,5},{5,1},{2,6},{6,2},{3,7},{7,3},{8,12},{12,8},{9,1... | collective-permute-start | bytes 6291464 | tf_op jit(solution)/shard_map/ppermute | solution.py:23
  7.5 4.6 %collective-permute-start = (s32[2,1,4,8]{3,2,1,0:T(4,128)}, s32[2,1,4,8]{3,2,1,0:T(4,128)S(1)}, u32[]{:S(2)}, u32[]{:S(2)}) collective-permute-start(s32[2,1,4,8]{3,2,1,0:T(4,128)} %mask_ref.3), channel_id=1, source_target_pairs={{0,4},{4,0},{1,5},{5,1},{2,6},{6,2},{3,7},{7,3},{8,12},{12,8},{9,1... | collective-permute-start | bytes 776 | tf_op jit(solution)/shard_map/ppermute | solution.py:23
  13.8 6.1 %collective-permute-start.4 = (s32[16]{0:T(128)S(1)}, s32[16]{0:T(128)S(1)}, u32[]{:S(2)}, u32[]{:S(2)}) collective-permute-start(s32[16]{0:T(128)S(1)} %plan.1.refs_4_), channel_id=1, source_target_pairs={{0,8},{8,16},{16,24},{1,9},{9,17},{17,25},{2,10},{10,18},{18,26},{... | collective-permute-start | bytes 200 | tf_op jit(solution)/shard_map/ppermute | solution.py:19
  22.0 11.1 %collective-permute-start.5 = (bf16[2,512,128]{2,1,0:T(8,128)(2,1)S(1)}, bf16[2,512,128]{2,1,0:T(8,128)(2,1)S(1)}, u32[]{:S(2)}, u32[]{:S(2)}) collective-permute-start(bf16[2,512,128]{2,1,0:T(8,128)(2,1)S(1)} %get-tuple-element.35), channel_id=1, source_target_pairs={{8,0},{16,8},{24,16},{9,1},{17,9},{25,17},{10,2},{18,10},{26,18},{... | collective-permute-start | bytes 786440 | tf_op jit(solution)/shard_map/ppermute | solution.py:19
  24.4 36.4 %collective-permute-start.15 = (bf16[2,512,256]{2,1,0:T(8,128)(2,1)S(1)}, bf16[2,512,256]{2,1,0:T(8,128)(2,1)S(1)}, u32[]{:S(2)}, u32[]{:S(2)}) collective-permute-start(bf16[2,512,256]{2,1,0:T(8,128)(2,1)S(1)} %shard_map.81), channel_id=1, source_target_pairs={{8,0},{16,8},{24,16},{9,1},{17,9},{25,17},{10,2},{18,10},{26,18},{... | collective-permute-start | bytes 1572872 | tf_op jit(solution)/shard_map/ppermute | solution.py:19
  27.3 33.6 %collective-permute-start.13 = (bf16[2,512,256]{2,1,0:T(8,128)(2,1)S(1)}, bf16[2,512,256]{2,1,0:T(8,128)(2,1)S(1)}, u32[]{:S(2)}, u32[]{:S(2)}) collective-permute-start(bf16[2,512,256]{2,1,0:T(8,128)(2,1)S(1)} %shard_map.80), channel_id=1, source_target_pairs={{8,0},{16,8},{24,16},{9,1},{17,9},{25,17},{10,2},{18,10},{26,18},{... | collective-permute-start | bytes 1572872 | tf_op jit(solution)/shard_map/ppermute | solution.py:19
  33.1 26.4 %collective-permute-start.7 = (bf16[2,512,128]{2,1,0:T(8,128)(2,1)S(1)}, bf16[2,512,128]{2,1,0:T(8,128)(2,1)S(1)}, u32[]{:S(2)}, u32[]{:S(2)}) collective-permute-start(bf16[2,512,128]{2,1,0:T(8,128)(2,1)S(1)} %get-tuple-element.36), channel_id=1, source_target_pairs={{8,0},{16,8},{24,16},{9,1},{17,9},{25,17},{10,2},{18,10},{26,18},{... | collective-permute-start | bytes 786440 | tf_op jit(solution)/shard_map/ppermute | solution.py:19
  59.5 8.5 %collective-permute-start.9 = (bf16[2,512,128]{2,1,0:T(8,128)(2,1)S(1)}, bf16[2,512,128]{2,1,0:T(8,128)(2,1)S(1)}, u32[]{:S(2)}, u32[]{:S(2)}) collective-permute-start(bf16[2,512,128]{2,1,0:T(8,128)(2,1)S(1)} %get-tuple-element.37), channel_id=1, source_target_pairs={{8,0},{16,8},{24,16},{9,1},{17,9},{25,17},{10,2},{18,10},{26,18},{... | collective-permute-start | bytes 786440 | tf_op jit(solution)/shard_map/ppermute | solution.py:19
  60.8 15.5 %collective-permute-start.16 = (bf16[2,512,256]{2,1,0:T(8,128)(2,1)S(1)}, bf16[2,512,256]{2,1,0:T(8,128)(2,1)S(1)}, u32[]{:S(2)}, u32[]{:S(2)}) collective-permute-start(bf16[2,512,256]{2,1,0:T(8,128)(2,1)S(1)} %collective-permute-done.15.refs_8_), channel_id=1, source_target_pairs={{0,4},{4,0},{1,5},{5,1},{2,6},{6,2},{3,7},{7,3},{8,12},{12,8},{9,1... | collective-permute-start | bytes 1572872 | tf_op jit(solution)/shard_map/ppermute | solution.py:23
  60.9 15.9 %collective-permute-start.14 = (bf16[2,512,256]{2,1,0:T(8,128)(2,1)S(1)}, bf16[2,512,256]{2,1,0:T(8,128)(2,1)S(1)}, u32[]{:S(2)}, u32[]{:S(2)}) collective-permute-start(bf16[2,512,256]{2,1,0:T(8,128)(2,1)S(1)} %collective-permute-done.13.refs_8_), channel_id=1, source_target_pairs={{0,4},{4,0},{1,5},{5,1},{2,6},{6,2},{3,7},{7,3},{8,12},{12,8},{9,1... | collective-permute-start | bytes 1572872 | tf_op jit(solution)/shard_map/ppermute | solution.py:23
  68.0 8.3 %collective-permute-start.11 = (bf16[2,512,128]{2,1,0:T(8,128)(2,1)S(1)}, bf16[2,512,128]{2,1,0:T(8,128)(2,1)S(1)}, u32[]{:S(2)}, u32[]{:S(2)}) collective-permute-start(bf16[2,512,128]{2,1,0:T(8,128)(2,1)S(1)} %get-tuple-element.38), channel_id=1, source_target_pairs={{8,0},{16,8},{24,16},{9,1},{17,9},{25,17},{10,2},{18,10},{26,18},{... | collective-permute-start | bytes 786440 | tf_op jit(solution)/shard_map/ppermute | solution.py:19
  76.2 18.1 %collective-permute-start.12 = (bf16[2,512,128]{2,1,0:T(8,128)(2,1)S(1)}, bf16[2,512,128]{2,1,0:T(8,128)(2,1)S(1)}, u32[]{:S(2)}, u32[]{:S(2)}) collective-permute-start(bf16[2,512,128]{2,1,0:T(8,128)(2,1)S(1)} %collective-permute-done.11.refs_8_), channel_id=1, source_target_pairs={{0,4},{4,0},{1,5},{5,1},{2,6},{6,2},{3,7},{7,3},{8,12},{12,8},{9,1... | collective-permute-start | bytes 786440 | tf_op jit(solution)/shard_map/ppermute | solution.py:23
  76.2 24.0 %collective-permute-start.10 = (bf16[2,512,128]{2,1,0:T(8,128)(2,1)S(1)}, bf16[2,512,128]{2,1,0:T(8,128)(2,1)S(1)}, u32[]{:S(2)}, u32[]{:S(2)}) collective-permute-start(bf16[2,512,128]{2,1,0:T(8,128)(2,1)S(1)} %collective-permute-done.9.refs_8_), channel_id=1, source_target_pairs={{0,4},{4,0},{1,5},{5,1},{2,6},{6,2},{3,7},{7,3},{8,12},{12,8},{9,1... | collective-permute-start | bytes 786440 | tf_op jit(solution)/shard_map/ppermute | solution.py:23
  76.8 29.3 %collective-permute-start.8 = (bf16[2,512,128]{2,1,0:T(8,128)(2,1)S(1)}, bf16[2,512,128]{2,1,0:T(8,128)(2,1)S(1)}, u32[]{:S(2)}, u32[]{:S(2)}) collective-permute-start(bf16[2,512,128]{2,1,0:T(8,128)(2,1)S(1)} %collective-permute-done.7.refs_8_), channel_id=1, source_target_pairs={{0,4},{4,0},{1,5},{5,1},{2,6},{6,2},{3,7},{7,3},{8,12},{12,8},{9,1... | collective-permute-start | bytes 786440 | tf_op jit(solution)/shard_map/ppermute | solution.py:23
  76.8 35.2 %collective-permute-start.6 = (bf16[2,512,128]{2,1,0:T(8,128)(2,1)S(1)}, bf16[2,512,128]{2,1,0:T(8,128)(2,1)S(1)}, u32[]{:S(2)}, u32[]{:S(2)}) collective-permute-start(bf16[2,512,128]{2,1,0:T(8,128)(2,1)S(1)} %collective-permute-done.5.refs_8_), channel_id=1, source_target_pairs={{0,4},{4,0},{1,5},{5,1},{2,6},{6,2},{3,7},{7,3},{8,12},{12,8},{9,1... | collective-permute-start | bytes 786440 | tf_op jit(solution)/shard_map/ppermute | solution.py:23
  118.4 34.0 %collective-permute-start.23 = (bf16[2,512,256]{2,1,0:T(8,128)(2,1)S(1)}, bf16[2,512,256]{2,1,0:T(8,128)(2,1)S(1)}, u32[]{:S(2)}, u32[]{:S(2)}) collective-permute-start(bf16[2,512,256]{2,1,0:T(8,128)(2,1)S(1)} %get-tuple-element.44), channel_id=1, source_target_pairs={{8,0},{16,8},{24,16},{9,1},{17,9},{25,17},{10,2},{18,10},{26,18},{... | collective-permute-start | bytes 1572872 | tf_op jit(solution)/shard_map/ppermute | solution.py:19
  119.7 32.8 %collective-permute-start.25 = (bf16[2,512,256]{2,1,0:T(8,128)(2,1)S(1)}, bf16[2,512,256]{2,1,0:T(8,128)(2,1)S(1)}, u32[]{:S(2)}, u32[]{:S(2)}) collective-permute-start(bf16[2,512,256]{2,1,0:T(8,128)(2,1)S(1)} %get-tuple-element.45), channel_id=1, source_target_pairs={{8,0},{16,8},{24,16},{9,1},{17,9},{25,17},{10,2},{18,10},{26,18},{... | collective-permute-start | bytes 1572872 | tf_op jit(solution)/shard_map/ppermute | solution.py:19
  121.0 33.3 %collective-permute-start.17 = (bf16[2,512,128]{2,1,0:T(8,128)(2,1)S(1)}, bf16[2,512,128]{2,1,0:T(8,128)(2,1)S(1)}, u32[]{:S(2)}, u32[]{:S(2)}) collective-permute-start(bf16[2,512,128]{2,1,0:T(8,128)(2,1)S(1)} %get-tuple-element.41), channel_id=1, source_target_pairs={{8,0},{16,8},{24,16},{9,1},{17,9},{25,17},{10,2},{18,10},{26,18},{... | collective-permute-start | bytes 786440 | tf_op jit(solution)/shard_map/ppermute | solution.py:19
  122.3 28.8 %collective-permute-start.1 = (s32[16]{0:T(128)S(1)}, s32[16]{0:T(128)S(1)}, u32[]{:S(2)}, u32[]{:S(2)}) collective-permute-start(s32[16]{0:T(128)S(1)} %plan.1.refs_4_), channel_id=1, source_target_pairs={{8,0},{16,8},{24,16},{9,1},{17,9},{25,17},{10,2},{18,10},{26,18},{... | collective-permute-start | bytes 200 | tf_op jit(solution)/shard_map/ppermute | solution.py:19
  151.1 11.1 %collective-permute-start.27 = (bf16[2,512,128]{2,1,0:T(8,128)(2,1)S(1)}, bf16[2,512,128]{2,1,0:T(8,128)(2,1)S(1)}, u32[]{:S(2)}, u32[]{:S(2)}) collective-permute-start(bf16[2,512,128]{2,1,0:T(8,128)(2,1)S(1)} %get-tuple-element.46), channel_id=1, source_target_pairs={{8,0},{16,8},{24,16},{9,1},{17,9},{25,17},{10,2},{18,10},{26,18},{... | collective-permute-start | bytes 786440 | tf_op jit(solution)/shard_map/ppermute | solution.py:19
  152.4 20.7 %collective-permute-start.24 = (bf16[2,512,256]{2,1,0:T(8,128)(2,1)S(1)}, bf16[2,512,256]{2,1,0:T(8,128)(2,1)S(1)}, u32[]{:S(2)}, u32[]{:S(2)}) collective-permute-start(bf16[2,512,256]{2,1,0:T(8,128)(2,1)S(1)} %collective-permute-done.23.refs_8_), channel_id=1, source_target_pairs={{0,4},{4,0},{1,5},{5,1},{2,6},{6,2},{3,7},{7,3},{8,12},{12,8},{9,1... | collective-permute-start | bytes 1572872 | tf_op jit(solution)/shard_map/ppermute | solution.py:23
  152.5 21.1 %collective-permute-start.26 = (bf16[2,512,256]{2,1,0:T(8,128)(2,1)S(1)}, bf16[2,512,256]{2,1,0:T(8,128)(2,1)S(1)}, u32[]{:S(2)}, u32[]{:S(2)}) collective-permute-start(bf16[2,512,256]{2,1,0:T(8,128)(2,1)S(1)} %collective-permute-done.25.refs_8_), channel_id=1, source_target_pairs={{0,4},{4,0},{1,5},{5,1},{2,6},{6,2},{3,7},{7,3},{8,12},{12,8},{9,1... | collective-permute-start | bytes 1572872 | tf_op jit(solution)/shard_map/ppermute | solution.py:23
  153.0 14.8 %collective-permute-start.19 = (bf16[2,512,128]{2,1,0:T(8,128)(2,1)S(1)}, bf16[2,512,128]{2,1,0:T(8,128)(2,1)S(1)}, u32[]{:S(2)}, u32[]{:S(2)}) collective-permute-start(bf16[2,512,128]{2,1,0:T(8,128)(2,1)S(1)} %get-tuple-element.42), channel_id=1, source_target_pairs={{8,0},{16,8},{24,16},{9,1},{17,9},{25,17},{10,2},{18,10},{26,18},{... | collective-permute-start | bytes 786440 | tf_op jit(solution)/shard_map/ppermute | solution.py:19
  154.3 17.3 %collective-permute-start.21 = (bf16[2,512,128]{2,1,0:T(8,128)(2,1)S(1)}, bf16[2,512,128]{2,1,0:T(8,128)(2,1)S(1)}, u32[]{:S(2)}, u32[]{:S(2)}) collective-permute-start(bf16[2,512,128]{2,1,0:T(8,128)(2,1)S(1)} %get-tuple-element.43), channel_id=1, source_target_pairs={{8,0},{16,8},{24,16},{9,1},{17,9},{25,17},{10,2},{18,10},{26,18},{... | collective-permute-start | bytes 786440 | tf_op jit(solution)/shard_map/ppermute | solution.py:19
  162.2 10.9 %collective-permute-start.28 = (bf16[2,512,128]{2,1,0:T(8,128)(2,1)S(1)}, bf16[2,512,128]{2,1,0:T(8,128)(2,1)S(1)}, u32[]{:S(2)}, u32[]{:S(2)}) collective-permute-start(bf16[2,512,128]{2,1,0:T(8,128)(2,1)S(1)} %collective-permute-done.27.refs_8_), channel_id=1, source_target_pairs={{0,4},{4,0},{1,5},{5,1},{2,6},{6,2},{3,7},{7,3},{8,12},{12,8},{9,1... | collective-permute-start | bytes 786440 | tf_op jit(solution)/shard_map/ppermute | solution.py:23
  167.8 44.6 %collective-permute-start.33 = (bf16[512,512]{1,0:T(8,128)(2,1)S(1)}, bf16[512,512]{1,0:T(8,128)(2,1)S(1)}, u32[]{:S(2)}, u32[]{:S(2)}) collective-permute-start(bf16[512,512]{1,0:T(8,128)(2,1)S(1)} %get-tuple-element.59), channel_id=1, source_target_pairs={{0,2},{1,3},{2,0},{3,1},{4,6},{5,7},{6,4},{7,5},{8,10},{9,11},{10,... | collective-permute-start | bytes 1572872 | tf_op jit(solution)/shard_map/ppermute | solution.py:23
  171.6 42.3 %collective-permute-start.34 = (bf16[512,512]{1,0:T(8,128)(2,1)S(1)}, bf16[512,512]{1,0:T(8,128)(2,1)S(1)}, u32[]{:S(2)}, u32[]{:S(2)}) collective-permute-start(bf16[512,512]{1,0:T(8,128)(2,1)S(1)} %get-tuple-element.61), channel_id=1, source_target_pairs={{0,1},{1,0},{2,3},{3,2},{4,5},{5,4},{6,7},{7,6},{8,9},{9,8},{10,11... | collective-permute-start | bytes 1572872 | tf_op jit(solution)/shard_map/ppermute | solution.py:23
  173.1 20.1 %collective-permute-start.22 = (bf16[2,512,128]{2,1,0:T(8,128)(2,1)S(1)}, bf16[2,512,128]{2,1,0:T(8,128)(2,1)S(1)}, u32[]{:S(2)}, u32[]{:S(2)}) collective-permute-start(bf16[2,512,128]{2,1,0:T(8,128)(2,1)S(1)} %collective-permute-done.21.refs_8_), channel_id=1, source_target_pairs={{0,4},{4,0},{1,5},{5,1},{2,6},{6,2},{3,7},{7,3},{8,12},{12,8},{9,1... | collective-permute-start | bytes 786440 | tf_op jit(solution)/shard_map/ppermute | solution.py:23
  173.1 24.6 %collective-permute-start.20 = (bf16[2,512,128]{2,1,0:T(8,128)(2,1)S(1)}, bf16[2,512,128]{2,1,0:T(8,128)(2,1)S(1)}, u32[]{:S(2)}, u32[]{:S(2)}) collective-permute-start(bf16[2,512,128]{2,1,0:T(8,128)(2,1)S(1)} %collective-permute-done.19.refs_8_), channel_id=1, source_target_pairs={{0,4},{4,0},{1,5},{5,1},{2,6},{6,2},{3,7},{7,3},{8,12},{12,8},{9,1... | collective-permute-start | bytes 786440 | tf_op jit(solution)/shard_map/ppermute | solution.py:23
  173.6 28.9 %collective-permute-start.18 = (bf16[2,512,128]{2,1,0:T(8,128)(2,1)S(1)}, bf16[2,512,128]{2,1,0:T(8,128)(2,1)S(1)}, u32[]{:S(2)}, u32[]{:S(2)}) collective-permute-start(bf16[2,512,128]{2,1,0:T(8,128)(2,1)S(1)} %collective-permute-done.17.refs_8_), channel_id=1, source_target_pairs={{0,4},{4,0},{1,5},{5,1},{2,6},{6,2},{3,7},{7,3},{8,12},{12,8},{9,1... | collective-permute-start | bytes 786440 | tf_op jit(solution)/shard_map/ppermute | solution.py:23
  206.1 9.2 %collective-permute-start.31 = (bf16[256,512]{1,0:T(8,128)(2,1)S(1)}, bf16[256,512]{1,0:T(8,128)(2,1)S(1)}, u32[]{:S(2)}, u32[]{:S(2)}) collective-permute-start(bf16[256,512]{1,0:T(8,128)(2,1)S(1)} %get-tuple-element.54), channel_id=1, source_target_pairs={{0,2},{1,3},{2,0},{3,1},{4,6},{5,7},{6,4},{7,5},{8,10},{9,11},{10,... | collective-permute-start | bytes 786440 | tf_op jit(solution)/shard_map/ppermute | solution.py:23
  207.7 9.2 %collective-permute-start.32 = (bf16[256,512]{1,0:T(8,128)(2,1)S(1)}, bf16[256,512]{1,0:T(8,128)(2,1)S(1)}, u32[]{:S(2)}, u32[]{:S(2)}) collective-permute-start(bf16[256,512]{1,0:T(8,128)(2,1)S(1)} %get-tuple-element.56), channel_id=1, source_target_pairs={{0,1},{1,0},{2,3},{3,2},{4,5},{5,4},{6,7},{7,6},{8,9},{9,8},{10,11... | collective-permute-start | bytes 786440 | tf_op jit(solution)/shard_map/ppermute | solution.py:23
  211.8 9.2 %collective-permute-start.29 = (bf16[256,512]{1,0:T(8,128)(2,1)S(1)}, bf16[256,512]{1,0:T(8,128)(2,1)S(1)}, u32[]{:S(2)}, u32[]{:S(2)}) collective-permute-start(bf16[256,512]{1,0:T(8,128)(2,1)S(1)} %get-tuple-element.50), channel_id=1, source_target_pairs={{0,2},{1,3},{2,0},{3,1},{4,6},{5,7},{6,4},{7,5},{8,10},{9,11},{10,... | collective-permute-start | bytes 786440 | tf_op jit(solution)/shard_map/ppermute | solution.py:23
  212.4 10.1 %collective-permute-start.30 = (bf16[256,512]{1,0:T(8,128)(2,1)S(1)}, bf16[256,512]{1,0:T(8,128)(2,1)S(1)}, u32[]{:S(2)}, u32[]{:S(2)}) collective-permute-start(bf16[256,512]{1,0:T(8,128)(2,1)S(1)} %get-tuple-element.52), channel_id=1, source_target_pairs={{0,1},{1,0},{2,3},{3,2},{4,5},{5,4},{6,7},{7,6},{8,9},{9,8},{10,11... | collective-permute-start | bytes 786440 | tf_op jit(solution)/shard_map/ppermute | solution.py:23
  214.0 14.1 %collective-permute-start.35 = (bf16[512,256]{1,0:T(8,128)(2,1)S(1)}, bf16[512,256]{1,0:T(8,128)(2,1)S(1)}, u32[]{:S(2)}, u32[]{:S(2)}) collective-permute-start(bf16[512,256]{1,0:T(8,128)(2,1)S(1)} %get-tuple-element.62), channel_id=1, source_target_pairs={{0,1},{1,0},{2,3},{3,2},{4,5},{5,4},{6,7},{7,6},{8,9},{9,8},{10,11... | collective-permute-start | bytes 786440 | tf_op jit(solution)/shard_map/ppermute | solution.py:23
  215.3 13.6 %collective-permute-start.36 = (bf16[512,256]{1,0:T(8,128)(2,1)S(1)}, bf16[512,256]{1,0:T(8,128)(2,1)S(1)}, u32[]{:S(2)}, u32[]{:S(2)}) collective-permute-start(bf16[512,256]{1,0:T(8,128)(2,1)S(1)} %get-tuple-element.63), channel_id=1, source_target_pairs={{0,2},{1,3},{2,0},{3,1},{4,6},{5,7},{6,4},{7,5},{8,10},{9,11},{10,... | collective-permute-start | bytes 786440 | tf_op jit(solution)/shard_map/ppermute | solution.py:23
  217.0 16.8 %collective-permute-start.37 = (bf16[256,256]{1,0:T(8,128)(2,1)S(1)}, bf16[256,256]{1,0:T(8,128)(2,1)S(1)}, u32[]{:S(2)}, u32[]{:S(2)}) collective-permute-start(bf16[256,256]{1,0:T(8,128)(2,1)S(1)} %get-tuple-element.64), channel_id=1, source_target_pairs={{0,1},{1,0},{2,3},{3,2},{4,5},{5,4},{6,7},{7,6},{8,9},{9,8},{10,11... | collective-permute-start | bytes 393224 | tf_op jit(solution)/shard_map/ppermute | solution.py:23
  222.6 10.3 %collective-permute-start.39 = (bf16[256,256]{1,0:T(8,128)(2,1)S(1)}, bf16[256,256]{1,0:T(8,128)(2,1)S(1)}, u32[]{:S(2)}, u32[]{:S(2)}) collective-permute-start(bf16[256,256]{1,0:T(8,128)(2,1)S(1)} %get-tuple-element.66), channel_id=1, source_target_pairs={{0,1},{1,0},{2,3},{3,2},{4,5},{5,4},{6,7},{7,6},{8,9},{9,8},{10,11... | collective-permute-start | bytes 393224 | tf_op jit(solution)/shard_map/ppermute | solution.py:23
  223.2 9.7 %collective-permute-start.40 = (bf16[256,256]{1,0:T(8,128)(2,1)S(1)}, bf16[256,256]{1,0:T(8,128)(2,1)S(1)}, u32[]{:S(2)}, u32[]{:S(2)}) collective-permute-start(bf16[256,256]{1,0:T(8,128)(2,1)S(1)} %get-tuple-element.67), channel_id=1, source_target_pairs={{0,2},{1,3},{2,0},{3,1},{4,6},{5,7},{6,4},{7,5},{8,10},{9,11},{10,... | collective-permute-start | bytes 393224 | tf_op jit(solution)/shard_map/ppermute | solution.py:23
  228.1 5.7 %collective-permute-start.38 = (bf16[256,256]{1,0:T(8,128)(2,1)S(1)}, bf16[256,256]{1,0:T(8,128)(2,1)S(1)}, u32[]{:S(2)}, u32[]{:S(2)}) collective-permute-start(bf16[256,256]{1,0:T(8,128)(2,1)S(1)} %get-tuple-element.65), channel_id=1, source_target_pairs={{0,2},{1,3},{2,0},{3,1},{4,6},{5,7},{6,4},{7,5},{8,10},{9,11},{10,... | collective-permute-start | bytes 393224 | tf_op jit(solution)/shard_map/ppermute | solution.py:23
